TPU v7x, 128 devices: a whole 4x4x4 slice. The times are simulated.
128 devices in a mesh: group: 8 (over y, core), within: 16 (over z, x).
Axes of the slice: x: 4, y: 4, z: 4, core: 2. Of those that a mesh axis runs over, the one named last changes fastest.
Arguments:
- tokens: bfloat16 [16384, 2048], P(('group', 'within')), may hold values from -6 to 6
- languages: int32 [16384], P(('group', 'within')), may hold values from 0 to 99, as said below
- lang_group: int32 [100], replicated, may hold values from 0 to 7, as said below
- group_gain: float32 [8, 2048], replicated, may hold values from 0.25 to 1.75
- group_w1: bfloat16 [8, 2048, 8192], P('group', None, 'within'), may hold values from -0.125 to 0.125
- group_b1: float32 [8, 8192], P('group', 'within'), may hold values from -3 to 3
- group_w2: bfloat16 [8, 8192, 2048], P('group', 'within'), may hold values from -0.0625 to 0.0625
- group_b2: float32 [8, 2048], replicated, may hold values from -3 to 3
- shared_gain: float32 [2048], replicated, may hold values from 0.25 to 1.75
- shared_w1: bfloat16 [2048, 8192], P(None, 'group'), may hold values from -0.125 to 0.125
- shared_b1: float32 [8192], P('group'), may hold values from -3 to 3
- shared_w2: bfloat16 [8192, 2048], P('group'), may hold values from -0.0625 to 0.0625
- shared_b2: float32 [2048], replicated, may hold values from -3 to 3
Outputs:
- encoded: bfloat16 [16384, 2048], P(('group', 'within'))
Inputs may be any that keep to these rules, and one draw needn't show every extreme that they name: `lang_group`: every language lies in one group and every group holds at least one language. Among the 128 tokens of one device (an aligned block), at most 24 have languages of one group, and in every block some group has exactly 24.
All inputs are finite; a program needn't handle non-finite values.
Results may differ from a plain program's by a relative error of at most 0.017.
Values may be sent and summed in bfloat16 or wider, within the bound.
No kernel may reach another device: no remote copies, remote signals or barrier semaphores. Data moves between devices by JAX's collectives and lax.ppermute only.
A program may use at most 128 MiB of HBM per device.

v0:
```python
import jax
import jax.numpy as jnp
from jax import lax
from jax.sharding import Mesh, PartitionSpec as P

X = ("xh", "xl")


def layer_norm(values, gains):
    centre = jnp.mean(values, axis=-1, keepdims=True)
    centred = values - centre
    spread = jnp.mean(centred * centred, axis=-1, keepdims=True)
    return centred * lax.rsqrt(spread + 1e-05) * gains


def shift(value, axis, step):
    size = lax.axis_size(axis)
    return lax.ppermute(value, axis, [(i, (i + step) % size) for i in range(size)])


def swap_column(value):
    return lax.ppermute(value, "xl", [(0, 1), (1, 0)])


def swap_blocks(value):
    return lax.ppermute(value, X, [(0, 3), (3, 0), (1, 2), (2, 1)])


def swap_core(value):
    return lax.ppermute(value, "core", [(0, 1), (1, 0)])


def up(value):
    return value.astype(jnp.float32)


def down(value):
    return value.astype(jnp.bfloat16)


def hold(*values):
    return lax.optimization_barrier(values)


def ring_scatter(own, prev, foll, far, axis, way):
    via = up(shift(far, axis, -way))
    if way == 1:
        prev = down(up(prev) + via)
    else:
        foll = down(up(foll) + via)
    return up(own) + up(shift(prev, axis, -1)) + up(shift(foll, axis, 1))


def on_device(
    tokens,
    languages,
    lang_group,
    group_gain,
    group_w1,
    group_b1,
    group_w2,
    group_b2,
    shared_gain,
    shared_w1,
    shared_b1,
    shared_w2,
    shared_b2,
):
    tok_dev = tokens.shape[0]
    width_model = tokens.shape[1]
    num_groups = group_gain.shape[0]
    num_langs = lang_group.shape[0]
    capacity = 3 * tok_dev // (2 * num_groups)
    bf16 = jnp.bfloat16

    half_model = width_model // 2
    b1_pair = swap_blocks(group_b1[0])
    w1_out, b1_pair = hold(group_w1[0], b1_pair)
    w1_pair = swap_blocks(w1_out)
    left, right = group_w2[0, :, :half_model], group_w2[0, :, half_model:]
    sw1_pair = swap_core(shared_w1)
    sb1_pair = swap_core(shared_b1)
    sw2_pair = swap_core(shared_w2)

    residual_in = tokens.astype(jnp.float32)
    lang_hit = (languages[:, None] == jnp.arange(num_langs, dtype=jnp.int32)[None, :]).astype(
        jnp.int32
    )
    group_of = jnp.sum(lang_hit * lang_group[None, :], axis=1)
    onehot = (group_of[:, None] == jnp.arange(num_groups, dtype=jnp.int32)[None, :]).astype(
        jnp.int32
    )
    earlier = jnp.cumsum(onehot, axis=0) - onehot
    slot_index = jnp.sum(earlier * onehot, axis=1)
    position = group_of * capacity + slot_index
    dispatch_map = (
        position[None, :] == jnp.arange(num_groups * capacity, dtype=jnp.int32)[:, None]
    ).astype(bf16)
    onehot_float = onehot.astype(jnp.float32)
    row_gains = jnp.dot(onehot_float, group_gain, precision=lax.Precision.HIGHEST)
    normed = layer_norm(residual_in, row_gains).astype(bf16)
    outgoing = jnp.dot(dispatch_map, normed, preferred_element_type=jnp.float32).astype(bf16)
    outgoing = outgoing.reshape(num_groups, capacity, width_model)
    slots = capacity // 2
    count = num_groups * slots

    def exchange(value):
        return lax.all_to_all(value, ("y", "core"), split_axis=0, concat_axis=0, tiled=True)

    arrived, sw1_pair, sw2_pair, sb1_pair = hold(exchange(outgoing), sw1_pair, sw2_pair, sb1_pair)
    a_own = arrived[:, :slots].reshape(count, width_model)
    b_own = arrived[:, slots:].reshape(count, width_model)
    a_prev, a_foll = shift(a_own, "z", 1), shift(a_own, "z", -1)
    a_far = shift(a_prev, "z", 1)
    b_pair = swap_column(b_own)
    a_near = jnp.concatenate([a_own, a_prev, a_foll], axis=0)
    a_near, b_pair = hold(a_near, b_pair)
    (b_own,) = hold(jnp.concatenate([b_own, b_pair], axis=0))
    b_prev, b_foll = shift(b_own, "z", 1), shift(b_own, "z", -1)
    b_far = shift(b_foll, "z", -1)
    near_pair = swap_column(a_near)
    far_own, w1_pair = hold(a_far, w1_pair)
    far_pair = swap_column(far_own)
    left_out, _ = hold(left, w1_pair)
    left_pair = swap_blocks(left_out)
    right_out, _ = hold(right, w1_pair, b_foll)[:2]
    right_pair = swap_blocks(right_out)
    w1 = jnp.concatenate([group_w1[0], w1_pair], axis=1)
    b1 = jnp.concatenate([group_b1[0], b1_pair])
    rows = jnp.concatenate([a_near, a_far, b_own, b_foll, b_prev, near_pair, far_pair, b_far], axis=0)
    rows, w1, left_pair = hold(rows, w1, left_pair)
    hidden = down(jax.nn.relu(jnp.dot(rows, w1, preferred_element_type=jnp.float32) + b1))

    def second(hidden, weight, weight_pair):
        weight = jnp.concatenate([weight, weight_pair], axis=0)
        return down(jnp.dot(hidden, weight, preferred_element_type=jnp.float32))

    def block(part, step):
        at = {"own": (0, 4, 10, 5), "prev": (1, 8, 11, 9), "foll": (2, 6, 12, 7), "far": (3, 14, 13, 15)}
        return jnp.concatenate([part[i * count : (i + 1) * count] for i in at[step]], axis=0)

    def sums(weight, weight_pair, hidden, after, way):
        part = second(hidden, weight, weight_pair)
        own, prev, foll = (block(part, step) for step in ("own", "prev", "foll"))
        via = shift(block(part, "far"), "z", -way)
        if way == 1:
            foll = shift(foll, "z", 1)
            via, foll, after = hold(via, foll, after)
            prev = down(up(prev) + up(via))
            hidden, prev = hold(hidden, prev)
            prev = shift(prev, "z", -1)
        else:
            prev = shift(prev, "z", -1)
            via, prev, after = hold(via, prev, after)
            foll = down(up(foll) + up(via))
            foll = shift(foll, "z", 1)
        summed = up(own) + up(prev) + up(foll)
        outer = down(summed[2 * count :])
        summed = summed[: 2 * count] + up(swap_column(outer))
        summed = down(summed).reshape(2, num_groups, slots, part.shape[1])
        return exchange(jnp.concatenate([summed[0], summed[1]], axis=1)), hidden, after, outer

    return_l, hidden, right_pair, outer = sums(left, left_pair, hidden, right_pair, 1)
    return_r, _, _, _ = sums(right, right_pair, hidden, outer, -1)
    returned = jnp.concatenate([return_l, return_r], axis=2)
    returned = returned.reshape(num_groups * capacity, width_model)
    group_out = lax.dot_general(
        dispatch_map, returned, (((0,), (0,)), ((), ())), preferred_element_type=jnp.float32
    )
    group_bias = jnp.dot(onehot_float, group_b2, precision=lax.Precision.HIGHEST)
    middle = residual_in + group_out + group_bias
    shared_in = layer_norm(middle, shared_gain).astype(bf16)

    def shared_forward(block):
        hidden = [
            down(jax.nn.relu(jnp.dot(block, w, preferred_element_type=jnp.float32) + b))
            for w, b in ((shared_w1, shared_b1), (sw1_pair, sb1_pair))
        ]
        hidden = hold(*hidden)
        return down(
            jnp.dot(hidden[0], shared_w2, preferred_element_type=jnp.float32)
            + jnp.dot(hidden[1], sw2_pair, preferred_element_type=jnp.float32)
        )

    def shared_gather(own, way):
        prev, foll = shift(own, "y", 1), shift(own, "y", -1)
        far = shift(prev if way == 1 else foll, "y", way)
        return jnp.concatenate([own, prev, foll, far], axis=0), (prev, foll)

    half_tok = tok_dev // 2
    first, near = shared_gather(shared_in[:half_tok], 1)
    second_in, near = hold(shared_in[half_tok:], near)
    other, _ = shared_gather(second_in, -1)
    first = ring_scatter(*jnp.split(shared_forward(first), 4), "y", 1)
    other = ring_scatter(*jnp.split(shared_forward(other), 4), "y", -1)
    shared_out = jnp.concatenate([first, other], axis=0)
    return (middle + shared_out + shared_b2).astype(bf16)


def solution(mesh):
    chips = Mesh(mesh.devices.reshape(4, 2, 4, 2, 2), ("y", "core", "z", "xh", "xl"))
    group = ("y", "core")
    within = ("z", "xh", "xl")
    both = group + within
    placed = (
        P(both, None),
        P(both),
        P(),
        P(),
        P(group, None, within),
        P(group, within),
        P(group, within, None),
        P(),
        P(),
        P(None, group),
        P(group),
        P(group, None),
        P(),
    )
    return jax.shard_map(
        on_device,
        mesh=chips,
        in_specs=placed,
        out_specs=P(both, None),
        check_vma=False,
    )
```

profile of v0, /device:TPU:0, one launch (start us, length us, event | category | flops | bytes accessed | tf_op | source)
XLA Modules:
  0.0 265.2 jit_solution(13234804261636507218)
XLA Ops:
  1.7 1.2 convert_reduce_fusion
  2.9 1.3 fusion.19
  4.3 2.2 fusion.2
  6.5 1.3 convolution_convert_fusion.2
  7.7 4.6 %all-to-all-start = ((bf16[8,24,2048]{2,1,0:T(8,128)(2,1)}), bf16[8,24,2048]{2,1,0:T(8,128)(2,1)S(1)}, u32[]{:S(2)}, u32[]{:S(2)}) async-start(bf16[8,24,2048]{2,1,0:T(8,128)(2,1)} %bitcast), calls=%async_computation | async-start | bytes 1572864 | tf_op jit(solution)/shard_map/all_to_all | solution.py:108
  12.3 2.8 %collective-permute-start.10 = (f32[512]{0:T(512)S(1)}, f32[512]{0:T(512)S(1)}, u32[]{:S(2)}, u32[]{:S(2)}) collective-permute-start(f32[512]{0:T(512)S(1)} %bitcast.33), channel_id=1, source_target_pairs={{0,3},{3,0},{1,2},{2,1},{4,7},{7,4},{5,6},{6,5},{8,11},{11,8},{9,1... | collective-permute-start | bytes 6152 | tf_op jit(solution)/shard_map/ppermute | solution.py:26
  15.1 2.0 collective-permute-done.10
  17.2 2.8 %collective-permute-start.11 = (bf16[2048,512]{1,0:T(8,128)(2,1)}, bf16[2048,512]{1,0:T(8,128)(2,1)}, u32[]{:S(2)}, u32[]{:S(2)}) collective-permute-start(bf16[2048,512]{1,0:T(8,128)(2,1)} %bitcast.31), channel_id=1, source_target_pairs={{0,3},{3,0},{1,2},{2,1},{4,7},{7,4},{5,6},{6,5},{8,11},{11,8},{9,1... | collective-permute-start | bytes 6291464 | tf_op jit(solution)/shard_map/ppermute | solution.py:26
  19.9 1.2 collective-permute-done.2
  21.1 4.3 %all-to-all-done = bf16[8,24,2048]{2,1,0:T(8,128)(2,1)S(1)} async-done(((bf16[8,24,2048]{2,1,0:T(8,128)(2,1)}), bf16[8,24,2048]{2,1,0:T(8,128)(2,1)S(1)}, u32[]{:S(2)}, u32[]{:S(2)}) %all-to-all-start) | async-done | bytes 786464 | tf_op jit(solution)/shard_map/all_to_all | solution.py:108
  26.4 1.1 reshape.61
  27.5 2.0 collective-permute-start.3
  29.5 2.2 collective-permute-start.4
  31.8 1.6 collective-permute-start.5
  33.6 7.0 %collective-permute-done.3 = bf16[96,2048]{1,0:T(8,128)(2,1)} collective-permute-done((bf16[96,2048]{1,0:T(8,128)(2,1)S(1)}, bf16[96,2048]{1,0:T(8,128)(2,1)}, u32[]{:S(2)}, u32[]{:S(2)}) %collective-permute-start.3) | collective-permute-done | bytes 393248 | tf_op jit(solution)/shard_map/ppermute | solution.py:18
  40.6 1.2 pad_maximum_fusion.1
  42.2 1.0 collective-permute-start.6
  43.3 2.3 collective-permute-start.7
  45.6 1.5 collective-permute-start.9
  47.2 18.3 %collective-permute-done.11 = bf16[2048,512]{1,0:T(8,128)(2,1)} collective-permute-done((bf16[2048,512]{1,0:T(8,128)(2,1)}, bf16[2048,512]{1,0:T(8,128)(2,1)}, u32[]{:S(2)}, u32[]{:S(2)}) %collective-permute-start.11) | collective-permute-done | bytes 2097184 | tf_op jit(solution)/shard_map/ppermute | solution.py:26
  65.6 2.8 %collective-permute-start.14 = (bf16[512,1024]{1,0:T(8,128)(2,1)S(1)}, bf16[512,1024]{1,0:T(8,128)(2,1)S(1)}, u32[]{:S(2)}, u32[]{:S(2)}) collective-permute-start(bf16[512,1024]{1,0:T(8,128)(2,1)S(1)} %get-tuple-element.38), channel_id=1, source_target_pairs={{0,3},{3,0},{1,2},{2,1},{4,7},{7,4},{5,6},{6,5},{8,11},{11,8},{9,1... | collective-permute-start | bytes 3145736 | tf_op jit(solution)/shard_map/ppermute | solution.py:26
  68.5 2.2 pad_maximum_fusion
  70.6 4.1 %collective-permute-start.13 = (bf16[192,2048]{1,0:T(8,128)(2,1)S(1)}, bf16[192,2048]{1,0:T(8,128)(2,1)S(1)}, u32[]{:S(2)}, u32[]{:S(2)}) collective-permute-start(bf16[192,2048]{1,0:T(8,128)(2,1)S(1)} %collective-permute-done.7), channel_id=1, source_target_pairs={{0,12},{4,0},{8,4},{12,8},{1,13},{5,1},{9,5},{13,9},{2,14},{6,2},{... | collective-permute-start | bytes 2359304 | tf_op jit(solution)/shard_map/ppermute | solution.py:18
  75.8 4.4 %collective-permute-done.12 = bf16[96,2048]{1,0:T(8,128)(2,1)S(1)} collective-permute-done((bf16[96,2048]{1,0:T(8,128)(2,1)S(1)}, bf16[96,2048]{1,0:T(8,128)(2,1)S(1)}, u32[]{:S(2)}, u32[]{:S(2)}) %collective-permute-start.12) | collective-permute-done | bytes 393248 | tf_op jit(solution)/shard_map/ppermute | solution.py:22
  80.2 9.7 %collective-permute-done.13 = bf16[192,2048]{1,0:T(8,128)(2,1)S(1)} collective-permute-done((bf16[192,2048]{1,0:T(8,128)(2,1)S(1)}, bf16[192,2048]{1,0:T(8,128)(2,1)S(1)}, u32[]{:S(2)}, u32[]{:S(2)}) %collective-permute-start.13) | collective-permute-done | bytes 786464 | tf_op jit(solution)/shard_map/ppermute | solution.py:18
  89.9 3.0 %collective-permute-done.14 = bf16[512,1024]{1,0:T(8,128)(2,1)S(1)} collective-permute-done((bf16[512,1024]{1,0:T(8,128)(2,1)S(1)}, bf16[512,1024]{1,0:T(8,128)(2,1)S(1)}, u32[]{:S(2)}, u32[]{:S(2)}) %collective-permute-start.14) | collective-permute-done | bytes 1048608 | tf_op jit(solution)/shard_map/ppermute | solution.py:26
  92.9 6.8 %maximum_convert_fusion = bf16[1536,1024]{1,0:T(8,128)(2,1)S(1)} fusion(bf16[1536,2048]{1,0:T(8,128)(2,1)S(1)} %constant_dynamic-update-slice_fusion, bf16[2048,1024]{1,0:T(8,128)(2,1)S(1)} %pad_maximum_fusion, f32[1024]{0:T(1024)S(1)} %pad_maximum_fusion.13), kind=kOutput, calls=%fused_computation | convolution fusion | flops 6447169536 | bytes 13635584 | tf_op jit(solution)/shard_map/dot_general | solution.py:132
  99.7 3.7 %convolution_convert_fusion.1 = bf16[1536,1024]{1,0:T(8,128)(2,1)S(1)} fusion(bf16[1536,1024]{1,0:T(8,128)(2,1)S(1)} %maximum_convert_fusion, bf16[512,1024]{1,0:T(8,128)(2,1)S(1)} %collective-permute-done.14, bf16[512,1024]{1,0:T(8,128)(2,1)S(1)} %get-tuple-element.38), kind=kOutput, calls=%fused_computation.3 | convolution fusion | flops 3226992640 | bytes 8388608 | tf_op jit(solution)/shard_map/dot_general | solution.py:136
  103.8 2.0 collective-permute-start.16
  105.9 2.2 collective-permute-start.15
  108.1 4.7 %collective-permute-done.17 = bf16[512,1024]{1,0:T(8,128)(2,1)S(1)} collective-permute-done((bf16[512,1024]{1,0:T(8,128)(2,1)S(1)}, bf16[512,1024]{1,0:T(8,128)(2,1)S(1)}, u32[]{:S(2)}, u32[]{:S(2)}) %collective-permute-start.17) | collective-permute-done | bytes 1048608 | tf_op jit(solution)/shard_map/ppermute | solution.py:26
  112.7 7.8 %collective-permute-done.16 = bf16[384,1024]{1,0:T(8,128)(2,1)S(1)} collective-permute-done((bf16[384,1024]{1,0:T(8,128)(2,1)S(1)}, bf16[384,1024]{1,0:T(8,128)(2,1)S(1)}, u32[]{:S(2)}, u32[]{:S(2)}) %collective-permute-start.16) | collective-permute-done | bytes 786464 | tf_op jit(solution)/shard_map/ppermute | solution.py:18
  120.5 2.0 collective-permute-done.15
  122.8 2.9 %collective-permute-start.18 = (bf16[384,1024]{1,0:T(8,128)(2,1)S(1)}, bf16[384,1024]{1,0:T(8,128)(2,1)S(1)}, u32[]{:S(2)}, u32[]{:S(2)}) collective-permute-start(bf16[384,1024]{1,0:T(8,128)(2,1)S(1)} %add_convert_fusion.1), channel_id=1, source_target_pairs={{0,12},{4,0},{8,4},{12,8},{1,13},{5,1},{9,5},{13,9},{2,14},{6,2},{... | collective-permute-start | bytes 2359304 | tf_op jit(solution)/shard_map/ppermute | solution.py:18
  125.8 3.6 %convolution_convert_fusion = bf16[1536,1024]{1,0:T(8,128)(2,1)S(1)} fusion(bf16[1536,1024]{1,0:T(8,128)(2,1)S(1)} %maximum_convert_fusion, bf16[512,1024]{1,0:T(8,128)(2,1)S(1)} %collective-permute-done.17, bf16[512,1024]{1,0:T(8,128)(2,1)S(1)} %get-tuple-element.43), kind=kOutput, calls=%fused_computation.2 | convolution fusion | flops 3226992640 | bytes 8388608 | tf_op jit(solution)/shard_map/dot_general | solution.py:136
  129.9 2.0 collective-permute-start.21
  132.1 11.9 %collective-permute-done.18 = bf16[384,1024]{1,0:T(8,128)(2,1)S(1)} collective-permute-done((bf16[384,1024]{1,0:T(8,128)(2,1)S(1)}, bf16[384,1024]{1,0:T(8,128)(2,1)S(1)}, u32[]{:S(2)}, u32[]{:S(2)}) %collective-permute-start.18) | collective-permute-done | bytes 786464 | tf_op jit(solution)/shard_map/ppermute | solution.py:18
  144.5 9.4 %collective-permute-done.21 = bf16[384,1024]{1,0:T(8,128)(2,1)S(1)} collective-permute-done((bf16[384,1024]{1,0:T(8,128)(2,1)S(1)}, bf16[384,1024]{1,0:T(8,128)(2,1)S(1)}, u32[]{:S(2)}, u32[]{:S(2)}) %collective-permute-start.21) | collective-permute-done | bytes 786464 | tf_op jit(solution)/shard_map/ppermute | solution.py:18
  154.2 1.8 collective-permute-start.22
  157.0 11.6 %collective-permute-done.22 = bf16[384,1024]{1,0:T(8,128)(2,1)S(1)} collective-permute-done((bf16[384,1024]{1,0:T(8,128)(2,1)S(1)}, bf16[384,1024]{1,0:T(8,128)(2,1)S(1)}, u32[]{:S(2)}, u32[]{:S(2)}) %collective-permute-start.22) | collective-permute-done | bytes 786464 | tf_op jit(solution)/shard_map/ppermute | solution.py:18
  169.0 1.0 collective-permute-start.23
  171.2 4.3 %all-to-all-start.1 = ((bf16[8,24,1024]{2,1,0:T(8,128)(2,1)}), bf16[8,24,1024]{2,1,0:T(8,128)(2,1)S(1)}, u32[]{:S(2)}, u32[]{:S(2)}) async-start(bf16[8,24,1024]{2,1,0:T(8,128)(2,1)} %pad_maximum_fusion.9), calls=%async_computation.1 | async-start | bytes 786432 | tf_op jit(solution)/shard_map/all_to_all | solution.py:108
  175.4 1.5 collective-permute-done.23
  177.2 7.1 %all-to-all-done.1 = bf16[8,24,1024]{2,1,0:T(8,128)(2,1)S(1)} async-done(((bf16[8,24,1024]{2,1,0:T(8,128)(2,1)}), bf16[8,24,1024]{2,1,0:T(8,128)(2,1)S(1)}, u32[]{:S(2)}, u32[]{:S(2)}) %all-to-all-start.1) | async-done | bytes 393248 | tf_op jit(solution)/shard_map/all_to_all | solution.py:108
  184.4 11.3 %all_to_all.15 = bf16[8,24,1024]{2,1,0:T(8,128)(2,1)S(1)} all-to-all(bf16[8,24,1024]{2,1,0:T(8,128)(2,1)S(1)} %pad_maximum_fusion.10), channel_id=1, replica_groups=mesh['y'=4,'core'=2,'z'=4,'xh'=2,'xl'=2] {'y','core'}, dimensions={0} | all-to-all | bytes 786432 | tf_op jit(solution)/shard_map/all_to_all | solution.py:108
  196.1 1.2 fusion.47
  198.5 2.7 %collective-permute-start.25 = (bf16[64,2048]{1,0:T(8,128)(2,1)S(1)}, bf16[64,2048]{1,0:T(8,128)(2,1)S(1)}, u32[]{:S(2)}, u32[]{:S(2)}) collective-permute-start(bf16[64,2048]{1,0:T(8,128)(2,1)S(1)} %get-tuple-element.99), channel_id=1, source_target_pairs={{0,96},{32,0},{64,32},{96,64},{1,97},{33,1},{65,33},{97,65},{2,98}... | collective-permute-start | bytes 786440 | tf_op jit(solution)/shard_map/ppermute | solution.py:18
  201.1 5.8 %collective-permute-done.24 = bf16[64,2048]{1,0:T(8,128)(2,1)S(1)} collective-permute-done((bf16[64,2048]{1,0:T(8,128)(2,1)S(1)}, bf16[64,2048]{1,0:T(8,128)(2,1)S(1)}, u32[]{:S(2)}, u32[]{:S(2)}) %collective-permute-start.24) | collective-permute-done | bytes 262176 | tf_op jit(solution)/shard_map/ppermute | solution.py:18
  207.0 3.3 %collective-permute-start.31 = (bf16[64,2048]{1,0:T(8,128)(2,1)S(1)}, bf16[64,2048]{1,0:T(8,128)(2,1)S(1)}, u32[]{:S(2)}, u32[]{:S(2)}) collective-permute-start(bf16[64,2048]{1,0:T(8,128)(2,1)S(1)} %get-tuple-element.56), channel_id=1, source_target_pairs={{0,96},{32,0},{64,32},{96,64},{1,97},{33,1},{65,33},{97,65},{2,98}... | collective-permute-start | bytes 786440 | tf_op jit(solution)/shard_map/ppermute | solution.py:18
  210.3 7.2 %collective-permute-done.26 = bf16[64,2048]{1,0:T(8,128)(2,1)S(1)} collective-permute-done((bf16[64,2048]{1,0:T(8,128)(2,1)S(1)}, bf16[64,2048]{1,0:T(8,128)(2,1)S(1)}, u32[]{:S(2)}, u32[]{:S(2)}) %collective-permute-start.26) | collective-permute-done | bytes 262176 | tf_op jit(solution)/shard_map/ppermute | solution.py:18
  217.4 1.3 fusion.13
  218.7 3.6 %fusion.14 = bf16[256,1024]{1,0:T(8,128)(2,1)S(1)} fusion(bf16[2048,1024]{1,0:T(8,128)(2,1)} %collective-permute-done, f32[1024]{0:T(1024)S(1)} %collective-permute-done.2, bf16[64,2048]{1,0:T(8,128)(2,1)S(1)} %collective-permute-done.26, bf16[64,2048]{1,0:T(8,128)(2,1)S(1)} %collective-permute-done.25, bf16[64,2048]{1,0:T(8,128)(2,1)S(1)} %collective-permute-done.24, ...), kind=kOutput, calls=%fused_computation.34 | convolution fusion | flops 1078722560 | bytes 5771264 | tf_op jit(solution)/shard_map/dot_general | solution.py:176
  222.3 1.3 fusion.48
  223.6 3.5 %fusion = bf16[256,2048]{1,0:T(8,128)(2,1)S(1)} fusion(f32[256,2048]{1,0:T(8,128)S(1)} %fusion.48, bf16[256,1024]{1,0:T(8,128)(2,1)S(1)} %fusion.14, bf16[1024,2048]{1,0:T(8,128)(2,1)} %collective-permute-done.1), kind=kOutput, calls=%fused_computation.6 | convolution fusion | flops 1074790400 | bytes 7864320 | tf_op jit(solution)/shard_map/dot_general | solution.py:182
  227.2 2.0 collective-permute-start.29
  229.3 1.3 collective-permute-start.32
  230.6 6.0 %collective-permute-done.32 = bf16[64,2048]{1,0:T(8,128)(2,1)S(1)} collective-permute-done((bf16[64,2048]{1,0:T(8,128)(2,1)S(1)}, bf16[64,2048]{1,0:T(8,128)(2,1)S(1)}, u32[]{:S(2)}, u32[]{:S(2)}) %collective-permute-start.32) | collective-permute-done | bytes 262176 | tf_op jit(solution)/shard_map/ppermute | solution.py:18
  236.6 3.5 %fusion.16 = bf16[256,1024]{1,0:T(8,128)(2,1)S(1)} fusion(bf16[256,2048]{1,0:T(8,128)(2,1)S(1)} %constant_dynamic-update-slice_fusion.8, bf16[2048,1024]{1,0:T(8,128)(2,1)} %collective-permute-done, f32[1024]{0:T(1024)S(1)} %collective-permute-done.2), kind=kOutput, calls=%fused_computation.36 | convolution fusion | flops 1074528256 | bytes 5771264 | tf_op jit(solution)/shard_map/dot_general | solution.py:176
  240.1 1.3 fusion.15
  241.3 1.3 fusion.49
  242.6 3.5 %fusion.1 = bf16[256,2048]{1,0:T(8,128)(2,1)S(1)} fusion(f32[256,2048]{1,0:T(8,128)S(1)} %fusion.49, bf16[256,1024]{1,0:T(8,128)(2,1)S(1)} %fusion.16, bf16[1024,2048]{1,0:T(8,128)(2,1)} %collective-permute-done.1), kind=kOutput, calls=%fused_computation.7 | convolution fusion | flops 1074790400 | bytes 7864320 | tf_op jit(solution)/shard_map/dot_general | solution.py:182
  246.3 3.3 %collective-permute-start.28 = (bf16[64,2048]{1,0:T(8,128)(2,1)S(1)}, bf16[64,2048]{1,0:T(8,128)(2,1)S(1)}, u32[]{:S(2)}, u32[]{:S(2)}) collective-permute-start(bf16[64,2048]{1,0:T(8,128)(2,1)S(1)} %add_convert_fusion.3), channel_id=1, source_target_pairs={{0,96},{32,0},{64,32},{96,64},{1,97},{33,1},{65,33},{97,65},{2,98}... | collective-permute-start | bytes 786440 | tf_op jit(solution)/shard_map/ppermute | solution.py:18
  250.0 6.5 %collective-permute-done.34 = bf16[64,2048]{1,0:T(8,128)(2,1)S(1)} collective-permute-done((bf16[64,2048]{1,0:T(8,128)(2,1)S(1)}, bf16[64,2048]{1,0:T(8,128)(2,1)S(1)}, u32[]{:S(2)}, u32[]{:S(2)}) %collective-permute-start.34) | collective-permute-done | bytes 262176 | tf_op jit(solution)/shard_map/ppermute | solution.py:18
  256.7 7.4 %collective-permute-done.35 = bf16[64,2048]{1,0:T(8,128)(2,1)S(1)} collective-permute-done((bf16[64,2048]{1,0:T(8,128)(2,1)S(1)}, bf16[64,2048]{1,0:T(8,128)(2,1)S(1)}, u32[]{:S(2)}, u32[]{:S(2)}) %collective-permute-start.35) | collective-permute-done | bytes 262176 | tf_op jit(solution)/shard_map/ppermute | solution.py:18
  (112 shorter events, 13.3 us)
Async XLA Ops:
  0.0 196.1 %copy-start = (f32[8,2048]{1,0:T(8,128)S(1)}, f32[8,2048]{1,0:T(8,128)}, u32[]{:S(2)}) copy-start(f32[8,2048]{1,0:T(8,128)} %param.20) | copy-start | bytes 196612
  0.0 25.4 %collective-permute-start = (bf16[2048,1024]{1,0:T(8,128)(2,1)}, bf16[2048,1024]{1,0:T(8,128)(2,1)}, u32[]{:S(2)}, u32[]{:S(2)}) collective-permute-start(bf16[2048,1024]{1,0:T(8,128)(2,1)} %param.22), channel_id=1, source_target_pairs={{0,16},{16,0},{1,17},{17,1},{2,18},{18,2},{3,19},{19,3},{4,20},{20... | collective-permute-start | bytes 12582920 | tf_op jit(solution)/shard_map/ppermute | solution.py:30
  0.0 25.4 %collective-permute-start.1 = (bf16[1024,2048]{1,0:T(8,128)(2,1)}, bf16[1024,2048]{1,0:T(8,128)(2,1)}, u32[]{:S(2)}, u32[]{:S(2)}) collective-permute-start(bf16[1024,2048]{1,0:T(8,128)(2,1)} %param.24), channel_id=1, source_target_pairs={{0,16},{16,0},{1,17},{17,1},{2,18},{18,2},{3,19},{19,3},{4,20},{20... | collective-permute-start | bytes 12582920 | tf_op jit(solution)/shard_map/ppermute | solution.py:30
  4.3 8.0 %copy-start.6 = (f32[1,512]{1,0:T(1,128)S(1)}, f32[1,512]{1,0:T(1,128)}, u32[]{:S(2)}) copy-start(f32[1,512]{1,0:T(1,128)} %param.18) | copy-start | bytes 6148
  4.3 15.7 %copy-start.9 = (f32[1024]{0:T(1024)S(1)}, f32[1024]{0:T(1024)}, u32[]{:S(2)}) copy-start(f32[1024]{0:T(1024)} %param.23) | copy-start | bytes 12292
  7.7 17.7 %all-to-all-start = ((bf16[8,24,2048]{2,1,0:T(8,128)(2,1)}), bf16[8,24,2048]{2,1,0:T(8,128)(2,1)S(1)}, u32[]{:S(2)}, u32[]{:S(2)}) async-start(bf16[8,24,2048]{2,1,0:T(8,128)(2,1)} %bitcast), calls=%async_computation | async-start | bytes 1572864 | tf_op jit(solution)/shard_map/all_to_all | solution.py:108
  12.3 21.1 %copy-start.2 = (bf16[1,512,2048]{2,1,0:T(8,128)(2,1)S(1)}, bf16[1,512,2048]{2,1,0:T(8,128)(2,1)}, u32[]{:S(2)}) copy-start(bf16[1,512,2048]{2,1,0:T(8,128)(2,1)} %param.19) | copy-start | bytes 6291460
  12.3 4.9 %collective-permute-start.10 = (f32[512]{0:T(512)S(1)}, f32[512]{0:T(512)S(1)}, u32[]{:S(2)}, u32[]{:S(2)}) collective-permute-start(f32[512]{0:T(512)S(1)} %bitcast.33), channel_id=1, source_target_pairs={{0,3},{3,0},{1,2},{2,1},{4,7},{7,4},{5,6},{6,5},{8,11},{11,8},{9,1... | collective-permute-start | bytes 6152 | tf_op jit(solution)/shard_map/ppermute | solution.py:26
  17.2 48.4 %collective-permute-start.11 = (bf16[2048,512]{1,0:T(8,128)(2,1)}, bf16[2048,512]{1,0:T(8,128)(2,1)}, u32[]{:S(2)}, u32[]{:S(2)}) collective-permute-start(bf16[2048,512]{1,0:T(8,128)(2,1)} %bitcast.31), channel_id=1, source_target_pairs={{0,3},{3,0},{1,2},{2,1},{4,7},{7,4},{5,6},{6,5},{8,11},{11,8},{9,1... | collective-permute-start | bytes 6291464 | tf_op jit(solution)/shard_map/ppermute | solution.py:26
  19.9 1.2 collective-permute-start.2
  27.5 13.1 %collective-permute-start.3 = (bf16[96,2048]{1,0:T(8,128)(2,1)S(1)}, bf16[96,2048]{1,0:T(8,128)(2,1)}, u32[]{:S(2)}, u32[]{:S(2)}) collective-permute-start(bf16[96,2048]{1,0:T(8,128)(2,1)S(1)} %reshape.61), channel_id=1, source_target_pairs={{0,4},{4,8},{8,12},{12,0},{1,5},{5,9},{9,13},{13,1},{2,6},{6,10},{... | collective-permute-start | bytes 1179656 | tf_op jit(solution)/shard_map/ppermute | solution.py:18
  29.5 11.1 %collective-permute-start.4 = (bf16[96,2048]{1,0:T(8,128)(2,1)S(1)}, bf16[96,2048]{1,0:T(8,128)(2,1)}, u32[]{:S(2)}, u32[]{:S(2)}) collective-permute-start(bf16[96,2048]{1,0:T(8,128)(2,1)S(1)} %reshape.61), channel_id=1, source_target_pairs={{0,12},{4,0},{8,4},{12,8},{1,13},{5,1},{9,5},{13,9},{2,14},{6,2},{... | collective-permute-start | bytes 1179656 | tf_op jit(solution)/shard_map/ppermute | solution.py:18
  31.8 10.5 %collective-permute-start.5 = (bf16[96,2048]{1,0:T(8,128)(2,1)S(1)}, bf16[96,2048]{1,0:T(8,128)(2,1)S(1)}, u32[]{:S(2)}, u32[]{:S(2)}) collective-permute-start(bf16[96,2048]{1,0:T(8,128)(2,1)S(1)} %reshape.62), channel_id=1, source_target_pairs={{0,1},{1,0},{2,3},{3,2},{4,5},{5,4},{6,7},{7,6},{8,9},{9,8},{10,11... | collective-permute-start | bytes 1179656 | tf_op jit(solution)/shard_map/ppermute | solution.py:22
  42.2 23.3 %collective-permute-start.6 = (bf16[96,2048]{1,0:T(8,128)(2,1)}, bf16[96,2048]{1,0:T(8,128)(2,1)S(1)}, u32[]{:S(2)}, u32[]{:S(2)}) collective-permute-start(bf16[96,2048]{1,0:T(8,128)(2,1)} %collective-permute-done.3), channel_id=1, source_target_pairs={{0,4},{4,8},{8,12},{12,0},{1,5},{5,9},{9,13},{13,1},{2,6},{6,10},{... | collective-permute-start | bytes 1179656 | tf_op jit(solution)/shard_map/ppermute | solution.py:18
  43.3 25.2 %copy-start.3 = (bf16[1,2048,512]{2,1,0:T(8,128)(2,1)S(1)}, bf16[1,2048,512]{2,1,0:T(8,128)(2,1)}, u32[]{:S(2)}) copy-start(bf16[1,2048,512]{2,1,0:T(8,128)(2,1)} %param.17) | copy-start | bytes 6291460
  43.3 27.3 %collective-permute-start.7 = (bf16[192,2048]{1,0:T(8,128)(2,1)S(1)}, bf16[192,2048]{1,0:T(8,128)(2,1)S(1)}, u32[]{:S(2)}, u32[]{:S(2)}) collective-permute-start(bf16[192,2048]{1,0:T(8,128)(2,1)S(1)} %pad_maximum_fusion.3), channel_id=1, source_target_pairs={{0,12},{4,0},{8,4},{12,8},{1,13},{5,1},{9,5},{13,9},{2,14},{6,2},{... | collective-permute-start | bytes 2359304 | tf_op jit(solution)/shard_map/ppermute | solution.py:18
  45.6 29.2 %collective-permute-start.8 = (bf16[192,2048]{1,0:T(8,128)(2,1)S(1)}, bf16[192,2048]{1,0:T(8,128)(2,1)S(1)}, u32[]{:S(2)}, u32[]{:S(2)}) collective-permute-start(bf16[192,2048]{1,0:T(8,128)(2,1)S(1)} %pad_maximum_fusion.3), channel_id=1, source_target_pairs={{0,4},{4,8},{8,12},{12,0},{1,5},{5,9},{9,13},{13,1},{2,6},{6,10},{... | collective-permute-start | bytes 2359304 | tf_op jit(solution)/shard_map/ppermute | solution.py:18
  45.6 30.0 %collective-permute-start.9 = (bf16[288,2048]{1,0:T(8,128)(2,1)S(1)}, bf16[288,2048]{1,0:T(8,128)(2,1)S(1)}, u32[]{:S(2)}, u32[]{:S(2)}) collective-permute-start(bf16[288,2048]{1,0:T(8,128)(2,1)S(1)} %pad_maximum_fusion.1), channel_id=1, source_target_pairs={{0,1},{1,0},{2,3},{3,2},{4,5},{5,4},{6,7},{7,6},{8,9},{9,8},{10,11... | collective-permute-start | bytes 3538952 | tf_op jit(solution)/shard_map/ppermute | solution.py:22
  65.6 14.5 %collective-permute-start.12 = (bf16[96,2048]{1,0:T(8,128)(2,1)S(1)}, bf16[96,2048]{1,0:T(8,128)(2,1)S(1)}, u32[]{:S(2)}, u32[]{:S(2)}) collective-permute-start(bf16[96,2048]{1,0:T(8,128)(2,1)S(1)} %collective-permute-done.6), channel_id=1, source_target_pairs={{0,1},{1,0},{2,3},{3,2},{4,5},{5,4},{6,7},{7,6},{8,9},{9,8},{10,11... | collective-permute-start | bytes 1179656 | tf_op jit(solution)/shard_map/ppermute | solution.py:22
  65.6 27.3 %collective-permute-start.14 = (bf16[512,1024]{1,0:T(8,128)(2,1)S(1)}, bf16[512,1024]{1,0:T(8,128)(2,1)S(1)}, u32[]{:S(2)}, u32[]{:S(2)}) collective-permute-start(bf16[512,1024]{1,0:T(8,128)(2,1)S(1)} %get-tuple-element.38), channel_id=1, source_target_pairs={{0,3},{3,0},{1,2},{2,1},{4,7},{7,4},{5,6},{6,5},{8,11},{11,8},{9,1... | collective-permute-start | bytes 3145736 | tf_op jit(solution)/shard_map/ppermute | solution.py:26
  70.6 19.2 %collective-permute-start.13 = (bf16[192,2048]{1,0:T(8,128)(2,1)S(1)}, bf16[192,2048]{1,0:T(8,128)(2,1)S(1)}, u32[]{:S(2)}, u32[]{:S(2)}) collective-permute-start(bf16[192,2048]{1,0:T(8,128)(2,1)S(1)} %collective-permute-done.7), channel_id=1, source_target_pairs={{0,12},{4,0},{8,4},{12,8},{1,13},{5,1},{9,5},{13,9},{2,14},{6,2},{... | collective-permute-start | bytes 2359304 | tf_op jit(solution)/shard_map/ppermute | solution.py:18
  74.8 37.9 %collective-permute-start.17 = (bf16[512,1024]{1,0:T(8,128)(2,1)S(1)}, bf16[512,1024]{1,0:T(8,128)(2,1)S(1)}, u32[]{:S(2)}, u32[]{:S(2)}) collective-permute-start(bf16[512,1024]{1,0:T(8,128)(2,1)S(1)} %get-tuple-element.43), channel_id=1, source_target_pairs={{0,3},{3,0},{1,2},{2,1},{4,7},{7,4},{5,6},{6,5},{8,11},{11,8},{9,1... | collective-permute-start | bytes 3145736 | tf_op jit(solution)/shard_map/ppermute | solution.py:26
  103.8 16.7 %collective-permute-start.16 = (bf16[384,1024]{1,0:T(8,128)(2,1)S(1)}, bf16[384,1024]{1,0:T(8,128)(2,1)S(1)}, u32[]{:S(2)}, u32[]{:S(2)}) collective-permute-start(bf16[384,1024]{1,0:T(8,128)(2,1)S(1)} %pad_maximum_fusion.5), channel_id=1, source_target_pairs={{0,4},{4,8},{8,12},{12,0},{1,5},{5,9},{9,13},{13,1},{2,6},{6,10},{... | collective-permute-start | bytes 2359304 | tf_op jit(solution)/shard_map/ppermute | solution.py:18
  105.9 16.7 %collective-permute-start.15 = (bf16[384,1024]{1,0:T(8,128)(2,1)S(1)}, bf16[384,1024]{1,0:T(8,128)(2,1)S(1)}, u32[]{:S(2)}, u32[]{:S(2)}) collective-permute-start(bf16[384,1024]{1,0:T(8,128)(2,1)S(1)} %pad_maximum_fusion.4), channel_id=1, source_target_pairs={{0,12},{4,0},{8,4},{12,8},{1,13},{5,1},{9,5},{13,9},{2,14},{6,2},{... | collective-permute-start | bytes 2359304 | tf_op jit(solution)/shard_map/ppermute | solution.py:18
  122.8 21.2 %collective-permute-start.18 = (bf16[384,1024]{1,0:T(8,128)(2,1)S(1)}, bf16[384,1024]{1,0:T(8,128)(2,1)S(1)}, u32[]{:S(2)}, u32[]{:S(2)}) collective-permute-start(bf16[384,1024]{1,0:T(8,128)(2,1)S(1)} %add_convert_fusion.1), channel_id=1, source_target_pairs={{0,12},{4,0},{8,4},{12,8},{1,13},{5,1},{9,5},{13,9},{2,14},{6,2},{... | collective-permute-start | bytes 2359304 | tf_op jit(solution)/shard_map/ppermute | solution.py:18
  129.9 24.0 %collective-permute-start.21 = (bf16[384,1024]{1,0:T(8,128)(2,1)S(1)}, bf16[384,1024]{1,0:T(8,128)(2,1)S(1)}, u32[]{:S(2)}, u32[]{:S(2)}) collective-permute-start(bf16[384,1024]{1,0:T(8,128)(2,1)S(1)} %pad_maximum_fusion.7), channel_id=1, source_target_pairs={{0,12},{4,0},{8,4},{12,8},{1,13},{5,1},{9,5},{13,9},{2,14},{6,2},{... | collective-permute-start | bytes 2359304 | tf_op jit(solution)/shard_map/ppermute | solution.py:18
  132.0 21.9 %collective-permute-start.20 = (bf16[384,1024]{1,0:T(8,128)(2,1)S(1)}, bf16[384,1024]{1,0:T(8,128)(2,1)S(1)}, u32[]{:S(2)}, u32[]{:S(2)}) collective-permute-start(bf16[384,1024]{1,0:T(8,128)(2,1)S(1)} %pad_maximum_fusion.6), channel_id=1, source_target_pairs={{0,4},{4,8},{8,12},{12,0},{1,5},{5,9},{9,13},{13,1},{2,6},{6,10},{... | collective-permute-start | bytes 2359304 | tf_op jit(solution)/shard_map/ppermute | solution.py:18
  154.2 14.3 %collective-permute-start.22 = (bf16[384,1024]{1,0:T(8,128)(2,1)S(1)}, bf16[384,1024]{1,0:T(8,128)(2,1)S(1)}, u32[]{:S(2)}, u32[]{:S(2)}) collective-permute-start(bf16[384,1024]{1,0:T(8,128)(2,1)S(1)} %add_convert_fusion), channel_id=1, source_target_pairs={{0,4},{4,8},{8,12},{12,0},{1,5},{5,9},{9,13},{13,1},{2,6},{6,10},{... | collective-permute-start | bytes 2359304 | tf_op jit(solution)/shard_map/ppermute | solution.py:18
  156.0 14.0 %collective-permute-start.19 = (bf16[192,1024]{1,0:T(8,128)(2,1)S(1)}, bf16[192,1024]{1,0:T(8,128)(2,1)S(1)}, u32[]{:S(2)}, u32[]{:S(2)}) collective-permute-start(bf16[192,1024]{1,0:T(8,128)(2,1)S(1)} %slice.243), channel_id=1, source_target_pairs={{0,1},{1,0},{2,3},{3,2},{4,5},{5,4},{6,7},{7,6},{8,9},{9,8},{10,11... | collective-permute-start | bytes 1179656 | tf_op jit(solution)/shard_map/ppermute | solution.py:22
  169.0 7.9 %collective-permute-start.23 = (bf16[192,1024]{1,0:T(8,128)(2,1)S(1)}, bf16[192,1024]{1,0:T(8,128)(2,1)S(1)}, u32[]{:S(2)}, u32[]{:S(2)}) collective-permute-start(bf16[192,1024]{1,0:T(8,128)(2,1)S(1)} %slice.242), channel_id=1, source_target_pairs={{0,1},{1,0},{2,3},{3,2},{4,5},{5,4},{6,7},{7,6},{8,9},{9,8},{10,11... | collective-permute-start | bytes 1179656 | tf_op jit(solution)/shard_map/ppermute | solution.py:22
  171.2 13.2 %all-to-all-start.1 = ((bf16[8,24,1024]{2,1,0:T(8,128)(2,1)}), bf16[8,24,1024]{2,1,0:T(8,128)(2,1)S(1)}, u32[]{:S(2)}, u32[]{:S(2)}) async-start(bf16[8,24,1024]{2,1,0:T(8,128)(2,1)} %pad_maximum_fusion.9), calls=%async_computation.1 | async-start | bytes 786432 | tf_op jit(solution)/shard_map/all_to_all | solution.py:108
  177.0 18.7 %copy-start.1 = (bf16[128,2048]{1,0:T(8,128)(2,1)S(1)}, bf16[128,2048]{1,0:T(8,128)(2,1)}, u32[]{:S(2)}) copy-start(bf16[128,2048]{1,0:T(8,128)(2,1)} %param.13) | copy-start | bytes 1572868
  196.1 1.5 copy-start.4
  197.3 20.1 %copy-start.7 = (bf16[2048,1024]{1,0:T(8,128)(2,1)S(1)}, bf16[2048,1024]{1,0:T(8,128)(2,1)}, u32[]{:S(2)}) copy-start(bf16[2048,1024]{1,0:T(8,128)(2,1)} %param.22) | copy-start | bytes 12582916
  197.8 9.1 %collective-permute-start.24 = (bf16[64,2048]{1,0:T(8,128)(2,1)S(1)}, bf16[64,2048]{1,0:T(8,128)(2,1)S(1)}, u32[]{:S(2)}, u32[]{:S(2)}) collective-permute-start(bf16[64,2048]{1,0:T(8,128)(2,1)S(1)} %get-tuple-element.99), channel_id=1, source_target_pairs={{0,32},{32,64},{64,96},{96,0},{1,33},{33,65},{65,97},{97,1},{2,34}... | collective-permute-start | bytes 786440 | tf_op jit(solution)/shard_map/ppermute | solution.py:18
  198.5 8.5 %collective-permute-start.25 = (bf16[64,2048]{1,0:T(8,128)(2,1)S(1)}, bf16[64,2048]{1,0:T(8,128)(2,1)S(1)}, u32[]{:S(2)}, u32[]{:S(2)}) collective-permute-start(bf16[64,2048]{1,0:T(8,128)(2,1)S(1)} %get-tuple-element.99), channel_id=1, source_target_pairs={{0,96},{32,0},{64,32},{96,64},{1,97},{33,1},{65,33},{97,65},{2,98}... | collective-permute-start | bytes 786440 | tf_op jit(solution)/shard_map/ppermute | solution.py:18
  207.0 10.5 %collective-permute-start.26 = (bf16[64,2048]{1,0:T(8,128)(2,1)S(1)}, bf16[64,2048]{1,0:T(8,128)(2,1)S(1)}, u32[]{:S(2)}, u32[]{:S(2)}) collective-permute-start(bf16[64,2048]{1,0:T(8,128)(2,1)S(1)} %collective-permute-done.24), channel_id=1, source_target_pairs={{0,32},{32,64},{64,96},{96,0},{1,33},{33,65},{65,97},{97,1},{2,34}... | collective-permute-start | bytes 786440 | tf_op jit(solution)/shard_map/ppermute | solution.py:18
  207.0 23.6 %collective-permute-start.30 = (bf16[64,2048]{1,0:T(8,128)(2,1)S(1)}, bf16[64,2048]{1,0:T(8,128)(2,1)S(1)}, u32[]{:S(2)}, u32[]{:S(2)}) collective-permute-start(bf16[64,2048]{1,0:T(8,128)(2,1)S(1)} %get-tuple-element.56), channel_id=1, source_target_pairs={{0,32},{32,64},{64,96},{96,0},{1,33},{33,65},{65,97},{97,1},{2,34}... | collective-permute-start | bytes 786440 | tf_op jit(solution)/shard_map/ppermute | solution.py:18
  207.0 22.3 %collective-permute-start.31 = (bf16[64,2048]{1,0:T(8,128)(2,1)S(1)}, bf16[64,2048]{1,0:T(8,128)(2,1)S(1)}, u32[]{:S(2)}, u32[]{:S(2)}) collective-permute-start(bf16[64,2048]{1,0:T(8,128)(2,1)S(1)} %get-tuple-element.56), channel_id=1, source_target_pairs={{0,96},{32,0},{64,32},{96,64},{1,97},{33,1},{65,33},{97,65},{2,98}... | collective-permute-start | bytes 786440 | tf_op jit(solution)/shard_map/ppermute | solution.py:18
  218.7 3.6 %copy-start.8 = (bf16[1024,2048]{1,0:T(8,128)(2,1)S(1)}, bf16[1024,2048]{1,0:T(8,128)(2,1)}, u32[]{:S(2)}) copy-start(bf16[1024,2048]{1,0:T(8,128)(2,1)} %param.24) | copy-start | bytes 12582916
  227.2 19.1 %collective-permute-start.27 = (bf16[64,2048]{1,0:T(8,128)(2,1)S(1)}, bf16[64,2048]{1,0:T(8,128)(2,1)S(1)}, u32[]{:S(2)}, u32[]{:S(2)}) collective-permute-start(bf16[64,2048]{1,0:T(8,128)(2,1)S(1)} %get-tuple-element.93), channel_id=1, source_target_pairs={{0,96},{32,0},{64,32},{96,64},{1,97},{33,1},{65,33},{97,65},{2,98}... | collective-permute-start | bytes 786440 | tf_op jit(solution)/shard_map/ppermute | solution.py:18
  227.2 29.3 %collective-permute-start.29 = (bf16[64,2048]{1,0:T(8,128)(2,1)S(1)}, bf16[64,2048]{1,0:T(8,128)(2,1)S(1)}, u32[]{:S(2)}, u32[]{:S(2)}) collective-permute-start(bf16[64,2048]{1,0:T(8,128)(2,1)S(1)} %get-tuple-element.94), channel_id=1, source_target_pairs={{0,32},{32,64},{64,96},{96,0},{1,33},{33,65},{65,97},{97,1},{2,34}... | collective-permute-start | bytes 786440 | tf_op jit(solution)/shard_map/ppermute | solution.py:18
  229.3 7.3 %collective-permute-start.32 = (bf16[64,2048]{1,0:T(8,128)(2,1)S(1)}, bf16[64,2048]{1,0:T(8,128)(2,1)S(1)}, u32[]{:S(2)}, u32[]{:S(2)}) collective-permute-start(bf16[64,2048]{1,0:T(8,128)(2,1)S(1)} %collective-permute-done.31), channel_id=1, source_target_pairs={{0,96},{32,0},{64,32},{96,64},{1,97},{33,1},{65,33},{97,65},{2,98}... | collective-permute-start | bytes 786440 | tf_op jit(solution)/shard_map/ppermute | solution.py:18
  246.2 18.1 %copy-start.5 = (f32[2048]{0:T(1024)S(1)}, f32[2048]{0:T(1024)}, u32[]{:S(2)}) copy-start(f32[2048]{0:T(1024)} %param.25) | copy-start | bytes 24580
  246.2 10.2 %collective-permute-start.34 = (bf16[64,2048]{1,0:T(8,128)(2,1)S(1)}, bf16[64,2048]{1,0:T(8,128)(2,1)S(1)}, u32[]{:S(2)}, u32[]{:S(2)}) collective-permute-start(bf16[64,2048]{1,0:T(8,128)(2,1)S(1)} %get-tuple-element.96), channel_id=1, source_target_pairs={{0,32},{32,64},{64,96},{96,0},{1,33},{33,65},{65,97},{97,1},{2,34}... | collective-permute-start | bytes 786440 | tf_op jit(solution)/shard_map/ppermute | solution.py:18
  246.3 10.2 %collective-permute-start.28 = (bf16[64,2048]{1,0:T(8,128)(2,1)S(1)}, bf16[64,2048]{1,0:T(8,128)(2,1)S(1)}, u32[]{:S(2)}, u32[]{:S(2)}) collective-permute-start(bf16[64,2048]{1,0:T(8,128)(2,1)S(1)} %add_convert_fusion.3), channel_id=1, source_target_pairs={{0,96},{32,0},{64,32},{96,64},{1,97},{33,1},{65,33},{97,65},{2,98}... | collective-permute-start | bytes 786440 | tf_op jit(solution)/shard_map/ppermute | solution.py:18
  249.6 7.1 %collective-permute-start.33 = (bf16[64,2048]{1,0:T(8,128)(2,1)S(1)}, bf16[64,2048]{1,0:T(8,128)(2,1)S(1)}, u32[]{:S(2)}, u32[]{:S(2)}) collective-permute-start(bf16[64,2048]{1,0:T(8,128)(2,1)S(1)} %get-tuple-element.95), channel_id=1, source_target_pairs={{0,96},{32,0},{64,32},{96,64},{1,97},{33,1},{65,33},{97,65},{2,98}... | collective-permute-start | bytes 786440 | tf_op jit(solution)/shard_map/ppermute | solution.py:18
  256.5 7.7 %collective-permute-start.35 = (bf16[64,2048]{1,0:T(8,128)(2,1)S(1)}, bf16[64,2048]{1,0:T(8,128)(2,1)S(1)}, u32[]{:S(2)}, u32[]{:S(2)}) collective-permute-start(bf16[64,2048]{1,0:T(8,128)(2,1)S(1)} %add_convert_fusion.2), channel_id=1, source_target_pairs={{0,32},{32,64},{64,96},{96,0},{1,33},{33,65},{65,97},{97,1},{2,34}... | collective-permute-start | bytes 786440 | tf_op jit(solution)/shard_map/ppermute | solution.py:18
where the time goes:
time: 266 us; the launch traced here: 265 us
  waiting for transfers between devices  139 us (52%)
  starting transfers between devices  59.9 us (23%)
  matrix products  38.2 us (14%)
  other arithmetic  11.8 us (4%)
  blocking collectives  11.3 us (4%)
  local copies, waits for them, and re-layouts  4.23 us (2%)
    ppermute x24, waiting for transfers between devices, shift(): lax.ppermute(value, axis, [(i, (i + step) % size) for i in range(size)])  92.3 us
    ppermute x24, starting transfers between devices, shift(): lax.ppermute(value, axis, [(i, (i + step) % size) for i in range(size)])  36.4 us
    ppermute x4, waiting for transfers between devices, swap_blocks(): return lax.ppermute(value, X, [(0, 3), (3, 0), (1, 2), (2, 1)])  28 us
    all_to_all x2, waiting for transfers between devices, exchange(): lax.all_to_all(value, ('y', 'core'), split_axis=0, concat_axis=0, tiled=T...  11.5 us
    all_to_all x1, blocking collectives, exchange(): lax.all_to_all(value, ('y', 'core'), split_axis=0, concat_axis=0, tiled=T...  11.3 us
    dot_general x4, matrix products, shared_forward(): jnp.dot(block, w, preferred_element_type=jnp.float32) + b  9.6 us
    ppermute x4, starting transfers between devices, swap_blocks(): return lax.ppermute(value, X, [(0, 3), (3, 0), (1, 2), (2, 1)])  9.07 us
    all_to_all x2, starting transfers between devices, exchange(): lax.all_to_all(value, ('y', 'core'), split_axis=0, concat_axis=0, tiled=T...  8.81 us
  transfers between devices with their start and end apart: 38, of which 22 were waited for; matrix products, arithmetic and copies ran while one was open for 19% of the time, Pallas kernels for 0%

commit v1 on v0

--- a/solution.py
+++ b/solution.py
@@ -49,6 +49,13 @@
     else:
         foll = down(up(foll) + via)
     return up(own) + up(shift(prev, axis, -1)) + up(shift(foll, axis, 1))
+
+
+def pick(index, table):
+    rows = jnp.broadcast_to(table[0], (index.shape[0], table.shape[1]))
+    for i in range(1, table.shape[0]):
+        rows = jnp.where((index == i)[:, None], table[i], rows)
+    return rows
 
 
 def on_device(
@@ -74,13 +81,13 @@
     bf16 = jnp.bfloat16
 
     half_model = width_model // 2
-    b1_pair = swap_blocks(group_b1[0])
-    w1_out, b1_pair = hold(group_w1[0], b1_pair)
-    w1_pair = swap_blocks(w1_out)
     left, right = group_w2[0, :, :half_model], group_w2[0, :, half_model:]
-    sw1_pair = swap_core(shared_w1)
-    sb1_pair = swap_core(shared_b1)
-    sw2_pair = swap_core(shared_w2)
+    rest, parts = group_b1[0], []
+    for _ in range(3):
+        parts.append(lax.reduce_precision(rest, 8, 7))
+        rest = rest - parts[-1]
+    parts = down(jnp.stack(parts + [jnp.zeros_like(rest)] * 5))
+    w1_pair = swap_blocks(jnp.concatenate([group_w1[0], parts], axis=0))
 
     residual_in = tokens.astype(jnp.float32)
     lang_hit = (languages[:, None] == jnp.arange(num_langs, dtype=jnp.int32)[None, :]).astype(
@@ -96,20 +103,20 @@
     dispatch_map = (
         position[None, :] == jnp.arange(num_groups * capacity, dtype=jnp.int32)[:, None]
     ).astype(bf16)
-    onehot_float = onehot.astype(jnp.float32)
-    row_gains = jnp.dot(onehot_float, group_gain, precision=lax.Precision.HIGHEST)
+    row_gains = pick(group_of, group_gain)
     normed = layer_norm(residual_in, row_gains).astype(bf16)
     outgoing = jnp.dot(dispatch_map, normed, preferred_element_type=jnp.float32).astype(bf16)
-    outgoing = outgoing.reshape(num_groups, capacity, width_model)
-    slots = capacity // 2
-    count = num_groups * slots
+    count = num_groups * capacity // 2
 
     def exchange(value):
-        return lax.all_to_all(value, ("y", "core"), split_axis=0, concat_axis=0, tiled=True)
-
-    arrived, sw1_pair, sw2_pair, sb1_pair = hold(exchange(outgoing), sw1_pair, sw2_pair, sb1_pair)
-    a_own = arrived[:, :slots].reshape(count, width_model)
-    b_own = arrived[:, slots:].reshape(count, width_model)
+        value = value.reshape(num_groups, capacity, value.shape[-1])
+        value = lax.all_to_all(value, ("y", "core"), split_axis=0, concat_axis=0, tiled=True)
+        return value.reshape(2 * count, value.shape[-1])
+
+    arrived, sw1_pair, sw2_pair, sb1_pair = hold(
+        exchange(outgoing), swap_core(shared_w1), swap_core(shared_w2), swap_core(shared_b1)
+    )
+    a_own, b_own = arrived[:count], arrived[count:]
     a_prev, a_foll = shift(a_own, "z", 1), shift(a_own, "z", -1)
     a_far = shift(a_prev, "z", 1)
     b_pair = swap_column(b_own)
@@ -117,18 +124,18 @@
     a_near, b_pair = hold(a_near, b_pair)
     (b_own,) = hold(jnp.concatenate([b_own, b_pair], axis=0))
     b_prev, b_foll = shift(b_own, "z", 1), shift(b_own, "z", -1)
+    b_foll, w1_pair = hold(b_foll, w1_pair)
     b_far = shift(b_foll, "z", -1)
     near_pair = swap_column(a_near)
-    far_own, w1_pair = hold(a_far, w1_pair)
-    far_pair = swap_column(far_own)
-    left_out, _ = hold(left, w1_pair)
+    far_pair = swap_column(a_far)
+    left_out, _ = hold(left, a_far)
     left_pair = swap_blocks(left_out)
-    right_out, _ = hold(right, w1_pair, b_foll)[:2]
+    right_out, _, _ = hold(right, w1_pair, b_prev)
     right_pair = swap_blocks(right_out)
-    w1 = jnp.concatenate([group_w1[0], w1_pair], axis=1)
+    b1_pair = jnp.sum(up(w1_pair[width_model:]), axis=0)
+    w1 = jnp.concatenate([group_w1[0], w1_pair[:width_model]], axis=1)
     b1 = jnp.concatenate([group_b1[0], b1_pair])
     rows = jnp.concatenate([a_near, a_far, b_own, b_foll, b_prev, near_pair, far_pair, b_far], axis=0)
-    rows, w1, left_pair = hold(rows, w1, left_pair)
     hidden = down(jax.nn.relu(jnp.dot(rows, w1, preferred_element_type=jnp.float32) + b1))
 
     def second(hidden, weight, weight_pair):
@@ -139,7 +146,7 @@
         at = {"own": (0, 4, 10, 5), "prev": (1, 8, 11, 9), "foll": (2, 6, 12, 7), "far": (3, 14, 13, 15)}
         return jnp.concatenate([part[i * count : (i + 1) * count] for i in at[step]], axis=0)
 
-    def sums(weight, weight_pair, hidden, after, way):
+    def ring(weight, weight_pair, hidden, way, after):
         part = second(hidden, weight, weight_pair)
         own, prev, foll = (block(part, step) for step in ("own", "prev", "foll"))
         via = shift(block(part, "far"), "z", -way)
@@ -151,23 +158,25 @@
             prev = shift(prev, "z", -1)
         else:
             prev = shift(prev, "z", -1)
-            via, prev, after = hold(via, prev, after)
-            foll = down(up(foll) + up(via))
-            foll = shift(foll, "z", 1)
-        summed = up(own) + up(prev) + up(foll)
-        outer = down(summed[2 * count :])
-        summed = summed[: 2 * count] + up(swap_column(outer))
-        summed = down(summed).reshape(2, num_groups, slots, part.shape[1])
-        return exchange(jnp.concatenate([summed[0], summed[1]], axis=1)), hidden, after, outer
-
-    return_l, hidden, right_pair, outer = sums(left, left_pair, hidden, right_pair, 1)
-    return_r, _, _, _ = sums(right, right_pair, hidden, outer, -1)
-    returned = jnp.concatenate([return_l, return_r], axis=2)
-    returned = returned.reshape(num_groups * capacity, width_model)
+            via, after = hold(via, after)
+            foll = shift(down(up(foll) + up(via)), "z", 1)
+        return up(own) + up(prev) + up(foll), hidden, after
+
+    def finish(summed, back):
+        return exchange(down(summed[: 2 * count] + up(back)))
+
+    sum_l, hidden, right_pair = ring(left, left_pair, hidden, 1, right_pair)
+    out_l = down(sum_l[2 * count :])
+    back_l = swap_column(out_l)
+    sum_r, _, back_l = ring(right, right_pair, hidden, -1, back_l)
+    return_l = finish(sum_l, back_l)
+    back_r = swap_column(down(sum_r[2 * count :]))
+    return_r = finish(sum_r, back_r)
+    returned = jnp.concatenate([return_l, return_r], axis=1)
     group_out = lax.dot_general(
         dispatch_map, returned, (((0,), (0,)), ((), ())), preferred_element_type=jnp.float32
     )
-    group_bias = jnp.dot(onehot_float, group_b2, precision=lax.Precision.HIGHEST)
+    group_bias = pick(group_of, group_b2)
     middle = residual_in + group_out + group_bias
     shared_in = layer_norm(middle, shared_gain).astype(bf16)
 
@@ -182,15 +191,17 @@
             + jnp.dot(hidden[1], sw2_pair, preferred_element_type=jnp.float32)
         )
 
-    def shared_gather(own, way):
-        prev, foll = shift(own, "y", 1), shift(own, "y", -1)
-        far = shift(prev if way == 1 else foll, "y", way)
-        return jnp.concatenate([own, prev, foll, far], axis=0), (prev, foll)
-
     half_tok = tok_dev // 2
-    first, near = shared_gather(shared_in[:half_tok], 1)
-    second_in, near = hold(shared_in[half_tok:], near)
-    other, _ = shared_gather(second_in, -1)
+    one, two = shared_in[:half_tok], shared_in[half_tok:]
+    prev, foll = shift(one, "y", 1), shift(one, "y", -1)
+    far = shift(prev, "y", 1)
+    first = jnp.concatenate([one, prev, foll, far], axis=0)
+    held, _, _ = hold(two, prev, foll)
+    foll = shift(held, "y", -1)
+    held, _ = hold(two, far)
+    prev = shift(held, "y", 1)
+    far = shift(foll, "y", -1)
+    other = jnp.concatenate([two, prev, foll, far], axis=0)
     first = ring_scatter(*jnp.split(shared_forward(first), 4), "y", 1)
     other = ring_scatter(*jnp.split(shared_forward(other), 4), "y", -1)
     shared_out = jnp.concatenate([first, other], axis=0)

time: 266 us -> 261 us (0.981)
  blocking collectives: 11.3 us -> 0 us
  starting transfers between devices: 59.9 us -> 70.5 us
  waiting for transfers between devices: 139 us -> 130 us
  local copies, waits for them, and re-layouts: 4.23 us -> 12.3 us
    ppermute x4 -> x3, waiting for transfers between devices: 28 us -> 10.6 us  [swap_blocks(): return lax.ppermute(value, X, [(0, 3), (3, 0), (1, 2), (2, 1)])]
    all_to_all x1 -> x0, blocking collectives: 11.3 us -> none  [exchange(): lax.all_to_all(value, ('y', 'core'), split_axis=0, concat_axis=0, tiled=T...]
    all_to_all x2 -> x3, waiting for transfers between devices: 11.5 us -> 19.1 us  [exchange(): lax.all_to_all(value, ('y', 'core'), split_axis=0, concat_axis=0, tiled=T...]
    concatenate x1, local copies, waits for them, and re-layouts: 0.02 us -> 7.54 us  [on_device(): w1_pair = swap_blocks(jnp.concatenate([group_w1[0], parts], axis=0))]
    all_to_all x2 -> x3, starting transfers between devices: 8.81 us -> 14.6 us  [exchange(): lax.all_to_all(value, ('y', 'core'), split_axis=0, concat_axis=0, tiled=T...]
    ppermute x24, waiting for transfers between devices: 92.3 us -> 96.8 us  [shift(): lax.ppermute(value, axis, [(i, (i + step) % size) for i in range(size)])]
    dot_general x2 -> x0, matrix products: 3.32 us -> none  [the longest x1 2.16 us: on_device(): jnp.dot(onehot_float, group_gain, precision=lax.Precision.HIGHEST)]
    concatenate x4 -> x0, other arithmetic: 3.16 us -> none  [the longest x1 2.16 us: on_device(): w1 = jnp.concatenate([group_w1[0], w1_pair], axis=1)]
  transfers between devices with their start and end apart: 38 -> 38, of which waited for: 22 -> 20; matrix products, arithmetic and copies ran while one was open for 19% -> 22% of each run, Pallas kernels for 0% -> 0%
where the time goes in v1:
time: 261 us; the launch traced here: 260 us
  waiting for transfers between devices  130 us (50%)
  starting transfers between devices  70.5 us (27%)
  matrix products  37.5 us (14%)
  local copies, waits for them, and re-layouts  12.3 us (5%)
  other arithmetic  9.8 us (4%)
    ppermute x24, waiting for transfers between devices, shift(): lax.ppermute(value, axis, [(i, (i + step) % size) for i in range(size)])  96.8 us
    ppermute x24, starting transfers between devices, shift(): lax.ppermute(value, axis, [(i, (i + step) % size) for i in range(size)])  38.8 us
    all_to_all x3, waiting for transfers between devices, exchange(): lax.all_to_all(value, ('y', 'core'), split_axis=0, concat_axis=0, tiled=T...  19.1 us
    all_to_all x3, starting transfers between devices, exchange(): lax.all_to_all(value, ('y', 'core'), split_axis=0, concat_axis=0, tiled=T...  14.6 us
    ppermute x3, waiting for transfers between devices, swap_blocks(): return lax.ppermute(value, X, [(0, 3), (3, 0), (1, 2), (2, 1)])  10.6 us
    dot_general x4, matrix products, shared_forward(): jnp.dot(block, w, preferred_element_type=jnp.float32) + b  9.6 us
    ppermute x3, starting transfers between devices, swap_blocks(): return lax.ppermute(value, X, [(0, 3), (3, 0), (1, 2), (2, 1)])  8.34 us
    ppermute x5, starting transfers between devices, swap_column(): return lax.ppermute(value, 'xl', [(0, 1), (1, 0)])  7.76 us
  transfers between devices with their start and end apart: 38, of which 20 were waited for; matrix products, arithmetic and copies ran while one was open for 22% of the time, Pallas kernels for 0%

profile of v1, /device:TPU:0, one launch (start us, length us, event | category | flops | bytes accessed | tf_op | source)
XLA Modules:
  0.0 260.3 jit_solution(15841444557310524240)
XLA Ops:
  1.7 1.2 convert_reduce_fusion
  2.9 1.3 fusion.22
  4.3 1.3 fusion.70
  5.6 2.8 %convolution_convert_fusion.2 = bf16[192,2048]{1,0:T(8,128)(2,1)} fusion(bf16[128,2048]{1,0:T(8,128)(2,1)} %param.13, f32[2048]{0:T(1024)S(1)} %bitcast.62, f32[2048]{0:T(1024)S(1)} %bitcast.63, f32[2048]{0:T(1024)S(1)} %bitcast.57, f32[2048]{0:T(1024)S(1)} %bitcast.58, f32[2048]{0:T(1024)S(1)} %bitcast.59, f32[2048]{0:T(1024)S(1)} %bitcast.60, ...), kind=kOutput, calls=%fused_computation.10 | convolution fusion | flops 104226816 | bytes 1378688 | tf_op jit(solution)/shard_map/dot_general | solution.py:108
  8.4 4.6 %all-to-all-start = ((bf16[8,24,2048]{2,1,0:T(8,128)(2,1)}), bf16[8,24,2048]{2,1,0:T(8,128)(2,1)S(1)}, u32[]{:S(2)}, u32[]{:S(2)}) async-start(bf16[8,24,2048]{2,1,0:T(8,128)(2,1)} %bitcast.8), calls=%async_computation | async-start | bytes 1572864 | tf_op jit(solution)/shard_map/all_to_all | solution.py:113
  13.5 7.5 %concatenate.63 = bf16[2056,512]{1,0:T(8,128)(2,1)S(1)} concatenate(bf16[2048,512]{1,0:T(8,128)(2,1)} %bitcast.44, bf16[1,512]{1,0:T(2,128)(2,1)S(1)} %get-tuple-element.110, bf16[1,512]{1,0:T(2,128)(2,1)S(1)} %get-tuple-element.111, bf16[1,512]{1,0:T(2,128)(2,1)S(1)} %get-tuple-element.109, bf16[1,512]{1,0:T(2,128)(2,1)S(1)} %stack_broadcast_in_dim.3, bf16[4,512]{1,0:T(4,128)(2,1)S(1)} %stack.3), dimensions={0} | concatenate | bytes 4210688 | tf_op jit(solution)/shard_map/concatenate | solution.py:90
  21.1 2.8 %collective-permute-start.8 = (bf16[2056,512]{1,0:T(8,128)(2,1)S(1)}, bf16[2056,512]{1,0:T(8,128)(2,1)}, u32[]{:S(2)}, u32[]{:S(2)}) collective-permute-start(bf16[2056,512]{1,0:T(8,128)(2,1)S(1)} %concatenate.63), channel_id=1, source_target_pairs={{0,3},{3,0},{1,2},{2,1},{4,7},{7,4},{5,6},{6,5},{8,11},{11,8},{9,1... | collective-permute-start | bytes 6316040 | tf_op jit(solution)/shard_map/ppermute | solution.py:26
  23.9 2.2 all-to-all-done
  26.2 2.0 collective-permute-start.3
  28.2 2.2 collective-permute-start.4
  30.4 1.5 collective-permute-start.5
  31.9 7.3 %collective-permute-done.3 = bf16[96,2048]{1,0:T(8,128)(2,1)S(1)} collective-permute-done((bf16[96,2048]{1,0:T(8,128)(2,1)S(1)}, bf16[96,2048]{1,0:T(8,128)(2,1)S(1)}, u32[]{:S(2)}, u32[]{:S(2)}) %collective-permute-start.3) | collective-permute-done | bytes 393248 | tf_op jit(solution)/shard_map/ppermute | solution.py:18
  39.3 1.4 collective-permute-done.5
  40.8 1.7 collective-permute-start.7
  43.2 1.6 collective-permute-start.10
  44.8 25.3 %collective-permute-done.6 = bf16[96,2048]{1,0:T(8,128)(2,1)S(1)} collective-permute-done((bf16[96,2048]{1,0:T(8,128)(2,1)S(1)}, bf16[96,2048]{1,0:T(8,128)(2,1)S(1)}, u32[]{:S(2)}, u32[]{:S(2)}) %collective-permute-start.6) | collective-permute-done | bytes 393248 | tf_op jit(solution)/shard_map/ppermute | solution.py:18
  70.2 2.8 %collective-permute-start.13 = (bf16[512,1024]{1,0:T(8,128)(2,1)S(1)}, bf16[512,1024]{1,0:T(8,128)(2,1)S(1)}, u32[]{:S(2)}, u32[]{:S(2)}) collective-permute-start(bf16[512,1024]{1,0:T(8,128)(2,1)S(1)} %get-tuple-element.33), channel_id=1, source_target_pairs={{0,3},{3,0},{1,2},{2,1},{4,7},{7,4},{5,6},{6,5},{8,11},{11,8},{9,1... | collective-permute-start | bytes 3145736 | tf_op jit(solution)/shard_map/ppermute | solution.py:26
  73.2 2.2 collective-permute-start.12
  75.4 1.7 slice.192
  77.2 2.7 %collective-permute-start.16 = (bf16[512,1024]{1,0:T(8,128)(2,1)S(1)}, bf16[512,1024]{1,0:T(8,128)(2,1)S(1)}, u32[]{:S(2)}, u32[]{:S(2)}) collective-permute-start(bf16[512,1024]{1,0:T(8,128)(2,1)S(1)} %get-tuple-element.34), channel_id=1, source_target_pairs={{0,3},{3,0},{1,2},{2,1},{4,7},{7,4},{5,6},{6,5},{8,11},{11,8},{9,1... | collective-permute-start | bytes 3145736 | tf_op jit(solution)/shard_map/ppermute | solution.py:26
  81.6 9.0 %collective-permute-done.12 = bf16[192,2048]{1,0:T(8,128)(2,1)S(1)} collective-permute-done((bf16[192,2048]{1,0:T(8,128)(2,1)S(1)}, bf16[192,2048]{1,0:T(8,128)(2,1)S(1)}, u32[]{:S(2)}, u32[]{:S(2)}) %collective-permute-start.12) | collective-permute-done | bytes 786464 | tf_op jit(solution)/shard_map/ppermute | solution.py:18
  90.6 7.3 %maximum_convert_fusion = bf16[1536,1024]{1,0:T(8,128)(2,1)S(1)} fusion(bf16[1536,2048]{1,0:T(8,128)(2,1)S(1)} %constant_dynamic-update-slice_fusion, bf16[2048,512]{1,0:T(8,128)(2,1)S(1)} %slice.192, bf16[2048,512]{1,0:T(8,128)(2,1)S(1)} %bitcast.45, f32[1024]{0:T(1024)S(1)} %pad_maximum_fusion.12), kind=kOutput, calls=%fused_computation | convolution fusion | flops 6455558144 | bytes 13635584 | tf_op jit(solution)/shard_map/dot_general | solution.py:139
  97.9 3.8 %convolution_convert_fusion.1 = bf16[1536,1024]{1,0:T(8,128)(2,1)S(1)} fusion(bf16[1536,1024]{1,0:T(8,128)(2,1)S(1)} %maximum_convert_fusion, bf16[512,1024]{1,0:T(8,128)(2,1)S(1)} %collective-permute-done.13, bf16[512,1024]{1,0:T(8,128)(2,1)S(1)} %get-tuple-element.33), kind=kOutput, calls=%fused_computation.5 | convolution fusion | flops 3226992640 | bytes 8388608 | tf_op jit(solution)/shard_map/dot_general | solution.py:143
  102.8 3.2 %collective-permute-start.14 = (bf16[384,1024]{1,0:T(8,128)(2,1)S(1)}, bf16[384,1024]{1,0:T(8,128)(2,1)S(1)}, u32[]{:S(2)}, u32[]{:S(2)}) collective-permute-start(bf16[384,1024]{1,0:T(8,128)(2,1)S(1)} %pad_maximum_fusion.4), channel_id=1, source_target_pairs={{0,12},{4,0},{8,4},{12,8},{1,13},{5,1},{9,5},{13,9},{2,14},{6,2},{... | collective-permute-start | bytes 2359304 | tf_op jit(solution)/shard_map/ppermute | solution.py:18
  106.0 10.6 %collective-permute-done.16 = bf16[512,1024]{1,0:T(8,128)(2,1)S(1)} collective-permute-done((bf16[512,1024]{1,0:T(8,128)(2,1)S(1)}, bf16[512,1024]{1,0:T(8,128)(2,1)S(1)}, u32[]{:S(2)}, u32[]{:S(2)}) %collective-permute-start.16) | collective-permute-done | bytes 1048608 | tf_op jit(solution)/shard_map/ppermute | solution.py:26
  116.6 4.2 %collective-permute-done.15 = bf16[384,1024]{1,0:T(8,128)(2,1)S(1)} collective-permute-done((bf16[384,1024]{1,0:T(8,128)(2,1)S(1)}, bf16[384,1024]{1,0:T(8,128)(2,1)S(1)}, u32[]{:S(2)}, u32[]{:S(2)}) %collective-permute-start.15) | collective-permute-done | bytes 786464 | tf_op jit(solution)/shard_map/ppermute | solution.py:18
  121.1 3.2 %collective-permute-start.17 = (bf16[384,1024]{1,0:T(8,128)(2,1)S(1)}, bf16[384,1024]{1,0:T(8,128)(2,1)S(1)}, u32[]{:S(2)}, u32[]{:S(2)}) collective-permute-start(bf16[384,1024]{1,0:T(8,128)(2,1)S(1)} %add_convert_fusion.1), channel_id=1, source_target_pairs={{0,12},{4,0},{8,4},{12,8},{1,13},{5,1},{9,5},{13,9},{2,14},{6,2},{... | collective-permute-start | bytes 2359304 | tf_op jit(solution)/shard_map/ppermute | solution.py:18
  124.2 3.8 %convolution_convert_fusion = bf16[1536,1024]{1,0:T(8,128)(2,1)S(1)} fusion(bf16[1536,1024]{1,0:T(8,128)(2,1)S(1)} %maximum_convert_fusion, bf16[512,1024]{1,0:T(8,128)(2,1)S(1)} %collective-permute-done.16, bf16[512,1024]{1,0:T(8,128)(2,1)S(1)} %get-tuple-element.34), kind=kOutput, calls=%fused_computation.4 | convolution fusion | flops 3226992640 | bytes 8388608 | tf_op jit(solution)/shard_map/dot_general | solution.py:143
  128.5 8.9 %collective-permute-done.17 = bf16[384,1024]{1,0:T(8,128)(2,1)S(1)} collective-permute-done((bf16[384,1024]{1,0:T(8,128)(2,1)S(1)}, bf16[384,1024]{1,0:T(8,128)(2,1)S(1)}, u32[]{:S(2)}, u32[]{:S(2)}) %collective-permute-start.17) | collective-permute-done | bytes 786464 | tf_op jit(solution)/shard_map/ppermute | solution.py:18
  137.9 2.5 collective-permute-start.19
  140.5 3.2 %collective-permute-start.20 = (bf16[384,1024]{1,0:T(8,128)(2,1)S(1)}, bf16[384,1024]{1,0:T(8,128)(2,1)S(1)}, u32[]{:S(2)}, u32[]{:S(2)}) collective-permute-start(bf16[384,1024]{1,0:T(8,128)(2,1)S(1)} %pad_maximum_fusion.7), channel_id=1, source_target_pairs={{0,12},{4,0},{8,4},{12,8},{1,13},{5,1},{9,5},{13,9},{2,14},{6,2},{... | collective-permute-start | bytes 2359304 | tf_op jit(solution)/shard_map/ppermute | solution.py:18
  143.7 1.5 collective-permute-done.18
  145.1 1.0 collective-permute-done.19
  146.5 2.1 collective-permute-start.21
  148.5 7.1 %collective-permute-done.20 = bf16[384,1024]{1,0:T(8,128)(2,1)S(1)} collective-permute-done((bf16[384,1024]{1,0:T(8,128)(2,1)S(1)}, bf16[384,1024]{1,0:T(8,128)(2,1)S(1)}, u32[]{:S(2)}, u32[]{:S(2)}) %collective-permute-start.20) | collective-permute-done | bytes 786464 | tf_op jit(solution)/shard_map/ppermute | solution.py:18
  155.6 6.4 %collective-permute-done.21 = bf16[384,1024]{1,0:T(8,128)(2,1)S(1)} collective-permute-done((bf16[384,1024]{1,0:T(8,128)(2,1)S(1)}, bf16[384,1024]{1,0:T(8,128)(2,1)S(1)}, u32[]{:S(2)}, u32[]{:S(2)}) %collective-permute-start.21) | collective-permute-done | bytes 786464 | tf_op jit(solution)/shard_map/ppermute | solution.py:18
  162.6 2.0 collective-permute-start.22
  164.7 0.9 fusion.28
  165.6 6.5 %all-to-all-start.1 = ((bf16[8,24,1024]{2,1,0:T(8,128)(2,1)}), bf16[8,24,1024]{2,1,0:T(8,128)(2,1)S(1)}, u32[]{:S(2)}, u32[]{:S(2)}) async-start(bf16[8,24,1024]{2,1,0:T(8,128)(2,1)} %bitcast.14), calls=%async_computation.1 | async-start | bytes 786432 | tf_op jit(solution)/shard_map/all_to_all | solution.py:113
  172.1 0.8 fusion.27
  173.0 8.1 %all-to-all-done.1 = bf16[8,24,1024]{2,1,0:T(8,128)(2,1)S(1)} async-done(((bf16[8,24,1024]{2,1,0:T(8,128)(2,1)}), bf16[8,24,1024]{2,1,0:T(8,128)(2,1)S(1)}, u32[]{:S(2)}, u32[]{:S(2)}) %all-to-all-start.1) | async-done | bytes 393248 | tf_op jit(solution)/shard_map/all_to_all | solution.py:113
  181.0 3.5 %all-to-all-start.2 = ((bf16[8,24,1024]{2,1,0:T(8,128)(2,1)}), bf16[8,24,1024]{2,1,0:T(8,128)(2,1)S(1)}, u32[]{:S(2)}, u32[]{:S(2)}) async-start(bf16[8,24,1024]{2,1,0:T(8,128)(2,1)} %bitcast.16), calls=%async_computation.2 | async-start | bytes 786432 | tf_op jit(solution)/shard_map/all_to_all | solution.py:113
  184.6 8.8 %all-to-all-done.2 = bf16[8,24,1024]{2,1,0:T(8,128)(2,1)S(1)} async-done(((bf16[8,24,1024]{2,1,0:T(8,128)(2,1)}), bf16[8,24,1024]{2,1,0:T(8,128)(2,1)S(1)}, u32[]{:S(2)}, u32[]{:S(2)}) %all-to-all-start.2) | async-done | bytes 393248 | tf_op jit(solution)/shard_map/all_to_all | solution.py:113
  193.4 0.8 fusion.71
  195.4 2.7 %collective-permute-start.24 = (bf16[64,2048]{1,0:T(8,128)(2,1)S(1)}, bf16[64,2048]{1,0:T(8,128)(2,1)S(1)}, u32[]{:S(2)}, u32[]{:S(2)}) collective-permute-start(bf16[64,2048]{1,0:T(8,128)(2,1)S(1)} %get-tuple-element.91), channel_id=1, source_target_pairs={{0,96},{32,0},{64,32},{96,64},{1,97},{33,1},{65,33},{97,65},{2,98}... | collective-permute-start | bytes 786440 | tf_op jit(solution)/shard_map/ppermute | solution.py:18
  198.0 5.8 %collective-permute-done.23 = bf16[64,2048]{1,0:T(8,128)(2,1)S(1)} collective-permute-done((bf16[64,2048]{1,0:T(8,128)(2,1)S(1)}, bf16[64,2048]{1,0:T(8,128)(2,1)S(1)}, u32[]{:S(2)}, u32[]{:S(2)}) %collective-permute-start.23) | collective-permute-done | bytes 262176 | tf_op jit(solution)/shard_map/ppermute | solution.py:18
  203.9 3.2 %collective-permute-start.30 = (bf16[64,2048]{1,0:T(8,128)(2,1)S(1)}, bf16[64,2048]{1,0:T(8,128)(2,1)S(1)}, u32[]{:S(2)}, u32[]{:S(2)}) collective-permute-start(bf16[64,2048]{1,0:T(8,128)(2,1)S(1)} %get-tuple-element.47), channel_id=1, source_target_pairs={{0,96},{32,0},{64,32},{96,64},{1,97},{33,1},{65,33},{97,65},{2,98}... | collective-permute-start | bytes 786440 | tf_op jit(solution)/shard_map/ppermute | solution.py:18
  207.1 4.9 %collective-permute-done.25 = bf16[64,2048]{1,0:T(8,128)(2,1)S(1)} collective-permute-done((bf16[64,2048]{1,0:T(8,128)(2,1)S(1)}, bf16[64,2048]{1,0:T(8,128)(2,1)S(1)}, u32[]{:S(2)}, u32[]{:S(2)}) %collective-permute-start.25) | collective-permute-done | bytes 262176 | tf_op jit(solution)/shard_map/ppermute | solution.py:18
  212.0 1.3 fusion.16
  213.3 3.6 %fusion.17 = bf16[256,1024]{1,0:T(8,128)(2,1)S(1)} fusion(bf16[2048,1024]{1,0:T(8,128)(2,1)} %collective-permute-done, f32[1024]{0:T(1024)S(1)} %collective-permute-done.2, bf16[64,2048]{1,0:T(8,128)(2,1)S(1)} %collective-permute-done.25, bf16[64,2048]{1,0:T(8,128)(2,1)S(1)} %collective-permute-done.24, bf16[64,2048]{1,0:T(8,128)(2,1)S(1)} %collective-permute-done.23, ...), kind=kOutput, calls=%fused_computation.34 | convolution fusion | flops 1078722560 | bytes 5771264 | tf_op jit(solution)/shard_map/dot_general | solution.py:185
  216.9 1.3 fusion.72
  218.3 3.5 %fusion.3 = bf16[256,2048]{1,0:T(8,128)(2,1)S(1)} fusion(f32[256,2048]{1,0:T(8,128)S(1)} %fusion.72, bf16[256,1024]{1,0:T(8,128)(2,1)S(1)} %fusion.17, bf16[1024,2048]{1,0:T(8,128)(2,1)} %collective-permute-done.1), kind=kOutput, calls=%fused_computation.8 | convolution fusion | flops 1074790400 | bytes 7864320 | tf_op jit(solution)/shard_map/dot_general | solution.py:191
  221.8 3.3 %collective-permute-start.31 = (bf16[64,2048]{1,0:T(8,128)(2,1)S(1)}, bf16[64,2048]{1,0:T(8,128)(2,1)S(1)}, u32[]{:S(2)}, u32[]{:S(2)}) collective-permute-start(bf16[64,2048]{1,0:T(8,128)(2,1)S(1)} %collective-permute-done.30), channel_id=1, source_target_pairs={{0,96},{32,0},{64,32},{96,64},{1,97},{33,1},{65,33},{97,65},{2,98}... | collective-permute-start | bytes 786440 | tf_op jit(solution)/shard_map/ppermute | solution.py:18
  225.2 2.0 collective-permute-start.28
  227.2 3.9 %collective-permute-done.31 = bf16[64,2048]{1,0:T(8,128)(2,1)S(1)} collective-permute-done((bf16[64,2048]{1,0:T(8,128)(2,1)S(1)}, bf16[64,2048]{1,0:T(8,128)(2,1)S(1)}, u32[]{:S(2)}, u32[]{:S(2)}) %collective-permute-start.31) | collective-permute-done | bytes 262176 | tf_op jit(solution)/shard_map/ppermute | solution.py:18
  231.2 3.5 %fusion.19 = bf16[256,1024]{1,0:T(8,128)(2,1)S(1)} fusion(bf16[2048,1024]{1,0:T(8,128)(2,1)} %collective-permute-done, f32[1024]{0:T(1024)S(1)} %collective-permute-done.2, bf16[64,2048]{1,0:T(8,128)(2,1)S(1)} %collective-permute-done.31, bf16[64,2048]{1,0:T(8,128)(2,1)S(1)} %collective-permute-done.30, bf16[64,2048]{1,0:T(8,128)(2,1)S(1)} %collective-permute-done.29, ...), kind=kOutput, calls=%fused_computation.36 | convolution fusion | flops 1078722560 | bytes 5771264 | tf_op jit(solution)/shard_map/dot_general | solution.py:185
  234.6 1.3 fusion.18
  235.9 1.3 fusion.73
  237.2 3.5 %fusion.4 = bf16[256,2048]{1,0:T(8,128)(2,1)S(1)} fusion(f32[256,2048]{1,0:T(8,128)S(1)} %fusion.73, bf16[256,1024]{1,0:T(8,128)(2,1)S(1)} %fusion.19, bf16[1024,2048]{1,0:T(8,128)(2,1)} %collective-permute-done.1), kind=kOutput, calls=%fused_computation.9 | convolution fusion | flops 1074790400 | bytes 7864320 | tf_op jit(solution)/shard_map/dot_general | solution.py:191
  240.9 3.8 %collective-permute-start.27 = (bf16[64,2048]{1,0:T(8,128)(2,1)S(1)}, bf16[64,2048]{1,0:T(8,128)(2,1)S(1)}, u32[]{:S(2)}, u32[]{:S(2)}) collective-permute-start(bf16[64,2048]{1,0:T(8,128)(2,1)S(1)} %add_convert_fusion.3), channel_id=1, source_target_pairs={{0,96},{32,0},{64,32},{96,64},{1,97},{33,1},{65,33},{97,65},{2,98}... | collective-permute-start | bytes 786440 | tf_op jit(solution)/shard_map/ppermute | solution.py:18
  244.6 2.0 collective-permute-start.32
  246.6 4.9 %collective-permute-done.33 = bf16[64,2048]{1,0:T(8,128)(2,1)S(1)} collective-permute-done((bf16[64,2048]{1,0:T(8,128)(2,1)S(1)}, bf16[64,2048]{1,0:T(8,128)(2,1)S(1)}, u32[]{:S(2)}, u32[]{:S(2)}) %collective-permute-start.33) | collective-permute-done | bytes 262176 | tf_op jit(solution)/shard_map/ppermute | solution.py:18
  251.8 7.4 %collective-permute-done.34 = bf16[64,2048]{1,0:T(8,128)(2,1)S(1)} collective-permute-done((bf16[64,2048]{1,0:T(8,128)(2,1)S(1)}, bf16[64,2048]{1,0:T(8,128)(2,1)S(1)}, u32[]{:S(2)}, u32[]{:S(2)}) %collective-permute-start.34) | collective-permute-done | bytes 262176 | tf_op jit(solution)/shard_map/ppermute | solution.py:18
  259.4 0.9 fusion.26
  (102 shorter events, 10.3 us)
Async XLA Ops:
  0.0 26.1 %collective-permute-start = (bf16[2048,1024]{1,0:T(8,128)(2,1)}, bf16[2048,1024]{1,0:T(8,128)(2,1)}, u32[]{:S(2)}, u32[]{:S(2)}) collective-permute-start(bf16[2048,1024]{1,0:T(8,128)(2,1)} %param.22), channel_id=1, source_target_pairs={{0,16},{16,0},{1,17},{17,1},{2,18},{18,2},{3,19},{19,3},{4,20},{20... | collective-permute-start | bytes 12582920 | tf_op jit(solution)/shard_map/ppermute | solution.py:30
  0.0 26.1 %collective-permute-start.1 = (bf16[1024,2048]{1,0:T(8,128)(2,1)}, bf16[1024,2048]{1,0:T(8,128)(2,1)}, u32[]{:S(2)}, u32[]{:S(2)}) collective-permute-start(bf16[1024,2048]{1,0:T(8,128)(2,1)} %param.24), channel_id=1, source_target_pairs={{0,16},{16,0},{1,17},{17,1},{2,18},{18,2},{3,19},{19,3},{4,20},{20... | collective-permute-start | bytes 12582920 | tf_op jit(solution)/shard_map/ppermute | solution.py:30
  5.6 7.4 %copy-start.9 = (f32[1024]{0:T(1024)S(1)}, f32[1024]{0:T(1024)}, u32[]{:S(2)}) copy-start(f32[1024]{0:T(1024)} %param.23) | copy-start | bytes 12292
  5.6 7.9 %copy-start.6 = (f32[1,512]{1,0:T(1,128)S(1)}, f32[1,512]{1,0:T(1,128)}, u32[]{:S(2)}) copy-start(f32[1,512]{1,0:T(1,128)} %param.18) | copy-start | bytes 6148
  8.4 17.7 %all-to-all-start = ((bf16[8,24,2048]{2,1,0:T(8,128)(2,1)}), bf16[8,24,2048]{2,1,0:T(8,128)(2,1)S(1)}, u32[]{:S(2)}, u32[]{:S(2)}) async-start(bf16[8,24,2048]{2,1,0:T(8,128)(2,1)} %bitcast.8), calls=%async_computation | async-start | bytes 1572864 | tf_op jit(solution)/shard_map/all_to_all | solution.py:113
  13.0 10.9 %collective-permute-start.2 = (f32[1024]{0:T(1024)S(1)}, f32[1024]{0:T(1024)S(1)}, u32[]{:S(2)}, u32[]{:S(2)}) collective-permute-start(f32[1024]{0:T(1024)S(1)} %copy-done.9), channel_id=1, source_target_pairs={{0,16},{16,0},{1,17},{17,1},{2,18},{18,2},{3,19},{19,3},{4,20},{20... | collective-permute-start | bytes 12296 | tf_op jit(solution)/shard_map/ppermute | solution.py:30
  21.1 52.0 %collective-permute-start.8 = (bf16[2056,512]{1,0:T(8,128)(2,1)S(1)}, bf16[2056,512]{1,0:T(8,128)(2,1)}, u32[]{:S(2)}, u32[]{:S(2)}) collective-permute-start(bf16[2056,512]{1,0:T(8,128)(2,1)S(1)} %concatenate.63), channel_id=1, source_target_pairs={{0,3},{3,0},{1,2},{2,1},{4,7},{7,4},{5,6},{6,5},{8,11},{11,8},{9,1... | collective-permute-start | bytes 6316040 | tf_op jit(solution)/shard_map/ppermute | solution.py:26
  26.2 16.8 %copy-start.1 = (bf16[1,512,2048]{2,1,0:T(8,128)(2,1)S(1)}, bf16[1,512,2048]{2,1,0:T(8,128)(2,1)}, u32[]{:S(2)}) copy-start(bf16[1,512,2048]{2,1,0:T(8,128)(2,1)} %param.19) | copy-start | bytes 6291460
  26.2 13.0 %collective-permute-start.3 = (bf16[96,2048]{1,0:T(8,128)(2,1)S(1)}, bf16[96,2048]{1,0:T(8,128)(2,1)S(1)}, u32[]{:S(2)}, u32[]{:S(2)}) collective-permute-start(bf16[96,2048]{1,0:T(8,128)(2,1)S(1)} %get-tuple-element.90), channel_id=1, source_target_pairs={{0,4},{4,8},{8,12},{12,0},{1,5},{5,9},{9,13},{13,1},{2,6},{6,10},{... | collective-permute-start | bytes 1179656 | tf_op jit(solution)/shard_map/ppermute | solution.py:18
  28.2 11.0 %collective-permute-start.4 = (bf16[96,2048]{1,0:T(8,128)(2,1)S(1)}, bf16[96,2048]{1,0:T(8,128)(2,1)S(1)}, u32[]{:S(2)}, u32[]{:S(2)}) collective-permute-start(bf16[96,2048]{1,0:T(8,128)(2,1)S(1)} %get-tuple-element.90), channel_id=1, source_target_pairs={{0,12},{4,0},{8,4},{12,8},{1,13},{5,1},{9,5},{13,9},{2,14},{6,2},{... | collective-permute-start | bytes 1179656 | tf_op jit(solution)/shard_map/ppermute | solution.py:18
  30.4 10.4 %collective-permute-start.5 = (bf16[96,2048]{1,0:T(8,128)(2,1)S(1)}, bf16[96,2048]{1,0:T(8,128)(2,1)S(1)}, u32[]{:S(2)}, u32[]{:S(2)}) collective-permute-start(bf16[96,2048]{1,0:T(8,128)(2,1)S(1)} %get-tuple-element.89), channel_id=1, source_target_pairs={{0,1},{1,0},{2,3},{3,2},{4,5},{5,4},{6,7},{7,6},{8,9},{9,8},{10,11... | collective-permute-start | bytes 1179656 | tf_op jit(solution)/shard_map/ppermute | solution.py:22
  40.8 32.4 %collective-permute-start.7 = (bf16[192,2048]{1,0:T(8,128)(2,1)S(1)}, bf16[192,2048]{1,0:T(8,128)(2,1)S(1)}, u32[]{:S(2)}, u32[]{:S(2)}) collective-permute-start(bf16[192,2048]{1,0:T(8,128)(2,1)S(1)} %pad_maximum_fusion.3), channel_id=1, source_target_pairs={{0,12},{4,0},{8,4},{12,8},{1,13},{5,1},{9,5},{13,9},{2,14},{6,2},{... | collective-permute-start | bytes 2359304 | tf_op jit(solution)/shard_map/ppermute | solution.py:18
  42.6 34.6 %collective-permute-start.9 = (bf16[192,2048]{1,0:T(8,128)(2,1)S(1)}, bf16[192,2048]{1,0:T(8,128)(2,1)S(1)}, u32[]{:S(2)}, u32[]{:S(2)}) collective-permute-start(bf16[192,2048]{1,0:T(8,128)(2,1)S(1)} %pad_maximum_fusion.3), channel_id=1, source_target_pairs={{0,4},{4,8},{8,12},{12,0},{1,5},{5,9},{9,13},{13,1},{2,6},{6,10},{... | collective-permute-start | bytes 2359304 | tf_op jit(solution)/shard_map/ppermute | solution.py:18
  42.9 27.2 %collective-permute-start.6 = (bf16[96,2048]{1,0:T(8,128)(2,1)S(1)}, bf16[96,2048]{1,0:T(8,128)(2,1)S(1)}, u32[]{:S(2)}, u32[]{:S(2)}) collective-permute-start(bf16[96,2048]{1,0:T(8,128)(2,1)S(1)} %collective-permute-done.3), channel_id=1, source_target_pairs={{0,4},{4,8},{8,12},{12,0},{1,5},{5,9},{9,13},{13,1},{2,6},{6,10},{... | collective-permute-start | bytes 1179656 | tf_op jit(solution)/shard_map/ppermute | solution.py:18
  43.2 37.6 %collective-permute-start.10 = (bf16[288,2048]{1,0:T(8,128)(2,1)S(1)}, bf16[288,2048]{1,0:T(8,128)(2,1)S(1)}, u32[]{:S(2)}, u32[]{:S(2)}) collective-permute-start(bf16[288,2048]{1,0:T(8,128)(2,1)S(1)} %pad_maximum_fusion), channel_id=1, source_target_pairs={{0,1},{1,0},{2,3},{3,2},{4,5},{5,4},{6,7},{7,6},{8,9},{9,8},{10,11... | collective-permute-start | bytes 3538952 | tf_op jit(solution)/shard_map/ppermute | solution.py:22
  70.2 27.7 %collective-permute-start.13 = (bf16[512,1024]{1,0:T(8,128)(2,1)S(1)}, bf16[512,1024]{1,0:T(8,128)(2,1)S(1)}, u32[]{:S(2)}, u32[]{:S(2)}) collective-permute-start(bf16[512,1024]{1,0:T(8,128)(2,1)S(1)} %get-tuple-element.33), channel_id=1, source_target_pairs={{0,3},{3,0},{1,2},{2,1},{4,7},{7,4},{5,6},{6,5},{8,11},{11,8},{9,1... | collective-permute-start | bytes 3145736 | tf_op jit(solution)/shard_map/ppermute | solution.py:26
  73.0 8.5 %collective-permute-start.11 = (bf16[96,2048]{1,0:T(8,128)(2,1)S(1)}, bf16[96,2048]{1,0:T(8,128)(2,1)S(1)}, u32[]{:S(2)}, u32[]{:S(2)}) collective-permute-start(bf16[96,2048]{1,0:T(8,128)(2,1)S(1)} %collective-permute-done.6), channel_id=1, source_target_pairs={{0,1},{1,0},{2,3},{3,2},{4,5},{5,4},{6,7},{7,6},{8,9},{9,8},{10,11... | collective-permute-start | bytes 1179656 | tf_op jit(solution)/shard_map/ppermute | solution.py:22
  73.2 17.3 %collective-permute-start.12 = (bf16[192,2048]{1,0:T(8,128)(2,1)S(1)}, bf16[192,2048]{1,0:T(8,128)(2,1)S(1)}, u32[]{:S(2)}, u32[]{:S(2)}) collective-permute-start(bf16[192,2048]{1,0:T(8,128)(2,1)S(1)} %collective-permute-done.7), channel_id=1, source_target_pairs={{0,12},{4,0},{8,4},{12,8},{1,13},{5,1},{9,5},{13,9},{2,14},{6,2},{... | collective-permute-start | bytes 2359304 | tf_op jit(solution)/shard_map/ppermute | solution.py:18
  77.2 39.4 %collective-permute-start.16 = (bf16[512,1024]{1,0:T(8,128)(2,1)S(1)}, bf16[512,1024]{1,0:T(8,128)(2,1)S(1)}, u32[]{:S(2)}, u32[]{:S(2)}) collective-permute-start(bf16[512,1024]{1,0:T(8,128)(2,1)S(1)} %get-tuple-element.34), channel_id=1, source_target_pairs={{0,3},{3,0},{1,2},{2,1},{4,7},{7,4},{5,6},{6,5},{8,11},{11,8},{9,1... | collective-permute-start | bytes 3145736 | tf_op jit(solution)/shard_map/ppermute | solution.py:26
  80.8 9.8 %copy-start = (bf16[1,2048,512]{2,1,0:T(8,128)(2,1)S(1)}, bf16[1,2048,512]{2,1,0:T(8,128)(2,1)}, u32[]{:S(2)}) copy-start(bf16[1,2048,512]{2,1,0:T(8,128)(2,1)} %param.17) | copy-start | bytes 6291460
  102.1 18.7 %collective-permute-start.15 = (bf16[384,1024]{1,0:T(8,128)(2,1)S(1)}, bf16[384,1024]{1,0:T(8,128)(2,1)S(1)}, u32[]{:S(2)}, u32[]{:S(2)}) collective-permute-start(bf16[384,1024]{1,0:T(8,128)(2,1)S(1)} %pad_maximum_fusion.5), channel_id=1, source_target_pairs={{0,4},{4,8},{8,12},{12,0},{1,5},{5,9},{9,13},{13,1},{2,6},{6,10},{... | collective-permute-start | bytes 2359304 | tf_op jit(solution)/shard_map/ppermute | solution.py:18
  102.8 18.0 %collective-permute-start.14 = (bf16[384,1024]{1,0:T(8,128)(2,1)S(1)}, bf16[384,1024]{1,0:T(8,128)(2,1)S(1)}, u32[]{:S(2)}, u32[]{:S(2)}) collective-permute-start(bf16[384,1024]{1,0:T(8,128)(2,1)S(1)} %pad_maximum_fusion.4), channel_id=1, source_target_pairs={{0,12},{4,0},{8,4},{12,8},{1,13},{5,1},{9,5},{13,9},{2,14},{6,2},{... | collective-permute-start | bytes 2359304 | tf_op jit(solution)/shard_map/ppermute | solution.py:18
  121.1 16.4 %collective-permute-start.17 = (bf16[384,1024]{1,0:T(8,128)(2,1)S(1)}, bf16[384,1024]{1,0:T(8,128)(2,1)S(1)}, u32[]{:S(2)}, u32[]{:S(2)}) collective-permute-start(bf16[384,1024]{1,0:T(8,128)(2,1)S(1)} %add_convert_fusion.1), channel_id=1, source_target_pairs={{0,12},{4,0},{8,4},{12,8},{1,13},{5,1},{9,5},{13,9},{2,14},{6,2},{... | collective-permute-start | bytes 2359304 | tf_op jit(solution)/shard_map/ppermute | solution.py:18
  128.4 16.7 %collective-permute-start.18 = (bf16[384,1024]{1,0:T(8,128)(2,1)S(1)}, bf16[384,1024]{1,0:T(8,128)(2,1)S(1)}, u32[]{:S(2)}, u32[]{:S(2)}) collective-permute-start(bf16[384,1024]{1,0:T(8,128)(2,1)S(1)} %pad_maximum_fusion.6), channel_id=1, source_target_pairs={{0,4},{4,8},{8,12},{12,0},{1,5},{5,9},{9,13},{13,1},{2,6},{6,10},{... | collective-permute-start | bytes 2359304 | tf_op jit(solution)/shard_map/ppermute | solution.py:18
  137.9 8.2 %collective-permute-start.19 = (bf16[192,1024]{1,0:T(8,128)(2,1)S(1)}, bf16[192,1024]{1,0:T(8,128)(2,1)S(1)}, u32[]{:S(2)}, u32[]{:S(2)}) collective-permute-start(bf16[192,1024]{1,0:T(8,128)(2,1)S(1)} %slice.292), channel_id=1, source_target_pairs={{0,1},{1,0},{2,3},{3,2},{4,5},{5,4},{6,7},{7,6},{8,9},{9,8},{10,11... | collective-permute-start | bytes 1179656 | tf_op jit(solution)/shard_map/ppermute | solution.py:22
  140.5 15.2 %collective-permute-start.20 = (bf16[384,1024]{1,0:T(8,128)(2,1)S(1)}, bf16[384,1024]{1,0:T(8,128)(2,1)S(1)}, u32[]{:S(2)}, u32[]{:S(2)}) collective-permute-start(bf16[384,1024]{1,0:T(8,128)(2,1)S(1)} %pad_maximum_fusion.7), channel_id=1, source_target_pairs={{0,12},{4,0},{8,4},{12,8},{1,13},{5,1},{9,5},{13,9},{2,14},{6,2},{... | collective-permute-start | bytes 2359304 | tf_op jit(solution)/shard_map/ppermute | solution.py:18
  146.5 15.6 %collective-permute-start.21 = (bf16[384,1024]{1,0:T(8,128)(2,1)S(1)}, bf16[384,1024]{1,0:T(8,128)(2,1)S(1)}, u32[]{:S(2)}, u32[]{:S(2)}) collective-permute-start(bf16[384,1024]{1,0:T(8,128)(2,1)S(1)} %add_convert_fusion), channel_id=1, source_target_pairs={{0,4},{4,8},{8,12},{12,0},{1,5},{5,9},{9,13},{13,1},{2,6},{6,10},{... | collective-permute-start | bytes 2359304 | tf_op jit(solution)/shard_map/ppermute | solution.py:18
  162.6 21.9 %copy-start.3 = (f32[8,2048]{1,0:T(8,128)S(1)}, f32[8,2048]{1,0:T(8,128)}, u32[]{:S(2)}) copy-start(f32[8,2048]{1,0:T(8,128)} %param.20) | copy-start | bytes 196612
  162.6 30.8 %copy-start.2 = (bf16[128,2048]{1,0:T(8,128)(2,1)S(1)}, bf16[128,2048]{1,0:T(8,128)(2,1)}, u32[]{:S(2)}) copy-start(bf16[128,2048]{1,0:T(8,128)(2,1)} %param.13) | copy-start | bytes 1572868
  162.6 9.5 %collective-permute-start.22 = (bf16[192,1024]{1,0:T(8,128)(2,1)S(1)}, bf16[192,1024]{1,0:T(8,128)(2,1)S(1)}, u32[]{:S(2)}, u32[]{:S(2)}) collective-permute-start(bf16[192,1024]{1,0:T(8,128)(2,1)S(1)} %slice.291), channel_id=1, source_target_pairs={{0,1},{1,0},{2,3},{3,2},{4,5},{5,4},{6,7},{7,6},{8,9},{9,8},{10,11... | collective-permute-start | bytes 1179656 | tf_op jit(solution)/shard_map/ppermute | solution.py:22
  165.6 15.5 %all-to-all-start.1 = ((bf16[8,24,1024]{2,1,0:T(8,128)(2,1)}), bf16[8,24,1024]{2,1,0:T(8,128)(2,1)S(1)}, u32[]{:S(2)}, u32[]{:S(2)}) async-start(bf16[8,24,1024]{2,1,0:T(8,128)(2,1)} %bitcast.14), calls=%async_computation.1 | async-start | bytes 786432 | tf_op jit(solution)/shard_map/all_to_all | solution.py:113
  181.0 12.3 %all-to-all-start.2 = ((bf16[8,24,1024]{2,1,0:T(8,128)(2,1)}), bf16[8,24,1024]{2,1,0:T(8,128)(2,1)S(1)}, u32[]{:S(2)}, u32[]{:S(2)}) async-start(bf16[8,24,1024]{2,1,0:T(8,128)(2,1)} %bitcast.16), calls=%async_computation.2 | async-start | bytes 786432 | tf_op jit(solution)/shard_map/all_to_all | solution.py:113
  193.4 1.1 copy-start.4
  193.4 18.6 %copy-start.7 = (bf16[2048,1024]{1,0:T(8,128)(2,1)S(1)}, bf16[2048,1024]{1,0:T(8,128)(2,1)}, u32[]{:S(2)}) copy-start(bf16[2048,1024]{1,0:T(8,128)(2,1)} %param.22) | copy-start | bytes 12582916
  194.7 9.1 %collective-permute-start.23 = (bf16[64,2048]{1,0:T(8,128)(2,1)S(1)}, bf16[64,2048]{1,0:T(8,128)(2,1)S(1)}, u32[]{:S(2)}, u32[]{:S(2)}) collective-permute-start(bf16[64,2048]{1,0:T(8,128)(2,1)S(1)} %get-tuple-element.91), channel_id=1, source_target_pairs={{0,32},{32,64},{64,96},{96,0},{1,33},{33,65},{65,97},{97,1},{2,34}... | collective-permute-start | bytes 786440 | tf_op jit(solution)/shard_map/ppermute | solution.py:18
  195.4 8.5 %collective-permute-start.24 = (bf16[64,2048]{1,0:T(8,128)(2,1)S(1)}, bf16[64,2048]{1,0:T(8,128)(2,1)S(1)}, u32[]{:S(2)}, u32[]{:S(2)}) collective-permute-start(bf16[64,2048]{1,0:T(8,128)(2,1)S(1)} %get-tuple-element.91), channel_id=1, source_target_pairs={{0,96},{32,0},{64,32},{96,64},{1,97},{33,1},{65,33},{97,65},{2,98}... | collective-permute-start | bytes 786440 | tf_op jit(solution)/shard_map/ppermute | solution.py:18
  203.8 8.2 %collective-permute-start.25 = (bf16[64,2048]{1,0:T(8,128)(2,1)S(1)}, bf16[64,2048]{1,0:T(8,128)(2,1)S(1)}, u32[]{:S(2)}, u32[]{:S(2)}) collective-permute-start(bf16[64,2048]{1,0:T(8,128)(2,1)S(1)} %collective-permute-done.23), channel_id=1, source_target_pairs={{0,32},{32,64},{64,96},{96,0},{1,33},{33,65},{65,97},{97,1},{2,34}... | collective-permute-start | bytes 786440 | tf_op jit(solution)/shard_map/ppermute | solution.py:18
  203.9 17.9 %collective-permute-start.30 = (bf16[64,2048]{1,0:T(8,128)(2,1)S(1)}, bf16[64,2048]{1,0:T(8,128)(2,1)S(1)}, u32[]{:S(2)}, u32[]{:S(2)}) collective-permute-start(bf16[64,2048]{1,0:T(8,128)(2,1)S(1)} %get-tuple-element.47), channel_id=1, source_target_pairs={{0,96},{32,0},{64,32},{96,64},{1,97},{33,1},{65,33},{97,65},{2,98}... | collective-permute-start | bytes 786440 | tf_op jit(solution)/shard_map/ppermute | solution.py:18
  213.3 3.6 %copy-start.8 = (bf16[1024,2048]{1,0:T(8,128)(2,1)S(1)}, bf16[1024,2048]{1,0:T(8,128)(2,1)}, u32[]{:S(2)}) copy-start(bf16[1024,2048]{1,0:T(8,128)(2,1)} %param.24) | copy-start | bytes 12582916
  218.2 9.0 %collective-permute-start.29 = (bf16[64,2048]{1,0:T(8,128)(2,1)S(1)}, bf16[64,2048]{1,0:T(8,128)(2,1)S(1)}, u32[]{:S(2)}, u32[]{:S(2)}) collective-permute-start(bf16[64,2048]{1,0:T(8,128)(2,1)S(1)} %get-tuple-element.47), channel_id=1, source_target_pairs={{0,32},{32,64},{64,96},{96,0},{1,33},{33,65},{65,97},{97,1},{2,34}... | collective-permute-start | bytes 786440 | tf_op jit(solution)/shard_map/ppermute | solution.py:18
  221.8 9.4 %collective-permute-start.31 = (bf16[64,2048]{1,0:T(8,128)(2,1)S(1)}, bf16[64,2048]{1,0:T(8,128)(2,1)S(1)}, u32[]{:S(2)}, u32[]{:S(2)}) collective-permute-start(bf16[64,2048]{1,0:T(8,128)(2,1)S(1)} %collective-permute-done.30), channel_id=1, source_target_pairs={{0,96},{32,0},{64,32},{96,64},{1,97},{33,1},{65,33},{97,65},{2,98}... | collective-permute-start | bytes 786440 | tf_op jit(solution)/shard_map/ppermute | solution.py:18
  225.1 15.7 %collective-permute-start.26 = (bf16[64,2048]{1,0:T(8,128)(2,1)S(1)}, bf16[64,2048]{1,0:T(8,128)(2,1)S(1)}, u32[]{:S(2)}, u32[]{:S(2)}) collective-permute-start(bf16[64,2048]{1,0:T(8,128)(2,1)S(1)} %get-tuple-element.85), channel_id=1, source_target_pairs={{0,96},{32,0},{64,32},{96,64},{1,97},{33,1},{65,33},{97,65},{2,98}... | collective-permute-start | bytes 786440 | tf_op jit(solution)/shard_map/ppermute | solution.py:18
  225.2 26.5 %collective-permute-start.28 = (bf16[64,2048]{1,0:T(8,128)(2,1)S(1)}, bf16[64,2048]{1,0:T(8,128)(2,1)S(1)}, u32[]{:S(2)}, u32[]{:S(2)}) collective-permute-start(bf16[64,2048]{1,0:T(8,128)(2,1)S(1)} %get-tuple-element.86), channel_id=1, source_target_pairs={{0,32},{32,64},{64,96},{96,0},{1,33},{33,65},{65,97},{97,1},{2,34}... | collective-permute-start | bytes 786440 | tf_op jit(solution)/shard_map/ppermute | solution.py:18
  240.7 18.7 %copy-start.5 = (f32[2048]{0:T(1024)S(1)}, f32[2048]{0:T(1024)}, u32[]{:S(2)}) copy-start(f32[2048]{0:T(1024)} %param.25) | copy-start | bytes 24580
  240.7 10.8 %collective-permute-start.33 = (bf16[64,2048]{1,0:T(8,128)(2,1)S(1)}, bf16[64,2048]{1,0:T(8,128)(2,1)S(1)}, u32[]{:S(2)}, u32[]{:S(2)}) collective-permute-start(bf16[64,2048]{1,0:T(8,128)(2,1)S(1)} %get-tuple-element.88), channel_id=1, source_target_pairs={{0,32},{32,64},{64,96},{96,0},{1,33},{33,65},{65,97},{97,1},{2,34}... | collective-permute-start | bytes 786440 | tf_op jit(solution)/shard_map/ppermute | solution.py:18
  240.9 10.8 %collective-permute-start.27 = (bf16[64,2048]{1,0:T(8,128)(2,1)S(1)}, bf16[64,2048]{1,0:T(8,128)(2,1)S(1)}, u32[]{:S(2)}, u32[]{:S(2)}) collective-permute-start(bf16[64,2048]{1,0:T(8,128)(2,1)S(1)} %add_convert_fusion.3), channel_id=1, source_target_pairs={{0,96},{32,0},{64,32},{96,64},{1,97},{33,1},{65,33},{97,65},{2,98}... | collective-permute-start | bytes 786440 | tf_op jit(solution)/shard_map/ppermute | solution.py:18
  244.6 7.2 %collective-permute-start.32 = (bf16[64,2048]{1,0:T(8,128)(2,1)S(1)}, bf16[64,2048]{1,0:T(8,128)(2,1)S(1)}, u32[]{:S(2)}, u32[]{:S(2)}) collective-permute-start(bf16[64,2048]{1,0:T(8,128)(2,1)S(1)} %get-tuple-element.87), channel_id=1, source_target_pairs={{0,96},{32,0},{64,32},{96,64},{1,97},{33,1},{65,33},{97,65},{2,98}... | collective-permute-start | bytes 786440 | tf_op jit(solution)/shard_map/ppermute | solution.py:18
  251.6 7.7 %collective-permute-start.34 = (bf16[64,2048]{1,0:T(8,128)(2,1)S(1)}, bf16[64,2048]{1,0:T(8,128)(2,1)S(1)}, u32[]{:S(2)}, u32[]{:S(2)}) collective-permute-start(bf16[64,2048]{1,0:T(8,128)(2,1)S(1)} %add_convert_fusion.2), channel_id=1, source_target_pairs={{0,32},{32,64},{64,96},{96,0},{1,33},{33,65},{65,97},{97,1},{2,34}... | collective-permute-start | bytes 786440 | tf_op jit(solution)/shard_map/ppermute | solution.py:18

commit v2 on v1

--- a/solution.py
+++ b/solution.py
@@ -1,6 +1,8 @@
 import jax
 import jax.numpy as jnp
 from jax import lax
+from jax.experimental import pallas as pl
+from jax.experimental.pallas import tpu as pltpu
 from jax.sharding import Mesh, PartitionSpec as P
 
 X = ("xh", "xl")
@@ -49,6 +51,20 @@
     else:
         foll = down(up(foll) + via)
     return up(own) + up(shift(prev, axis, -1)) + up(shift(foll, axis, 1))
+
+
+def on_chip(value):
+    def copy(source, target):
+        pltpu.sync_copy(source, target)
+
+    return pl.pallas_call(
+        copy,
+        in_specs=[pl.BlockSpec(memory_space=pl.ANY)],
+        out_specs=pl.BlockSpec(memory_space=pltpu.VMEM),
+        out_shape=pltpu.VMEM(value.shape, value.dtype),
+        compiler_params=pltpu.CompilerParams(vmem_limit_bytes=262144),
+        name="on_chip",
+    )(value)
 
 
 def pick(index, table):
@@ -82,12 +98,8 @@
 
     half_model = width_model // 2
     left, right = group_w2[0, :, :half_model], group_w2[0, :, half_model:]
-    rest, parts = group_b1[0], []
-    for _ in range(3):
-        parts.append(lax.reduce_precision(rest, 8, 7))
-        rest = rest - parts[-1]
-    parts = down(jnp.stack(parts + [jnp.zeros_like(rest)] * 5))
-    w1_pair = swap_blocks(jnp.concatenate([group_w1[0], parts], axis=0))
+    w1_out, b1_pair = hold(group_w1[0], swap_blocks(group_b1[0]))
+    w1_pair = swap_blocks(w1_out)
 
     residual_in = tokens.astype(jnp.float32)
     lang_hit = (languages[:, None] == jnp.arange(num_langs, dtype=jnp.int32)[None, :]).astype(
@@ -123,8 +135,12 @@
     a_near = jnp.concatenate([a_own, a_prev, a_foll], axis=0)
     a_near, b_pair = hold(a_near, b_pair)
     (b_own,) = hold(jnp.concatenate([b_own, b_pair], axis=0))
-    b_prev, b_foll = shift(b_own, "z", 1), shift(b_own, "z", -1)
-    b_foll, w1_pair = hold(b_foll, w1_pair)
+    b_foll = shift(b_own, "z", -1)
+    held, a_far = hold(b_own, a_far)
+    b_prev = shift(held, "z", 1)
+    sw1_pair, sw2_pair, _ = hold(sw1_pair, sw2_pair, b_own)
+    sw1_pair, sw2_pair = on_chip(sw1_pair), on_chip(sw2_pair)
+    b_foll, w1_pair, sw1_pair, sw2_pair = hold(b_foll, w1_pair, sw1_pair, sw2_pair)
     b_far = shift(b_foll, "z", -1)
     near_pair = swap_column(a_near)
     far_pair = swap_column(a_far)
@@ -132,8 +148,7 @@
     left_pair = swap_blocks(left_out)
     right_out, _, _ = hold(right, w1_pair, b_prev)
     right_pair = swap_blocks(right_out)
-    b1_pair = jnp.sum(up(w1_pair[width_model:]), axis=0)
-    w1 = jnp.concatenate([group_w1[0], w1_pair[:width_model]], axis=1)
+    w1 = jnp.concatenate([group_w1[0], w1_pair], axis=1)
     b1 = jnp.concatenate([group_b1[0], b1_pair])
     rows = jnp.concatenate([a_near, a_far, b_own, b_foll, b_prev, near_pair, far_pair, b_far], axis=0)
     hidden = down(jax.nn.relu(jnp.dot(rows, w1, preferred_element_type=jnp.float32) + b1))
@@ -170,6 +185,7 @@
     back_l = swap_column(out_l)
     sum_r, _, back_l = ring(right, right_pair, hidden, -1, back_l)
     return_l = finish(sum_l, back_l)
+    sum_r, return_l = hold(sum_r, return_l)
     back_r = swap_column(down(sum_r[2 * count :]))
     return_r = finish(sum_r, back_r)
     returned = jnp.concatenate([return_l, return_r], axis=1)
@@ -180,12 +196,13 @@
     middle = residual_in + group_out + group_bias
     shared_in = layer_norm(middle, shared_gain).astype(bf16)
 
-    def shared_forward(block):
-        hidden = [
+    def shared_first(block):
+        return tuple(
             down(jax.nn.relu(jnp.dot(block, w, preferred_element_type=jnp.float32) + b))
             for w, b in ((shared_w1, shared_b1), (sw1_pair, sb1_pair))
-        ]
-        hidden = hold(*hidden)
+        )
+
+    def shared_second(hidden):
         return down(
             jnp.dot(hidden[0], shared_w2, preferred_element_type=jnp.float32)
             + jnp.dot(hidden[1], sw2_pair, preferred_element_type=jnp.float32)
@@ -202,8 +219,14 @@
     prev = shift(held, "y", 1)
     far = shift(foll, "y", -1)
     other = jnp.concatenate([two, prev, foll, far], axis=0)
-    first = ring_scatter(*jnp.split(shared_forward(first), 4), "y", 1)
-    other = ring_scatter(*jnp.split(shared_forward(other), 4), "y", -1)
+    *hidden, _ = hold(*shared_first(first), foll)
+    own, prev, foll, via = jnp.split(shared_second(hidden), 4)
+    via = shift(via, "y", -1)
+    foll = shift(foll, "y", 1)
+    prev = down(up(prev) + up(via))
+    *hidden, prev_out, foll = hold(*shared_first(other), prev, foll)
+    first = up(own) + up(shift(prev_out, "y", -1)) + up(foll)
+    other = ring_scatter(*jnp.split(shared_second(hidden), 4), "y", -1)
     shared_out = jnp.concatenate([first, other], axis=0)
     return (middle + shared_out + shared_b2).astype(bf16)
 

time: 261 us -> 244 us (0.935)
  waiting for transfers between devices: 130 us -> 122 us
  matrix products: 37.5 us -> 30.2 us
  Pallas kernels: 0 us -> 4.38 us
  local copies, waits for them, and re-layouts: 12.3 us -> 7.95 us
  starting transfers between devices: 70.5 us -> 67.7 us
    ppermute x24, waiting for transfers between devices: 96.8 us -> 73.3 us  [shift(): lax.ppermute(value, axis, [(i, (i + step) % size) for i in range(size)])]
    ppermute x5, waiting for transfers between devices: 3.13 us -> 16.9 us  [swap_column(): return lax.ppermute(value, 'xl', [(0, 1), (1, 0)])]
    concatenate x1 -> x0, local copies, waits for them, and re-layouts: 7.54 us -> none  [on_device(): w1_pair = swap_blocks(jnp.concatenate([group_w1[0], parts], axis=0))]
    dot_general x8, matrix products: 19.1 us -> 11.7 us  [the longest x4 6.58 us: shared_first(): jnp.dot(block, w, preferred_element_type=jnp.float32) + b]
    ppermute x3 -> x4, waiting for transfers between devices: 10.6 us -> 17.5 us  [swap_blocks(): return lax.ppermute(value, X, [(0, 3), (3, 0), (1, 2), (2, 1)])]
    unnamed x27 -> x53, local copies, waits for them, and re-layouts: 0.42 us -> 5.31 us
    all_to_all x3, waiting for transfers between devices: 19.1 us -> 14.7 us  [exchange(): lax.all_to_all(value, ('y', 'core'), split_axis=0, concat_axis=0, tiled=T...]
    pallas_call x0 -> x2, Pallas kernels: none -> 4.38 us  [on_chip(): pl.pallas_call(copy, in_specs=[pl.BlockSpec(memory_space=pl.ANY)], out_sp...]
  transfers between devices with their start and end apart: 38 -> 39, of which waited for: 20 -> 23; matrix products, arithmetic and copies ran while one was open for 22% -> 15% of each run, Pallas kernels for 0% -> 2%
where the time goes in v2:
time: 244 us; the launch traced here: 243 us
  waiting for transfers between devices  122 us (50%)
  starting transfers between devices  67.7 us (28%)
  matrix products  30.2 us (12%)
  other arithmetic  10.1 us (4%)
  local copies, waits for them, and re-layouts  7.95 us (3%)
  Pallas kernels  4.38 us (2%)
    ppermute x24, waiting for transfers between devices, shift(): lax.ppermute(value, axis, [(i, (i + step) % size) for i in range(size)])  73.3 us
    ppermute x24, starting transfers between devices, shift(): lax.ppermute(value, axis, [(i, (i + step) % size) for i in range(size)])  39.8 us
    ppermute x4, waiting for transfers between devices, swap_blocks(): return lax.ppermute(value, X, [(0, 3), (3, 0), (1, 2), (2, 1)])  17.5 us
    ppermute x5, waiting for transfers between devices, swap_column(): return lax.ppermute(value, 'xl', [(0, 1), (1, 0)])  16.9 us
    all_to_all x3, waiting for transfers between devices, exchange(): lax.all_to_all(value, ('y', 'core'), split_axis=0, concat_axis=0, tiled=T...  14.7 us
    all_to_all x3, starting transfers between devices, exchange(): lax.all_to_all(value, ('y', 'core'), split_axis=0, concat_axis=0, tiled=T...  13.3 us
    ppermute x4, starting transfers between devices, swap_blocks(): return lax.ppermute(value, X, [(0, 3), (3, 0), (1, 2), (2, 1)])  9.01 us
    dot_general x2, matrix products, second(): return down(jnp.dot(hidden, weight, preferred_element_type=jnp.float32))  7.53 us
  transfers between devices with their start and end apart: 39, of which 23 were waited for; matrix products, arithmetic and copies ran while one was open for 15% of the time, Pallas kernels for 2%

profile of v2, /device:TPU:0, one launch (start us, length us, event | category | flops | bytes accessed | tf_op | source)
XLA Modules:
  0.0 243.4 jit_solution(4448368780626270384)
XLA Ops:
  2.9 1.3 fusion.22
  4.3 1.3 fusion.67
  5.7 2.8 %convolution_convert_fusion.2 = bf16[192,2048]{1,0:T(8,128)(2,1)} fusion(bf16[128,2048]{1,0:T(8,128)(2,1)} %param.13, f32[2048]{0:T(1024)S(1)} %bitcast.61, f32[2048]{0:T(1024)S(1)} %bitcast.62, f32[2048]{0:T(1024)S(1)} %bitcast.56, f32[2048]{0:T(1024)S(1)} %bitcast.57, f32[2048]{0:T(1024)S(1)} %bitcast.58, f32[2048]{0:T(1024)S(1)} %bitcast.59, ...), kind=kOutput, calls=%fused_computation.10 | convolution fusion | flops 104226816 | bytes 1378688 | tf_op jit(solution)/shard_map/dot_general | solution.py:120
  8.5 4.7 %all-to-all-start = ((bf16[8,24,2048]{2,1,0:T(8,128)(2,1)}), bf16[8,24,2048]{2,1,0:T(8,128)(2,1)S(1)}, u32[]{:S(2)}, u32[]{:S(2)}) async-start(bf16[8,24,2048]{2,1,0:T(8,128)(2,1)} %bitcast.44), calls=%async_computation | async-start | bytes 1572864 | tf_op jit(solution)/shard_map/all_to_all | solution.py:125
  13.7 2.8 %collective-permute-start.8 = (f32[512]{0:T(512)S(1)}, f32[512]{0:T(512)S(1)}, u32[]{:S(2)}, u32[]{:S(2)}) collective-permute-start(f32[512]{0:T(512)S(1)} %bitcast.63), channel_id=1, source_target_pairs={{0,3},{3,0},{1,2},{2,1},{4,7},{7,4},{5,6},{6,5},{8,11},{11,8},{9,1... | collective-permute-start | bytes 6152 | tf_op jit(solution)/shard_map/ppermute | solution.py:28
  16.4 2.0 collective-permute-done.8
  18.5 2.8 %collective-permute-start.9 = (bf16[2048,512]{1,0:T(8,128)(2,1)}, bf16[2048,512]{1,0:T(8,128)(2,1)}, u32[]{:S(2)}, u32[]{:S(2)}) collective-permute-start(bf16[2048,512]{1,0:T(8,128)(2,1)} %bitcast.65), channel_id=1, source_target_pairs={{0,3},{3,0},{1,2},{2,1},{4,7},{7,4},{5,6},{6,5},{8,11},{11,8},{9,1... | collective-permute-start | bytes 6291464 | tf_op jit(solution)/shard_map/ppermute | solution.py:28
  21.2 5.1 %all-to-all-done = bf16[8,24,2048]{2,1,0:T(8,128)(2,1)S(1)} async-done(((bf16[8,24,2048]{2,1,0:T(8,128)(2,1)}), bf16[8,24,2048]{2,1,0:T(8,128)(2,1)S(1)}, u32[]{:S(2)}, u32[]{:S(2)}) %all-to-all-start) | async-done | bytes 786464 | tf_op jit(solution)/shard_map/all_to_all | solution.py:125
  26.4 2.0 collective-permute-start.3
  28.4 2.2 collective-permute-start.4
  30.6 1.5 collective-permute-start.5
  32.3 7.1 %collective-permute-done.3 = bf16[96,2048]{1,0:T(8,128)(2,1)S(1)} collective-permute-done((bf16[96,2048]{1,0:T(8,128)(2,1)S(1)}, bf16[96,2048]{1,0:T(8,128)(2,1)S(1)}, u32[]{:S(2)}, u32[]{:S(2)}) %collective-permute-start.3) | collective-permute-done | bytes 393248 | tf_op jit(solution)/shard_map/ppermute | solution.py:20
  39.5 1.4 collective-permute-done.5
  41.0 1.9 collective-permute-start.7
  42.9 1.5 collective-permute-start.11
  44.4 6.4 %collective-permute-done.6 = bf16[96,2048]{1,0:T(8,128)(2,1)S(1)} collective-permute-done((bf16[96,2048]{1,0:T(8,128)(2,1)S(1)}, bf16[96,2048]{1,0:T(8,128)(2,1)S(1)}, u32[]{:S(2)}, u32[]{:S(2)}) %collective-permute-start.6) | collective-permute-done | bytes 393248 | tf_op jit(solution)/shard_map/ppermute | solution.py:20
  50.9 2.2 on_chip.2
  53.1 2.0 copy-done.2
  55.1 2.2 on_chip.3
  57.3 2.0 copy-done
  59.3 1.4 collective-permute-start.12
  60.8 5.7 %collective-permute-done.9 = bf16[2048,512]{1,0:T(8,128)(2,1)} collective-permute-done((bf16[2048,512]{1,0:T(8,128)(2,1)}, bf16[2048,512]{1,0:T(8,128)(2,1)}, u32[]{:S(2)}, u32[]{:S(2)}) %collective-permute-start.9) | collective-permute-done | bytes 2097184 | tf_op jit(solution)/shard_map/ppermute | solution.py:28
  66.5 2.8 %collective-permute-start.14 = (bf16[512,1024]{1,0:T(8,128)(2,1)S(1)}, bf16[512,1024]{1,0:T(8,128)(2,1)S(1)}, u32[]{:S(2)}, u32[]{:S(2)}) collective-permute-start(bf16[512,1024]{1,0:T(8,128)(2,1)S(1)} %get-tuple-element.53), channel_id=1, source_target_pairs={{0,3},{3,0},{1,2},{2,1},{4,7},{7,4},{5,6},{6,5},{8,11},{11,8},{9,1... | collective-permute-start | bytes 3145736 | tf_op jit(solution)/shard_map/ppermute | solution.py:28
  69.2 4.0 %collective-permute-start.13 = (bf16[192,2048]{1,0:T(8,128)(2,1)S(1)}, bf16[192,2048]{1,0:T(8,128)(2,1)S(1)}, u32[]{:S(2)}, u32[]{:S(2)}) collective-permute-start(bf16[192,2048]{1,0:T(8,128)(2,1)S(1)} %collective-permute-done.7), channel_id=1, source_target_pairs={{0,12},{4,0},{8,4},{12,8},{1,13},{5,1},{9,5},{13,9},{2,14},{6,2},{... | collective-permute-start | bytes 2359304 | tf_op jit(solution)/shard_map/ppermute | solution.py:20
  74.3 3.6 %collective-permute-done.12 = bf16[96,2048]{1,0:T(8,128)(2,1)S(1)} collective-permute-done((bf16[96,2048]{1,0:T(8,128)(2,1)S(1)}, bf16[96,2048]{1,0:T(8,128)(2,1)S(1)}, u32[]{:S(2)}, u32[]{:S(2)}) %collective-permute-start.12) | collective-permute-done | bytes 393248 | tf_op jit(solution)/shard_map/ppermute | solution.py:24
  77.9 10.1 %collective-permute-done.13 = bf16[192,2048]{1,0:T(8,128)(2,1)S(1)} collective-permute-done((bf16[192,2048]{1,0:T(8,128)(2,1)S(1)}, bf16[192,2048]{1,0:T(8,128)(2,1)S(1)}, u32[]{:S(2)}, u32[]{:S(2)}) %collective-permute-start.13) | collective-permute-done | bytes 786464 | tf_op jit(solution)/shard_map/ppermute | solution.py:20
  88.1 7.3 %maximum_convert_fusion = bf16[1536,1024]{1,0:T(8,128)(2,1)S(1)} fusion(bf16[1536,2048]{1,0:T(8,128)(2,1)S(1)} %constant_dynamic-update-slice_fusion, bf16[2048,512]{1,0:T(8,128)(2,1)} %collective-permute-done.9, bf16[2048,512]{1,0:T(8,128)(2,1)S(1)} %bitcast.66, f32[1024]{0:T(1024)S(1)} %pad_maximum_fusion.12), kind=kOutput, calls=%fused_computation | convolution fusion | flops 6455558144 | bytes 13635584 | tf_op jit(solution)/shard_map/dot_general | solution.py:154
  95.4 3.8 %convolution_convert_fusion.1 = bf16[1536,1024]{1,0:T(8,128)(2,1)S(1)} fusion(bf16[1536,1024]{1,0:T(8,128)(2,1)S(1)} %maximum_convert_fusion, bf16[512,1024]{1,0:T(8,128)(2,1)S(1)} %collective-permute-done.14, bf16[512,1024]{1,0:T(8,128)(2,1)S(1)} %get-tuple-element.53), kind=kOutput, calls=%fused_computation.5 | convolution fusion | flops 3226992640 | bytes 8388608 | tf_op jit(solution)/shard_map/dot_general | solution.py:158
  100.3 3.2 %collective-permute-start.15 = (bf16[384,1024]{1,0:T(8,128)(2,1)S(1)}, bf16[384,1024]{1,0:T(8,128)(2,1)S(1)}, u32[]{:S(2)}, u32[]{:S(2)}) collective-permute-start(bf16[384,1024]{1,0:T(8,128)(2,1)S(1)} %pad_maximum_fusion.4), channel_id=1, source_target_pairs={{0,12},{4,0},{8,4},{12,8},{1,13},{5,1},{9,5},{13,9},{2,14},{6,2},{... | collective-permute-start | bytes 2359304 | tf_op jit(solution)/shard_map/ppermute | solution.py:20
  103.5 9.7 %collective-permute-done.17 = bf16[512,1024]{1,0:T(8,128)(2,1)S(1)} collective-permute-done((bf16[512,1024]{1,0:T(8,128)(2,1)S(1)}, bf16[512,1024]{1,0:T(8,128)(2,1)S(1)}, u32[]{:S(2)}, u32[]{:S(2)}) %collective-permute-start.17) | collective-permute-done | bytes 1048608 | tf_op jit(solution)/shard_map/ppermute | solution.py:28
  113.2 4.7 %collective-permute-done.16 = bf16[384,1024]{1,0:T(8,128)(2,1)S(1)} collective-permute-done((bf16[384,1024]{1,0:T(8,128)(2,1)S(1)}, bf16[384,1024]{1,0:T(8,128)(2,1)S(1)}, u32[]{:S(2)}, u32[]{:S(2)}) %collective-permute-start.16) | collective-permute-done | bytes 786464 | tf_op jit(solution)/shard_map/ppermute | solution.py:20
  118.2 3.2 %collective-permute-start.20 = (bf16[384,1024]{1,0:T(8,128)(2,1)S(1)}, bf16[384,1024]{1,0:T(8,128)(2,1)S(1)}, u32[]{:S(2)}, u32[]{:S(2)}) collective-permute-start(bf16[384,1024]{1,0:T(8,128)(2,1)S(1)} %add_convert_fusion.1), channel_id=1, source_target_pairs={{0,12},{4,0},{8,4},{12,8},{1,13},{5,1},{9,5},{13,9},{2,14},{6,2},{... | collective-permute-start | bytes 2359304 | tf_op jit(solution)/shard_map/ppermute | solution.py:20
  121.4 3.8 %convolution_convert_fusion = bf16[1536,1024]{1,0:T(8,128)(2,1)S(1)} fusion(bf16[1536,1024]{1,0:T(8,128)(2,1)S(1)} %maximum_convert_fusion, bf16[512,1024]{1,0:T(8,128)(2,1)S(1)} %collective-permute-done.17, bf16[512,1024]{1,0:T(8,128)(2,1)S(1)} %get-tuple-element.54), kind=kOutput, calls=%fused_computation.4 | convolution fusion | flops 3226992640 | bytes 8388608 | tf_op jit(solution)/shard_map/dot_general | solution.py:158
  125.7 9.4 %collective-permute-done.20 = bf16[384,1024]{1,0:T(8,128)(2,1)S(1)} collective-permute-done((bf16[384,1024]{1,0:T(8,128)(2,1)S(1)}, bf16[384,1024]{1,0:T(8,128)(2,1)S(1)}, u32[]{:S(2)}, u32[]{:S(2)}) %collective-permute-start.20) | collective-permute-done | bytes 786464 | tf_op jit(solution)/shard_map/ppermute | solution.py:20
  135.8 3.3 %collective-permute-start.18 = (bf16[384,1024]{1,0:T(8,128)(2,1)S(1)}, bf16[384,1024]{1,0:T(8,128)(2,1)S(1)}, u32[]{:S(2)}, u32[]{:S(2)}) collective-permute-start(bf16[384,1024]{1,0:T(8,128)(2,1)S(1)} %pad_maximum_fusion.6), channel_id=1, source_target_pairs={{0,12},{4,0},{8,4},{12,8},{1,13},{5,1},{9,5},{13,9},{2,14},{6,2},{... | collective-permute-start | bytes 2359304 | tf_op jit(solution)/shard_map/ppermute | solution.py:20
  139.1 3.1 %collective-permute-done.19 = bf16[384,1024]{1,0:T(8,128)(2,1)S(1)} collective-permute-done((bf16[384,1024]{1,0:T(8,128)(2,1)S(1)}, bf16[384,1024]{1,0:T(8,128)(2,1)S(1)}, u32[]{:S(2)}, u32[]{:S(2)}) %collective-permute-start.19) | collective-permute-done | bytes 786464 | tf_op jit(solution)/shard_map/ppermute | solution.py:20
  142.2 1.3 collective-permute-done.21
  143.8 2.6 %collective-permute-start.22 = (bf16[384,1024]{1,0:T(8,128)(2,1)S(1)}, bf16[384,1024]{1,0:T(8,128)(2,1)}, u32[]{:S(2)}, u32[]{:S(2)}) collective-permute-start(bf16[384,1024]{1,0:T(8,128)(2,1)S(1)} %add_convert_fusion), channel_id=1, source_target_pairs={{0,4},{4,8},{8,12},{12,0},{1,5},{5,9},{9,13},{13,1},{2,6},{6,10},{... | collective-permute-start | bytes 2359304 | tf_op jit(solution)/shard_map/ppermute | solution.py:20
  147.2 5.2 %all-to-all-start.1 = ((bf16[8,24,1024]{2,1,0:T(8,128)(2,1)}), bf16[8,24,1024]{2,1,0:T(8,128)(2,1)S(1)}, u32[]{:S(2)}, u32[]{:S(2)}) async-start(bf16[8,24,1024]{2,1,0:T(8,128)(2,1)} %bitcast.14), calls=%async_computation.1 | async-start | bytes 786432 | tf_op jit(solution)/shard_map/all_to_all | solution.py:125
  152.4 6.5 %collective-permute-done.22 = bf16[384,1024]{1,0:T(8,128)(2,1)} collective-permute-done((bf16[384,1024]{1,0:T(8,128)(2,1)S(1)}, bf16[384,1024]{1,0:T(8,128)(2,1)}, u32[]{:S(2)}, u32[]{:S(2)}) %collective-permute-start.22) | collective-permute-done | bytes 786464 | tf_op jit(solution)/shard_map/ppermute | solution.py:20
  158.9 1.6 convert_add_fusion
  161.5 10.6 %collective-permute-done.23 = bf16[192,1024]{1,0:T(8,128)(2,1)S(1)} collective-permute-done((bf16[192,1024]{1,0:T(8,128)(2,1)S(1)}, bf16[192,1024]{1,0:T(8,128)(2,1)S(1)}, u32[]{:S(2)}, u32[]{:S(2)}) %collective-permute-start.23) | collective-permute-done | bytes 393248 | tf_op jit(solution)/shard_map/ppermute | solution.py:24
  172.9 3.5 %all-to-all-start.2 = ((bf16[8,24,1024]{2,1,0:T(8,128)(2,1)}), bf16[8,24,1024]{2,1,0:T(8,128)(2,1)S(1)}, u32[]{:S(2)}, u32[]{:S(2)}) async-start(bf16[8,24,1024]{2,1,0:T(8,128)(2,1)} %bitcast.16), calls=%async_computation.2 | async-start | bytes 786432 | tf_op jit(solution)/shard_map/all_to_all | solution.py:125
  176.5 8.8 %all-to-all-done.2 = bf16[8,24,1024]{2,1,0:T(8,128)(2,1)S(1)} async-done(((bf16[8,24,1024]{2,1,0:T(8,128)(2,1)}), bf16[8,24,1024]{2,1,0:T(8,128)(2,1)S(1)}, u32[]{:S(2)}, u32[]{:S(2)}) %all-to-all-start.2) | async-done | bytes 393248 | tf_op jit(solution)/shard_map/all_to_all | solution.py:125
  187.3 2.7 %collective-permute-start.25 = (bf16[64,2048]{1,0:T(8,128)(2,1)S(1)}, bf16[64,2048]{1,0:T(8,128)(2,1)S(1)}, u32[]{:S(2)}, u32[]{:S(2)}) collective-permute-start(bf16[64,2048]{1,0:T(8,128)(2,1)S(1)} %get-tuple-element.115), channel_id=1, source_target_pairs={{0,96},{32,0},{64,32},{96,64},{1,97},{33,1},{65,33},{97,65},{2,98}... | collective-permute-start | bytes 786440 | tf_op jit(solution)/shard_map/ppermute | solution.py:20
  190.0 5.8 %collective-permute-done.24 = bf16[64,2048]{1,0:T(8,128)(2,1)S(1)} collective-permute-done((bf16[64,2048]{1,0:T(8,128)(2,1)S(1)}, bf16[64,2048]{1,0:T(8,128)(2,1)S(1)}, u32[]{:S(2)}, u32[]{:S(2)}) %collective-permute-start.24) | collective-permute-done | bytes 262176 | tf_op jit(solution)/shard_map/ppermute | solution.py:20
  195.8 3.2 %collective-permute-start.27 = (bf16[64,2048]{1,0:T(8,128)(2,1)S(1)}, bf16[64,2048]{1,0:T(8,128)(2,1)S(1)}, u32[]{:S(2)}, u32[]{:S(2)}) collective-permute-start(bf16[64,2048]{1,0:T(8,128)(2,1)S(1)} %get-tuple-element.70), channel_id=1, source_target_pairs={{0,96},{32,0},{64,32},{96,64},{1,97},{33,1},{65,33},{97,65},{2,98}... | collective-permute-start | bytes 786440 | tf_op jit(solution)/shard_map/ppermute | solution.py:20
  199.1 4.9 %collective-permute-done.26 = bf16[64,2048]{1,0:T(8,128)(2,1)S(1)} collective-permute-done((bf16[64,2048]{1,0:T(8,128)(2,1)S(1)}, bf16[64,2048]{1,0:T(8,128)(2,1)S(1)}, u32[]{:S(2)}, u32[]{:S(2)}) %collective-permute-start.26) | collective-permute-done | bytes 262176 | tf_op jit(solution)/shard_map/ppermute | solution.py:20
  204.0 1.3 fusion.16
  205.3 2.1 fusion.17
  207.5 1.3 fusion.69
  209.6 1.3 fusion.3
  210.9 2.5 %collective-permute-start.29 = (bf16[64,2048]{1,0:T(8,128)(2,1)S(1)}, bf16[64,2048]{1,0:T(8,128)(2,1)S(1)}, u32[]{:S(2)}, u32[]{:S(2)}) collective-permute-start(bf16[64,2048]{1,0:T(8,128)(2,1)S(1)} %collective-permute-done.27), channel_id=1, source_target_pairs={{0,96},{32,0},{64,32},{96,64},{1,97},{33,1},{65,33},{97,65},{2,98}... | collective-permute-start | bytes 786440 | tf_op jit(solution)/shard_map/ppermute | solution.py:20
  213.5 2.0 collective-permute-start.31
  215.6 4.3 %collective-permute-done.29 = bf16[64,2048]{1,0:T(8,128)(2,1)S(1)} collective-permute-done((bf16[64,2048]{1,0:T(8,128)(2,1)S(1)}, bf16[64,2048]{1,0:T(8,128)(2,1)S(1)}, u32[]{:S(2)}, u32[]{:S(2)}) %collective-permute-start.29) | collective-permute-done | bytes 262176 | tf_op jit(solution)/shard_map/ppermute | solution.py:20
  219.8 1.9 fusion.19
  221.8 1.3 fusion.18
  223.2 1.3 fusion.70
  224.4 1.3 fusion.4
  225.9 3.4 %collective-permute-start.32 = (bf16[64,2048]{1,0:T(8,128)(2,1)S(1)}, bf16[64,2048]{1,0:T(8,128)(2,1)S(1)}, u32[]{:S(2)}, u32[]{:S(2)}) collective-permute-start(bf16[64,2048]{1,0:T(8,128)(2,1)S(1)} %add_convert_fusion.4), channel_id=1, source_target_pairs={{0,96},{32,0},{64,32},{96,64},{1,97},{33,1},{65,33},{97,65},{2,98}... | collective-permute-start | bytes 786440 | tf_op jit(solution)/shard_map/ppermute | solution.py:20
  229.3 1.9 collective-permute-start.33
  231.2 3.0 %collective-permute-done.34 = bf16[64,2048]{1,0:T(8,128)(2,1)S(1)} collective-permute-done((bf16[64,2048]{1,0:T(8,128)(2,1)S(1)}, bf16[64,2048]{1,0:T(8,128)(2,1)S(1)}, u32[]{:S(2)}, u32[]{:S(2)}) %collective-permute-start.34) | collective-permute-done | bytes 262176 | tf_op jit(solution)/shard_map/ppermute | solution.py:20
  234.5 2.3 collective-permute-done.33
  236.8 5.5 %collective-permute-done.35 = bf16[64,2048]{1,0:T(8,128)(2,1)S(1)} collective-permute-done((bf16[64,2048]{1,0:T(8,128)(2,1)S(1)}, bf16[64,2048]{1,0:T(8,128)(2,1)S(1)}, u32[]{:S(2)}, u32[]{:S(2)}) %collective-permute-start.35) | collective-permute-done | bytes 262176 | tf_op jit(solution)/shard_map/ppermute | solution.py:20
  (126 shorter events, 15.1 us)
Async XLA Ops:
  0.0 26.3 %collective-permute-start = (bf16[2048,1024]{1,0:T(8,128)(2,1)}, bf16[2048,1024]{1,0:T(8,128)(2,1)}, u32[]{:S(2)}, u32[]{:S(2)}) collective-permute-start(bf16[2048,1024]{1,0:T(8,128)(2,1)} %param.22), channel_id=1, source_target_pairs={{0,16},{16,0},{1,17},{17,1},{2,18},{18,2},{3,19},{19,3},{4,20},{20... | collective-permute-start | bytes 12582920 | tf_op jit(solution)/shard_map/ppermute | solution.py:32
  0.0 26.3 %collective-permute-start.1 = (bf16[1024,2048]{1,0:T(8,128)(2,1)}, bf16[1024,2048]{1,0:T(8,128)(2,1)}, u32[]{:S(2)}, u32[]{:S(2)}) collective-permute-start(bf16[1024,2048]{1,0:T(8,128)(2,1)} %param.24), channel_id=1, source_target_pairs={{0,16},{16,0},{1,17},{17,1},{2,18},{18,2},{3,19},{19,3},{4,20},{20... | collective-permute-start | bytes 12582920 | tf_op jit(solution)/shard_map/ppermute | solution.py:32
  4.3 4.2 %copy-start.21 = (s32[128]{0:T(128)}, s32[128]{0:T(128)S(1)}, u32[]{:S(2)}) copy-start(s32[128]{0:T(128)S(1)} %multiply_add_fusion) | copy-start | bytes 1540
  4.3 4.1 %copy-start.10 = (pred[128]{0:T(512)(128)(4,1)}, pred[128]{0:T(512)(128)(4,1)S(1)}, u32[]{:S(2)}) copy-start(pred[128]{0:T(512)(128)(4,1)S(1)} %get-tuple-element.137) | copy-start | bytes 388
  4.3 4.1 %copy-start.12 = (pred[128]{0:T(512)(128)(4,1)}, pred[128]{0:T(512)(128)(4,1)S(1)}, u32[]{:S(2)}) copy-start(pred[128]{0:T(512)(128)(4,1)S(1)} %get-tuple-element.138) | copy-start | bytes 388
  4.3 4.1 %copy-start.14 = (pred[128]{0:T(512)(128)(4,1)}, pred[128]{0:T(512)(128)(4,1)S(1)}, u32[]{:S(2)}) copy-start(pred[128]{0:T(512)(128)(4,1)S(1)} %get-tuple-element.139) | copy-start | bytes 388
  5.6 7.5 %copy-start.19 = (f32[1024]{0:T(1024)S(1)}, f32[1024]{0:T(1024)}, u32[]{:S(2)}) copy-start(f32[1024]{0:T(1024)} %param.23) | copy-start | bytes 12292
  5.6 8.0 %copy-start.9 = (f32[1,512]{1,0:T(1,128)S(1)}, f32[1,512]{1,0:T(1,128)}, u32[]{:S(2)}) copy-start(f32[1,512]{1,0:T(1,128)} %param.18) | copy-start | bytes 6148
  8.5 23.6 %copy-start.4 = (bf16[1,512,2048]{2,1,0:T(8,128)(2,1)S(1)}, bf16[1,512,2048]{2,1,0:T(8,128)(2,1)}, u32[]{:S(2)}) copy-start(bf16[1,512,2048]{2,1,0:T(8,128)(2,1)} %param.19) | copy-start | bytes 6291460
  8.5 17.9 %all-to-all-start = ((bf16[8,24,2048]{2,1,0:T(8,128)(2,1)}), bf16[8,24,2048]{2,1,0:T(8,128)(2,1)S(1)}, u32[]{:S(2)}, u32[]{:S(2)}) async-start(bf16[8,24,2048]{2,1,0:T(8,128)(2,1)} %bitcast.44), calls=%async_computation | async-start | bytes 1572864 | tf_op jit(solution)/shard_map/all_to_all | solution.py:125
  13.2 8.1 %collective-permute-start.2 = (f32[1024]{0:T(1024)S(1)}, f32[1024]{0:T(1024)}, u32[]{:S(2)}, u32[]{:S(2)}) collective-permute-start(f32[1024]{0:T(1024)S(1)} %copy-done.19), channel_id=1, source_target_pairs={{0,16},{16,0},{1,17},{17,1},{2,18},{18,2},{3,19},{19,3},{4,20},{20... | collective-permute-start | bytes 12296 | tf_op jit(solution)/shard_map/ppermute | solution.py:32
  13.7 4.8 %collective-permute-start.8 = (f32[512]{0:T(512)S(1)}, f32[512]{0:T(512)S(1)}, u32[]{:S(2)}, u32[]{:S(2)}) collective-permute-start(f32[512]{0:T(512)S(1)} %bitcast.63), channel_id=1, source_target_pairs={{0,3},{3,0},{1,2},{2,1},{4,7},{7,4},{5,6},{6,5},{8,11},{11,8},{9,1... | collective-permute-start | bytes 6152 | tf_op jit(solution)/shard_map/ppermute | solution.py:28
  18.5 48.0 %collective-permute-start.9 = (bf16[2048,512]{1,0:T(8,128)(2,1)}, bf16[2048,512]{1,0:T(8,128)(2,1)}, u32[]{:S(2)}, u32[]{:S(2)}) collective-permute-start(bf16[2048,512]{1,0:T(8,128)(2,1)} %bitcast.65), channel_id=1, source_target_pairs={{0,3},{3,0},{1,2},{2,1},{4,7},{7,4},{5,6},{6,5},{8,11},{11,8},{9,1... | collective-permute-start | bytes 6291464 | tf_op jit(solution)/shard_map/ppermute | solution.py:28
  26.4 13.0 %collective-permute-start.3 = (bf16[96,2048]{1,0:T(8,128)(2,1)S(1)}, bf16[96,2048]{1,0:T(8,128)(2,1)S(1)}, u32[]{:S(2)}, u32[]{:S(2)}) collective-permute-start(bf16[96,2048]{1,0:T(8,128)(2,1)S(1)} %get-tuple-element.114), channel_id=1, source_target_pairs={{0,4},{4,8},{8,12},{12,0},{1,5},{5,9},{9,13},{13,1},{2,6},{6,10},{... | collective-permute-start | bytes 1179656 | tf_op jit(solution)/shard_map/ppermute | solution.py:20
  28.4 11.0 %collective-permute-start.4 = (bf16[96,2048]{1,0:T(8,128)(2,1)S(1)}, bf16[96,2048]{1,0:T(8,128)(2,1)S(1)}, u32[]{:S(2)}, u32[]{:S(2)}) collective-permute-start(bf16[96,2048]{1,0:T(8,128)(2,1)S(1)} %get-tuple-element.114), channel_id=1, source_target_pairs={{0,12},{4,0},{8,4},{12,8},{1,13},{5,1},{9,5},{13,9},{2,14},{6,2},{... | collective-permute-start | bytes 1179656 | tf_op jit(solution)/shard_map/ppermute | solution.py:20
  30.6 10.4 %collective-permute-start.5 = (bf16[96,2048]{1,0:T(8,128)(2,1)S(1)}, bf16[96,2048]{1,0:T(8,128)(2,1)S(1)}, u32[]{:S(2)}, u32[]{:S(2)}) collective-permute-start(bf16[96,2048]{1,0:T(8,128)(2,1)S(1)} %get-tuple-element.113), channel_id=1, source_target_pairs={{0,1},{1,0},{2,3},{3,2},{4,5},{5,4},{6,7},{7,6},{8,9},{9,8},{10,11... | collective-permute-start | bytes 1179656 | tf_op jit(solution)/shard_map/ppermute | solution.py:24
  39.4 11.4 %collective-permute-start.6 = (bf16[96,2048]{1,0:T(8,128)(2,1)S(1)}, bf16[96,2048]{1,0:T(8,128)(2,1)S(1)}, u32[]{:S(2)}, u32[]{:S(2)}) collective-permute-start(bf16[96,2048]{1,0:T(8,128)(2,1)S(1)} %collective-permute-done.3), channel_id=1, source_target_pairs={{0,4},{4,8},{8,12},{12,0},{1,5},{5,9},{9,13},{13,1},{2,6},{6,10},{... | collective-permute-start | bytes 1179656 | tf_op jit(solution)/shard_map/ppermute | solution.py:20
  41.0 28.2 %collective-permute-start.7 = (bf16[192,2048]{1,0:T(8,128)(2,1)S(1)}, bf16[192,2048]{1,0:T(8,128)(2,1)S(1)}, u32[]{:S(2)}, u32[]{:S(2)}) collective-permute-start(bf16[192,2048]{1,0:T(8,128)(2,1)S(1)} %pad_maximum_fusion.3), channel_id=1, source_target_pairs={{0,12},{4,0},{8,4},{12,8},{1,13},{5,1},{9,5},{13,9},{2,14},{6,2},{... | collective-permute-start | bytes 2359304 | tf_op jit(solution)/shard_map/ppermute | solution.py:20
  42.9 31.3 %collective-permute-start.11 = (bf16[288,2048]{1,0:T(8,128)(2,1)S(1)}, bf16[288,2048]{1,0:T(8,128)(2,1)S(1)}, u32[]{:S(2)}, u32[]{:S(2)}) collective-permute-start(bf16[288,2048]{1,0:T(8,128)(2,1)S(1)} %pad_maximum_fusion), channel_id=1, source_target_pairs={{0,1},{1,0},{2,3},{3,2},{4,5},{5,4},{6,7},{7,6},{8,9},{9,8},{10,11... | collective-permute-start | bytes 3538952 | tf_op jit(solution)/shard_map/ppermute | solution.py:24
  50.8 22.6 %collective-permute-start.10 = (bf16[192,2048]{1,0:T(8,128)(2,1)S(1)}, bf16[192,2048]{1,0:T(8,128)(2,1)S(1)}, u32[]{:S(2)}, u32[]{:S(2)}) collective-permute-start(bf16[192,2048]{1,0:T(8,128)(2,1)S(1)} %pad_maximum_fusion.3), channel_id=1, source_target_pairs={{0,4},{4,8},{8,12},{12,0},{1,5},{5,9},{9,13},{13,1},{2,6},{6,10},{... | collective-permute-start | bytes 2359304 | tf_op jit(solution)/shard_map/ppermute | solution.py:20
  53.1 2.0 copy-start.2
  57.3 2.0 copy-start
  59.3 18.6 %collective-permute-start.12 = (bf16[96,2048]{1,0:T(8,128)(2,1)S(1)}, bf16[96,2048]{1,0:T(8,128)(2,1)S(1)}, u32[]{:S(2)}, u32[]{:S(2)}) collective-permute-start(bf16[96,2048]{1,0:T(8,128)(2,1)S(1)} %collective-permute-done.6), channel_id=1, source_target_pairs={{0,1},{1,0},{2,3},{3,2},{4,5},{5,4},{6,7},{7,6},{8,9},{9,8},{10,11... | collective-permute-start | bytes 1179656 | tf_op jit(solution)/shard_map/ppermute | solution.py:24
  66.5 28.9 %collective-permute-start.14 = (bf16[512,1024]{1,0:T(8,128)(2,1)S(1)}, bf16[512,1024]{1,0:T(8,128)(2,1)S(1)}, u32[]{:S(2)}, u32[]{:S(2)}) collective-permute-start(bf16[512,1024]{1,0:T(8,128)(2,1)S(1)} %get-tuple-element.53), channel_id=1, source_target_pairs={{0,3},{3,0},{1,2},{2,1},{4,7},{7,4},{5,6},{6,5},{8,11},{11,8},{9,1... | collective-permute-start | bytes 3145736 | tf_op jit(solution)/shard_map/ppermute | solution.py:28
  69.2 18.7 %collective-permute-start.13 = (bf16[192,2048]{1,0:T(8,128)(2,1)S(1)}, bf16[192,2048]{1,0:T(8,128)(2,1)S(1)}, u32[]{:S(2)}, u32[]{:S(2)}) collective-permute-start(bf16[192,2048]{1,0:T(8,128)(2,1)S(1)} %collective-permute-done.7), channel_id=1, source_target_pairs={{0,12},{4,0},{8,4},{12,8},{1,13},{5,1},{9,5},{13,9},{2,14},{6,2},{... | collective-permute-start | bytes 2359304 | tf_op jit(solution)/shard_map/ppermute | solution.py:20
  73.4 39.9 %collective-permute-start.17 = (bf16[512,1024]{1,0:T(8,128)(2,1)S(1)}, bf16[512,1024]{1,0:T(8,128)(2,1)S(1)}, u32[]{:S(2)}, u32[]{:S(2)}) collective-permute-start(bf16[512,1024]{1,0:T(8,128)(2,1)S(1)} %get-tuple-element.54), channel_id=1, source_target_pairs={{0,3},{3,0},{1,2},{2,1},{4,7},{7,4},{5,6},{6,5},{8,11},{11,8},{9,1... | collective-permute-start | bytes 3145736 | tf_op jit(solution)/shard_map/ppermute | solution.py:28
  74.2 13.9 %copy-start.18 = (bf16[1,2048,512]{2,1,0:T(8,128)(2,1)S(1)}, bf16[1,2048,512]{2,1,0:T(8,128)(2,1)}, u32[]{:S(2)}) copy-start(bf16[1,2048,512]{2,1,0:T(8,128)(2,1)} %param.17) | copy-start | bytes 6291460
  99.6 18.3 %collective-permute-start.16 = (bf16[384,1024]{1,0:T(8,128)(2,1)S(1)}, bf16[384,1024]{1,0:T(8,128)(2,1)S(1)}, u32[]{:S(2)}, u32[]{:S(2)}) collective-permute-start(bf16[384,1024]{1,0:T(8,128)(2,1)S(1)} %pad_maximum_fusion.5), channel_id=1, source_target_pairs={{0,4},{4,8},{8,12},{12,0},{1,5},{5,9},{9,13},{13,1},{2,6},{6,10},{... | collective-permute-start | bytes 2359304 | tf_op jit(solution)/shard_map/ppermute | solution.py:20
  100.3 17.6 %collective-permute-start.15 = (bf16[384,1024]{1,0:T(8,128)(2,1)S(1)}, bf16[384,1024]{1,0:T(8,128)(2,1)S(1)}, u32[]{:S(2)}, u32[]{:S(2)}) collective-permute-start(bf16[384,1024]{1,0:T(8,128)(2,1)S(1)} %pad_maximum_fusion.4), channel_id=1, source_target_pairs={{0,12},{4,0},{8,4},{12,8},{1,13},{5,1},{9,5},{13,9},{2,14},{6,2},{... | collective-permute-start | bytes 2359304 | tf_op jit(solution)/shard_map/ppermute | solution.py:20
  118.2 16.9 %collective-permute-start.20 = (bf16[384,1024]{1,0:T(8,128)(2,1)S(1)}, bf16[384,1024]{1,0:T(8,128)(2,1)S(1)}, u32[]{:S(2)}, u32[]{:S(2)}) collective-permute-start(bf16[384,1024]{1,0:T(8,128)(2,1)S(1)} %add_convert_fusion.1), channel_id=1, source_target_pairs={{0,12},{4,0},{8,4},{12,8},{1,13},{5,1},{9,5},{13,9},{2,14},{6,2},{... | collective-permute-start | bytes 2359304 | tf_op jit(solution)/shard_map/ppermute | solution.py:20
  125.6 16.6 %collective-permute-start.19 = (bf16[384,1024]{1,0:T(8,128)(2,1)S(1)}, bf16[384,1024]{1,0:T(8,128)(2,1)S(1)}, u32[]{:S(2)}, u32[]{:S(2)}) collective-permute-start(bf16[384,1024]{1,0:T(8,128)(2,1)S(1)} %pad_maximum_fusion.7), channel_id=1, source_target_pairs={{0,4},{4,8},{8,12},{12,0},{1,5},{5,9},{9,13},{13,1},{2,6},{6,10},{... | collective-permute-start | bytes 2359304 | tf_op jit(solution)/shard_map/ppermute | solution.py:20
  135.6 7.9 %collective-permute-start.21 = (bf16[192,1024]{1,0:T(8,128)(2,1)S(1)}, bf16[192,1024]{1,0:T(8,128)(2,1)S(1)}, u32[]{:S(2)}, u32[]{:S(2)}) collective-permute-start(bf16[192,1024]{1,0:T(8,128)(2,1)S(1)} %slice.280), channel_id=1, source_target_pairs={{0,1},{1,0},{2,3},{3,2},{4,5},{5,4},{6,7},{7,6},{8,9},{9,8},{10,11... | collective-permute-start | bytes 1179656 | tf_op jit(solution)/shard_map/ppermute | solution.py:24
  135.8 16.6 %collective-permute-start.18 = (bf16[384,1024]{1,0:T(8,128)(2,1)S(1)}, bf16[384,1024]{1,0:T(8,128)(2,1)S(1)}, u32[]{:S(2)}, u32[]{:S(2)}) collective-permute-start(bf16[384,1024]{1,0:T(8,128)(2,1)S(1)} %pad_maximum_fusion.6), channel_id=1, source_target_pairs={{0,12},{4,0},{8,4},{12,8},{1,13},{5,1},{9,5},{13,9},{2,14},{6,2},{... | collective-permute-start | bytes 2359304 | tf_op jit(solution)/shard_map/ppermute | solution.py:20
  143.8 15.1 %collective-permute-start.22 = (bf16[384,1024]{1,0:T(8,128)(2,1)S(1)}, bf16[384,1024]{1,0:T(8,128)(2,1)}, u32[]{:S(2)}, u32[]{:S(2)}) collective-permute-start(bf16[384,1024]{1,0:T(8,128)(2,1)S(1)} %add_convert_fusion), channel_id=1, source_target_pairs={{0,4},{4,8},{8,12},{12,0},{1,5},{5,9},{9,13},{13,1},{2,6},{6,10},{... | collective-permute-start | bytes 2359304 | tf_op jit(solution)/shard_map/ppermute | solution.py:20
  147.2 14.1 %all-to-all-start.1 = ((bf16[8,24,1024]{2,1,0:T(8,128)(2,1)}), bf16[8,24,1024]{2,1,0:T(8,128)(2,1)S(1)}, u32[]{:S(2)}, u32[]{:S(2)}) async-start(bf16[8,24,1024]{2,1,0:T(8,128)(2,1)} %bitcast.14), calls=%async_computation.1 | async-start | bytes 786432 | tf_op jit(solution)/shard_map/all_to_all | solution.py:125
  160.4 16.0 %copy-start.6 = (f32[8,2048]{1,0:T(8,128)S(1)}, f32[8,2048]{1,0:T(8,128)}, u32[]{:S(2)}) copy-start(f32[8,2048]{1,0:T(8,128)} %param.20) | copy-start | bytes 196612
  160.5 24.8 %copy-start.5 = (bf16[128,2048]{1,0:T(8,128)(2,1)S(1)}, bf16[128,2048]{1,0:T(8,128)(2,1)}, u32[]{:S(2)}) copy-start(bf16[128,2048]{1,0:T(8,128)(2,1)} %param.13) | copy-start | bytes 1572868
  160.5 24.8 %copy-start.11 = (pred[128]{0:T(512)(128)(4,1)S(1)}, pred[128]{0:T(512)(128)(4,1)}, u32[]{:S(2)}) copy-start(pred[128]{0:T(512)(128)(4,1)} %copy-done.10) | copy-start | bytes 388
  160.5 24.8 %copy-start.13 = (pred[128]{0:T(512)(128)(4,1)S(1)}, pred[128]{0:T(512)(128)(4,1)}, u32[]{:S(2)}) copy-start(pred[128]{0:T(512)(128)(4,1)} %copy-done.12) | copy-start | bytes 388
  160.5 24.8 %copy-start.15 = (pred[128]{0:T(512)(128)(4,1)S(1)}, pred[128]{0:T(512)(128)(4,1)}, u32[]{:S(2)}) copy-start(pred[128]{0:T(512)(128)(4,1)} %copy-done.14) | copy-start | bytes 388
  160.5 24.8 %copy-start.22 = (s32[128]{0:T(128)S(1)}, s32[128]{0:T(128)}, u32[]{:S(2)}) copy-start(s32[128]{0:T(128)} %copy-done.21) | copy-start | bytes 1540
  161.4 10.7 %collective-permute-start.23 = (bf16[192,1024]{1,0:T(8,128)(2,1)S(1)}, bf16[192,1024]{1,0:T(8,128)(2,1)S(1)}, u32[]{:S(2)}, u32[]{:S(2)}) collective-permute-start(bf16[192,1024]{1,0:T(8,128)(2,1)S(1)} %slice.279), channel_id=1, source_target_pairs={{0,1},{1,0},{2,3},{3,2},{4,5},{5,4},{6,7},{7,6},{8,9},{9,8},{10,11... | collective-permute-start | bytes 1179656 | tf_op jit(solution)/shard_map/ppermute | solution.py:24
  172.9 12.3 %all-to-all-start.2 = ((bf16[8,24,1024]{2,1,0:T(8,128)(2,1)}), bf16[8,24,1024]{2,1,0:T(8,128)(2,1)S(1)}, u32[]{:S(2)}, u32[]{:S(2)}) async-start(bf16[8,24,1024]{2,1,0:T(8,128)(2,1)} %bitcast.16), calls=%async_computation.2 | async-start | bytes 786432 | tf_op jit(solution)/shard_map/all_to_all | solution.py:125
  185.3 1.1 copy-start.7
  185.3 18.7 %copy-start.16 = (bf16[2048,1024]{1,0:T(8,128)(2,1)S(1)}, bf16[2048,1024]{1,0:T(8,128)(2,1)}, u32[]{:S(2)}) copy-start(bf16[2048,1024]{1,0:T(8,128)(2,1)} %param.22) | copy-start | bytes 12582916
  186.1 17.8 %copy-start.20 = (f32[1024]{0:T(1024)S(1)}, f32[1024]{0:T(1024)}, u32[]{:S(2)}) copy-start(f32[1024]{0:T(1024)} %param.23) | copy-start | bytes 12292
  186.7 9.1 %collective-permute-start.24 = (bf16[64,2048]{1,0:T(8,128)(2,1)S(1)}, bf16[64,2048]{1,0:T(8,128)(2,1)S(1)}, u32[]{:S(2)}, u32[]{:S(2)}) collective-permute-start(bf16[64,2048]{1,0:T(8,128)(2,1)S(1)} %get-tuple-element.115), channel_id=1, source_target_pairs={{0,32},{32,64},{64,96},{96,0},{1,33},{33,65},{65,97},{97,1},{2,34}... | collective-permute-start | bytes 786440 | tf_op jit(solution)/shard_map/ppermute | solution.py:20
  187.3 8.5 %collective-permute-start.25 = (bf16[64,2048]{1,0:T(8,128)(2,1)S(1)}, bf16[64,2048]{1,0:T(8,128)(2,1)S(1)}, u32[]{:S(2)}, u32[]{:S(2)}) collective-permute-start(bf16[64,2048]{1,0:T(8,128)(2,1)S(1)} %get-tuple-element.115), channel_id=1, source_target_pairs={{0,96},{32,0},{64,32},{96,64},{1,97},{33,1},{65,33},{97,65},{2,98}... | collective-permute-start | bytes 786440 | tf_op jit(solution)/shard_map/ppermute | solution.py:20
  195.8 8.2 %collective-permute-start.26 = (bf16[64,2048]{1,0:T(8,128)(2,1)S(1)}, bf16[64,2048]{1,0:T(8,128)(2,1)S(1)}, u32[]{:S(2)}, u32[]{:S(2)}) collective-permute-start(bf16[64,2048]{1,0:T(8,128)(2,1)S(1)} %collective-permute-done.24), channel_id=1, source_target_pairs={{0,32},{32,64},{64,96},{96,0},{1,33},{33,65},{65,97},{97,1},{2,34}... | collective-permute-start | bytes 786440 | tf_op jit(solution)/shard_map/ppermute | solution.py:20
  195.8 9.4 %copy-start.3 = (bf16[2048,1024]{1,0:T(8,128)(2,1)S(1)}, bf16[2048,1024]{1,0:T(8,128)(2,1)}, u32[]{:S(2)}) copy-start(bf16[2048,1024]{1,0:T(8,128)(2,1)} %copy-done.2) | copy-start | bytes 12582916
  195.8 11.6 %collective-permute-start.27 = (bf16[64,2048]{1,0:T(8,128)(2,1)S(1)}, bf16[64,2048]{1,0:T(8,128)(2,1)S(1)}, u32[]{:S(2)}, u32[]{:S(2)}) collective-permute-start(bf16[64,2048]{1,0:T(8,128)(2,1)S(1)} %get-tuple-element.70), channel_id=1, source_target_pairs={{0,96},{32,0},{64,32},{96,64},{1,97},{33,1},{65,33},{97,65},{2,98}... | collective-permute-start | bytes 786440 | tf_op jit(solution)/shard_map/ppermute | solution.py:20
  205.3 2.2 copy-start.1
  207.4 2.2 copy-start.17
  207.4 8.1 %collective-permute-start.28 = (bf16[64,2048]{1,0:T(8,128)(2,1)S(1)}, bf16[64,2048]{1,0:T(8,128)(2,1)S(1)}, u32[]{:S(2)}, u32[]{:S(2)}) collective-permute-start(bf16[64,2048]{1,0:T(8,128)(2,1)S(1)} %get-tuple-element.70), channel_id=1, source_target_pairs={{0,32},{32,64},{64,96},{96,0},{1,33},{33,65},{65,97},{97,1},{2,34}... | collective-permute-start | bytes 786440 | tf_op jit(solution)/shard_map/ppermute | solution.py:20
  210.9 8.9 %collective-permute-start.29 = (bf16[64,2048]{1,0:T(8,128)(2,1)S(1)}, bf16[64,2048]{1,0:T(8,128)(2,1)S(1)}, u32[]{:S(2)}, u32[]{:S(2)}) collective-permute-start(bf16[64,2048]{1,0:T(8,128)(2,1)S(1)} %collective-permute-done.27), channel_id=1, source_target_pairs={{0,96},{32,0},{64,32},{96,64},{1,97},{33,1},{65,33},{97,65},{2,98}... | collective-permute-start | bytes 786440 | tf_op jit(solution)/shard_map/ppermute | solution.py:20
  213.5 9.6 %collective-permute-start.30 = (bf16[64,2048]{1,0:T(8,128)(2,1)S(1)}, bf16[64,2048]{1,0:T(8,128)(2,1)S(1)}, u32[]{:S(2)}, u32[]{:S(2)}) collective-permute-start(bf16[64,2048]{1,0:T(8,128)(2,1)S(1)} %get-tuple-element.112), channel_id=1, source_target_pairs={{0,96},{32,0},{64,32},{96,64},{1,97},{33,1},{65,33},{97,65},{2,98}... | collective-permute-start | bytes 786440 | tf_op jit(solution)/shard_map/ppermute | solution.py:20
  213.5 9.6 %collective-permute-start.31 = (bf16[64,2048]{1,0:T(8,128)(2,1)S(1)}, bf16[64,2048]{1,0:T(8,128)(2,1)S(1)}, u32[]{:S(2)}, u32[]{:S(2)}) collective-permute-start(bf16[64,2048]{1,0:T(8,128)(2,1)S(1)} %get-tuple-element.111), channel_id=1, source_target_pairs={{0,32},{32,64},{64,96},{96,0},{1,33},{33,65},{65,97},{97,1},{2,34}... | collective-permute-start | bytes 786440 | tf_op jit(solution)/shard_map/ppermute | solution.py:20
  225.7 16.7 %copy-start.8 = (f32[2048]{0:T(1024)S(1)}, f32[2048]{0:T(1024)}, u32[]{:S(2)}) copy-start(f32[2048]{0:T(1024)} %param.25) | copy-start | bytes 24580
  225.8 8.4 %collective-permute-start.34 = (bf16[64,2048]{1,0:T(8,128)(2,1)S(1)}, bf16[64,2048]{1,0:T(8,128)(2,1)S(1)}, u32[]{:S(2)}, u32[]{:S(2)}) collective-permute-start(bf16[64,2048]{1,0:T(8,128)(2,1)S(1)} %get-tuple-element.110), channel_id=1, source_target_pairs={{0,32},{32,64},{64,96},{96,0},{1,33},{33,65},{65,97},{97,1},{2,34}... | collective-permute-start | bytes 786440 | tf_op jit(solution)/shard_map/ppermute | solution.py:20
  225.9 8.5 %collective-permute-start.32 = (bf16[64,2048]{1,0:T(8,128)(2,1)S(1)}, bf16[64,2048]{1,0:T(8,128)(2,1)S(1)}, u32[]{:S(2)}, u32[]{:S(2)}) collective-permute-start(bf16[64,2048]{1,0:T(8,128)(2,1)S(1)} %add_convert_fusion.4), channel_id=1, source_target_pairs={{0,96},{32,0},{64,32},{96,64},{1,97},{33,1},{65,33},{97,65},{2,98}... | collective-permute-start | bytes 786440 | tf_op jit(solution)/shard_map/ppermute | solution.py:20
  229.3 7.5 %collective-permute-start.33 = (bf16[64,2048]{1,0:T(8,128)(2,1)S(1)}, bf16[64,2048]{1,0:T(8,128)(2,1)S(1)}, u32[]{:S(2)}, u32[]{:S(2)}) collective-permute-start(bf16[64,2048]{1,0:T(8,128)(2,1)S(1)} %get-tuple-element.109), channel_id=1, source_target_pairs={{0,96},{32,0},{64,32},{96,64},{1,97},{33,1},{65,33},{97,65},{2,98}... | collective-permute-start | bytes 786440 | tf_op jit(solution)/shard_map/ppermute | solution.py:20
  234.3 8.1 %collective-permute-start.35 = (bf16[64,2048]{1,0:T(8,128)(2,1)S(1)}, bf16[64,2048]{1,0:T(8,128)(2,1)S(1)}, u32[]{:S(2)}, u32[]{:S(2)}) collective-permute-start(bf16[64,2048]{1,0:T(8,128)(2,1)S(1)} %add_convert_fusion.3), channel_id=1, source_target_pairs={{0,32},{32,64},{64,96},{96,0},{1,33},{33,65},{65,97},{97,1},{2,34}... | collective-permute-start | bytes 786440 | tf_op jit(solution)/shard_map/ppermute | solution.py:20

commit v3 on v2

--- a/solution.py
+++ b/solution.py
@@ -96,8 +96,8 @@
     capacity = 3 * tok_dev // (2 * num_groups)
     bf16 = jnp.bfloat16
 
-    half_model = width_model // 2
-    left, right = group_w2[0, :, :half_model], group_w2[0, :, half_model:]
+    cut = 5 * width_model // 8
+    left, right = group_w2[0, :, :cut], group_w2[0, :, cut:]
     w1_out, b1_pair = hold(group_w1[0], swap_blocks(group_b1[0]))
     w1_pair = swap_blocks(w1_out)
 
@@ -140,18 +140,24 @@
     b_prev = shift(held, "z", 1)
     sw1_pair, sw2_pair, _ = hold(sw1_pair, sw2_pair, b_own)
     sw1_pair, sw2_pair = on_chip(sw1_pair), on_chip(sw2_pair)
-    b_foll, w1_pair, sw1_pair, sw2_pair = hold(b_foll, w1_pair, sw1_pair, sw2_pair)
     b_far = shift(b_foll, "z", -1)
     near_pair = swap_column(a_near)
-    far_pair = swap_column(a_far)
+    far_out, near_pair = hold(a_far, near_pair)
+    far_pair = swap_column(far_out)
     left_out, _ = hold(left, a_far)
+    w1_pair, near_pair, sw1_pair, sw2_pair = hold(w1_pair, near_pair, sw1_pair, sw2_pair)
     left_pair = swap_blocks(left_out)
-    right_out, _, _ = hold(right, w1_pair, b_prev)
+    right_out, _ = hold(right, b_prev)
     right_pair = swap_blocks(right_out)
     w1 = jnp.concatenate([group_w1[0], w1_pair], axis=1)
     b1 = jnp.concatenate([group_b1[0], b1_pair])
-    rows = jnp.concatenate([a_near, a_far, b_own, b_foll, b_prev, near_pair, far_pair, b_far], axis=0)
-    hidden = down(jax.nn.relu(jnp.dot(rows, w1, preferred_element_type=jnp.float32) + b1))
+    early = jnp.concatenate([a_near, a_far, b_own, b_foll, b_prev, near_pair], axis=0)
+    late = jnp.concatenate([far_pair, b_far], axis=0)
+
+    def first(rows):
+        return down(jax.nn.relu(jnp.dot(rows, w1, preferred_element_type=jnp.float32) + b1))
+
+    hidden = jnp.concatenate([first(early), first(late)], axis=0)
 
     def second(hidden, weight, weight_pair):
         weight = jnp.concatenate([weight, weight_pair], axis=0)

time: 244 us -> 253 us (1.037)
  waiting for transfers between devices: 122 us -> 130 us
    ppermute x4, waiting for transfers between devices: 17.5 us -> 29.9 us  [swap_blocks(): return lax.ppermute(value, X, [(0, 3), (3, 0), (1, 2), (2, 1)])]
    ppermute x24, waiting for transfers between devices: 73.3 us -> 65.7 us  [shift(): lax.ppermute(value, axis, [(i, (i + step) % size) for i in range(size)])]
    all_to_all x3, waiting for transfers between devices: 14.7 us -> 17.5 us  [exchange(): lax.all_to_all(value, ('y', 'core'), split_axis=0, concat_axis=0, tiled=T...]
    dot_general x1 -> x2, matrix products: 7.31 us -> 8.98 us  [first(): jnp.dot(rows, w1, preferred_element_type=jnp.float32) + b1]
    unnamed x53 -> x55, local copies, waits for them, and re-layouts: 5.31 us -> 5.38 us
  transfers between devices with their start and end apart: 39 -> 39, of which waited for: 23 -> 25; matrix products, arithmetic and copies ran while one was open for 15% -> 12% of each run, Pallas kernels for 2% -> 2%
where the time goes in v3:
time: 253 us; the launch traced here: 251 us
  waiting for transfers between devices  130 us (51%)
  starting transfers between devices  67.3 us (27%)
  matrix products  32 us (13%)
  other arithmetic  8.73 us (3%)
  local copies, waits for them, and re-layouts  7.66 us (3%)
  Pallas kernels  4.38 us (2%)
    ppermute x24, waiting for transfers between devices, shift(): lax.ppermute(value, axis, [(i, (i + step) % size) for i in range(size)])  65.7 us
    ppermute x24, starting transfers between devices, shift(): lax.ppermute(value, axis, [(i, (i + step) % size) for i in range(size)])  38.1 us
    ppermute x4, waiting for transfers between devices, swap_blocks(): return lax.ppermute(value, X, [(0, 3), (3, 0), (1, 2), (2, 1)])  29.9 us
    all_to_all x3, waiting for transfers between devices, exchange(): lax.all_to_all(value, ('y', 'core'), split_axis=0, concat_axis=0, tiled=T...  17.5 us
    ppermute x5, waiting for transfers between devices, swap_column(): return lax.ppermute(value, 'xl', [(0, 1), (1, 0)])  17 us
    all_to_all x3, starting transfers between devices, exchange(): lax.all_to_all(value, ('y', 'core'), split_axis=0, concat_axis=0, tiled=T...  13.4 us
    ppermute x4, starting transfers between devices, swap_blocks(): return lax.ppermute(value, X, [(0, 3), (3, 0), (1, 2), (2, 1)])  11.1 us
    dot_general x2, matrix products, first(): jnp.dot(rows, w1, preferred_element_type=jnp.float32) + b1  8.98 us
  transfers between devices with their start and end apart: 39, of which 25 were waited for; matrix products, arithmetic and copies ran while one was open for 12% of the time, Pallas kernels for 2%

profile of v3, /device:TPU:0, one launch (start us, length us, event | category | flops | bytes accessed | tf_op | source)
XLA Modules:
  0.0 250.9 jit_solution(6680671559082149776)
XLA Ops:
  2.9 1.3 fusion.26
  4.3 1.3 fusion.72
  5.7 2.8 %convolution_convert_fusion.2 = bf16[192,2048]{1,0:T(8,128)(2,1)} fusion(bf16[128,2048]{1,0:T(8,128)(2,1)} %param.13, f32[2048]{0:T(1024)S(1)} %bitcast.59, f32[2048]{0:T(1024)S(1)} %bitcast.60, f32[2048]{0:T(1024)S(1)} %bitcast.54, f32[2048]{0:T(1024)S(1)} %bitcast.55, f32[2048]{0:T(1024)S(1)} %bitcast.56, f32[2048]{0:T(1024)S(1)} %bitcast.57, ...), kind=kOutput, calls=%fused_computation.13 | convolution fusion | flops 104226816 | bytes 1378688 | tf_op jit(solution)/shard_map/dot_general | solution.py:120
  8.5 4.7 %all-to-all-start = ((bf16[8,24,2048]{2,1,0:T(8,128)(2,1)}), bf16[8,24,2048]{2,1,0:T(8,128)(2,1)S(1)}, u32[]{:S(2)}, u32[]{:S(2)}) async-start(bf16[8,24,2048]{2,1,0:T(8,128)(2,1)} %bitcast.43), calls=%async_computation | async-start | bytes 1572864 | tf_op jit(solution)/shard_map/all_to_all | solution.py:125
  13.7 2.8 %collective-permute-start.9 = (f32[512]{0:T(512)S(1)}, f32[512]{0:T(512)S(1)}, u32[]{:S(2)}, u32[]{:S(2)}) collective-permute-start(f32[512]{0:T(512)S(1)} %bitcast.61), channel_id=1, source_target_pairs={{0,3},{3,0},{1,2},{2,1},{4,7},{7,4},{5,6},{6,5},{8,11},{11,8},{9,1... | collective-permute-start | bytes 6152 | tf_op jit(solution)/shard_map/ppermute | solution.py:28
  16.4 2.0 collective-permute-done.9
  18.5 2.8 %collective-permute-start.10 = (bf16[2048,512]{1,0:T(8,128)(2,1)}, bf16[2048,512]{1,0:T(8,128)(2,1)}, u32[]{:S(2)}, u32[]{:S(2)}) collective-permute-start(bf16[2048,512]{1,0:T(8,128)(2,1)} %bitcast.63), channel_id=1, source_target_pairs={{0,3},{3,0},{1,2},{2,1},{4,7},{7,4},{5,6},{6,5},{8,11},{11,8},{9,1... | collective-permute-start | bytes 6291464 | tf_op jit(solution)/shard_map/ppermute | solution.py:28
  21.3 5.1 %all-to-all-done = bf16[8,24,2048]{2,1,0:T(8,128)(2,1)S(1)} async-done(((bf16[8,24,2048]{2,1,0:T(8,128)(2,1)}), bf16[8,24,2048]{2,1,0:T(8,128)(2,1)S(1)}, u32[]{:S(2)}, u32[]{:S(2)}) %all-to-all-start) | async-done | bytes 786464 | tf_op jit(solution)/shard_map/all_to_all | solution.py:125
  26.4 2.0 collective-permute-start.3
  28.4 2.2 collective-permute-start.4
  30.6 1.5 collective-permute-start.5
  32.2 7.2 %collective-permute-done.3 = bf16[96,2048]{1,0:T(8,128)(2,1)S(1)} collective-permute-done((bf16[96,2048]{1,0:T(8,128)(2,1)S(1)}, bf16[96,2048]{1,0:T(8,128)(2,1)S(1)}, u32[]{:S(2)}, u32[]{:S(2)}) %collective-permute-start.3) | collective-permute-done | bytes 393248 | tf_op jit(solution)/shard_map/ppermute | solution.py:20
  39.6 1.4 collective-permute-done.5
  41.0 1.5 collective-permute-start.11
  42.5 2.0 collective-permute-start.7
  44.5 6.3 %collective-permute-done.6 = bf16[96,2048]{1,0:T(8,128)(2,1)S(1)} collective-permute-done((bf16[96,2048]{1,0:T(8,128)(2,1)S(1)}, bf16[96,2048]{1,0:T(8,128)(2,1)S(1)}, u32[]{:S(2)}, u32[]{:S(2)}) %collective-permute-start.6) | collective-permute-done | bytes 393248 | tf_op jit(solution)/shard_map/ppermute | solution.py:20
  50.9 2.2 on_chip.2
  53.1 2.0 copy-done.2
  55.1 2.2 on_chip.3
  57.3 2.0 copy-done
  59.3 2.8 %collective-permute-start.14 = (bf16[512,1280]{1,0:T(8,128)(2,1)S(1)}, bf16[512,1280]{1,0:T(8,128)(2,1)S(1)}, u32[]{:S(2)}, u32[]{:S(2)}) collective-permute-start(bf16[512,1280]{1,0:T(8,128)(2,1)S(1)} %slice_bitcast_fusion), channel_id=1, source_target_pairs={{0,3},{3,0},{1,2},{2,1},{4,7},{7,4},{5,6},{6,5},{8,11},{11,8},{9,1... | collective-permute-start | bytes 3932168 | tf_op jit(solution)/shard_map/ppermute | solution.py:28
  62.1 3.3 %collective-permute-start.13 = (bf16[192,2048]{1,0:T(8,128)(2,1)S(1)}, bf16[192,2048]{1,0:T(8,128)(2,1)S(1)}, u32[]{:S(2)}, u32[]{:S(2)}) collective-permute-start(bf16[192,2048]{1,0:T(8,128)(2,1)S(1)} %collective-permute-done.7), channel_id=1, source_target_pairs={{0,12},{4,0},{8,4},{12,8},{1,13},{5,1},{9,5},{13,9},{2,14},{6,2},{... | collective-permute-start | bytes 2359304 | tf_op jit(solution)/shard_map/ppermute | solution.py:20
  65.5 1.9 collective-permute-done.11
  70.0 6.0 %maximum_convert_fusion = bf16[1248,1024]{1,0:T(8,128)(2,1)S(1)} fusion(bf16[1248,2048]{1,0:T(8,128)(2,1)S(1)} %constant_dynamic-update-slice_fusion, bf16[2048,512]{1,0:T(8,128)(2,1)} %collective-permute-done.10, bf16[2048,512]{1,0:T(8,128)(2,1)S(1)} %bitcast.64, f32[1024]{0:T(1024)S(1)} %pad_maximum_fusion.22), kind=kOutput, calls=%fused_computation.1 | convolution fusion | flops 5246713856 | bytes 11866112 | tf_op jit(solution)/shard_map/dot_general | solution.py:158
  76.0 4.2 %collective-permute-done.13 = bf16[192,2048]{1,0:T(8,128)(2,1)S(1)} collective-permute-done((bf16[192,2048]{1,0:T(8,128)(2,1)S(1)}, bf16[192,2048]{1,0:T(8,128)(2,1)S(1)}, u32[]{:S(2)}, u32[]{:S(2)}) %collective-permute-start.13) | collective-permute-done | bytes 786464 | tf_op jit(solution)/shard_map/ppermute | solution.py:20
  80.2 3.0 %fusion.12 = bf16[288,1024]{1,0:T(8,128)(2,1)S(1)} fusion(bf16[2048,512]{1,0:T(8,128)(2,1)} %collective-permute-done.10, bf16[2048,512]{1,0:T(8,128)(2,1)S(1)} %bitcast.65, bf16[192,2048]{1,0:T(8,128)(2,1)S(1)} %collective-permute-done.13, bf16[96,2048]{1,0:T(8,128)(2,1)S(1)} %collective-permute-done.12, f32[1024]{0:T(1024)S(1)} %pad_maximum_fusion.22), kind=kOutput, calls=%fused_computation.25 | convolution fusion | flops 1219592192 | bytes 5967872 | tf_op jit(solution)/shard_map/dot_general | solution.py:158
  83.2 11.3 %collective-permute-done.14 = bf16[512,1280]{1,0:T(8,128)(2,1)S(1)} collective-permute-done((bf16[512,1280]{1,0:T(8,128)(2,1)S(1)}, bf16[512,1280]{1,0:T(8,128)(2,1)S(1)}, u32[]{:S(2)}, u32[]{:S(2)}) %collective-permute-start.14) | collective-permute-done | bytes 1310752 | tf_op jit(solution)/shard_map/ppermute | solution.py:28
  94.5 5.2 %convolution_convert_fusion = bf16[1536,1280]{1,0:T(8,128)(2,1)S(1)} fusion(bf16[512,1280]{1,0:T(8,128)(2,1)S(1)} %collective-permute-done.14, bf16[512,1280]{1,0:T(8,128)(2,1)S(1)} %slice_bitcast_fusion, bf16[288,1024]{1,0:T(8,128)(2,1)S(1)} %fusion.12, bf16[1248,1024]{1,0:T(8,128)(2,1)S(1)} %maximum_convert_fusion), kind=kOutput, calls=%fused_computation | convolution fusion | flops 4040032256 | bytes 9699328 | tf_op jit(solution)/shard_map/dot_general | solution.py:164
  100.0 2.0 collective-permute-start.16
  102.1 2.2 collective-permute-start.15
  104.4 2.8 %collective-permute-start.17 = (bf16[512,768]{1,0:T(8,128)(2,1)S(1)}, bf16[512,768]{1,0:T(8,128)(2,1)S(1)}, u32[]{:S(2)}, u32[]{:S(2)}) collective-permute-start(bf16[512,768]{1,0:T(8,128)(2,1)S(1)} %slice_bitcast_fusion.1), channel_id=1, source_target_pairs={{0,3},{3,0},{1,2},{2,1},{4,7},{7,4},{5,6},{6,5},{8,11},{11,8},{9,1... | collective-permute-start | bytes 2359304 | tf_op jit(solution)/shard_map/ppermute | solution.py:28
  107.5 15.3 %collective-permute-done.17 = bf16[512,768]{1,0:T(8,128)(2,1)S(1)} collective-permute-done((bf16[512,768]{1,0:T(8,128)(2,1)S(1)}, bf16[512,768]{1,0:T(8,128)(2,1)S(1)}, u32[]{:S(2)}, u32[]{:S(2)}) %collective-permute-start.17) | collective-permute-done | bytes 786464 | tf_op jit(solution)/shard_map/ppermute | solution.py:28
  124.3 3.2 %collective-permute-start.20 = (bf16[384,1280]{1,0:T(8,128)(2,1)S(1)}, bf16[384,1280]{1,0:T(8,128)(2,1)S(1)}, u32[]{:S(2)}, u32[]{:S(2)}) collective-permute-start(bf16[384,1280]{1,0:T(8,128)(2,1)S(1)} %add_convert_fusion), channel_id=1, source_target_pairs={{0,12},{4,0},{8,4},{12,8},{1,13},{5,1},{9,5},{13,9},{2,14},{6,2},{... | collective-permute-start | bytes 2949128 | tf_op jit(solution)/shard_map/ppermute | solution.py:20
  127.5 2.8 %convolution_convert_fusion.1 = bf16[1536,768]{1,0:T(8,128)(2,1)S(1)} fusion(bf16[1536,1024]{1,0:T(8,128)(2,1)S(1)} %pad_maximum_fusion.1, bf16[512,768]{1,0:T(8,128)(2,1)S(1)} %collective-permute-done.17, bf16[512,768]{1,0:T(8,128)(2,1)S(1)} %slice_bitcast_fusion.1), kind=kOutput, calls=%fused_computation.3 | convolution fusion | flops 2420244480 | bytes 7077888 | tf_op jit(solution)/shard_map/dot_general | solution.py:164
  130.6 15.2 %collective-permute-done.20 = bf16[384,1280]{1,0:T(8,128)(2,1)S(1)} collective-permute-done((bf16[384,1280]{1,0:T(8,128)(2,1)S(1)}, bf16[384,1280]{1,0:T(8,128)(2,1)S(1)}, u32[]{:S(2)}, u32[]{:S(2)}) %collective-permute-start.20) | collective-permute-done | bytes 983072 | tf_op jit(solution)/shard_map/ppermute | solution.py:20
  146.3 3.8 %collective-permute-start.18 = (bf16[384,768]{1,0:T(8,128)(2,1)S(1)}, bf16[384,768]{1,0:T(8,128)(2,1)S(1)}, u32[]{:S(2)}, u32[]{:S(2)}) collective-permute-start(bf16[384,768]{1,0:T(8,128)(2,1)S(1)} %pad_maximum_fusion.16), channel_id=1, source_target_pairs={{0,12},{4,0},{8,4},{12,8},{1,13},{5,1},{9,5},{13,9},{2,14},{6,2},{... | collective-permute-start | bytes 1769480 | tf_op jit(solution)/shard_map/ppermute | solution.py:20
  150.1 5.5 %collective-permute-done.21 = bf16[192,1280]{1,0:T(8,128)(2,1)S(1)} collective-permute-done((bf16[192,1280]{1,0:T(8,128)(2,1)S(1)}, bf16[192,1280]{1,0:T(8,128)(2,1)S(1)}, u32[]{:S(2)}, u32[]{:S(2)}) %collective-permute-start.21) | collective-permute-done | bytes 491552 | tf_op jit(solution)/shard_map/ppermute | solution.py:24
  157.7 5.3 %all-to-all-start.1 = ((bf16[8,24,1280]{2,1,0:T(8,128)(2,1)}), bf16[8,24,1280]{2,1,0:T(8,128)(2,1)}, u32[]{:S(2)}, u32[]{:S(2)}) async-start(bf16[8,24,1280]{2,1,0:T(8,128)(2,1)} %bitcast.14), calls=%async_computation.1 | async-start | bytes 983040 | tf_op jit(solution)/shard_map/all_to_all | solution.py:125
  163.0 5.2 %collective-permute-done.22 = bf16[384,768]{1,0:T(8,128)(2,1)S(1)} collective-permute-done((bf16[384,768]{1,0:T(8,128)(2,1)S(1)}, bf16[384,768]{1,0:T(8,128)(2,1)S(1)}, u32[]{:S(2)}, u32[]{:S(2)}) %collective-permute-start.22) | collective-permute-done | bytes 589856 | tf_op jit(solution)/shard_map/ppermute | solution.py:20
  168.5 4.6 %all-to-all-done.1 = bf16[8,24,1280]{2,1,0:T(8,128)(2,1)} async-done(((bf16[8,24,1280]{2,1,0:T(8,128)(2,1)}), bf16[8,24,1280]{2,1,0:T(8,128)(2,1)}, u32[]{:S(2)}, u32[]{:S(2)}) %all-to-all-start.1) | async-done | bytes 491552 | tf_op jit(solution)/shard_map/all_to_all | solution.py:125
  173.5 8.3 %collective-permute-done.23 = bf16[192,768]{1,0:T(8,128)(2,1)S(1)} collective-permute-done((bf16[192,768]{1,0:T(8,128)(2,1)S(1)}, bf16[192,768]{1,0:T(8,128)(2,1)S(1)}, u32[]{:S(2)}, u32[]{:S(2)}) %collective-permute-start.23) | collective-permute-done | bytes 294944 | tf_op jit(solution)/shard_map/ppermute | solution.py:24
  182.6 3.4 %all-to-all-start.2 = ((bf16[8,24,768]{2,1,0:T(8,128)(2,1)}), bf16[8,24,768]{2,1,0:T(8,128)(2,1)S(1)}, u32[]{:S(2)}, u32[]{:S(2)}) async-start(bf16[8,24,768]{2,1,0:T(8,128)(2,1)} %bitcast.16), calls=%async_computation.2 | async-start | bytes 589824 | tf_op jit(solution)/shard_map/all_to_all | solution.py:125
  186.1 7.7 %all-to-all-done.2 = bf16[8,24,768]{2,1,0:T(8,128)(2,1)S(1)} async-done(((bf16[8,24,768]{2,1,0:T(8,128)(2,1)}), bf16[8,24,768]{2,1,0:T(8,128)(2,1)S(1)}, u32[]{:S(2)}, u32[]{:S(2)}) %all-to-all-start.2) | async-done | bytes 294944 | tf_op jit(solution)/shard_map/all_to_all | solution.py:125
  193.9 2.0 fusion.73
  197.0 2.7 %collective-permute-start.25 = (bf16[64,2048]{1,0:T(8,128)(2,1)S(1)}, bf16[64,2048]{1,0:T(8,128)(2,1)S(1)}, u32[]{:S(2)}, u32[]{:S(2)}) collective-permute-start(bf16[64,2048]{1,0:T(8,128)(2,1)S(1)} %get-tuple-element.117), channel_id=1, source_target_pairs={{0,96},{32,0},{64,32},{96,64},{1,97},{33,1},{65,33},{97,65},{2,98}... | collective-permute-start | bytes 786440 | tf_op jit(solution)/shard_map/ppermute | solution.py:20
  199.7 5.6 %collective-permute-done.24 = bf16[64,2048]{1,0:T(8,128)(2,1)S(1)} collective-permute-done((bf16[64,2048]{1,0:T(8,128)(2,1)S(1)}, bf16[64,2048]{1,0:T(8,128)(2,1)S(1)}, u32[]{:S(2)}, u32[]{:S(2)}) %collective-permute-start.24) | collective-permute-done | bytes 262176 | tf_op jit(solution)/shard_map/ppermute | solution.py:20
  205.3 3.2 %collective-permute-start.27 = (bf16[64,2048]{1,0:T(8,128)(2,1)S(1)}, bf16[64,2048]{1,0:T(8,128)(2,1)S(1)}, u32[]{:S(2)}, u32[]{:S(2)}) collective-permute-start(bf16[64,2048]{1,0:T(8,128)(2,1)S(1)} %get-tuple-element.74), channel_id=1, source_target_pairs={{0,96},{32,0},{64,32},{96,64},{1,97},{33,1},{65,33},{97,65},{2,98}... | collective-permute-start | bytes 786440 | tf_op jit(solution)/shard_map/ppermute | solution.py:20
  208.5 4.7 %collective-permute-done.26 = bf16[64,2048]{1,0:T(8,128)(2,1)S(1)} collective-permute-done((bf16[64,2048]{1,0:T(8,128)(2,1)S(1)}, bf16[64,2048]{1,0:T(8,128)(2,1)S(1)}, u32[]{:S(2)}, u32[]{:S(2)}) %collective-permute-start.26) | collective-permute-done | bytes 262176 | tf_op jit(solution)/shard_map/ppermute | solution.py:20
  213.2 1.3 fusion.17
  214.5 1.3 fusion.18
  216.7 1.3 fusion.74
  218.2 1.3 fusion.4
  219.5 2.3 collective-permute-start.29
  221.9 2.0 collective-permute-start.31
  223.9 4.3 %collective-permute-done.29 = bf16[64,2048]{1,0:T(8,128)(2,1)S(1)} collective-permute-done((bf16[64,2048]{1,0:T(8,128)(2,1)S(1)}, bf16[64,2048]{1,0:T(8,128)(2,1)S(1)}, u32[]{:S(2)}, u32[]{:S(2)}) %collective-permute-start.29) | collective-permute-done | bytes 262176 | tf_op jit(solution)/shard_map/ppermute | solution.py:20
  228.2 1.3 fusion.20
  229.5 1.3 fusion.19
  231.1 1.3 fusion.75
  232.4 1.3 fusion.5
  233.8 3.2 %collective-permute-start.32 = (bf16[64,2048]{1,0:T(8,128)(2,1)S(1)}, bf16[64,2048]{1,0:T(8,128)(2,1)S(1)}, u32[]{:S(2)}, u32[]{:S(2)}) collective-permute-start(bf16[64,2048]{1,0:T(8,128)(2,1)S(1)} %add_convert_fusion.4), channel_id=1, source_target_pairs={{0,96},{32,0},{64,32},{96,64},{1,97},{33,1},{65,33},{97,65},{2,98}... | collective-permute-start | bytes 786440 | tf_op jit(solution)/shard_map/ppermute | solution.py:20
  237.0 1.9 collective-permute-start.33
  238.9 2.9 %collective-permute-done.34 = bf16[64,2048]{1,0:T(8,128)(2,1)S(1)} collective-permute-done((bf16[64,2048]{1,0:T(8,128)(2,1)S(1)}, bf16[64,2048]{1,0:T(8,128)(2,1)S(1)}, u32[]{:S(2)}, u32[]{:S(2)}) %collective-permute-start.34) | collective-permute-done | bytes 262176 | tf_op jit(solution)/shard_map/ppermute | solution.py:20
  242.1 2.6 %collective-permute-done.33 = bf16[64,2048]{1,0:T(8,128)(2,1)S(1)} collective-permute-done((bf16[64,2048]{1,0:T(8,128)(2,1)S(1)}, bf16[64,2048]{1,0:T(8,128)(2,1)S(1)}, u32[]{:S(2)}, u32[]{:S(2)}) %collective-permute-start.33) | collective-permute-done | bytes 262176 | tf_op jit(solution)/shard_map/ppermute | solution.py:20
  244.7 5.1 %collective-permute-done.35 = bf16[64,2048]{1,0:T(8,128)(2,1)S(1)} collective-permute-done((bf16[64,2048]{1,0:T(8,128)(2,1)S(1)}, bf16[64,2048]{1,0:T(8,128)(2,1)S(1)}, u32[]{:S(2)}, u32[]{:S(2)}) %collective-permute-start.35) | collective-permute-done | bytes 262176 | tf_op jit(solution)/shard_map/ppermute | solution.py:20
  (131 shorter events, 17.4 us)
Async XLA Ops:
  0.0 26.3 %collective-permute-start = (bf16[2048,1024]{1,0:T(8,128)(2,1)}, bf16[2048,1024]{1,0:T(8,128)(2,1)}, u32[]{:S(2)}, u32[]{:S(2)}) collective-permute-start(bf16[2048,1024]{1,0:T(8,128)(2,1)} %param.22), channel_id=1, source_target_pairs={{0,16},{16,0},{1,17},{17,1},{2,18},{18,2},{3,19},{19,3},{4,20},{20... | collective-permute-start | bytes 12582920 | tf_op jit(solution)/shard_map/ppermute | solution.py:32
  0.0 26.3 %collective-permute-start.1 = (bf16[1024,2048]{1,0:T(8,128)(2,1)}, bf16[1024,2048]{1,0:T(8,128)(2,1)}, u32[]{:S(2)}, u32[]{:S(2)}) collective-permute-start(bf16[1024,2048]{1,0:T(8,128)(2,1)} %param.24), channel_id=1, source_target_pairs={{0,16},{16,0},{1,17},{17,1},{2,18},{18,2},{3,19},{19,3},{4,20},{20... | collective-permute-start | bytes 12582920 | tf_op jit(solution)/shard_map/ppermute | solution.py:32
  4.3 1.4 copy-start.23
  4.3 4.2 %copy-start.10 = (pred[128]{0:T(512)(128)(4,1)}, pred[128]{0:T(512)(128)(4,1)S(1)}, u32[]{:S(2)}) copy-start(pred[128]{0:T(512)(128)(4,1)S(1)} %get-tuple-element.139) | copy-start | bytes 388
  4.3 4.1 %copy-start.12 = (pred[128]{0:T(512)(128)(4,1)}, pred[128]{0:T(512)(128)(4,1)S(1)}, u32[]{:S(2)}) copy-start(pred[128]{0:T(512)(128)(4,1)S(1)} %get-tuple-element.140) | copy-start | bytes 388
  4.3 4.1 %copy-start.14 = (pred[128]{0:T(512)(128)(4,1)}, pred[128]{0:T(512)(128)(4,1)S(1)}, u32[]{:S(2)}) copy-start(pred[128]{0:T(512)(128)(4,1)S(1)} %get-tuple-element.141) | copy-start | bytes 388
  5.6 7.5 %copy-start.19 = (f32[1024]{0:T(1024)S(1)}, f32[1024]{0:T(1024)}, u32[]{:S(2)}) copy-start(f32[1024]{0:T(1024)} %param.23) | copy-start | bytes 12292
  5.7 8.0 %copy-start.9 = (f32[1,512]{1,0:T(1,128)S(1)}, f32[1,512]{1,0:T(1,128)}, u32[]{:S(2)}) copy-start(f32[1,512]{1,0:T(1,128)} %param.18) | copy-start | bytes 6148
  8.5 23.6 %copy-start.4 = (bf16[1,512,2048]{2,1,0:T(8,128)(2,1)S(1)}, bf16[1,512,2048]{2,1,0:T(8,128)(2,1)}, u32[]{:S(2)}) copy-start(bf16[1,512,2048]{2,1,0:T(8,128)(2,1)} %param.19) | copy-start | bytes 6291460
  8.5 17.9 %all-to-all-start = ((bf16[8,24,2048]{2,1,0:T(8,128)(2,1)}), bf16[8,24,2048]{2,1,0:T(8,128)(2,1)S(1)}, u32[]{:S(2)}, u32[]{:S(2)}) async-start(bf16[8,24,2048]{2,1,0:T(8,128)(2,1)} %bitcast.43), calls=%async_computation | async-start | bytes 1572864 | tf_op jit(solution)/shard_map/all_to_all | solution.py:125
  13.2 8.1 %collective-permute-start.2 = (f32[1024]{0:T(1024)S(1)}, f32[1024]{0:T(1024)S(1)}, u32[]{:S(2)}, u32[]{:S(2)}) collective-permute-start(f32[1024]{0:T(1024)S(1)} %copy-done.19), channel_id=1, source_target_pairs={{0,16},{16,0},{1,17},{17,1},{2,18},{18,2},{3,19},{19,3},{4,20},{20... | collective-permute-start | bytes 12296 | tf_op jit(solution)/shard_map/ppermute | solution.py:32
  13.7 4.8 %collective-permute-start.9 = (f32[512]{0:T(512)S(1)}, f32[512]{0:T(512)S(1)}, u32[]{:S(2)}, u32[]{:S(2)}) collective-permute-start(f32[512]{0:T(512)S(1)} %bitcast.61), channel_id=1, source_target_pairs={{0,3},{3,0},{1,2},{2,1},{4,7},{7,4},{5,6},{6,5},{8,11},{11,8},{9,1... | collective-permute-start | bytes 6152 | tf_op jit(solution)/shard_map/ppermute | solution.py:28
  18.5 50.1 %collective-permute-start.10 = (bf16[2048,512]{1,0:T(8,128)(2,1)}, bf16[2048,512]{1,0:T(8,128)(2,1)}, u32[]{:S(2)}, u32[]{:S(2)}) collective-permute-start(bf16[2048,512]{1,0:T(8,128)(2,1)} %bitcast.63), channel_id=1, source_target_pairs={{0,3},{3,0},{1,2},{2,1},{4,7},{7,4},{5,6},{6,5},{8,11},{11,8},{9,1... | collective-permute-start | bytes 6291464 | tf_op jit(solution)/shard_map/ppermute | solution.py:28
  21.2 11.0 %copy-start.21 = (f32[1024]{0:T(1024)}, f32[1024]{0:T(1024)S(1)}, u32[]{:S(2)}) copy-start(f32[1024]{0:T(1024)S(1)} %collective-permute-done.2) | copy-start | bytes 12292
  26.4 13.0 %collective-permute-start.3 = (bf16[96,2048]{1,0:T(8,128)(2,1)S(1)}, bf16[96,2048]{1,0:T(8,128)(2,1)S(1)}, u32[]{:S(2)}, u32[]{:S(2)}) collective-permute-start(bf16[96,2048]{1,0:T(8,128)(2,1)S(1)} %get-tuple-element.116), channel_id=1, source_target_pairs={{0,4},{4,8},{8,12},{12,0},{1,5},{5,9},{9,13},{13,1},{2,6},{6,10},{... | collective-permute-start | bytes 1179656 | tf_op jit(solution)/shard_map/ppermute | solution.py:20
  28.4 11.0 %collective-permute-start.4 = (bf16[96,2048]{1,0:T(8,128)(2,1)S(1)}, bf16[96,2048]{1,0:T(8,128)(2,1)S(1)}, u32[]{:S(2)}, u32[]{:S(2)}) collective-permute-start(bf16[96,2048]{1,0:T(8,128)(2,1)S(1)} %get-tuple-element.116), channel_id=1, source_target_pairs={{0,12},{4,0},{8,4},{12,8},{1,13},{5,1},{9,5},{13,9},{2,14},{6,2},{... | collective-permute-start | bytes 1179656 | tf_op jit(solution)/shard_map/ppermute | solution.py:20
  30.6 10.4 %collective-permute-start.5 = (bf16[96,2048]{1,0:T(8,128)(2,1)S(1)}, bf16[96,2048]{1,0:T(8,128)(2,1)S(1)}, u32[]{:S(2)}, u32[]{:S(2)}) collective-permute-start(bf16[96,2048]{1,0:T(8,128)(2,1)S(1)} %get-tuple-element.115), channel_id=1, source_target_pairs={{0,1},{1,0},{2,3},{3,2},{4,5},{5,4},{6,7},{7,6},{8,9},{9,8},{10,11... | collective-permute-start | bytes 1179656 | tf_op jit(solution)/shard_map/ppermute | solution.py:24
  39.4 11.4 %collective-permute-start.6 = (bf16[96,2048]{1,0:T(8,128)(2,1)S(1)}, bf16[96,2048]{1,0:T(8,128)(2,1)S(1)}, u32[]{:S(2)}, u32[]{:S(2)}) collective-permute-start(bf16[96,2048]{1,0:T(8,128)(2,1)S(1)} %collective-permute-done.3), channel_id=1, source_target_pairs={{0,4},{4,8},{8,12},{12,0},{1,5},{5,9},{9,13},{13,1},{2,6},{6,10},{... | collective-permute-start | bytes 1179656 | tf_op jit(solution)/shard_map/ppermute | solution.py:20
  41.0 26.4 %collective-permute-start.11 = (bf16[288,2048]{1,0:T(8,128)(2,1)S(1)}, bf16[288,2048]{1,0:T(8,128)(2,1)S(1)}, u32[]{:S(2)}, u32[]{:S(2)}) collective-permute-start(bf16[288,2048]{1,0:T(8,128)(2,1)S(1)} %pad_maximum_fusion.10), channel_id=1, source_target_pairs={{0,1},{1,0},{2,3},{3,2},{4,5},{5,4},{6,7},{7,6},{8,9},{9,8},{10,11... | collective-permute-start | bytes 3538952 | tf_op jit(solution)/shard_map/ppermute | solution.py:24
  42.5 19.6 %collective-permute-start.7 = (bf16[192,2048]{1,0:T(8,128)(2,1)S(1)}, bf16[192,2048]{1,0:T(8,128)(2,1)S(1)}, u32[]{:S(2)}, u32[]{:S(2)}) collective-permute-start(bf16[192,2048]{1,0:T(8,128)(2,1)S(1)} %pad_maximum_fusion.15), channel_id=1, source_target_pairs={{0,12},{4,0},{8,4},{12,8},{1,13},{5,1},{9,5},{13,9},{2,14},{6,2},{... | collective-permute-start | bytes 2359304 | tf_op jit(solution)/shard_map/ppermute | solution.py:20
  50.8 19.0 %collective-permute-start.8 = (bf16[192,2048]{1,0:T(8,128)(2,1)S(1)}, bf16[192,2048]{1,0:T(8,128)(2,1)S(1)}, u32[]{:S(2)}, u32[]{:S(2)}) collective-permute-start(bf16[192,2048]{1,0:T(8,128)(2,1)S(1)} %pad_maximum_fusion.15), channel_id=1, source_target_pairs={{0,4},{4,8},{8,12},{12,0},{1,5},{5,9},{9,13},{13,1},{2,6},{6,10},{... | collective-permute-start | bytes 2359304 | tf_op jit(solution)/shard_map/ppermute | solution.py:20
  53.1 2.0 copy-start.2
  57.3 2.0 copy-start
  59.3 35.2 %collective-permute-start.14 = (bf16[512,1280]{1,0:T(8,128)(2,1)S(1)}, bf16[512,1280]{1,0:T(8,128)(2,1)S(1)}, u32[]{:S(2)}, u32[]{:S(2)}) collective-permute-start(bf16[512,1280]{1,0:T(8,128)(2,1)S(1)} %slice_bitcast_fusion), channel_id=1, source_target_pairs={{0,3},{3,0},{1,2},{2,1},{4,7},{7,4},{5,6},{6,5},{8,11},{11,8},{9,1... | collective-permute-start | bytes 3932168 | tf_op jit(solution)/shard_map/ppermute | solution.py:28
  62.1 18.1 %collective-permute-start.13 = (bf16[192,2048]{1,0:T(8,128)(2,1)S(1)}, bf16[192,2048]{1,0:T(8,128)(2,1)S(1)}, u32[]{:S(2)}, u32[]{:S(2)}) collective-permute-start(bf16[192,2048]{1,0:T(8,128)(2,1)S(1)} %collective-permute-done.7), channel_id=1, source_target_pairs={{0,12},{4,0},{8,4},{12,8},{1,13},{5,1},{9,5},{13,9},{2,14},{6,2},{... | collective-permute-start | bytes 2359304 | tf_op jit(solution)/shard_map/ppermute | solution.py:20
  65.5 4.5 %copy-start.18 = (bf16[1,2048,512]{2,1,0:T(8,128)(2,1)S(1)}, bf16[1,2048,512]{2,1,0:T(8,128)(2,1)}, u32[]{:S(2)}) copy-start(bf16[1,2048,512]{2,1,0:T(8,128)(2,1)} %param.17) | copy-start | bytes 6291460
  68.6 11.6 %collective-permute-start.12 = (bf16[96,2048]{1,0:T(8,128)(2,1)S(1)}, bf16[96,2048]{1,0:T(8,128)(2,1)S(1)}, u32[]{:S(2)}, u32[]{:S(2)}) collective-permute-start(bf16[96,2048]{1,0:T(8,128)(2,1)S(1)} %collective-permute-done.6), channel_id=1, source_target_pairs={{0,1},{1,0},{2,3},{3,2},{4,5},{5,4},{6,7},{7,6},{8,9},{9,8},{10,11... | collective-permute-start | bytes 1179656 | tf_op jit(solution)/shard_map/ppermute | solution.py:24
  100.0 24.0 %collective-permute-start.16 = (bf16[384,1280]{1,0:T(8,128)(2,1)S(1)}, bf16[384,1280]{1,0:T(8,128)(2,1)S(1)}, u32[]{:S(2)}, u32[]{:S(2)}) collective-permute-start(bf16[384,1280]{1,0:T(8,128)(2,1)S(1)} %pad_maximum_fusion.14), channel_id=1, source_target_pairs={{0,4},{4,8},{8,12},{12,0},{1,5},{5,9},{9,13},{13,1},{2,6},{6,10},{... | collective-permute-start | bytes 2949128 | tf_op jit(solution)/shard_map/ppermute | solution.py:20
  102.1 22.0 %collective-permute-start.15 = (bf16[384,1280]{1,0:T(8,128)(2,1)S(1)}, bf16[384,1280]{1,0:T(8,128)(2,1)S(1)}, u32[]{:S(2)}, u32[]{:S(2)}) collective-permute-start(bf16[384,1280]{1,0:T(8,128)(2,1)S(1)} %pad_maximum_fusion.13), channel_id=1, source_target_pairs={{0,12},{4,0},{8,4},{12,8},{1,13},{5,1},{9,5},{13,9},{2,14},{6,2},{... | collective-permute-start | bytes 2949128 | tf_op jit(solution)/shard_map/ppermute | solution.py:20
  104.4 18.5 %collective-permute-start.17 = (bf16[512,768]{1,0:T(8,128)(2,1)S(1)}, bf16[512,768]{1,0:T(8,128)(2,1)S(1)}, u32[]{:S(2)}, u32[]{:S(2)}) collective-permute-start(bf16[512,768]{1,0:T(8,128)(2,1)S(1)} %slice_bitcast_fusion.1), channel_id=1, source_target_pairs={{0,3},{3,0},{1,2},{2,1},{4,7},{7,4},{5,6},{6,5},{8,11},{11,8},{9,1... | collective-permute-start | bytes 2359304 | tf_op jit(solution)/shard_map/ppermute | solution.py:28
  124.3 21.4 %collective-permute-start.20 = (bf16[384,1280]{1,0:T(8,128)(2,1)S(1)}, bf16[384,1280]{1,0:T(8,128)(2,1)S(1)}, u32[]{:S(2)}, u32[]{:S(2)}) collective-permute-start(bf16[384,1280]{1,0:T(8,128)(2,1)S(1)} %add_convert_fusion), channel_id=1, source_target_pairs={{0,12},{4,0},{8,4},{12,8},{1,13},{5,1},{9,5},{13,9},{2,14},{6,2},{... | collective-permute-start | bytes 2949128 | tf_op jit(solution)/shard_map/ppermute | solution.py:20
  130.6 19.5 %collective-permute-start.19 = (bf16[384,768]{1,0:T(8,128)(2,1)S(1)}, bf16[384,768]{1,0:T(8,128)(2,1)S(1)}, u32[]{:S(2)}, u32[]{:S(2)}) collective-permute-start(bf16[384,768]{1,0:T(8,128)(2,1)S(1)} %pad_maximum_fusion.17), channel_id=1, source_target_pairs={{0,4},{4,8},{8,12},{12,0},{1,5},{5,9},{9,13},{13,1},{2,6},{6,10},{... | collective-permute-start | bytes 1769480 | tf_op jit(solution)/shard_map/ppermute | solution.py:20
  146.2 9.4 %collective-permute-start.21 = (bf16[192,1280]{1,0:T(8,128)(2,1)S(1)}, bf16[192,1280]{1,0:T(8,128)(2,1)S(1)}, u32[]{:S(2)}, u32[]{:S(2)}) collective-permute-start(bf16[192,1280]{1,0:T(8,128)(2,1)S(1)} %slice.279), channel_id=1, source_target_pairs={{0,1},{1,0},{2,3},{3,2},{4,5},{5,4},{6,7},{7,6},{8,9},{9,8},{10,11... | collective-permute-start | bytes 1474568 | tf_op jit(solution)/shard_map/ppermute | solution.py:24
  146.3 16.7 %collective-permute-start.18 = (bf16[384,768]{1,0:T(8,128)(2,1)S(1)}, bf16[384,768]{1,0:T(8,128)(2,1)S(1)}, u32[]{:S(2)}, u32[]{:S(2)}) collective-permute-start(bf16[384,768]{1,0:T(8,128)(2,1)S(1)} %pad_maximum_fusion.16), channel_id=1, source_target_pairs={{0,12},{4,0},{8,4},{12,8},{1,13},{5,1},{9,5},{13,9},{2,14},{6,2},{... | collective-permute-start | bytes 1769480 | tf_op jit(solution)/shard_map/ppermute | solution.py:20
  155.7 12.5 %collective-permute-start.22 = (bf16[384,768]{1,0:T(8,128)(2,1)S(1)}, bf16[384,768]{1,0:T(8,128)(2,1)S(1)}, u32[]{:S(2)}, u32[]{:S(2)}) collective-permute-start(bf16[384,768]{1,0:T(8,128)(2,1)S(1)} %add_convert_fusion.1), channel_id=1, source_target_pairs={{0,4},{4,8},{8,12},{12,0},{1,5},{5,9},{9,13},{13,1},{2,6},{6,10},{... | collective-permute-start | bytes 1769480 | tf_op jit(solution)/shard_map/ppermute | solution.py:20
  157.7 15.4 %all-to-all-start.1 = ((bf16[8,24,1280]{2,1,0:T(8,128)(2,1)}), bf16[8,24,1280]{2,1,0:T(8,128)(2,1)}, u32[]{:S(2)}, u32[]{:S(2)}) async-start(bf16[8,24,1280]{2,1,0:T(8,128)(2,1)} %bitcast.14), calls=%async_computation.1 | async-start | bytes 983040 | tf_op jit(solution)/shard_map/all_to_all | solution.py:125
  168.2 17.8 %copy-start.6 = (f32[8,2048]{1,0:T(8,128)S(1)}, f32[8,2048]{1,0:T(8,128)}, u32[]{:S(2)}) copy-start(f32[8,2048]{1,0:T(8,128)} %param.20) | copy-start | bytes 196612
  168.2 25.6 %copy-start.5 = (bf16[128,2048]{1,0:T(8,128)(2,1)S(1)}, bf16[128,2048]{1,0:T(8,128)(2,1)}, u32[]{:S(2)}) copy-start(bf16[128,2048]{1,0:T(8,128)(2,1)} %param.13) | copy-start | bytes 1572868
  168.4 25.4 %copy-start.11 = (pred[128]{0:T(512)(128)(4,1)S(1)}, pred[128]{0:T(512)(128)(4,1)}, u32[]{:S(2)}) copy-start(pred[128]{0:T(512)(128)(4,1)} %copy-done.10) | copy-start | bytes 388
  168.4 25.4 %copy-start.13 = (pred[128]{0:T(512)(128)(4,1)S(1)}, pred[128]{0:T(512)(128)(4,1)}, u32[]{:S(2)}) copy-start(pred[128]{0:T(512)(128)(4,1)} %copy-done.12) | copy-start | bytes 388
  168.4 25.4 %copy-start.15 = (pred[128]{0:T(512)(128)(4,1)S(1)}, pred[128]{0:T(512)(128)(4,1)}, u32[]{:S(2)}) copy-start(pred[128]{0:T(512)(128)(4,1)} %copy-done.14) | copy-start | bytes 388
  168.5 25.4 %copy-start.24 = (s32[128]{0:T(128)S(1)}, s32[128]{0:T(128)}, u32[]{:S(2)}) copy-start(s32[128]{0:T(128)} %copy-done.23) | copy-start | bytes 1540
  173.2 8.6 %collective-permute-start.23 = (bf16[192,768]{1,0:T(8,128)(2,1)S(1)}, bf16[192,768]{1,0:T(8,128)(2,1)S(1)}, u32[]{:S(2)}, u32[]{:S(2)}) collective-permute-start(bf16[192,768]{1,0:T(8,128)(2,1)S(1)} %slice.280), channel_id=1, source_target_pairs={{0,1},{1,0},{2,3},{3,2},{4,5},{5,4},{6,7},{7,6},{8,9},{9,8},{10,11... | collective-permute-start | bytes 884744 | tf_op jit(solution)/shard_map/ppermute | solution.py:24
  182.6 11.2 %all-to-all-start.2 = ((bf16[8,24,768]{2,1,0:T(8,128)(2,1)}), bf16[8,24,768]{2,1,0:T(8,128)(2,1)S(1)}, u32[]{:S(2)}, u32[]{:S(2)}) async-start(bf16[8,24,768]{2,1,0:T(8,128)(2,1)} %bitcast.16), calls=%async_computation.2 | async-start | bytes 589824 | tf_op jit(solution)/shard_map/all_to_all | solution.py:125
  193.8 2.3 copy-start.7
  193.8 19.4 %copy-start.16 = (bf16[2048,1024]{1,0:T(8,128)(2,1)S(1)}, bf16[2048,1024]{1,0:T(8,128)(2,1)}, u32[]{:S(2)}) copy-start(bf16[2048,1024]{1,0:T(8,128)(2,1)} %param.22) | copy-start | bytes 12582916
  195.8 17.4 %copy-start.20 = (f32[1024]{0:T(1024)S(1)}, f32[1024]{0:T(1024)}, u32[]{:S(2)}) copy-start(f32[1024]{0:T(1024)} %param.23) | copy-start | bytes 12292
  196.4 8.9 %collective-permute-start.24 = (bf16[64,2048]{1,0:T(8,128)(2,1)S(1)}, bf16[64,2048]{1,0:T(8,128)(2,1)S(1)}, u32[]{:S(2)}, u32[]{:S(2)}) collective-permute-start(bf16[64,2048]{1,0:T(8,128)(2,1)S(1)} %get-tuple-element.117), channel_id=1, source_target_pairs={{0,32},{32,64},{64,96},{96,0},{1,33},{33,65},{65,97},{97,1},{2,34}... | collective-permute-start | bytes 786440 | tf_op jit(solution)/shard_map/ppermute | solution.py:20
  197.0 8.3 %collective-permute-start.25 = (bf16[64,2048]{1,0:T(8,128)(2,1)S(1)}, bf16[64,2048]{1,0:T(8,128)(2,1)S(1)}, u32[]{:S(2)}, u32[]{:S(2)}) collective-permute-start(bf16[64,2048]{1,0:T(8,128)(2,1)S(1)} %get-tuple-element.117), channel_id=1, source_target_pairs={{0,96},{32,0},{64,32},{96,64},{1,97},{33,1},{65,33},{97,65},{2,98}... | collective-permute-start | bytes 786440 | tf_op jit(solution)/shard_map/ppermute | solution.py:20
  205.3 7.9 %collective-permute-start.26 = (bf16[64,2048]{1,0:T(8,128)(2,1)S(1)}, bf16[64,2048]{1,0:T(8,128)(2,1)S(1)}, u32[]{:S(2)}, u32[]{:S(2)}) collective-permute-start(bf16[64,2048]{1,0:T(8,128)(2,1)S(1)} %collective-permute-done.24), channel_id=1, source_target_pairs={{0,32},{32,64},{64,96},{96,0},{1,33},{33,65},{65,97},{97,1},{2,34}... | collective-permute-start | bytes 786440 | tf_op jit(solution)/shard_map/ppermute | solution.py:20
  205.3 9.2 %copy-start.3 = (bf16[2048,1024]{1,0:T(8,128)(2,1)S(1)}, bf16[2048,1024]{1,0:T(8,128)(2,1)}, u32[]{:S(2)}) copy-start(bf16[2048,1024]{1,0:T(8,128)(2,1)} %copy-done.2) | copy-start | bytes 12582916
  205.3 9.2 %copy-start.22 = (f32[1024]{0:T(1024)S(1)}, f32[1024]{0:T(1024)}, u32[]{:S(2)}) copy-start(f32[1024]{0:T(1024)} %copy-done.21) | copy-start | bytes 12292
  205.3 10.5 %collective-permute-start.27 = (bf16[64,2048]{1,0:T(8,128)(2,1)S(1)}, bf16[64,2048]{1,0:T(8,128)(2,1)S(1)}, u32[]{:S(2)}, u32[]{:S(2)}) collective-permute-start(bf16[64,2048]{1,0:T(8,128)(2,1)S(1)} %get-tuple-element.74), channel_id=1, source_target_pairs={{0,96},{32,0},{64,32},{96,64},{1,97},{33,1},{65,33},{97,65},{2,98}... | collective-permute-start | bytes 786440 | tf_op jit(solution)/shard_map/ppermute | solution.py:20
  214.5 2.2 copy-start.1
  215.8 2.4 copy-start.17
  215.8 8.1 %collective-permute-start.28 = (bf16[64,2048]{1,0:T(8,128)(2,1)S(1)}, bf16[64,2048]{1,0:T(8,128)(2,1)S(1)}, u32[]{:S(2)}, u32[]{:S(2)}) collective-permute-start(bf16[64,2048]{1,0:T(8,128)(2,1)S(1)} %get-tuple-element.74), channel_id=1, source_target_pairs={{0,32},{32,64},{64,96},{96,0},{1,33},{33,65},{65,97},{97,1},{2,34}... | collective-permute-start | bytes 786440 | tf_op jit(solution)/shard_map/ppermute | solution.py:20
  219.5 8.7 %collective-permute-start.29 = (bf16[64,2048]{1,0:T(8,128)(2,1)S(1)}, bf16[64,2048]{1,0:T(8,128)(2,1)S(1)}, u32[]{:S(2)}, u32[]{:S(2)}) collective-permute-start(bf16[64,2048]{1,0:T(8,128)(2,1)S(1)} %collective-permute-done.27), channel_id=1, source_target_pairs={{0,96},{32,0},{64,32},{96,64},{1,97},{33,1},{65,33},{97,65},{2,98}... | collective-permute-start | bytes 786440 | tf_op jit(solution)/shard_map/ppermute | solution.py:20
  221.8 9.2 %collective-permute-start.30 = (bf16[64,2048]{1,0:T(8,128)(2,1)S(1)}, bf16[64,2048]{1,0:T(8,128)(2,1)S(1)}, u32[]{:S(2)}, u32[]{:S(2)}) collective-permute-start(bf16[64,2048]{1,0:T(8,128)(2,1)S(1)} %get-tuple-element.114), channel_id=1, source_target_pairs={{0,96},{32,0},{64,32},{96,64},{1,97},{33,1},{65,33},{97,65},{2,98}... | collective-permute-start | bytes 786440 | tf_op jit(solution)/shard_map/ppermute | solution.py:20
  221.9 9.2 %collective-permute-start.31 = (bf16[64,2048]{1,0:T(8,128)(2,1)S(1)}, bf16[64,2048]{1,0:T(8,128)(2,1)S(1)}, u32[]{:S(2)}, u32[]{:S(2)}) collective-permute-start(bf16[64,2048]{1,0:T(8,128)(2,1)S(1)} %get-tuple-element.113), channel_id=1, source_target_pairs={{0,32},{32,64},{64,96},{96,0},{1,33},{33,65},{65,97},{97,1},{2,34}... | collective-permute-start | bytes 786440 | tf_op jit(solution)/shard_map/ppermute | solution.py:20
  233.7 16.3 %copy-start.8 = (f32[2048]{0:T(1024)S(1)}, f32[2048]{0:T(1024)}, u32[]{:S(2)}) copy-start(f32[2048]{0:T(1024)} %param.25) | copy-start | bytes 24580
  233.7 8.1 %collective-permute-start.34 = (bf16[64,2048]{1,0:T(8,128)(2,1)S(1)}, bf16[64,2048]{1,0:T(8,128)(2,1)S(1)}, u32[]{:S(2)}, u32[]{:S(2)}) collective-permute-start(bf16[64,2048]{1,0:T(8,128)(2,1)S(1)} %get-tuple-element.112), channel_id=1, source_target_pairs={{0,32},{32,64},{64,96},{96,0},{1,33},{33,65},{65,97},{97,1},{2,34}... | collective-permute-start | bytes 786440 | tf_op jit(solution)/shard_map/ppermute | solution.py:20
  233.8 8.2 %collective-permute-start.32 = (bf16[64,2048]{1,0:T(8,128)(2,1)S(1)}, bf16[64,2048]{1,0:T(8,128)(2,1)S(1)}, u32[]{:S(2)}, u32[]{:S(2)}) collective-permute-start(bf16[64,2048]{1,0:T(8,128)(2,1)S(1)} %add_convert_fusion.4), channel_id=1, source_target_pairs={{0,96},{32,0},{64,32},{96,64},{1,97},{33,1},{65,33},{97,65},{2,98}... | collective-permute-start | bytes 786440 | tf_op jit(solution)/shard_map/ppermute | solution.py:20
  237.0 7.7 %collective-permute-start.33 = (bf16[64,2048]{1,0:T(8,128)(2,1)S(1)}, bf16[64,2048]{1,0:T(8,128)(2,1)S(1)}, u32[]{:S(2)}, u32[]{:S(2)}) collective-permute-start(bf16[64,2048]{1,0:T(8,128)(2,1)S(1)} %get-tuple-element.111), channel_id=1, source_target_pairs={{0,96},{32,0},{64,32},{96,64},{1,97},{33,1},{65,33},{97,65},{2,98}... | collective-permute-start | bytes 786440 | tf_op jit(solution)/shard_map/ppermute | solution.py:20
  241.9 7.9 %collective-permute-start.35 = (bf16[64,2048]{1,0:T(8,128)(2,1)S(1)}, bf16[64,2048]{1,0:T(8,128)(2,1)S(1)}, u32[]{:S(2)}, u32[]{:S(2)}) collective-permute-start(bf16[64,2048]{1,0:T(8,128)(2,1)S(1)} %add_convert_fusion.3), channel_id=1, source_target_pairs={{0,32},{32,64},{64,96},{96,0},{1,33},{33,65},{65,97},{97,1},{2,34}... | collective-permute-start | bytes 786440 | tf_op jit(solution)/shard_map/ppermute | solution.py:20

commit v4 on v3

--- a/solution.py
+++ b/solution.py
@@ -96,7 +96,7 @@
     capacity = 3 * tok_dev // (2 * num_groups)
     bf16 = jnp.bfloat16
 
-    cut = 5 * width_model // 8
+    cut = width_model // 2
     left, right = group_w2[0, :, :cut], group_w2[0, :, cut:]
     w1_out, b1_pair = hold(group_w1[0], swap_blocks(group_b1[0]))
     w1_pair = swap_blocks(w1_out)

time: 253 us -> 239 us (0.945)
  waiting for transfers between devices: 130 us -> 115 us
    ppermute x4, waiting for transfers between devices: 29.9 us -> 22 us  [swap_blocks(): return lax.ppermute(value, X, [(0, 3), (3, 0), (1, 2), (2, 1)])]
    ppermute x5, waiting for transfers between devices: 17 us -> 13.4 us  [swap_column(): return lax.ppermute(value, 'xl', [(0, 1), (1, 0)])]
    all_to_all x3, waiting for transfers between devices: 17.5 us -> 13.9 us  [exchange(): lax.all_to_all(value, ('y', 'core'), split_axis=0, concat_axis=0, tiled=T...]
    unnamed x55 -> x51, local copies, waits for them, and re-layouts: 5.38 us -> 5.26 us
  transfers between devices with their start and end apart: 39 -> 39, of which waited for: 25 -> 26; matrix products, arithmetic and copies ran while one was open for 12% -> 17% of each run, Pallas kernels for 2% -> 2%
where the time goes in v4:
time: 239 us
  waiting for transfers between devices  115 us (48%)
  starting transfers between devices  68.2 us (29%)
  matrix products  32.5 us (14%)
  other arithmetic  10.4 us (4%)
  local copies, waits for them, and re-layouts  7.91 us (3%)
  Pallas kernels  4.38 us (2%)
    ppermute x24, waiting for transfers between devices, shift(): lax.ppermute(value, axis, [(i, (i + step) % size) for i in range(size)])  65.2 us
    ppermute x24, starting transfers between devices, shift(): lax.ppermute(value, axis, [(i, (i + step) % size) for i in range(size)])  39.1 us
    ppermute x4, waiting for transfers between devices, swap_blocks(): return lax.ppermute(value, X, [(0, 3), (3, 0), (1, 2), (2, 1)])  22 us
    all_to_all x3, waiting for transfers between devices, exchange(): lax.all_to_all(value, ('y', 'core'), split_axis=0, concat_axis=0, tiled=T...  13.9 us
    all_to_all x3, starting transfers between devices, exchange(): lax.all_to_all(value, ('y', 'core'), split_axis=0, concat_axis=0, tiled=T...  13.6 us
    ppermute x5, waiting for transfers between devices, swap_column(): return lax.ppermute(value, 'xl', [(0, 1), (1, 0)])  13.4 us
    ppermute x4, starting transfers between devices, swap_blocks(): return lax.ppermute(value, X, [(0, 3), (3, 0), (1, 2), (2, 1)])  11 us
    dot_general x2, matrix products, first(): jnp.dot(rows, w1, preferred_element_type=jnp.float32) + b1  9 us
  transfers between devices with their start and end apart: 39, of which 26 were waited for; matrix products, arithmetic and copies ran while one was open for 17% of the time, Pallas kernels for 2%

profile of v4, /device:TPU:0, one launch (start us, length us, event | category | flops | bytes accessed | tf_op | source)
XLA Modules:
  0.0 238.6 jit_solution(13765944187184035450)
XLA Ops:
  2.9 1.3 fusion.26
  4.3 1.3 fusion.72
  5.7 2.8 %convolution_convert_fusion.2 = bf16[192,2048]{1,0:T(8,128)(2,1)} fusion(bf16[128,2048]{1,0:T(8,128)(2,1)} %param.13, f32[2048]{0:T(1024)S(1)} %bitcast.60, f32[2048]{0:T(1024)S(1)} %bitcast.61, f32[2048]{0:T(1024)S(1)} %bitcast.55, f32[2048]{0:T(1024)S(1)} %bitcast.56, f32[2048]{0:T(1024)S(1)} %bitcast.57, f32[2048]{0:T(1024)S(1)} %bitcast.58, ...), kind=kOutput, calls=%fused_computation.10 | convolution fusion | flops 104226816 | bytes 1378688 | tf_op jit(solution)/shard_map/dot_general | solution.py:120
  8.5 4.7 %all-to-all-start = ((bf16[8,24,2048]{2,1,0:T(8,128)(2,1)}), bf16[8,24,2048]{2,1,0:T(8,128)(2,1)S(1)}, u32[]{:S(2)}, u32[]{:S(2)}) async-start(bf16[8,24,2048]{2,1,0:T(8,128)(2,1)} %bitcast.43), calls=%async_computation | async-start | bytes 1572864 | tf_op jit(solution)/shard_map/all_to_all | solution.py:125
  13.7 2.8 %collective-permute-start.9 = (f32[512]{0:T(512)S(1)}, f32[512]{0:T(512)S(1)}, u32[]{:S(2)}, u32[]{:S(2)}) collective-permute-start(f32[512]{0:T(512)S(1)} %bitcast.62), channel_id=1, source_target_pairs={{0,3},{3,0},{1,2},{2,1},{4,7},{7,4},{5,6},{6,5},{8,11},{11,8},{9,1... | collective-permute-start | bytes 6152 | tf_op jit(solution)/shard_map/ppermute | solution.py:28
  16.4 2.0 collective-permute-done.9
  18.5 2.8 %collective-permute-start.10 = (bf16[2048,512]{1,0:T(8,128)(2,1)}, bf16[2048,512]{1,0:T(8,128)(2,1)}, u32[]{:S(2)}, u32[]{:S(2)}) collective-permute-start(bf16[2048,512]{1,0:T(8,128)(2,1)} %bitcast.64), channel_id=1, source_target_pairs={{0,3},{3,0},{1,2},{2,1},{4,7},{7,4},{5,6},{6,5},{8,11},{11,8},{9,1... | collective-permute-start | bytes 6291464 | tf_op jit(solution)/shard_map/ppermute | solution.py:28
  21.2 5.1 %all-to-all-done = bf16[8,24,2048]{2,1,0:T(8,128)(2,1)S(1)} async-done(((bf16[8,24,2048]{2,1,0:T(8,128)(2,1)}), bf16[8,24,2048]{2,1,0:T(8,128)(2,1)S(1)}, u32[]{:S(2)}, u32[]{:S(2)}) %all-to-all-start) | async-done | bytes 786464 | tf_op jit(solution)/shard_map/all_to_all | solution.py:125
  26.4 2.0 collective-permute-start.3
  28.4 2.2 collective-permute-start.4
  30.6 1.5 collective-permute-start.5
  32.3 7.1 %collective-permute-done.3 = bf16[96,2048]{1,0:T(8,128)(2,1)S(1)} collective-permute-done((bf16[96,2048]{1,0:T(8,128)(2,1)S(1)}, bf16[96,2048]{1,0:T(8,128)(2,1)S(1)}, u32[]{:S(2)}, u32[]{:S(2)}) %collective-permute-start.3) | collective-permute-done | bytes 393248 | tf_op jit(solution)/shard_map/ppermute | solution.py:20
  39.5 1.4 collective-permute-done.5
  41.0 1.5 collective-permute-start.11
  42.5 2.0 collective-permute-start.7
  44.5 6.3 %collective-permute-done.6 = bf16[96,2048]{1,0:T(8,128)(2,1)S(1)} collective-permute-done((bf16[96,2048]{1,0:T(8,128)(2,1)S(1)}, bf16[96,2048]{1,0:T(8,128)(2,1)S(1)}, u32[]{:S(2)}, u32[]{:S(2)}) %collective-permute-start.6) | collective-permute-done | bytes 393248 | tf_op jit(solution)/shard_map/ppermute | solution.py:20
  50.9 2.2 on_chip.2
  53.1 2.0 copy-done.2
  55.1 2.2 on_chip.3
  57.3 2.0 copy-done
  59.3 2.8 %collective-permute-start.14 = (bf16[512,1024]{1,0:T(8,128)(2,1)S(1)}, bf16[512,1024]{1,0:T(8,128)(2,1)S(1)}, u32[]{:S(2)}, u32[]{:S(2)}) collective-permute-start(bf16[512,1024]{1,0:T(8,128)(2,1)S(1)} %get-tuple-element.57), channel_id=1, source_target_pairs={{0,3},{3,0},{1,2},{2,1},{4,7},{7,4},{5,6},{6,5},{8,11},{11,8},{9,1... | collective-permute-start | bytes 3145736 | tf_op jit(solution)/shard_map/ppermute | solution.py:28
  62.2 3.3 %collective-permute-start.13 = (bf16[192,2048]{1,0:T(8,128)(2,1)S(1)}, bf16[192,2048]{1,0:T(8,128)(2,1)S(1)}, u32[]{:S(2)}, u32[]{:S(2)}) collective-permute-start(bf16[192,2048]{1,0:T(8,128)(2,1)S(1)} %collective-permute-done.7), channel_id=1, source_target_pairs={{0,12},{4,0},{8,4},{12,8},{1,13},{5,1},{9,5},{13,9},{2,14},{6,2},{... | collective-permute-start | bytes 2359304 | tf_op jit(solution)/shard_map/ppermute | solution.py:20
  65.6 1.8 collective-permute-done.11
  69.8 2.8 %collective-permute-start.17 = (bf16[512,1024]{1,0:T(8,128)(2,1)S(1)}, bf16[512,1024]{1,0:T(8,128)(2,1)S(1)}, u32[]{:S(2)}, u32[]{:S(2)}) collective-permute-start(bf16[512,1024]{1,0:T(8,128)(2,1)S(1)} %get-tuple-element.58), channel_id=1, source_target_pairs={{0,3},{3,0},{1,2},{2,1},{4,7},{7,4},{5,6},{6,5},{8,11},{11,8},{9,1... | collective-permute-start | bytes 3145736 | tf_op jit(solution)/shard_map/ppermute | solution.py:28
  72.8 6.0 %maximum_convert_fusion = bf16[1248,1024]{1,0:T(8,128)(2,1)S(1)} fusion(bf16[1248,2048]{1,0:T(8,128)(2,1)S(1)} %constant_dynamic-update-slice_fusion, bf16[2048,512]{1,0:T(8,128)(2,1)} %collective-permute-done.10, bf16[2048,512]{1,0:T(8,128)(2,1)S(1)} %bitcast.65, f32[1024]{0:T(1024)S(1)} %pad_maximum_fusion.22), kind=kOutput, calls=%fused_computation | convolution fusion | flops 5246713856 | bytes 11866112 | tf_op jit(solution)/shard_map/dot_general | solution.py:158
  78.8 1.4 collective-permute-done.13
  80.2 3.0 %fusion.12 = bf16[288,1024]{1,0:T(8,128)(2,1)S(1)} fusion(bf16[2048,512]{1,0:T(8,128)(2,1)} %collective-permute-done.10, bf16[2048,512]{1,0:T(8,128)(2,1)S(1)} %bitcast.66, bf16[192,2048]{1,0:T(8,128)(2,1)S(1)} %collective-permute-done.13, bf16[96,2048]{1,0:T(8,128)(2,1)S(1)} %collective-permute-done.12, f32[1024]{0:T(1024)S(1)} %pad_maximum_fusion.22), kind=kOutput, calls=%fused_computation.27 | convolution fusion | flops 1219592192 | bytes 5967872 | tf_op jit(solution)/shard_map/dot_general | solution.py:158
  83.2 7.7 %collective-permute-done.14 = bf16[512,1024]{1,0:T(8,128)(2,1)S(1)} collective-permute-done((bf16[512,1024]{1,0:T(8,128)(2,1)S(1)}, bf16[512,1024]{1,0:T(8,128)(2,1)S(1)}, u32[]{:S(2)}, u32[]{:S(2)}) %collective-permute-start.14) | collective-permute-done | bytes 1048608 | tf_op jit(solution)/shard_map/ppermute | solution.py:28
  90.9 4.3 %convolution_convert_fusion.1 = bf16[1536,1024]{1,0:T(8,128)(2,1)S(1)} fusion(bf16[512,1024]{1,0:T(8,128)(2,1)S(1)} %collective-permute-done.14, bf16[512,1024]{1,0:T(8,128)(2,1)S(1)} %get-tuple-element.57, bf16[288,1024]{1,0:T(8,128)(2,1)S(1)} %fusion.12, bf16[1248,1024]{1,0:T(8,128)(2,1)S(1)} %maximum_convert_fusion), kind=kOutput, calls=%fused_computation.3 | convolution fusion | flops 3233284096 | bytes 8388608 | tf_op jit(solution)/shard_map/dot_general | solution.py:164
  95.7 2.0 collective-permute-start.16
  97.8 2.2 collective-permute-start.15
  100.3 11.0 %collective-permute-done.17 = bf16[512,1024]{1,0:T(8,128)(2,1)S(1)} collective-permute-done((bf16[512,1024]{1,0:T(8,128)(2,1)S(1)}, bf16[512,1024]{1,0:T(8,128)(2,1)S(1)}, u32[]{:S(2)}, u32[]{:S(2)}) %collective-permute-start.17) | collective-permute-done | bytes 1048608 | tf_op jit(solution)/shard_map/ppermute | solution.py:28
  111.3 2.1 collective-permute-done.16
  114.0 3.0 %collective-permute-start.20 = (bf16[384,1024]{1,0:T(8,128)(2,1)S(1)}, bf16[384,1024]{1,0:T(8,128)(2,1)S(1)}, u32[]{:S(2)}, u32[]{:S(2)}) collective-permute-start(bf16[384,1024]{1,0:T(8,128)(2,1)S(1)} %add_convert_fusion.1), channel_id=1, source_target_pairs={{0,12},{4,0},{8,4},{12,8},{1,13},{5,1},{9,5},{13,9},{2,14},{6,2},{... | collective-permute-start | bytes 2359304 | tf_op jit(solution)/shard_map/ppermute | solution.py:20
  116.9 3.8 %convolution_convert_fusion = bf16[1536,1024]{1,0:T(8,128)(2,1)S(1)} fusion(bf16[1536,1024]{1,0:T(8,128)(2,1)S(1)} %pad_maximum_fusion.1, bf16[512,1024]{1,0:T(8,128)(2,1)S(1)} %collective-permute-done.17, bf16[512,1024]{1,0:T(8,128)(2,1)S(1)} %get-tuple-element.58), kind=kOutput, calls=%fused_computation.2 | convolution fusion | flops 3226992640 | bytes 8388608 | tf_op jit(solution)/shard_map/dot_general | solution.py:164
  121.2 9.5 %collective-permute-done.20 = bf16[384,1024]{1,0:T(8,128)(2,1)S(1)} collective-permute-done((bf16[384,1024]{1,0:T(8,128)(2,1)S(1)}, bf16[384,1024]{1,0:T(8,128)(2,1)S(1)}, u32[]{:S(2)}, u32[]{:S(2)}) %collective-permute-start.20) | collective-permute-done | bytes 786464 | tf_op jit(solution)/shard_map/ppermute | solution.py:20
  131.4 3.8 %collective-permute-start.18 = (bf16[384,1024]{1,0:T(8,128)(2,1)S(1)}, bf16[384,1024]{1,0:T(8,128)(2,1)S(1)}, u32[]{:S(2)}, u32[]{:S(2)}) collective-permute-start(bf16[384,1024]{1,0:T(8,128)(2,1)S(1)} %pad_maximum_fusion.16), channel_id=1, source_target_pairs={{0,12},{4,0},{8,4},{12,8},{1,13},{5,1},{9,5},{13,9},{2,14},{6,2},{... | collective-permute-start | bytes 2359304 | tf_op jit(solution)/shard_map/ppermute | solution.py:20
  135.1 3.3 %collective-permute-done.19 = bf16[384,1024]{1,0:T(8,128)(2,1)S(1)} collective-permute-done((bf16[384,1024]{1,0:T(8,128)(2,1)S(1)}, bf16[384,1024]{1,0:T(8,128)(2,1)S(1)}, u32[]{:S(2)}, u32[]{:S(2)}) %collective-permute-start.19) | collective-permute-done | bytes 786464 | tf_op jit(solution)/shard_map/ppermute | solution.py:20
  139.4 1.9 collective-permute-start.22
  142.1 5.4 %all-to-all-start.1 = ((bf16[8,24,1024]{2,1,0:T(8,128)(2,1)}), bf16[8,24,1024]{2,1,0:T(8,128)(2,1)S(1)}, u32[]{:S(2)}, u32[]{:S(2)}) async-start(bf16[8,24,1024]{2,1,0:T(8,128)(2,1)} %bitcast.14), calls=%async_computation.1 | async-start | bytes 786432 | tf_op jit(solution)/shard_map/all_to_all | solution.py:125
  148.0 7.9 %collective-permute-done.22 = bf16[384,1024]{1,0:T(8,128)(2,1)} collective-permute-done((bf16[384,1024]{1,0:T(8,128)(2,1)S(1)}, bf16[384,1024]{1,0:T(8,128)(2,1)}, u32[]{:S(2)}, u32[]{:S(2)}) %collective-permute-start.22) | collective-permute-done | bytes 786464 | tf_op jit(solution)/shard_map/ppermute | solution.py:20
  155.9 1.6 convert_add_fusion
  157.7 9.5 %collective-permute-done.23 = bf16[192,1024]{1,0:T(8,128)(2,1)S(1)} collective-permute-done((bf16[192,1024]{1,0:T(8,128)(2,1)S(1)}, bf16[192,1024]{1,0:T(8,128)(2,1)S(1)}, u32[]{:S(2)}, u32[]{:S(2)}) %collective-permute-start.23) | collective-permute-done | bytes 393248 | tf_op jit(solution)/shard_map/ppermute | solution.py:24
  168.1 3.5 %all-to-all-start.2 = ((bf16[8,24,1024]{2,1,0:T(8,128)(2,1)}), bf16[8,24,1024]{2,1,0:T(8,128)(2,1)S(1)}, u32[]{:S(2)}, u32[]{:S(2)}) async-start(bf16[8,24,1024]{2,1,0:T(8,128)(2,1)} %bitcast.16), calls=%async_computation.2 | async-start | bytes 786432 | tf_op jit(solution)/shard_map/all_to_all | solution.py:125
  171.7 8.8 %all-to-all-done.2 = bf16[8,24,1024]{2,1,0:T(8,128)(2,1)S(1)} async-done(((bf16[8,24,1024]{2,1,0:T(8,128)(2,1)}), bf16[8,24,1024]{2,1,0:T(8,128)(2,1)S(1)}, u32[]{:S(2)}, u32[]{:S(2)}) %all-to-all-start.2) | async-done | bytes 393248 | tf_op jit(solution)/shard_map/all_to_all | solution.py:125
  182.5 2.7 %collective-permute-start.25 = (bf16[64,2048]{1,0:T(8,128)(2,1)S(1)}, bf16[64,2048]{1,0:T(8,128)(2,1)S(1)}, u32[]{:S(2)}, u32[]{:S(2)}) collective-permute-start(bf16[64,2048]{1,0:T(8,128)(2,1)S(1)} %get-tuple-element.119), channel_id=1, source_target_pairs={{0,96},{32,0},{64,32},{96,64},{1,97},{33,1},{65,33},{97,65},{2,98}... | collective-permute-start | bytes 786440 | tf_op jit(solution)/shard_map/ppermute | solution.py:20
  185.2 5.8 %collective-permute-done.24 = bf16[64,2048]{1,0:T(8,128)(2,1)S(1)} collective-permute-done((bf16[64,2048]{1,0:T(8,128)(2,1)S(1)}, bf16[64,2048]{1,0:T(8,128)(2,1)S(1)}, u32[]{:S(2)}, u32[]{:S(2)}) %collective-permute-start.24) | collective-permute-done | bytes 262176 | tf_op jit(solution)/shard_map/ppermute | solution.py:20
  191.0 3.2 %collective-permute-start.27 = (bf16[64,2048]{1,0:T(8,128)(2,1)S(1)}, bf16[64,2048]{1,0:T(8,128)(2,1)S(1)}, u32[]{:S(2)}, u32[]{:S(2)}) collective-permute-start(bf16[64,2048]{1,0:T(8,128)(2,1)S(1)} %get-tuple-element.74), channel_id=1, source_target_pairs={{0,96},{32,0},{64,32},{96,64},{1,97},{33,1},{65,33},{97,65},{2,98}... | collective-permute-start | bytes 786440 | tf_op jit(solution)/shard_map/ppermute | solution.py:20
  194.3 4.9 %collective-permute-done.26 = bf16[64,2048]{1,0:T(8,128)(2,1)S(1)} collective-permute-done((bf16[64,2048]{1,0:T(8,128)(2,1)S(1)}, bf16[64,2048]{1,0:T(8,128)(2,1)S(1)}, u32[]{:S(2)}, u32[]{:S(2)}) %collective-permute-start.26) | collective-permute-done | bytes 262176 | tf_op jit(solution)/shard_map/ppermute | solution.py:20
  200.5 2.1 fusion.18
  202.7 1.3 fusion.74
  204.8 1.3 fusion.1
  206.1 2.5 %collective-permute-start.29 = (bf16[64,2048]{1,0:T(8,128)(2,1)S(1)}, bf16[64,2048]{1,0:T(8,128)(2,1)S(1)}, u32[]{:S(2)}, u32[]{:S(2)}) collective-permute-start(bf16[64,2048]{1,0:T(8,128)(2,1)S(1)} %collective-permute-done.27), channel_id=1, source_target_pairs={{0,96},{32,0},{64,32},{96,64},{1,97},{33,1},{65,33},{97,65},{2,98}... | collective-permute-start | bytes 786440 | tf_op jit(solution)/shard_map/ppermute | solution.py:20
  208.8 2.0 collective-permute-start.31
  210.8 4.3 %collective-permute-done.29 = bf16[64,2048]{1,0:T(8,128)(2,1)S(1)} collective-permute-done((bf16[64,2048]{1,0:T(8,128)(2,1)S(1)}, bf16[64,2048]{1,0:T(8,128)(2,1)S(1)}, u32[]{:S(2)}, u32[]{:S(2)}) %collective-permute-start.29) | collective-permute-done | bytes 262176 | tf_op jit(solution)/shard_map/ppermute | solution.py:20
  215.0 1.9 fusion.20
  217.0 1.3 fusion.19
  218.4 1.3 fusion.75
  219.6 1.3 fusion.2
  221.1 3.4 %collective-permute-start.32 = (bf16[64,2048]{1,0:T(8,128)(2,1)S(1)}, bf16[64,2048]{1,0:T(8,128)(2,1)S(1)}, u32[]{:S(2)}, u32[]{:S(2)}) collective-permute-start(bf16[64,2048]{1,0:T(8,128)(2,1)S(1)} %add_convert_fusion.4), channel_id=1, source_target_pairs={{0,96},{32,0},{64,32},{96,64},{1,97},{33,1},{65,33},{97,65},{2,98}... | collective-permute-start | bytes 786440 | tf_op jit(solution)/shard_map/ppermute | solution.py:20
  224.5 1.9 collective-permute-start.33
  226.4 3.0 %collective-permute-done.34 = bf16[64,2048]{1,0:T(8,128)(2,1)S(1)} collective-permute-done((bf16[64,2048]{1,0:T(8,128)(2,1)S(1)}, bf16[64,2048]{1,0:T(8,128)(2,1)S(1)}, u32[]{:S(2)}, u32[]{:S(2)}) %collective-permute-start.34) | collective-permute-done | bytes 262176 | tf_op jit(solution)/shard_map/ppermute | solution.py:20
  229.7 2.3 collective-permute-done.33
  232.0 5.6 %collective-permute-done.35 = bf16[64,2048]{1,0:T(8,128)(2,1)S(1)} collective-permute-done((bf16[64,2048]{1,0:T(8,128)(2,1)S(1)}, bf16[64,2048]{1,0:T(8,128)(2,1)S(1)}, u32[]{:S(2)}, u32[]{:S(2)}) %collective-permute-start.35) | collective-permute-done | bytes 262176 | tf_op jit(solution)/shard_map/ppermute | solution.py:20
  (126 shorter events, 18.3 us)
Async XLA Ops:
  0.0 26.3 %collective-permute-start = (bf16[2048,1024]{1,0:T(8,128)(2,1)}, bf16[2048,1024]{1,0:T(8,128)(2,1)}, u32[]{:S(2)}, u32[]{:S(2)}) collective-permute-start(bf16[2048,1024]{1,0:T(8,128)(2,1)} %param.22), channel_id=1, source_target_pairs={{0,16},{16,0},{1,17},{17,1},{2,18},{18,2},{3,19},{19,3},{4,20},{20... | collective-permute-start | bytes 12582920 | tf_op jit(solution)/shard_map/ppermute | solution.py:32
  0.0 26.3 %collective-permute-start.1 = (bf16[1024,2048]{1,0:T(8,128)(2,1)}, bf16[1024,2048]{1,0:T(8,128)(2,1)}, u32[]{:S(2)}, u32[]{:S(2)}) collective-permute-start(bf16[1024,2048]{1,0:T(8,128)(2,1)} %param.24), channel_id=1, source_target_pairs={{0,16},{16,0},{1,17},{17,1},{2,18},{18,2},{3,19},{19,3},{4,20},{20... | collective-permute-start | bytes 12582920 | tf_op jit(solution)/shard_map/ppermute | solution.py:32
  4.3 4.2 %copy-start.21 = (s32[128]{0:T(128)}, s32[128]{0:T(128)S(1)}, u32[]{:S(2)}) copy-start(s32[128]{0:T(128)S(1)} %multiply_add_fusion) | copy-start | bytes 1540
  4.3 4.1 %copy-start.10 = (pred[128]{0:T(512)(128)(4,1)}, pred[128]{0:T(512)(128)(4,1)S(1)}, u32[]{:S(2)}) copy-start(pred[128]{0:T(512)(128)(4,1)S(1)} %get-tuple-element.141) | copy-start | bytes 388
  4.3 4.1 %copy-start.12 = (pred[128]{0:T(512)(128)(4,1)}, pred[128]{0:T(512)(128)(4,1)S(1)}, u32[]{:S(2)}) copy-start(pred[128]{0:T(512)(128)(4,1)S(1)} %get-tuple-element.142) | copy-start | bytes 388
  4.3 4.1 %copy-start.14 = (pred[128]{0:T(512)(128)(4,1)}, pred[128]{0:T(512)(128)(4,1)S(1)}, u32[]{:S(2)}) copy-start(pred[128]{0:T(512)(128)(4,1)S(1)} %get-tuple-element.143) | copy-start | bytes 388
  5.6 7.5 %copy-start.19 = (f32[1024]{0:T(1024)S(1)}, f32[1024]{0:T(1024)}, u32[]{:S(2)}) copy-start(f32[1024]{0:T(1024)} %param.23) | copy-start | bytes 12292
  5.6 8.0 %copy-start.9 = (f32[1,512]{1,0:T(1,128)S(1)}, f32[1,512]{1,0:T(1,128)}, u32[]{:S(2)}) copy-start(f32[1,512]{1,0:T(1,128)} %param.18) | copy-start | bytes 6148
  8.5 23.6 %copy-start.4 = (bf16[1,512,2048]{2,1,0:T(8,128)(2,1)S(1)}, bf16[1,512,2048]{2,1,0:T(8,128)(2,1)}, u32[]{:S(2)}) copy-start(bf16[1,512,2048]{2,1,0:T(8,128)(2,1)} %param.19) | copy-start | bytes 6291460
  8.5 17.9 %all-to-all-start = ((bf16[8,24,2048]{2,1,0:T(8,128)(2,1)}), bf16[8,24,2048]{2,1,0:T(8,128)(2,1)S(1)}, u32[]{:S(2)}, u32[]{:S(2)}) async-start(bf16[8,24,2048]{2,1,0:T(8,128)(2,1)} %bitcast.43), calls=%async_computation | async-start | bytes 1572864 | tf_op jit(solution)/shard_map/all_to_all | solution.py:125
  13.2 8.1 %collective-permute-start.2 = (f32[1024]{0:T(1024)S(1)}, f32[1024]{0:T(1024)}, u32[]{:S(2)}, u32[]{:S(2)}) collective-permute-start(f32[1024]{0:T(1024)S(1)} %copy-done.19), channel_id=1, source_target_pairs={{0,16},{16,0},{1,17},{17,1},{2,18},{18,2},{3,19},{19,3},{4,20},{20... | collective-permute-start | bytes 12296 | tf_op jit(solution)/shard_map/ppermute | solution.py:32
  13.7 4.8 %collective-permute-start.9 = (f32[512]{0:T(512)S(1)}, f32[512]{0:T(512)S(1)}, u32[]{:S(2)}, u32[]{:S(2)}) collective-permute-start(f32[512]{0:T(512)S(1)} %bitcast.62), channel_id=1, source_target_pairs={{0,3},{3,0},{1,2},{2,1},{4,7},{7,4},{5,6},{6,5},{8,11},{11,8},{9,1... | collective-permute-start | bytes 6152 | tf_op jit(solution)/shard_map/ppermute | solution.py:28
  18.5 50.1 %collective-permute-start.10 = (bf16[2048,512]{1,0:T(8,128)(2,1)}, bf16[2048,512]{1,0:T(8,128)(2,1)}, u32[]{:S(2)}, u32[]{:S(2)}) collective-permute-start(bf16[2048,512]{1,0:T(8,128)(2,1)} %bitcast.64), channel_id=1, source_target_pairs={{0,3},{3,0},{1,2},{2,1},{4,7},{7,4},{5,6},{6,5},{8,11},{11,8},{9,1... | collective-permute-start | bytes 6291464 | tf_op jit(solution)/shard_map/ppermute | solution.py:28
  26.4 13.0 %collective-permute-start.3 = (bf16[96,2048]{1,0:T(8,128)(2,1)S(1)}, bf16[96,2048]{1,0:T(8,128)(2,1)S(1)}, u32[]{:S(2)}, u32[]{:S(2)}) collective-permute-start(bf16[96,2048]{1,0:T(8,128)(2,1)S(1)} %get-tuple-element.118), channel_id=1, source_target_pairs={{0,4},{4,8},{8,12},{12,0},{1,5},{5,9},{9,13},{13,1},{2,6},{6,10},{... | collective-permute-start | bytes 1179656 | tf_op jit(solution)/shard_map/ppermute | solution.py:20
  28.4 11.0 %collective-permute-start.4 = (bf16[96,2048]{1,0:T(8,128)(2,1)S(1)}, bf16[96,2048]{1,0:T(8,128)(2,1)S(1)}, u32[]{:S(2)}, u32[]{:S(2)}) collective-permute-start(bf16[96,2048]{1,0:T(8,128)(2,1)S(1)} %get-tuple-element.118), channel_id=1, source_target_pairs={{0,12},{4,0},{8,4},{12,8},{1,13},{5,1},{9,5},{13,9},{2,14},{6,2},{... | collective-permute-start | bytes 1179656 | tf_op jit(solution)/shard_map/ppermute | solution.py:20
  30.6 10.4 %collective-permute-start.5 = (bf16[96,2048]{1,0:T(8,128)(2,1)S(1)}, bf16[96,2048]{1,0:T(8,128)(2,1)S(1)}, u32[]{:S(2)}, u32[]{:S(2)}) collective-permute-start(bf16[96,2048]{1,0:T(8,128)(2,1)S(1)} %get-tuple-element.117), channel_id=1, source_target_pairs={{0,1},{1,0},{2,3},{3,2},{4,5},{5,4},{6,7},{7,6},{8,9},{9,8},{10,11... | collective-permute-start | bytes 1179656 | tf_op jit(solution)/shard_map/ppermute | solution.py:24
  39.4 11.4 %collective-permute-start.6 = (bf16[96,2048]{1,0:T(8,128)(2,1)S(1)}, bf16[96,2048]{1,0:T(8,128)(2,1)S(1)}, u32[]{:S(2)}, u32[]{:S(2)}) collective-permute-start(bf16[96,2048]{1,0:T(8,128)(2,1)S(1)} %collective-permute-done.3), channel_id=1, source_target_pairs={{0,4},{4,8},{8,12},{12,0},{1,5},{5,9},{9,13},{13,1},{2,6},{6,10},{... | collective-permute-start | bytes 1179656 | tf_op jit(solution)/shard_map/ppermute | solution.py:20
  41.0 26.4 %collective-permute-start.11 = (bf16[288,2048]{1,0:T(8,128)(2,1)S(1)}, bf16[288,2048]{1,0:T(8,128)(2,1)S(1)}, u32[]{:S(2)}, u32[]{:S(2)}) collective-permute-start(bf16[288,2048]{1,0:T(8,128)(2,1)S(1)} %pad_maximum_fusion.10), channel_id=1, source_target_pairs={{0,1},{1,0},{2,3},{3,2},{4,5},{5,4},{6,7},{7,6},{8,9},{9,8},{10,11... | collective-permute-start | bytes 3538952 | tf_op jit(solution)/shard_map/ppermute | solution.py:24
  42.5 19.7 %collective-permute-start.7 = (bf16[192,2048]{1,0:T(8,128)(2,1)S(1)}, bf16[192,2048]{1,0:T(8,128)(2,1)S(1)}, u32[]{:S(2)}, u32[]{:S(2)}) collective-permute-start(bf16[192,2048]{1,0:T(8,128)(2,1)S(1)} %pad_maximum_fusion.13), channel_id=1, source_target_pairs={{0,12},{4,0},{8,4},{12,8},{1,13},{5,1},{9,5},{13,9},{2,14},{6,2},{... | collective-permute-start | bytes 2359304 | tf_op jit(solution)/shard_map/ppermute | solution.py:20
  50.8 19.0 %collective-permute-start.8 = (bf16[192,2048]{1,0:T(8,128)(2,1)S(1)}, bf16[192,2048]{1,0:T(8,128)(2,1)S(1)}, u32[]{:S(2)}, u32[]{:S(2)}) collective-permute-start(bf16[192,2048]{1,0:T(8,128)(2,1)S(1)} %pad_maximum_fusion.13), channel_id=1, source_target_pairs={{0,4},{4,8},{8,12},{12,0},{1,5},{5,9},{9,13},{13,1},{2,6},{6,10},{... | collective-permute-start | bytes 2359304 | tf_op jit(solution)/shard_map/ppermute | solution.py:20
  53.1 2.0 copy-start.2
  57.3 2.0 copy-start
  59.3 31.6 %collective-permute-start.14 = (bf16[512,1024]{1,0:T(8,128)(2,1)S(1)}, bf16[512,1024]{1,0:T(8,128)(2,1)S(1)}, u32[]{:S(2)}, u32[]{:S(2)}) collective-permute-start(bf16[512,1024]{1,0:T(8,128)(2,1)S(1)} %get-tuple-element.57), channel_id=1, source_target_pairs={{0,3},{3,0},{1,2},{2,1},{4,7},{7,4},{5,6},{6,5},{8,11},{11,8},{9,1... | collective-permute-start | bytes 3145736 | tf_op jit(solution)/shard_map/ppermute | solution.py:28
  62.2 18.1 %collective-permute-start.13 = (bf16[192,2048]{1,0:T(8,128)(2,1)S(1)}, bf16[192,2048]{1,0:T(8,128)(2,1)S(1)}, u32[]{:S(2)}, u32[]{:S(2)}) collective-permute-start(bf16[192,2048]{1,0:T(8,128)(2,1)S(1)} %collective-permute-done.7), channel_id=1, source_target_pairs={{0,12},{4,0},{8,4},{12,8},{1,13},{5,1},{9,5},{13,9},{2,14},{6,2},{... | collective-permute-start | bytes 2359304 | tf_op jit(solution)/shard_map/ppermute | solution.py:20
  65.6 7.2 %copy-start.18 = (bf16[1,2048,512]{2,1,0:T(8,128)(2,1)S(1)}, bf16[1,2048,512]{2,1,0:T(8,128)(2,1)}, u32[]{:S(2)}) copy-start(bf16[1,2048,512]{2,1,0:T(8,128)(2,1)} %param.17) | copy-start | bytes 6291460
  68.6 11.7 %collective-permute-start.12 = (bf16[96,2048]{1,0:T(8,128)(2,1)S(1)}, bf16[96,2048]{1,0:T(8,128)(2,1)S(1)}, u32[]{:S(2)}, u32[]{:S(2)}) collective-permute-start(bf16[96,2048]{1,0:T(8,128)(2,1)S(1)} %collective-permute-done.6), channel_id=1, source_target_pairs={{0,1},{1,0},{2,3},{3,2},{4,5},{5,4},{6,7},{7,6},{8,9},{9,8},{10,11... | collective-permute-start | bytes 1179656 | tf_op jit(solution)/shard_map/ppermute | solution.py:24
  69.8 41.5 %collective-permute-start.17 = (bf16[512,1024]{1,0:T(8,128)(2,1)S(1)}, bf16[512,1024]{1,0:T(8,128)(2,1)S(1)}, u32[]{:S(2)}, u32[]{:S(2)}) collective-permute-start(bf16[512,1024]{1,0:T(8,128)(2,1)S(1)} %get-tuple-element.58), channel_id=1, source_target_pairs={{0,3},{3,0},{1,2},{2,1},{4,7},{7,4},{5,6},{6,5},{8,11},{11,8},{9,1... | collective-permute-start | bytes 3145736 | tf_op jit(solution)/shard_map/ppermute | solution.py:28
  95.7 17.7 %collective-permute-start.16 = (bf16[384,1024]{1,0:T(8,128)(2,1)S(1)}, bf16[384,1024]{1,0:T(8,128)(2,1)S(1)}, u32[]{:S(2)}, u32[]{:S(2)}) collective-permute-start(bf16[384,1024]{1,0:T(8,128)(2,1)S(1)} %pad_maximum_fusion.15), channel_id=1, source_target_pairs={{0,4},{4,8},{8,12},{12,0},{1,5},{5,9},{9,13},{13,1},{2,6},{6,10},{... | collective-permute-start | bytes 2359304 | tf_op jit(solution)/shard_map/ppermute | solution.py:20
  97.8 15.9 %collective-permute-start.15 = (bf16[384,1024]{1,0:T(8,128)(2,1)S(1)}, bf16[384,1024]{1,0:T(8,128)(2,1)S(1)}, u32[]{:S(2)}, u32[]{:S(2)}) collective-permute-start(bf16[384,1024]{1,0:T(8,128)(2,1)S(1)} %pad_maximum_fusion.14), channel_id=1, source_target_pairs={{0,12},{4,0},{8,4},{12,8},{1,13},{5,1},{9,5},{13,9},{2,14},{6,2},{... | collective-permute-start | bytes 2359304 | tf_op jit(solution)/shard_map/ppermute | solution.py:20
  114.0 16.8 %collective-permute-start.20 = (bf16[384,1024]{1,0:T(8,128)(2,1)S(1)}, bf16[384,1024]{1,0:T(8,128)(2,1)S(1)}, u32[]{:S(2)}, u32[]{:S(2)}) collective-permute-start(bf16[384,1024]{1,0:T(8,128)(2,1)S(1)} %add_convert_fusion.1), channel_id=1, source_target_pairs={{0,12},{4,0},{8,4},{12,8},{1,13},{5,1},{9,5},{13,9},{2,14},{6,2},{... | collective-permute-start | bytes 2359304 | tf_op jit(solution)/shard_map/ppermute | solution.py:20
  121.1 17.3 %collective-permute-start.19 = (bf16[384,1024]{1,0:T(8,128)(2,1)S(1)}, bf16[384,1024]{1,0:T(8,128)(2,1)S(1)}, u32[]{:S(2)}, u32[]{:S(2)}) collective-permute-start(bf16[384,1024]{1,0:T(8,128)(2,1)S(1)} %pad_maximum_fusion.17), channel_id=1, source_target_pairs={{0,4},{4,8},{8,12},{12,0},{1,5},{5,9},{9,13},{13,1},{2,6},{6,10},{... | collective-permute-start | bytes 2359304 | tf_op jit(solution)/shard_map/ppermute | solution.py:20
  131.2 7.9 %collective-permute-start.21 = (bf16[192,1024]{1,0:T(8,128)(2,1)S(1)}, bf16[192,1024]{1,0:T(8,128)(2,1)S(1)}, u32[]{:S(2)}, u32[]{:S(2)}) collective-permute-start(bf16[192,1024]{1,0:T(8,128)(2,1)S(1)} %slice.280), channel_id=1, source_target_pairs={{0,1},{1,0},{2,3},{3,2},{4,5},{5,4},{6,7},{7,6},{8,9},{9,8},{10,11... | collective-permute-start | bytes 1179656 | tf_op jit(solution)/shard_map/ppermute | solution.py:24
  131.4 16.6 %collective-permute-start.18 = (bf16[384,1024]{1,0:T(8,128)(2,1)S(1)}, bf16[384,1024]{1,0:T(8,128)(2,1)S(1)}, u32[]{:S(2)}, u32[]{:S(2)}) collective-permute-start(bf16[384,1024]{1,0:T(8,128)(2,1)S(1)} %pad_maximum_fusion.16), channel_id=1, source_target_pairs={{0,12},{4,0},{8,4},{12,8},{1,13},{5,1},{9,5},{13,9},{2,14},{6,2},{... | collective-permute-start | bytes 2359304 | tf_op jit(solution)/shard_map/ppermute | solution.py:20
  139.4 16.5 %collective-permute-start.22 = (bf16[384,1024]{1,0:T(8,128)(2,1)S(1)}, bf16[384,1024]{1,0:T(8,128)(2,1)}, u32[]{:S(2)}, u32[]{:S(2)}) collective-permute-start(bf16[384,1024]{1,0:T(8,128)(2,1)S(1)} %add_convert_fusion), channel_id=1, source_target_pairs={{0,4},{4,8},{8,12},{12,0},{1,5},{5,9},{9,13},{13,1},{2,6},{6,10},{... | collective-permute-start | bytes 2359304 | tf_op jit(solution)/shard_map/ppermute | solution.py:20
  142.1 15.4 %all-to-all-start.1 = ((bf16[8,24,1024]{2,1,0:T(8,128)(2,1)}), bf16[8,24,1024]{2,1,0:T(8,128)(2,1)S(1)}, u32[]{:S(2)}, u32[]{:S(2)}) async-start(bf16[8,24,1024]{2,1,0:T(8,128)(2,1)} %bitcast.14), calls=%async_computation.1 | async-start | bytes 786432 | tf_op jit(solution)/shard_map/all_to_all | solution.py:125
  157.4 14.1 %copy-start.6 = (f32[8,2048]{1,0:T(8,128)S(1)}, f32[8,2048]{1,0:T(8,128)}, u32[]{:S(2)}) copy-start(f32[8,2048]{1,0:T(8,128)} %param.20) | copy-start | bytes 196612
  157.5 23.0 %copy-start.5 = (bf16[128,2048]{1,0:T(8,128)(2,1)S(1)}, bf16[128,2048]{1,0:T(8,128)(2,1)}, u32[]{:S(2)}) copy-start(bf16[128,2048]{1,0:T(8,128)(2,1)} %param.13) | copy-start | bytes 1572868
  157.5 23.0 %copy-start.11 = (pred[128]{0:T(512)(128)(4,1)S(1)}, pred[128]{0:T(512)(128)(4,1)}, u32[]{:S(2)}) copy-start(pred[128]{0:T(512)(128)(4,1)} %copy-done.10) | copy-start | bytes 388
  157.5 23.0 %copy-start.13 = (pred[128]{0:T(512)(128)(4,1)S(1)}, pred[128]{0:T(512)(128)(4,1)}, u32[]{:S(2)}) copy-start(pred[128]{0:T(512)(128)(4,1)} %copy-done.12) | copy-start | bytes 388
  157.5 23.0 %copy-start.15 = (pred[128]{0:T(512)(128)(4,1)S(1)}, pred[128]{0:T(512)(128)(4,1)}, u32[]{:S(2)}) copy-start(pred[128]{0:T(512)(128)(4,1)} %copy-done.14) | copy-start | bytes 388
  157.5 23.0 %copy-start.22 = (s32[128]{0:T(128)S(1)}, s32[128]{0:T(128)}, u32[]{:S(2)}) copy-start(s32[128]{0:T(128)} %copy-done.21) | copy-start | bytes 1540
  157.6 9.7 %collective-permute-start.23 = (bf16[192,1024]{1,0:T(8,128)(2,1)S(1)}, bf16[192,1024]{1,0:T(8,128)(2,1)S(1)}, u32[]{:S(2)}, u32[]{:S(2)}) collective-permute-start(bf16[192,1024]{1,0:T(8,128)(2,1)S(1)} %slice.279), channel_id=1, source_target_pairs={{0,1},{1,0},{2,3},{3,2},{4,5},{5,4},{6,7},{7,6},{8,9},{9,8},{10,11... | collective-permute-start | bytes 1179656 | tf_op jit(solution)/shard_map/ppermute | solution.py:24
  168.1 12.3 %all-to-all-start.2 = ((bf16[8,24,1024]{2,1,0:T(8,128)(2,1)}), bf16[8,24,1024]{2,1,0:T(8,128)(2,1)S(1)}, u32[]{:S(2)}, u32[]{:S(2)}) async-start(bf16[8,24,1024]{2,1,0:T(8,128)(2,1)} %bitcast.16), calls=%async_computation.2 | async-start | bytes 786432 | tf_op jit(solution)/shard_map/all_to_all | solution.py:125
  180.5 1.1 copy-start.7
  180.5 18.7 %copy-start.16 = (bf16[2048,1024]{1,0:T(8,128)(2,1)S(1)}, bf16[2048,1024]{1,0:T(8,128)(2,1)}, u32[]{:S(2)}) copy-start(bf16[2048,1024]{1,0:T(8,128)(2,1)} %param.22) | copy-start | bytes 12582916
  181.3 17.8 %copy-start.20 = (f32[1024]{0:T(1024)S(1)}, f32[1024]{0:T(1024)}, u32[]{:S(2)}) copy-start(f32[1024]{0:T(1024)} %param.23) | copy-start | bytes 12292
  181.9 9.1 %collective-permute-start.24 = (bf16[64,2048]{1,0:T(8,128)(2,1)S(1)}, bf16[64,2048]{1,0:T(8,128)(2,1)S(1)}, u32[]{:S(2)}, u32[]{:S(2)}) collective-permute-start(bf16[64,2048]{1,0:T(8,128)(2,1)S(1)} %get-tuple-element.119), channel_id=1, source_target_pairs={{0,32},{32,64},{64,96},{96,0},{1,33},{33,65},{65,97},{97,1},{2,34}... | collective-permute-start | bytes 786440 | tf_op jit(solution)/shard_map/ppermute | solution.py:20
  182.5 8.5 %collective-permute-start.25 = (bf16[64,2048]{1,0:T(8,128)(2,1)S(1)}, bf16[64,2048]{1,0:T(8,128)(2,1)S(1)}, u32[]{:S(2)}, u32[]{:S(2)}) collective-permute-start(bf16[64,2048]{1,0:T(8,128)(2,1)S(1)} %get-tuple-element.119), channel_id=1, source_target_pairs={{0,96},{32,0},{64,32},{96,64},{1,97},{33,1},{65,33},{97,65},{2,98}... | collective-permute-start | bytes 786440 | tf_op jit(solution)/shard_map/ppermute | solution.py:20
  191.0 8.2 %collective-permute-start.26 = (bf16[64,2048]{1,0:T(8,128)(2,1)S(1)}, bf16[64,2048]{1,0:T(8,128)(2,1)S(1)}, u32[]{:S(2)}, u32[]{:S(2)}) collective-permute-start(bf16[64,2048]{1,0:T(8,128)(2,1)S(1)} %collective-permute-done.24), channel_id=1, source_target_pairs={{0,32},{32,64},{64,96},{96,0},{1,33},{33,65},{65,97},{97,1},{2,34}... | collective-permute-start | bytes 786440 | tf_op jit(solution)/shard_map/ppermute | solution.py:20
  191.0 9.4 %copy-start.3 = (bf16[2048,1024]{1,0:T(8,128)(2,1)S(1)}, bf16[2048,1024]{1,0:T(8,128)(2,1)}, u32[]{:S(2)}) copy-start(bf16[2048,1024]{1,0:T(8,128)(2,1)} %copy-done.2) | copy-start | bytes 12582916
  191.0 11.6 %collective-permute-start.27 = (bf16[64,2048]{1,0:T(8,128)(2,1)S(1)}, bf16[64,2048]{1,0:T(8,128)(2,1)S(1)}, u32[]{:S(2)}, u32[]{:S(2)}) collective-permute-start(bf16[64,2048]{1,0:T(8,128)(2,1)S(1)} %get-tuple-element.74), channel_id=1, source_target_pairs={{0,96},{32,0},{64,32},{96,64},{1,97},{33,1},{65,33},{97,65},{2,98}... | collective-permute-start | bytes 786440 | tf_op jit(solution)/shard_map/ppermute | solution.py:20
  200.5 2.2 copy-start.1
  202.6 2.2 copy-start.17
  202.6 8.2 %collective-permute-start.28 = (bf16[64,2048]{1,0:T(8,128)(2,1)S(1)}, bf16[64,2048]{1,0:T(8,128)(2,1)S(1)}, u32[]{:S(2)}, u32[]{:S(2)}) collective-permute-start(bf16[64,2048]{1,0:T(8,128)(2,1)S(1)} %get-tuple-element.74), channel_id=1, source_target_pairs={{0,32},{32,64},{64,96},{96,0},{1,33},{33,65},{65,97},{97,1},{2,34}... | collective-permute-start | bytes 786440 | tf_op jit(solution)/shard_map/ppermute | solution.py:20
  206.1 8.9 %collective-permute-start.29 = (bf16[64,2048]{1,0:T(8,128)(2,1)S(1)}, bf16[64,2048]{1,0:T(8,128)(2,1)S(1)}, u32[]{:S(2)}, u32[]{:S(2)}) collective-permute-start(bf16[64,2048]{1,0:T(8,128)(2,1)S(1)} %collective-permute-done.27), channel_id=1, source_target_pairs={{0,96},{32,0},{64,32},{96,64},{1,97},{33,1},{65,33},{97,65},{2,98}... | collective-permute-start | bytes 786440 | tf_op jit(solution)/shard_map/ppermute | solution.py:20
  208.7 9.6 %collective-permute-start.30 = (bf16[64,2048]{1,0:T(8,128)(2,1)S(1)}, bf16[64,2048]{1,0:T(8,128)(2,1)S(1)}, u32[]{:S(2)}, u32[]{:S(2)}) collective-permute-start(bf16[64,2048]{1,0:T(8,128)(2,1)S(1)} %get-tuple-element.116), channel_id=1, source_target_pairs={{0,96},{32,0},{64,32},{96,64},{1,97},{33,1},{65,33},{97,65},{2,98}... | collective-permute-start | bytes 786440 | tf_op jit(solution)/shard_map/ppermute | solution.py:20
  208.8 9.6 %collective-permute-start.31 = (bf16[64,2048]{1,0:T(8,128)(2,1)S(1)}, bf16[64,2048]{1,0:T(8,128)(2,1)S(1)}, u32[]{:S(2)}, u32[]{:S(2)}) collective-permute-start(bf16[64,2048]{1,0:T(8,128)(2,1)S(1)} %get-tuple-element.115), channel_id=1, source_target_pairs={{0,32},{32,64},{64,96},{96,0},{1,33},{33,65},{65,97},{97,1},{2,34}... | collective-permute-start | bytes 786440 | tf_op jit(solution)/shard_map/ppermute | solution.py:20
  220.9 16.7 %copy-start.8 = (f32[2048]{0:T(1024)S(1)}, f32[2048]{0:T(1024)}, u32[]{:S(2)}) copy-start(f32[2048]{0:T(1024)} %param.25) | copy-start | bytes 24580
  221.0 8.4 %collective-permute-start.34 = (bf16[64,2048]{1,0:T(8,128)(2,1)S(1)}, bf16[64,2048]{1,0:T(8,128)(2,1)S(1)}, u32[]{:S(2)}, u32[]{:S(2)}) collective-permute-start(bf16[64,2048]{1,0:T(8,128)(2,1)S(1)} %get-tuple-element.114), channel_id=1, source_target_pairs={{0,32},{32,64},{64,96},{96,0},{1,33},{33,65},{65,97},{97,1},{2,34}... | collective-permute-start | bytes 786440 | tf_op jit(solution)/shard_map/ppermute | solution.py:20
  221.1 8.5 %collective-permute-start.32 = (bf16[64,2048]{1,0:T(8,128)(2,1)S(1)}, bf16[64,2048]{1,0:T(8,128)(2,1)S(1)}, u32[]{:S(2)}, u32[]{:S(2)}) collective-permute-start(bf16[64,2048]{1,0:T(8,128)(2,1)S(1)} %add_convert_fusion.4), channel_id=1, source_target_pairs={{0,96},{32,0},{64,32},{96,64},{1,97},{33,1},{65,33},{97,65},{2,98}... | collective-permute-start | bytes 786440 | tf_op jit(solution)/shard_map/ppermute | solution.py:20
  224.5 7.5 %collective-permute-start.33 = (bf16[64,2048]{1,0:T(8,128)(2,1)S(1)}, bf16[64,2048]{1,0:T(8,128)(2,1)S(1)}, u32[]{:S(2)}, u32[]{:S(2)}) collective-permute-start(bf16[64,2048]{1,0:T(8,128)(2,1)S(1)} %get-tuple-element.113), channel_id=1, source_target_pairs={{0,96},{32,0},{64,32},{96,64},{1,97},{33,1},{65,33},{97,65},{2,98}... | collective-permute-start | bytes 786440 | tf_op jit(solution)/shard_map/ppermute | solution.py:20
  229.5 8.1 %collective-permute-start.35 = (bf16[64,2048]{1,0:T(8,128)(2,1)S(1)}, bf16[64,2048]{1,0:T(8,128)(2,1)S(1)}, u32[]{:S(2)}, u32[]{:S(2)}) collective-permute-start(bf16[64,2048]{1,0:T(8,128)(2,1)S(1)} %add_convert_fusion.3), channel_id=1, source_target_pairs={{0,32},{32,64},{64,96},{96,0},{1,33},{33,65},{65,97},{97,1},{2,34}... | collective-permute-start | bytes 786440 | tf_op jit(solution)/shard_map/ppermute | solution.py:20

commit v5 on v4

--- a/solution.py
+++ b/solution.py
@@ -51,6 +51,58 @@
     else:
         foll = down(up(foll) + via)
     return up(own) + up(shift(prev, axis, -1)) + up(shift(foll, axis, 1))
+
+
+def dispatch(tokens, group_of, group_gain, capacity):
+    num_tok, width = tokens.shape
+    num_groups = group_gain.shape[0]
+    num_slots = num_groups * capacity
+
+    def body(tokens_ref, group_ref, gain_ref, out_ref, position_ref, rows_ref):
+        group = group_ref[...]
+        member = (lax.broadcasted_iota(jnp.int32, (num_groups, num_tok), 0) == group).astype(
+            jnp.float32
+        )
+        before = (
+            lax.broadcasted_iota(jnp.int32, (num_tok, num_tok), 0)
+            < lax.broadcasted_iota(jnp.int32, (num_tok, num_tok), 1)
+        ).astype(jnp.float32)
+        earlier = jnp.dot(
+            member.astype(jnp.bfloat16),
+            before.astype(jnp.bfloat16),
+            preferred_element_type=jnp.float32,
+        )
+        slot = jnp.sum(earlier * member, axis=0, keepdims=True)
+        position = group * capacity + slot.astype(jnp.int32)
+        position_ref[...] = position
+        chosen = lax.broadcasted_iota(jnp.int32, (num_slots, num_tok), 0) == position
+        rows_ref[...] = jnp.dot(
+            chosen.astype(jnp.float32).astype(jnp.bfloat16),
+            tokens_ref[...],
+            preferred_element_type=jnp.float32,
+        )
+        for start in range(0, num_slots, 16):
+            rows = rows_ref[start : start + 16]
+            gains = [
+                jnp.broadcast_to(gain_ref[at // capacity : at // capacity + 1], (8, width))
+                for at in (start, start + 8)
+            ]
+            normed = layer_norm(rows, jnp.concatenate(gains, axis=0))
+            out_ref[start : start + 16] = normed.astype(jnp.bfloat16)
+
+    outgoing, position = pl.pallas_call(
+        body,
+        in_specs=[pl.BlockSpec(memory_space=pltpu.VMEM)] * 3,
+        out_specs=[pl.BlockSpec(memory_space=pltpu.VMEM)] * 2,
+        out_shape=[
+            jax.ShapeDtypeStruct((num_slots, width), jnp.bfloat16),
+            jax.ShapeDtypeStruct((1, num_tok), jnp.int32),
+        ],
+        scratch_shapes=[pltpu.VMEM((num_slots, width), jnp.float32)],
+        compiler_params=pltpu.CompilerParams(vmem_limit_bytes=16 * 1024 * 1024),
+        name="dispatch",
+    )(tokens, group_of.reshape(1, num_tok), group_gain)
+    return outgoing, position[0]
 
 
 def on_chip(value):
@@ -106,18 +158,10 @@
         jnp.int32
     )
     group_of = jnp.sum(lang_hit * lang_group[None, :], axis=1)
-    onehot = (group_of[:, None] == jnp.arange(num_groups, dtype=jnp.int32)[None, :]).astype(
-        jnp.int32
-    )
-    earlier = jnp.cumsum(onehot, axis=0) - onehot
-    slot_index = jnp.sum(earlier * onehot, axis=1)
-    position = group_of * capacity + slot_index
+    outgoing, position = dispatch(tokens, group_of, group_gain, capacity)
     dispatch_map = (
         position[None, :] == jnp.arange(num_groups * capacity, dtype=jnp.int32)[:, None]
     ).astype(bf16)
-    row_gains = pick(group_of, group_gain)
-    normed = layer_norm(residual_in, row_gains).astype(bf16)
-    outgoing = jnp.dot(dispatch_map, normed, preferred_element_type=jnp.float32).astype(bf16)
     count = num_groups * capacity // 2
 
     def exchange(value):

time: 239 us -> 235 us (0.983)
  matrix products: 32.5 us -> 29.3 us
  other arithmetic: 10.4 us -> 7.46 us
    dot_general x1 -> x0, matrix products: 2.78 us -> none  [on_device(): jnp.dot(dispatch_map, normed, preferred_element_type=jnp.float32)]
    unnamed x51 -> x37, local copies, waits for them, and re-layouts: 5.26 us -> 7.29 us
  transfers between devices with their start and end apart: 39 -> 39, of which waited for: 26 -> 28; matrix products, arithmetic and copies ran while one was open for 17% -> 13% of each run, Pallas kernels for 2% -> 3%
where the time goes in v5:
time: 235 us; the launch traced here: 234 us
  waiting for transfers between devices  115 us (49%)
  starting transfers between devices  67.7 us (29%)
  matrix products  29.3 us (12%)
  local copies, waits for them, and re-layouts  8.59 us (4%)
  other arithmetic  7.46 us (3%)
  Pallas kernels  6.15 us (3%)
    ppermute x24, waiting for transfers between devices, shift(): lax.ppermute(value, axis, [(i, (i + step) % size) for i in range(size)])  65.1 us
    ppermute x24, starting transfers between devices, shift(): lax.ppermute(value, axis, [(i, (i + step) % size) for i in range(size)])  38.7 us
    ppermute x4, waiting for transfers between devices, swap_blocks(): return lax.ppermute(value, X, [(0, 3), (3, 0), (1, 2), (2, 1)])  22 us
    all_to_all x3, waiting for transfers between devices, exchange(): lax.all_to_all(value, ('y', 'core'), split_axis=0, concat_axis=0, tiled=T...  13.9 us
    ppermute x5, waiting for transfers between devices, swap_column(): return lax.ppermute(value, 'xl', [(0, 1), (1, 0)])  13.6 us
    all_to_all x3, starting transfers between devices, exchange(): lax.all_to_all(value, ('y', 'core'), split_axis=0, concat_axis=0, tiled=T...  13.4 us
    ppermute x4, starting transfers between devices, swap_blocks(): return lax.ppermute(value, X, [(0, 3), (3, 0), (1, 2), (2, 1)])  11 us
    dot_general x2, matrix products, first(): jnp.dot(rows, w1, preferred_element_type=jnp.float32) + b1  9 us
  transfers between devices with their start and end apart: 39, of which 28 were waited for; matrix products, arithmetic and copies ran while one was open for 13% of the time, Pallas kernels for 3%

profile of v5, /device:TPU:0, one launch (start us, length us, event | category | flops | bytes accessed | tf_op | source)
XLA Modules:
  0.0 234.3 jit_solution(2476181660896533860)
XLA Ops:
  3.2 1.8 dispatch.1
  4.9 4.6 %all-to-all-start = ((bf16[8,24,2048]{2,1,0:T(8,128)(2,1)}), bf16[8,24,2048]{2,1,0:T(8,128)(2,1)S(1)}, u32[]{:S(2)}, u32[]{:S(2)}) async-start(bf16[8,24,2048]{2,1,0:T(8,128)(2,1)} %bitcast.2), calls=%async_computation | async-start | bytes 1572864 | tf_op jit(solution)/shard_map/all_to_all | solution.py:169
  10.0 2.8 %collective-permute-start.9 = (f32[512]{0:T(512)S(1)}, f32[512]{0:T(512)S(1)}, u32[]{:S(2)}, u32[]{:S(2)}) collective-permute-start(f32[512]{0:T(512)S(1)} %bitcast.48), channel_id=1, source_target_pairs={{0,3},{3,0},{1,2},{2,1},{4,7},{7,4},{5,6},{6,5},{8,11},{11,8},{9,1... | collective-permute-start | bytes 6152 | tf_op jit(solution)/shard_map/ppermute | solution.py:28
  12.8 2.0 collective-permute-done.9
  14.8 2.8 %collective-permute-start.10 = (bf16[2048,512]{1,0:T(8,128)(2,1)}, bf16[2048,512]{1,0:T(8,128)(2,1)}, u32[]{:S(2)}, u32[]{:S(2)}) collective-permute-start(bf16[2048,512]{1,0:T(8,128)(2,1)} %bitcast.50), channel_id=1, source_target_pairs={{0,3},{3,0},{1,2},{2,1},{4,7},{7,4},{5,6},{6,5},{8,11},{11,8},{9,1... | collective-permute-start | bytes 6291464 | tf_op jit(solution)/shard_map/ppermute | solution.py:28
  17.6 5.1 %all-to-all-done = bf16[8,24,2048]{2,1,0:T(8,128)(2,1)S(1)} async-done(((bf16[8,24,2048]{2,1,0:T(8,128)(2,1)}), bf16[8,24,2048]{2,1,0:T(8,128)(2,1)S(1)}, u32[]{:S(2)}, u32[]{:S(2)}) %all-to-all-start) | async-done | bytes 786464 | tf_op jit(solution)/shard_map/all_to_all | solution.py:169
  22.7 2.0 collective-permute-start.3
  24.7 2.2 collective-permute-start.4
  26.9 1.5 collective-permute-start.5
  28.6 7.2 %collective-permute-done.3 = bf16[96,2048]{1,0:T(8,128)(2,1)S(1)} collective-permute-done((bf16[96,2048]{1,0:T(8,128)(2,1)S(1)}, bf16[96,2048]{1,0:T(8,128)(2,1)S(1)}, u32[]{:S(2)}, u32[]{:S(2)}) %collective-permute-start.3) | collective-permute-done | bytes 393248 | tf_op jit(solution)/shard_map/ppermute | solution.py:20
  35.9 1.4 collective-permute-done.5
  37.3 1.5 collective-permute-start.11
  38.9 2.0 collective-permute-start.7
  40.8 6.3 %collective-permute-done.6 = bf16[96,2048]{1,0:T(8,128)(2,1)S(1)} collective-permute-done((bf16[96,2048]{1,0:T(8,128)(2,1)S(1)}, bf16[96,2048]{1,0:T(8,128)(2,1)S(1)}, u32[]{:S(2)}, u32[]{:S(2)}) %collective-permute-start.6) | collective-permute-done | bytes 393248 | tf_op jit(solution)/shard_map/ppermute | solution.py:20
  47.3 2.2 on_chip.2
  49.5 2.0 copy-done.2
  51.4 2.2 on_chip.3
  53.6 2.0 copy-done
  55.6 2.8 %collective-permute-start.14 = (bf16[512,1024]{1,0:T(8,128)(2,1)S(1)}, bf16[512,1024]{1,0:T(8,128)(2,1)S(1)}, u32[]{:S(2)}, u32[]{:S(2)}) collective-permute-start(bf16[512,1024]{1,0:T(8,128)(2,1)S(1)} %get-tuple-element.61), channel_id=1, source_target_pairs={{0,3},{3,0},{1,2},{2,1},{4,7},{7,4},{5,6},{6,5},{8,11},{11,8},{9,1... | collective-permute-start | bytes 3145736 | tf_op jit(solution)/shard_map/ppermute | solution.py:28
  58.5 3.3 %collective-permute-start.13 = (bf16[192,2048]{1,0:T(8,128)(2,1)S(1)}, bf16[192,2048]{1,0:T(8,128)(2,1)S(1)}, u32[]{:S(2)}, u32[]{:S(2)}) collective-permute-start(bf16[192,2048]{1,0:T(8,128)(2,1)S(1)} %collective-permute-done.7), channel_id=1, source_target_pairs={{0,12},{4,0},{8,4},{12,8},{1,13},{5,1},{9,5},{13,9},{2,14},{6,2},{... | collective-permute-start | bytes 2359304 | tf_op jit(solution)/shard_map/ppermute | solution.py:20
  61.9 1.8 collective-permute-done.11
  66.1 2.8 %collective-permute-start.17 = (bf16[512,1024]{1,0:T(8,128)(2,1)S(1)}, bf16[512,1024]{1,0:T(8,128)(2,1)S(1)}, u32[]{:S(2)}, u32[]{:S(2)}) collective-permute-start(bf16[512,1024]{1,0:T(8,128)(2,1)S(1)} %get-tuple-element.62), channel_id=1, source_target_pairs={{0,3},{3,0},{1,2},{2,1},{4,7},{7,4},{5,6},{6,5},{8,11},{11,8},{9,1... | collective-permute-start | bytes 3145736 | tf_op jit(solution)/shard_map/ppermute | solution.py:28
  69.1 6.0 %maximum_convert_fusion = bf16[1248,1024]{1,0:T(8,128)(2,1)S(1)} fusion(bf16[1248,2048]{1,0:T(8,128)(2,1)S(1)} %constant_dynamic-update-slice_fusion, bf16[2048,512]{1,0:T(8,128)(2,1)} %collective-permute-done.10, bf16[2048,512]{1,0:T(8,128)(2,1)S(1)} %bitcast.51, f32[1024]{0:T(1024)S(1)} %pad_maximum_fusion.22), kind=kOutput, calls=%fused_computation | convolution fusion | flops 5246713856 | bytes 11866112 | tf_op jit(solution)/shard_map/dot_general | solution.py:202
  75.1 1.4 collective-permute-done.13
  76.6 3.0 %fusion.12 = bf16[288,1024]{1,0:T(8,128)(2,1)S(1)} fusion(bf16[2048,512]{1,0:T(8,128)(2,1)} %collective-permute-done.10, bf16[2048,512]{1,0:T(8,128)(2,1)S(1)} %bitcast.52, bf16[192,2048]{1,0:T(8,128)(2,1)S(1)} %collective-permute-done.13, bf16[96,2048]{1,0:T(8,128)(2,1)S(1)} %collective-permute-done.12, f32[1024]{0:T(1024)S(1)} %pad_maximum_fusion.22), kind=kOutput, calls=%fused_computation.24 | convolution fusion | flops 1219592192 | bytes 5967872 | tf_op jit(solution)/shard_map/dot_general | solution.py:202
  79.5 7.7 %collective-permute-done.14 = bf16[512,1024]{1,0:T(8,128)(2,1)S(1)} collective-permute-done((bf16[512,1024]{1,0:T(8,128)(2,1)S(1)}, bf16[512,1024]{1,0:T(8,128)(2,1)S(1)}, u32[]{:S(2)}, u32[]{:S(2)}) %collective-permute-start.14) | collective-permute-done | bytes 1048608 | tf_op jit(solution)/shard_map/ppermute | solution.py:28
  87.3 4.3 %convolution_convert_fusion.1 = bf16[1536,1024]{1,0:T(8,128)(2,1)S(1)} fusion(bf16[512,1024]{1,0:T(8,128)(2,1)S(1)} %collective-permute-done.14, bf16[512,1024]{1,0:T(8,128)(2,1)S(1)} %get-tuple-element.61, bf16[288,1024]{1,0:T(8,128)(2,1)S(1)} %fusion.12, bf16[1248,1024]{1,0:T(8,128)(2,1)S(1)} %maximum_convert_fusion), kind=kOutput, calls=%fused_computation.3 | convolution fusion | flops 3233284096 | bytes 8388608 | tf_op jit(solution)/shard_map/dot_general | solution.py:208
  92.0 2.0 collective-permute-start.16
  94.1 2.2 collective-permute-start.15
  96.6 11.0 %collective-permute-done.17 = bf16[512,1024]{1,0:T(8,128)(2,1)S(1)} collective-permute-done((bf16[512,1024]{1,0:T(8,128)(2,1)S(1)}, bf16[512,1024]{1,0:T(8,128)(2,1)S(1)}, u32[]{:S(2)}, u32[]{:S(2)}) %collective-permute-start.17) | collective-permute-done | bytes 1048608 | tf_op jit(solution)/shard_map/ppermute | solution.py:28
  107.6 2.1 collective-permute-done.16
  110.3 3.0 %collective-permute-start.20 = (bf16[384,1024]{1,0:T(8,128)(2,1)S(1)}, bf16[384,1024]{1,0:T(8,128)(2,1)S(1)}, u32[]{:S(2)}, u32[]{:S(2)}) collective-permute-start(bf16[384,1024]{1,0:T(8,128)(2,1)S(1)} %add_convert_fusion.1), channel_id=1, source_target_pairs={{0,12},{4,0},{8,4},{12,8},{1,13},{5,1},{9,5},{13,9},{2,14},{6,2},{... | collective-permute-start | bytes 2359304 | tf_op jit(solution)/shard_map/ppermute | solution.py:20
  113.3 3.8 %convolution_convert_fusion = bf16[1536,1024]{1,0:T(8,128)(2,1)S(1)} fusion(bf16[1536,1024]{1,0:T(8,128)(2,1)S(1)} %pad_maximum_fusion.1, bf16[512,1024]{1,0:T(8,128)(2,1)S(1)} %collective-permute-done.17, bf16[512,1024]{1,0:T(8,128)(2,1)S(1)} %get-tuple-element.62), kind=kOutput, calls=%fused_computation.2 | convolution fusion | flops 3226992640 | bytes 8388608 | tf_op jit(solution)/shard_map/dot_general | solution.py:208
  117.5 9.5 %collective-permute-done.20 = bf16[384,1024]{1,0:T(8,128)(2,1)S(1)} collective-permute-done((bf16[384,1024]{1,0:T(8,128)(2,1)S(1)}, bf16[384,1024]{1,0:T(8,128)(2,1)S(1)}, u32[]{:S(2)}, u32[]{:S(2)}) %collective-permute-start.20) | collective-permute-done | bytes 786464 | tf_op jit(solution)/shard_map/ppermute | solution.py:20
  127.7 3.8 %collective-permute-start.18 = (bf16[384,1024]{1,0:T(8,128)(2,1)S(1)}, bf16[384,1024]{1,0:T(8,128)(2,1)S(1)}, u32[]{:S(2)}, u32[]{:S(2)}) collective-permute-start(bf16[384,1024]{1,0:T(8,128)(2,1)S(1)} %pad_maximum_fusion.16), channel_id=1, source_target_pairs={{0,12},{4,0},{8,4},{12,8},{1,13},{5,1},{9,5},{13,9},{2,14},{6,2},{... | collective-permute-start | bytes 2359304 | tf_op jit(solution)/shard_map/ppermute | solution.py:20
  131.4 3.3 %collective-permute-done.19 = bf16[384,1024]{1,0:T(8,128)(2,1)S(1)} collective-permute-done((bf16[384,1024]{1,0:T(8,128)(2,1)S(1)}, bf16[384,1024]{1,0:T(8,128)(2,1)S(1)}, u32[]{:S(2)}, u32[]{:S(2)}) %collective-permute-start.19) | collective-permute-done | bytes 786464 | tf_op jit(solution)/shard_map/ppermute | solution.py:20
  135.7 1.9 collective-permute-start.22
  138.5 5.4 %all-to-all-start.1 = ((bf16[8,24,1024]{2,1,0:T(8,128)(2,1)}), bf16[8,24,1024]{2,1,0:T(8,128)(2,1)}, u32[]{:S(2)}, u32[]{:S(2)}) async-start(bf16[8,24,1024]{2,1,0:T(8,128)(2,1)} %bitcast.8), calls=%async_computation.1 | async-start | bytes 786432 | tf_op jit(solution)/shard_map/all_to_all | solution.py:169
  144.3 7.9 %collective-permute-done.22 = bf16[384,1024]{1,0:T(8,128)(2,1)} collective-permute-done((bf16[384,1024]{1,0:T(8,128)(2,1)S(1)}, bf16[384,1024]{1,0:T(8,128)(2,1)}, u32[]{:S(2)}, u32[]{:S(2)}) %collective-permute-start.22) | collective-permute-done | bytes 786464 | tf_op jit(solution)/shard_map/ppermute | solution.py:20
  152.2 1.6 convert_add_fusion
  154.0 9.7 %collective-permute-done.23 = bf16[192,1024]{1,0:T(8,128)(2,1)S(1)} collective-permute-done((bf16[192,1024]{1,0:T(8,128)(2,1)S(1)}, bf16[192,1024]{1,0:T(8,128)(2,1)S(1)}, u32[]{:S(2)}, u32[]{:S(2)}) %collective-permute-start.23) | collective-permute-done | bytes 393248 | tf_op jit(solution)/shard_map/ppermute | solution.py:24
  164.6 3.5 %all-to-all-start.2 = ((bf16[8,24,1024]{2,1,0:T(8,128)(2,1)}), bf16[8,24,1024]{2,1,0:T(8,128)(2,1)S(1)}, u32[]{:S(2)}, u32[]{:S(2)}) async-start(bf16[8,24,1024]{2,1,0:T(8,128)(2,1)} %bitcast.10), calls=%async_computation.2 | async-start | bytes 786432 | tf_op jit(solution)/shard_map/all_to_all | solution.py:169
  168.1 8.8 %all-to-all-done.2 = bf16[8,24,1024]{2,1,0:T(8,128)(2,1)S(1)} async-done(((bf16[8,24,1024]{2,1,0:T(8,128)(2,1)}), bf16[8,24,1024]{2,1,0:T(8,128)(2,1)S(1)}, u32[]{:S(2)}, u32[]{:S(2)}) %all-to-all-start.2) | async-done | bytes 393248 | tf_op jit(solution)/shard_map/all_to_all | solution.py:169
  176.9 2.0 fusion.47
  180.1 2.7 %collective-permute-start.25 = (bf16[64,2048]{1,0:T(8,128)(2,1)S(1)}, bf16[64,2048]{1,0:T(8,128)(2,1)S(1)}, u32[]{:S(2)}, u32[]{:S(2)}) collective-permute-start(bf16[64,2048]{1,0:T(8,128)(2,1)S(1)} %get-tuple-element.123), channel_id=1, source_target_pairs={{0,96},{32,0},{64,32},{96,64},{1,97},{33,1},{65,33},{97,65},{2,98}... | collective-permute-start | bytes 786440 | tf_op jit(solution)/shard_map/ppermute | solution.py:20
  182.7 5.8 %collective-permute-done.24 = bf16[64,2048]{1,0:T(8,128)(2,1)S(1)} collective-permute-done((bf16[64,2048]{1,0:T(8,128)(2,1)S(1)}, bf16[64,2048]{1,0:T(8,128)(2,1)S(1)}, u32[]{:S(2)}, u32[]{:S(2)}) %collective-permute-start.24) | collective-permute-done | bytes 262176 | tf_op jit(solution)/shard_map/ppermute | solution.py:20
  188.6 3.2 %collective-permute-start.27 = (bf16[64,2048]{1,0:T(8,128)(2,1)S(1)}, bf16[64,2048]{1,0:T(8,128)(2,1)S(1)}, u32[]{:S(2)}, u32[]{:S(2)}) collective-permute-start(bf16[64,2048]{1,0:T(8,128)(2,1)S(1)} %get-tuple-element.78), channel_id=1, source_target_pairs={{0,96},{32,0},{64,32},{96,64},{1,97},{33,1},{65,33},{97,65},{2,98}... | collective-permute-start | bytes 786440 | tf_op jit(solution)/shard_map/ppermute | solution.py:20
  191.8 4.9 %collective-permute-done.26 = bf16[64,2048]{1,0:T(8,128)(2,1)S(1)} collective-permute-done((bf16[64,2048]{1,0:T(8,128)(2,1)S(1)}, bf16[64,2048]{1,0:T(8,128)(2,1)S(1)}, u32[]{:S(2)}, u32[]{:S(2)}) %collective-permute-start.26) | collective-permute-done | bytes 262176 | tf_op jit(solution)/shard_map/ppermute | solution.py:20
  196.7 1.3 fusion.17
  198.0 1.3 fusion.18
  200.2 1.3 fusion.48
  201.7 1.3 fusion.1
  203.0 2.3 collective-permute-start.29
  205.4 2.0 collective-permute-start.31
  207.4 4.5 %collective-permute-done.29 = bf16[64,2048]{1,0:T(8,128)(2,1)S(1)} collective-permute-done((bf16[64,2048]{1,0:T(8,128)(2,1)S(1)}, bf16[64,2048]{1,0:T(8,128)(2,1)S(1)}, u32[]{:S(2)}, u32[]{:S(2)}) %collective-permute-start.29) | collective-permute-done | bytes 262176 | tf_op jit(solution)/shard_map/ppermute | solution.py:20
  211.9 1.3 fusion.20
  213.2 1.3 fusion.19
  214.8 1.3 fusion.49
  216.1 1.3 fusion.2
  217.5 3.2 %collective-permute-start.32 = (bf16[64,2048]{1,0:T(8,128)(2,1)S(1)}, bf16[64,2048]{1,0:T(8,128)(2,1)S(1)}, u32[]{:S(2)}, u32[]{:S(2)}) collective-permute-start(bf16[64,2048]{1,0:T(8,128)(2,1)S(1)} %add_convert_fusion.4), channel_id=1, source_target_pairs={{0,96},{32,0},{64,32},{96,64},{1,97},{33,1},{65,33},{97,65},{2,98}... | collective-permute-start | bytes 786440 | tf_op jit(solution)/shard_map/ppermute | solution.py:20
  220.7 1.9 collective-permute-start.33
  222.6 2.7 %collective-permute-done.34 = bf16[64,2048]{1,0:T(8,128)(2,1)S(1)} collective-permute-done((bf16[64,2048]{1,0:T(8,128)(2,1)S(1)}, bf16[64,2048]{1,0:T(8,128)(2,1)S(1)}, u32[]{:S(2)}, u32[]{:S(2)}) %collective-permute-start.34) | collective-permute-done | bytes 262176 | tf_op jit(solution)/shard_map/ppermute | solution.py:20
  226.0 2.7 %collective-permute-done.33 = bf16[64,2048]{1,0:T(8,128)(2,1)S(1)} collective-permute-done((bf16[64,2048]{1,0:T(8,128)(2,1)S(1)}, bf16[64,2048]{1,0:T(8,128)(2,1)S(1)}, u32[]{:S(2)}, u32[]{:S(2)}) %collective-permute-start.33) | collective-permute-done | bytes 262176 | tf_op jit(solution)/shard_map/ppermute | solution.py:20
  228.7 4.6 %collective-permute-done.35 = bf16[64,2048]{1,0:T(8,128)(2,1)S(1)} collective-permute-done((bf16[64,2048]{1,0:T(8,128)(2,1)S(1)}, bf16[64,2048]{1,0:T(8,128)(2,1)S(1)}, u32[]{:S(2)}, u32[]{:S(2)}) %collective-permute-start.35) | collective-permute-done | bytes 262176 | tf_op jit(solution)/shard_map/ppermute | solution.py:20
  (103 shorter events, 17.3 us)
Async XLA Ops:
  0.0 10.0 %copy-start.11 = (f32[1,512]{1,0:T(1,128)S(1)}, f32[1,512]{1,0:T(1,128)}, u32[]{:S(2)}) copy-start(f32[1,512]{1,0:T(1,128)} %param.18) | copy-start | bytes 6148
  0.0 22.7 %collective-permute-start = (bf16[2048,1024]{1,0:T(8,128)(2,1)}, bf16[2048,1024]{1,0:T(8,128)(2,1)}, u32[]{:S(2)}, u32[]{:S(2)}) collective-permute-start(bf16[2048,1024]{1,0:T(8,128)(2,1)} %param.22), channel_id=1, source_target_pairs={{0,16},{16,0},{1,17},{17,1},{2,18},{18,2},{3,19},{19,3},{4,20},{20... | collective-permute-start | bytes 12582920 | tf_op jit(solution)/shard_map/ppermute | solution.py:32
  0.0 22.7 %collective-permute-start.1 = (bf16[1024,2048]{1,0:T(8,128)(2,1)}, bf16[1024,2048]{1,0:T(8,128)(2,1)}, u32[]{:S(2)}, u32[]{:S(2)}) collective-permute-start(bf16[1024,2048]{1,0:T(8,128)(2,1)} %param.24), channel_id=1, source_target_pairs={{0,16},{16,0},{1,17},{17,1},{2,18},{18,2},{3,19},{19,3},{4,20},{20... | collective-permute-start | bytes 12582920 | tf_op jit(solution)/shard_map/ppermute | solution.py:32
  1.3 1.0 copy-start.4
  2.3 0.8 copy-start.6
  3.2 6.3 %copy-start.15 = (f32[1024]{0:T(1024)S(1)}, f32[1024]{0:T(1024)}, u32[]{:S(2)}) copy-start(f32[1024]{0:T(1024)} %param.23) | copy-start | bytes 12292
  3.2 25.2 %copy-start.7 = (bf16[1,512,2048]{2,1,0:T(8,128)(2,1)S(1)}, bf16[1,512,2048]{2,1,0:T(8,128)(2,1)}, u32[]{:S(2)}) copy-start(bf16[1,512,2048]{2,1,0:T(8,128)(2,1)} %param.19) | copy-start | bytes 6291460
  4.9 17.7 %all-to-all-start = ((bf16[8,24,2048]{2,1,0:T(8,128)(2,1)}), bf16[8,24,2048]{2,1,0:T(8,128)(2,1)S(1)}, u32[]{:S(2)}, u32[]{:S(2)}) async-start(bf16[8,24,2048]{2,1,0:T(8,128)(2,1)} %bitcast.2), calls=%async_computation | async-start | bytes 1572864 | tf_op jit(solution)/shard_map/all_to_all | solution.py:169
  9.5 8.1 %collective-permute-start.2 = (f32[1024]{0:T(1024)S(1)}, f32[1024]{0:T(1024)S(1)}, u32[]{:S(2)}, u32[]{:S(2)}) collective-permute-start(f32[1024]{0:T(1024)S(1)} %copy-done.15), channel_id=1, source_target_pairs={{0,16},{16,0},{1,17},{17,1},{2,18},{18,2},{3,19},{19,3},{4,20},{20... | collective-permute-start | bytes 12296 | tf_op jit(solution)/shard_map/ppermute | solution.py:32
  10.0 4.8 %collective-permute-start.9 = (f32[512]{0:T(512)S(1)}, f32[512]{0:T(512)S(1)}, u32[]{:S(2)}, u32[]{:S(2)}) collective-permute-start(f32[512]{0:T(512)S(1)} %bitcast.48), channel_id=1, source_target_pairs={{0,3},{3,0},{1,2},{2,1},{4,7},{7,4},{5,6},{6,5},{8,11},{11,8},{9,1... | collective-permute-start | bytes 6152 | tf_op jit(solution)/shard_map/ppermute | solution.py:28
  14.8 50.1 %collective-permute-start.10 = (bf16[2048,512]{1,0:T(8,128)(2,1)}, bf16[2048,512]{1,0:T(8,128)(2,1)}, u32[]{:S(2)}, u32[]{:S(2)}) collective-permute-start(bf16[2048,512]{1,0:T(8,128)(2,1)} %bitcast.50), channel_id=1, source_target_pairs={{0,3},{3,0},{1,2},{2,1},{4,7},{7,4},{5,6},{6,5},{8,11},{11,8},{9,1... | collective-permute-start | bytes 6291464 | tf_op jit(solution)/shard_map/ppermute | solution.py:28
  22.7 13.0 %collective-permute-start.3 = (bf16[96,2048]{1,0:T(8,128)(2,1)S(1)}, bf16[96,2048]{1,0:T(8,128)(2,1)S(1)}, u32[]{:S(2)}, u32[]{:S(2)}) collective-permute-start(bf16[96,2048]{1,0:T(8,128)(2,1)S(1)} %get-tuple-element.122), channel_id=1, source_target_pairs={{0,4},{4,8},{8,12},{12,0},{1,5},{5,9},{9,13},{13,1},{2,6},{6,10},{... | collective-permute-start | bytes 1179656 | tf_op jit(solution)/shard_map/ppermute | solution.py:20
  24.7 11.0 %collective-permute-start.4 = (bf16[96,2048]{1,0:T(8,128)(2,1)S(1)}, bf16[96,2048]{1,0:T(8,128)(2,1)S(1)}, u32[]{:S(2)}, u32[]{:S(2)}) collective-permute-start(bf16[96,2048]{1,0:T(8,128)(2,1)S(1)} %get-tuple-element.122), channel_id=1, source_target_pairs={{0,12},{4,0},{8,4},{12,8},{1,13},{5,1},{9,5},{13,9},{2,14},{6,2},{... | collective-permute-start | bytes 1179656 | tf_op jit(solution)/shard_map/ppermute | solution.py:20
  26.9 10.4 %collective-permute-start.5 = (bf16[96,2048]{1,0:T(8,128)(2,1)S(1)}, bf16[96,2048]{1,0:T(8,128)(2,1)S(1)}, u32[]{:S(2)}, u32[]{:S(2)}) collective-permute-start(bf16[96,2048]{1,0:T(8,128)(2,1)S(1)} %get-tuple-element.121), channel_id=1, source_target_pairs={{0,1},{1,0},{2,3},{3,2},{4,5},{5,4},{6,7},{7,6},{8,9},{9,8},{10,11... | collective-permute-start | bytes 1179656 | tf_op jit(solution)/shard_map/ppermute | solution.py:24
  35.7 11.4 %collective-permute-start.6 = (bf16[96,2048]{1,0:T(8,128)(2,1)S(1)}, bf16[96,2048]{1,0:T(8,128)(2,1)S(1)}, u32[]{:S(2)}, u32[]{:S(2)}) collective-permute-start(bf16[96,2048]{1,0:T(8,128)(2,1)S(1)} %collective-permute-done.3), channel_id=1, source_target_pairs={{0,4},{4,8},{8,12},{12,0},{1,5},{5,9},{9,13},{13,1},{2,6},{6,10},{... | collective-permute-start | bytes 1179656 | tf_op jit(solution)/shard_map/ppermute | solution.py:20
  37.3 26.4 %collective-permute-start.11 = (bf16[288,2048]{1,0:T(8,128)(2,1)S(1)}, bf16[288,2048]{1,0:T(8,128)(2,1)S(1)}, u32[]{:S(2)}, u32[]{:S(2)}) collective-permute-start(bf16[288,2048]{1,0:T(8,128)(2,1)S(1)} %pad_maximum_fusion.10), channel_id=1, source_target_pairs={{0,1},{1,0},{2,3},{3,2},{4,5},{5,4},{6,7},{7,6},{8,9},{9,8},{10,11... | collective-permute-start | bytes 3538952 | tf_op jit(solution)/shard_map/ppermute | solution.py:24
  38.9 19.6 %collective-permute-start.7 = (bf16[192,2048]{1,0:T(8,128)(2,1)S(1)}, bf16[192,2048]{1,0:T(8,128)(2,1)S(1)}, u32[]{:S(2)}, u32[]{:S(2)}) collective-permute-start(bf16[192,2048]{1,0:T(8,128)(2,1)S(1)} %pad_maximum_fusion.13), channel_id=1, source_target_pairs={{0,12},{4,0},{8,4},{12,8},{1,13},{5,1},{9,5},{13,9},{2,14},{6,2},{... | collective-permute-start | bytes 2359304 | tf_op jit(solution)/shard_map/ppermute | solution.py:20
  47.1 19.0 %collective-permute-start.8 = (bf16[192,2048]{1,0:T(8,128)(2,1)S(1)}, bf16[192,2048]{1,0:T(8,128)(2,1)S(1)}, u32[]{:S(2)}, u32[]{:S(2)}) collective-permute-start(bf16[192,2048]{1,0:T(8,128)(2,1)S(1)} %pad_maximum_fusion.13), channel_id=1, source_target_pairs={{0,4},{4,8},{8,12},{12,0},{1,5},{5,9},{9,13},{13,1},{2,6},{6,10},{... | collective-permute-start | bytes 2359304 | tf_op jit(solution)/shard_map/ppermute | solution.py:20
  49.5 2.0 copy-start.2
  53.6 2.0 copy-start
  55.6 31.6 %collective-permute-start.14 = (bf16[512,1024]{1,0:T(8,128)(2,1)S(1)}, bf16[512,1024]{1,0:T(8,128)(2,1)S(1)}, u32[]{:S(2)}, u32[]{:S(2)}) collective-permute-start(bf16[512,1024]{1,0:T(8,128)(2,1)S(1)} %get-tuple-element.61), channel_id=1, source_target_pairs={{0,3},{3,0},{1,2},{2,1},{4,7},{7,4},{5,6},{6,5},{8,11},{11,8},{9,1... | collective-permute-start | bytes 3145736 | tf_op jit(solution)/shard_map/ppermute | solution.py:28
  58.5 18.1 %collective-permute-start.13 = (bf16[192,2048]{1,0:T(8,128)(2,1)S(1)}, bf16[192,2048]{1,0:T(8,128)(2,1)S(1)}, u32[]{:S(2)}, u32[]{:S(2)}) collective-permute-start(bf16[192,2048]{1,0:T(8,128)(2,1)S(1)} %collective-permute-done.7), channel_id=1, source_target_pairs={{0,12},{4,0},{8,4},{12,8},{1,13},{5,1},{9,5},{13,9},{2,14},{6,2},{... | collective-permute-start | bytes 2359304 | tf_op jit(solution)/shard_map/ppermute | solution.py:20
  61.9 7.2 %copy-start.14 = (bf16[1,2048,512]{2,1,0:T(8,128)(2,1)S(1)}, bf16[1,2048,512]{2,1,0:T(8,128)(2,1)}, u32[]{:S(2)}) copy-start(bf16[1,2048,512]{2,1,0:T(8,128)(2,1)} %param.17) | copy-start | bytes 6291460
  64.9 11.7 %collective-permute-start.12 = (bf16[96,2048]{1,0:T(8,128)(2,1)S(1)}, bf16[96,2048]{1,0:T(8,128)(2,1)S(1)}, u32[]{:S(2)}, u32[]{:S(2)}) collective-permute-start(bf16[96,2048]{1,0:T(8,128)(2,1)S(1)} %collective-permute-done.6), channel_id=1, source_target_pairs={{0,1},{1,0},{2,3},{3,2},{4,5},{5,4},{6,7},{7,6},{8,9},{9,8},{10,11... | collective-permute-start | bytes 1179656 | tf_op jit(solution)/shard_map/ppermute | solution.py:24
  66.1 41.5 %collective-permute-start.17 = (bf16[512,1024]{1,0:T(8,128)(2,1)S(1)}, bf16[512,1024]{1,0:T(8,128)(2,1)S(1)}, u32[]{:S(2)}, u32[]{:S(2)}) collective-permute-start(bf16[512,1024]{1,0:T(8,128)(2,1)S(1)} %get-tuple-element.62), channel_id=1, source_target_pairs={{0,3},{3,0},{1,2},{2,1},{4,7},{7,4},{5,6},{6,5},{8,11},{11,8},{9,1... | collective-permute-start | bytes 3145736 | tf_op jit(solution)/shard_map/ppermute | solution.py:28
  92.0 17.7 %collective-permute-start.16 = (bf16[384,1024]{1,0:T(8,128)(2,1)S(1)}, bf16[384,1024]{1,0:T(8,128)(2,1)S(1)}, u32[]{:S(2)}, u32[]{:S(2)}) collective-permute-start(bf16[384,1024]{1,0:T(8,128)(2,1)S(1)} %pad_maximum_fusion.15), channel_id=1, source_target_pairs={{0,4},{4,8},{8,12},{12,0},{1,5},{5,9},{9,13},{13,1},{2,6},{6,10},{... | collective-permute-start | bytes 2359304 | tf_op jit(solution)/shard_map/ppermute | solution.py:20
  94.1 15.9 %collective-permute-start.15 = (bf16[384,1024]{1,0:T(8,128)(2,1)S(1)}, bf16[384,1024]{1,0:T(8,128)(2,1)S(1)}, u32[]{:S(2)}, u32[]{:S(2)}) collective-permute-start(bf16[384,1024]{1,0:T(8,128)(2,1)S(1)} %pad_maximum_fusion.14), channel_id=1, source_target_pairs={{0,12},{4,0},{8,4},{12,8},{1,13},{5,1},{9,5},{13,9},{2,14},{6,2},{... | collective-permute-start | bytes 2359304 | tf_op jit(solution)/shard_map/ppermute | solution.py:20
  110.3 16.8 %collective-permute-start.20 = (bf16[384,1024]{1,0:T(8,128)(2,1)S(1)}, bf16[384,1024]{1,0:T(8,128)(2,1)S(1)}, u32[]{:S(2)}, u32[]{:S(2)}) collective-permute-start(bf16[384,1024]{1,0:T(8,128)(2,1)S(1)} %add_convert_fusion.1), channel_id=1, source_target_pairs={{0,12},{4,0},{8,4},{12,8},{1,13},{5,1},{9,5},{13,9},{2,14},{6,2},{... | collective-permute-start | bytes 2359304 | tf_op jit(solution)/shard_map/ppermute | solution.py:20
  117.4 17.3 %collective-permute-start.19 = (bf16[384,1024]{1,0:T(8,128)(2,1)S(1)}, bf16[384,1024]{1,0:T(8,128)(2,1)S(1)}, u32[]{:S(2)}, u32[]{:S(2)}) collective-permute-start(bf16[384,1024]{1,0:T(8,128)(2,1)S(1)} %pad_maximum_fusion.17), channel_id=1, source_target_pairs={{0,4},{4,8},{8,12},{12,0},{1,5},{5,9},{9,13},{13,1},{2,6},{6,10},{... | collective-permute-start | bytes 2359304 | tf_op jit(solution)/shard_map/ppermute | solution.py:20
  127.5 7.9 %collective-permute-start.21 = (bf16[192,1024]{1,0:T(8,128)(2,1)S(1)}, bf16[192,1024]{1,0:T(8,128)(2,1)S(1)}, u32[]{:S(2)}, u32[]{:S(2)}) collective-permute-start(bf16[192,1024]{1,0:T(8,128)(2,1)S(1)} %slice.248), channel_id=1, source_target_pairs={{0,1},{1,0},{2,3},{3,2},{4,5},{5,4},{6,7},{7,6},{8,9},{9,8},{10,11... | collective-permute-start | bytes 1179656 | tf_op jit(solution)/shard_map/ppermute | solution.py:24
  127.7 16.6 %collective-permute-start.18 = (bf16[384,1024]{1,0:T(8,128)(2,1)S(1)}, bf16[384,1024]{1,0:T(8,128)(2,1)S(1)}, u32[]{:S(2)}, u32[]{:S(2)}) collective-permute-start(bf16[384,1024]{1,0:T(8,128)(2,1)S(1)} %pad_maximum_fusion.16), channel_id=1, source_target_pairs={{0,12},{4,0},{8,4},{12,8},{1,13},{5,1},{9,5},{13,9},{2,14},{6,2},{... | collective-permute-start | bytes 2359304 | tf_op jit(solution)/shard_map/ppermute | solution.py:20
  135.7 16.5 %collective-permute-start.22 = (bf16[384,1024]{1,0:T(8,128)(2,1)S(1)}, bf16[384,1024]{1,0:T(8,128)(2,1)}, u32[]{:S(2)}, u32[]{:S(2)}) collective-permute-start(bf16[384,1024]{1,0:T(8,128)(2,1)S(1)} %add_convert_fusion), channel_id=1, source_target_pairs={{0,4},{4,8},{8,12},{12,0},{1,5},{5,9},{9,13},{13,1},{2,6},{6,10},{... | collective-permute-start | bytes 2359304 | tf_op jit(solution)/shard_map/ppermute | solution.py:20
  138.5 15.3 %all-to-all-start.1 = ((bf16[8,24,1024]{2,1,0:T(8,128)(2,1)}), bf16[8,24,1024]{2,1,0:T(8,128)(2,1)}, u32[]{:S(2)}, u32[]{:S(2)}) async-start(bf16[8,24,1024]{2,1,0:T(8,128)(2,1)} %bitcast.8), calls=%async_computation.1 | async-start | bytes 786432 | tf_op jit(solution)/shard_map/all_to_all | solution.py:169
  153.8 14.3 %copy-start.8 = (f32[8,2048]{1,0:T(8,128)S(1)}, f32[8,2048]{1,0:T(8,128)}, u32[]{:S(2)}) copy-start(f32[8,2048]{1,0:T(8,128)} %param.20) | copy-start | bytes 196612
  153.8 23.1 %copy-start.5 = (bf16[128,2048]{1,0:T(8,128)(2,1)S(1)}, bf16[128,2048]{1,0:T(8,128)(2,1)}, u32[]{:S(2)}) copy-start(bf16[128,2048]{1,0:T(8,128)(2,1)} %tokens_ref.1) | copy-start | bytes 1572868
  153.9 9.9 %collective-permute-start.23 = (bf16[192,1024]{1,0:T(8,128)(2,1)S(1)}, bf16[192,1024]{1,0:T(8,128)(2,1)S(1)}, u32[]{:S(2)}, u32[]{:S(2)}) collective-permute-start(bf16[192,1024]{1,0:T(8,128)(2,1)S(1)} %slice.247), channel_id=1, source_target_pairs={{0,1},{1,0},{2,3},{3,2},{4,5},{5,4},{6,7},{7,6},{8,9},{9,8},{10,11... | collective-permute-start | bytes 1179656 | tf_op jit(solution)/shard_map/ppermute | solution.py:24
  164.6 12.3 %all-to-all-start.2 = ((bf16[8,24,1024]{2,1,0:T(8,128)(2,1)}), bf16[8,24,1024]{2,1,0:T(8,128)(2,1)S(1)}, u32[]{:S(2)}, u32[]{:S(2)}) async-start(bf16[8,24,1024]{2,1,0:T(8,128)(2,1)} %bitcast.10), calls=%async_computation.2 | async-start | bytes 786432 | tf_op jit(solution)/shard_map/all_to_all | solution.py:169
  176.9 2.3 copy-start.9
  176.9 19.8 %copy-start.12 = (bf16[2048,1024]{1,0:T(8,128)(2,1)S(1)}, bf16[2048,1024]{1,0:T(8,128)(2,1)}, u32[]{:S(2)}) copy-start(bf16[2048,1024]{1,0:T(8,128)(2,1)} %param.22) | copy-start | bytes 12582916
  179.4 9.1 %collective-permute-start.24 = (bf16[64,2048]{1,0:T(8,128)(2,1)S(1)}, bf16[64,2048]{1,0:T(8,128)(2,1)S(1)}, u32[]{:S(2)}, u32[]{:S(2)}) collective-permute-start(bf16[64,2048]{1,0:T(8,128)(2,1)S(1)} %get-tuple-element.123), channel_id=1, source_target_pairs={{0,32},{32,64},{64,96},{96,0},{1,33},{33,65},{65,97},{97,1},{2,34}... | collective-permute-start | bytes 786440 | tf_op jit(solution)/shard_map/ppermute | solution.py:20
  180.1 8.5 %collective-permute-start.25 = (bf16[64,2048]{1,0:T(8,128)(2,1)S(1)}, bf16[64,2048]{1,0:T(8,128)(2,1)S(1)}, u32[]{:S(2)}, u32[]{:S(2)}) collective-permute-start(bf16[64,2048]{1,0:T(8,128)(2,1)S(1)} %get-tuple-element.123), channel_id=1, source_target_pairs={{0,96},{32,0},{64,32},{96,64},{1,97},{33,1},{65,33},{97,65},{2,98}... | collective-permute-start | bytes 786440 | tf_op jit(solution)/shard_map/ppermute | solution.py:20
  188.5 8.2 %collective-permute-start.26 = (bf16[64,2048]{1,0:T(8,128)(2,1)S(1)}, bf16[64,2048]{1,0:T(8,128)(2,1)S(1)}, u32[]{:S(2)}, u32[]{:S(2)}) collective-permute-start(bf16[64,2048]{1,0:T(8,128)(2,1)S(1)} %collective-permute-done.24), channel_id=1, source_target_pairs={{0,32},{32,64},{64,96},{96,0},{1,33},{33,65},{65,97},{97,1},{2,34}... | collective-permute-start | bytes 786440 | tf_op jit(solution)/shard_map/ppermute | solution.py:20
  188.6 9.4 %copy-start.3 = (bf16[2048,1024]{1,0:T(8,128)(2,1)S(1)}, bf16[2048,1024]{1,0:T(8,128)(2,1)}, u32[]{:S(2)}) copy-start(bf16[2048,1024]{1,0:T(8,128)(2,1)} %copy-done.2) | copy-start | bytes 12582916
  188.6 10.7 %collective-permute-start.27 = (bf16[64,2048]{1,0:T(8,128)(2,1)S(1)}, bf16[64,2048]{1,0:T(8,128)(2,1)S(1)}, u32[]{:S(2)}, u32[]{:S(2)}) collective-permute-start(bf16[64,2048]{1,0:T(8,128)(2,1)S(1)} %get-tuple-element.78), channel_id=1, source_target_pairs={{0,96},{32,0},{64,32},{96,64},{1,97},{33,1},{65,33},{97,65},{2,98}... | collective-permute-start | bytes 786440 | tf_op jit(solution)/shard_map/ppermute | solution.py:20
  198.0 2.2 copy-start.1
  199.3 2.4 %copy-start.13 = (bf16[1024,2048]{1,0:T(8,128)(2,1)S(1)}, bf16[1024,2048]{1,0:T(8,128)(2,1)}, u32[]{:S(2)}) copy-start(bf16[1024,2048]{1,0:T(8,128)(2,1)} %param.24) | copy-start | bytes 12582916
  199.3 8.1 %collective-permute-start.28 = (bf16[64,2048]{1,0:T(8,128)(2,1)S(1)}, bf16[64,2048]{1,0:T(8,128)(2,1)S(1)}, u32[]{:S(2)}, u32[]{:S(2)}) collective-permute-start(bf16[64,2048]{1,0:T(8,128)(2,1)S(1)} %get-tuple-element.78), channel_id=1, source_target_pairs={{0,32},{32,64},{64,96},{96,0},{1,33},{33,65},{65,97},{97,1},{2,34}... | collective-permute-start | bytes 786440 | tf_op jit(solution)/shard_map/ppermute | solution.py:20
  203.0 8.9 %collective-permute-start.29 = (bf16[64,2048]{1,0:T(8,128)(2,1)S(1)}, bf16[64,2048]{1,0:T(8,128)(2,1)S(1)}, u32[]{:S(2)}, u32[]{:S(2)}) collective-permute-start(bf16[64,2048]{1,0:T(8,128)(2,1)S(1)} %collective-permute-done.27), channel_id=1, source_target_pairs={{0,96},{32,0},{64,32},{96,64},{1,97},{33,1},{65,33},{97,65},{2,98}... | collective-permute-start | bytes 786440 | tf_op jit(solution)/shard_map/ppermute | solution.py:20
  205.3 9.4 %collective-permute-start.30 = (bf16[64,2048]{1,0:T(8,128)(2,1)S(1)}, bf16[64,2048]{1,0:T(8,128)(2,1)S(1)}, u32[]{:S(2)}, u32[]{:S(2)}) collective-permute-start(bf16[64,2048]{1,0:T(8,128)(2,1)S(1)} %get-tuple-element.120), channel_id=1, source_target_pairs={{0,96},{32,0},{64,32},{96,64},{1,97},{33,1},{65,33},{97,65},{2,98}... | collective-permute-start | bytes 786440 | tf_op jit(solution)/shard_map/ppermute | solution.py:20
  205.4 9.4 %collective-permute-start.31 = (bf16[64,2048]{1,0:T(8,128)(2,1)S(1)}, bf16[64,2048]{1,0:T(8,128)(2,1)S(1)}, u32[]{:S(2)}, u32[]{:S(2)}) collective-permute-start(bf16[64,2048]{1,0:T(8,128)(2,1)S(1)} %get-tuple-element.119), channel_id=1, source_target_pairs={{0,32},{32,64},{64,96},{96,0},{1,33},{33,65},{65,97},{97,1},{2,34}... | collective-permute-start | bytes 786440 | tf_op jit(solution)/shard_map/ppermute | solution.py:20
  217.4 16.0 %copy-start.10 = (f32[2048]{0:T(1024)S(1)}, f32[2048]{0:T(1024)}, u32[]{:S(2)}) copy-start(f32[2048]{0:T(1024)} %param.25) | copy-start | bytes 24580
  217.4 7.9 %collective-permute-start.34 = (bf16[64,2048]{1,0:T(8,128)(2,1)S(1)}, bf16[64,2048]{1,0:T(8,128)(2,1)S(1)}, u32[]{:S(2)}, u32[]{:S(2)}) collective-permute-start(bf16[64,2048]{1,0:T(8,128)(2,1)S(1)} %get-tuple-element.118), channel_id=1, source_target_pairs={{0,32},{32,64},{64,96},{96,0},{1,33},{33,65},{65,97},{97,1},{2,34}... | collective-permute-start | bytes 786440 | tf_op jit(solution)/shard_map/ppermute | solution.py:20
  217.5 8.4 %collective-permute-start.32 = (bf16[64,2048]{1,0:T(8,128)(2,1)S(1)}, bf16[64,2048]{1,0:T(8,128)(2,1)S(1)}, u32[]{:S(2)}, u32[]{:S(2)}) collective-permute-start(bf16[64,2048]{1,0:T(8,128)(2,1)S(1)} %add_convert_fusion.4), channel_id=1, source_target_pairs={{0,96},{32,0},{64,32},{96,64},{1,97},{33,1},{65,33},{97,65},{2,98}... | collective-permute-start | bytes 786440 | tf_op jit(solution)/shard_map/ppermute | solution.py:20
  220.7 8.0 %collective-permute-start.33 = (bf16[64,2048]{1,0:T(8,128)(2,1)S(1)}, bf16[64,2048]{1,0:T(8,128)(2,1)S(1)}, u32[]{:S(2)}, u32[]{:S(2)}) collective-permute-start(bf16[64,2048]{1,0:T(8,128)(2,1)S(1)} %get-tuple-element.117), channel_id=1, source_target_pairs={{0,96},{32,0},{64,32},{96,64},{1,97},{33,1},{65,33},{97,65},{2,98}... | collective-permute-start | bytes 786440 | tf_op jit(solution)/shard_map/ppermute | solution.py:20
  225.4 7.9 %collective-permute-start.35 = (bf16[64,2048]{1,0:T(8,128)(2,1)S(1)}, bf16[64,2048]{1,0:T(8,128)(2,1)S(1)}, u32[]{:S(2)}, u32[]{:S(2)}) collective-permute-start(bf16[64,2048]{1,0:T(8,128)(2,1)S(1)} %add_convert_fusion.3), channel_id=1, source_target_pairs={{0,32},{32,64},{64,96},{96,0},{1,33},{33,65},{65,97},{97,1},{2,34}... | collective-permute-start | bytes 786440 | tf_op jit(solution)/shard_map/ppermute | solution.py:20

commit v6 on v5

--- a/solution.py
+++ b/solution.py
@@ -159,6 +159,7 @@
     )
     group_of = jnp.sum(lang_hit * lang_group[None, :], axis=1)
     outgoing, position = dispatch(tokens, group_of, group_gain, capacity)
+    outgoing, b1_pair = hold(outgoing, b1_pair)
     dispatch_map = (
         position[None, :] == jnp.arange(num_groups * capacity, dtype=jnp.int32)[:, None]
     ).astype(bf16)

time: 235 us -> 238 us (1.013)
  waiting for transfers between devices: 115 us -> 125 us
  starting transfers between devices: 67.7 us -> 60.2 us
    all_to_all x3, waiting for transfers between devices: 13.9 us -> 20.7 us  [exchange(): lax.all_to_all(value, ('y', 'core'), split_axis=0, concat_axis=0, tiled=T...]
    ppermute x24, waiting for transfers between devices: 65.1 us -> 71.8 us  [shift(): lax.ppermute(value, axis, [(i, (i + step) % size) for i in range(size)])]
    ppermute x4, starting transfers between devices: 11 us -> 4.56 us  [swap_blocks(): return lax.ppermute(value, X, [(0, 3), (3, 0), (1, 2), (2, 1)])]
    ppermute x4, waiting for transfers between devices: 22 us -> 17.9 us  [swap_blocks(): return lax.ppermute(value, X, [(0, 3), (3, 0), (1, 2), (2, 1)])]
    all_to_all x3, starting transfers between devices: 13.4 us -> 16.1 us  [exchange(): lax.all_to_all(value, ('y', 'core'), split_axis=0, concat_axis=0, tiled=T...]
  transfers between devices with their start and end apart: 39 -> 39, of which waited for: 28 -> 26; matrix products, arithmetic and copies ran while one was open for 13% -> 13% of each run, Pallas kernels for 3% -> 3%
where the time goes in v6:
time: 238 us; the launch traced here: 237 us
  waiting for transfers between devices  125 us (53%)
  starting transfers between devices  60.2 us (25%)
  matrix products  29.2 us (12%)
  local copies, waits for them, and re-layouts  8.63 us (4%)
  other arithmetic  7.46 us (3%)
  Pallas kernels  6.16 us (3%)
    ppermute x24, waiting for transfers between devices, shift(): lax.ppermute(value, axis, [(i, (i + step) % size) for i in range(size)])  71.8 us
    ppermute x24, starting transfers between devices, shift(): lax.ppermute(value, axis, [(i, (i + step) % size) for i in range(size)])  37.2 us
    all_to_all x3, waiting for transfers between devices, exchange(): lax.all_to_all(value, ('y', 'core'), split_axis=0, concat_axis=0, tiled=T...  20.7 us
    ppermute x4, waiting for transfers between devices, swap_blocks(): return lax.ppermute(value, X, [(0, 3), (3, 0), (1, 2), (2, 1)])  17.9 us
    all_to_all x3, starting transfers between devices, exchange(): lax.all_to_all(value, ('y', 'core'), split_axis=0, concat_axis=0, tiled=T...  16.1 us
    ppermute x5, waiting for transfers between devices, swap_column(): return lax.ppermute(value, 'xl', [(0, 1), (1, 0)])  14.3 us
    dot_general x2, matrix products, first(): jnp.dot(rows, w1, preferred_element_type=jnp.float32) + b1  9 us
    dot_general x2, matrix products, second(): return down(jnp.dot(hidden, weight, preferred_element_type=jnp.float32))  8.1 us
  transfers between devices with their start and end apart: 39, of which 26 were waited for; matrix products, arithmetic and copies ran while one was open for 13% of the time, Pallas kernels for 3%

profile of v6, /device:TPU:0, one launch (start us, length us, event | category | flops | bytes accessed | tf_op | source)
XLA Modules:
  0.0 237.1 jit_solution(8209533010262463469)
XLA Ops:
  0.5 2.8 %collective-permute-start = (f32[512]{0:T(512)}, f32[512]{0:T(512)S(1)}, u32[]{:S(2)}, u32[]{:S(2)}) collective-permute-start(f32[512]{0:T(512)} %bitcast.48), channel_id=1, source_target_pairs={{0,3},{3,0},{1,2},{2,1},{4,7},{7,4},{5,6},{6,5},{8,11},{11,8},{9,1... | collective-permute-start | bytes 6152 | tf_op jit(solution)/shard_map/ppermute | solution.py:28
  4.1 1.0 copy-done.4
  6.0 1.8 dispatch.1
  7.8 4.5 %all-to-all-start = ((bf16[8,24,2048]{2,1,0:T(8,128)(2,1)}), bf16[8,24,2048]{2,1,0:T(8,128)(2,1)S(1)}, u32[]{:S(2)}, u32[]{:S(2)}) async-start(bf16[8,24,2048]{2,1,0:T(8,128)(2,1)} %bitcast.4), calls=%async_computation | async-start | bytes 1572864 | tf_op jit(solution)/shard_map/all_to_all | solution.py:170
  13.6 11.8 %all-to-all-done = bf16[8,24,2048]{2,1,0:T(8,128)(2,1)S(1)} async-done(((bf16[8,24,2048]{2,1,0:T(8,128)(2,1)}), bf16[8,24,2048]{2,1,0:T(8,128)(2,1)S(1)}, u32[]{:S(2)}, u32[]{:S(2)}) %all-to-all-start) | async-done | bytes 786464 | tf_op jit(solution)/shard_map/all_to_all | solution.py:170
  25.5 2.0 collective-permute-start.4
  27.5 2.2 collective-permute-start.5
  30.1 8.4 %collective-permute-done.4 = bf16[96,2048]{1,0:T(8,128)(2,1)S(1)} collective-permute-done((bf16[96,2048]{1,0:T(8,128)(2,1)S(1)}, bf16[96,2048]{1,0:T(8,128)(2,1)S(1)}, u32[]{:S(2)}, u32[]{:S(2)}) %collective-permute-start.4) | collective-permute-done | bytes 393248 | tf_op jit(solution)/shard_map/ppermute | solution.py:20
  38.7 1.4 collective-permute-done.6
  40.4 1.9 collective-permute-start.8
  42.4 7.6 %collective-permute-done.7 = bf16[96,2048]{1,0:T(8,128)(2,1)S(1)} collective-permute-done((bf16[96,2048]{1,0:T(8,128)(2,1)S(1)}, bf16[96,2048]{1,0:T(8,128)(2,1)S(1)}, u32[]{:S(2)}, u32[]{:S(2)}) %collective-permute-start.7) | collective-permute-done | bytes 393248 | tf_op jit(solution)/shard_map/ppermute | solution.py:20
  50.0 2.2 on_chip.2
  52.2 2.0 copy-done.2
  54.2 2.2 on_chip.3
  56.4 2.0 copy-done
  59.1 3.3 %collective-permute-start.13 = (bf16[192,2048]{1,0:T(8,128)(2,1)S(1)}, bf16[192,2048]{1,0:T(8,128)(2,1)S(1)}, u32[]{:S(2)}, u32[]{:S(2)}) collective-permute-start(bf16[192,2048]{1,0:T(8,128)(2,1)S(1)} %collective-permute-done.8), channel_id=1, source_target_pairs={{0,12},{4,0},{8,4},{12,8},{1,13},{5,1},{9,5},{13,9},{2,14},{6,2},{... | collective-permute-start | bytes 2359304 | tf_op jit(solution)/shard_map/ppermute | solution.py:20
  62.5 4.0 %collective-permute-done.11 = bf16[288,2048]{1,0:T(8,128)(2,1)S(1)} collective-permute-done((bf16[288,2048]{1,0:T(8,128)(2,1)S(1)}, bf16[288,2048]{1,0:T(8,128)(2,1)S(1)}, u32[]{:S(2)}, u32[]{:S(2)}) %collective-permute-start.11) | collective-permute-done | bytes 1179680 | tf_op jit(solution)/shard_map/ppermute | solution.py:24
  66.8 2.1 collective-permute-done.9
  69.7 6.0 %maximum_convert_fusion = bf16[1248,1024]{1,0:T(8,128)(2,1)S(1)} fusion(bf16[1248,2048]{1,0:T(8,128)(2,1)S(1)} %constant_dynamic-update-slice_fusion, bf16[2048,512]{1,0:T(8,128)(2,1)} %collective-permute-done.10, bf16[2048,512]{1,0:T(8,128)(2,1)S(1)} %bitcast.51, f32[1024]{0:T(1024)S(1)} %pad_maximum_fusion.22), kind=kOutput, calls=%fused_computation | convolution fusion | flops 5246713856 | bytes 11866112 | tf_op jit(solution)/shard_map/dot_general | solution.py:203
  75.7 1.4 collective-permute-done.13
  77.2 3.0 %fusion.12 = bf16[288,1024]{1,0:T(8,128)(2,1)S(1)} fusion(bf16[2048,512]{1,0:T(8,128)(2,1)} %collective-permute-done.10, bf16[2048,512]{1,0:T(8,128)(2,1)S(1)} %bitcast.52, bf16[192,2048]{1,0:T(8,128)(2,1)S(1)} %collective-permute-done.13, bf16[96,2048]{1,0:T(8,128)(2,1)S(1)} %collective-permute-done.12, f32[1024]{0:T(1024)S(1)} %pad_maximum_fusion.22), kind=kOutput, calls=%fused_computation.24 | convolution fusion | flops 1219592192 | bytes 5967872 | tf_op jit(solution)/shard_map/dot_general | solution.py:203
  80.1 5.6 %collective-permute-done.14 = bf16[512,1024]{1,0:T(8,128)(2,1)S(1)} collective-permute-done((bf16[512,1024]{1,0:T(8,128)(2,1)S(1)}, bf16[512,1024]{1,0:T(8,128)(2,1)S(1)}, u32[]{:S(2)}, u32[]{:S(2)}) %collective-permute-start.14) | collective-permute-done | bytes 1048608 | tf_op jit(solution)/shard_map/ppermute | solution.py:28
  85.7 4.3 %convolution_convert_fusion.1 = bf16[1536,1024]{1,0:T(8,128)(2,1)S(1)} fusion(bf16[512,1024]{1,0:T(8,128)(2,1)S(1)} %collective-permute-done.14, bf16[512,1024]{1,0:T(8,128)(2,1)S(1)} %get-tuple-element.65, bf16[288,1024]{1,0:T(8,128)(2,1)S(1)} %fusion.12, bf16[1248,1024]{1,0:T(8,128)(2,1)S(1)} %maximum_convert_fusion), kind=kOutput, calls=%fused_computation.3 | convolution fusion | flops 3233284096 | bytes 8388608 | tf_op jit(solution)/shard_map/dot_general | solution.py:209
  90.5 1.4 collective-permute-start.16
  92.0 2.2 collective-permute-start.15
  94.5 12.3 %collective-permute-done.17 = bf16[512,1024]{1,0:T(8,128)(2,1)S(1)} collective-permute-done((bf16[512,1024]{1,0:T(8,128)(2,1)S(1)}, bf16[512,1024]{1,0:T(8,128)(2,1)S(1)}, u32[]{:S(2)}, u32[]{:S(2)}) %collective-permute-start.17) | collective-permute-done | bytes 1048608 | tf_op jit(solution)/shard_map/ppermute | solution.py:28
  106.7 3.4 %collective-permute-done.16 = bf16[384,1024]{1,0:T(8,128)(2,1)S(1)} collective-permute-done((bf16[384,1024]{1,0:T(8,128)(2,1)S(1)}, bf16[384,1024]{1,0:T(8,128)(2,1)S(1)}, u32[]{:S(2)}, u32[]{:S(2)}) %collective-permute-start.16) | collective-permute-done | bytes 786464 | tf_op jit(solution)/shard_map/ppermute | solution.py:20
  110.4 3.2 %collective-permute-start.20 = (bf16[384,1024]{1,0:T(8,128)(2,1)S(1)}, bf16[384,1024]{1,0:T(8,128)(2,1)S(1)}, u32[]{:S(2)}, u32[]{:S(2)}) collective-permute-start(bf16[384,1024]{1,0:T(8,128)(2,1)S(1)} %add_convert_fusion.1), channel_id=1, source_target_pairs={{0,12},{4,0},{8,4},{12,8},{1,13},{5,1},{9,5},{13,9},{2,14},{6,2},{... | collective-permute-start | bytes 2359304 | tf_op jit(solution)/shard_map/ppermute | solution.py:20
  113.6 3.8 %convolution_convert_fusion = bf16[1536,1024]{1,0:T(8,128)(2,1)S(1)} fusion(bf16[1536,1024]{1,0:T(8,128)(2,1)S(1)} %pad_maximum_fusion.1, bf16[512,1024]{1,0:T(8,128)(2,1)S(1)} %collective-permute-done.17, bf16[512,1024]{1,0:T(8,128)(2,1)S(1)} %get-tuple-element.66), kind=kOutput, calls=%fused_computation.2 | convolution fusion | flops 3226992640 | bytes 8388608 | tf_op jit(solution)/shard_map/dot_general | solution.py:209
  117.9 10.2 %collective-permute-done.20 = bf16[384,1024]{1,0:T(8,128)(2,1)S(1)} collective-permute-done((bf16[384,1024]{1,0:T(8,128)(2,1)S(1)}, bf16[384,1024]{1,0:T(8,128)(2,1)S(1)}, u32[]{:S(2)}, u32[]{:S(2)}) %collective-permute-start.20) | collective-permute-done | bytes 786464 | tf_op jit(solution)/shard_map/ppermute | solution.py:20
  128.7 3.8 %collective-permute-start.18 = (bf16[384,1024]{1,0:T(8,128)(2,1)S(1)}, bf16[384,1024]{1,0:T(8,128)(2,1)S(1)}, u32[]{:S(2)}, u32[]{:S(2)}) collective-permute-start(bf16[384,1024]{1,0:T(8,128)(2,1)S(1)} %pad_maximum_fusion.16), channel_id=1, source_target_pairs={{0,12},{4,0},{8,4},{12,8},{1,13},{5,1},{9,5},{13,9},{2,14},{6,2},{... | collective-permute-start | bytes 2359304 | tf_op jit(solution)/shard_map/ppermute | solution.py:20
  132.4 3.3 %collective-permute-done.19 = bf16[384,1024]{1,0:T(8,128)(2,1)S(1)} collective-permute-done((bf16[384,1024]{1,0:T(8,128)(2,1)S(1)}, bf16[384,1024]{1,0:T(8,128)(2,1)S(1)}, u32[]{:S(2)}, u32[]{:S(2)}) %collective-permute-start.19) | collective-permute-done | bytes 786464 | tf_op jit(solution)/shard_map/ppermute | solution.py:20
  136.7 0.9 collective-permute-start.22
  137.6 0.9 fusion.26
  138.4 5.6 %all-to-all-start.1 = ((bf16[8,24,1024]{2,1,0:T(8,128)(2,1)}), bf16[8,24,1024]{2,1,0:T(8,128)(2,1)}, u32[]{:S(2)}, u32[]{:S(2)}) async-start(bf16[8,24,1024]{2,1,0:T(8,128)(2,1)} %bitcast.8), calls=%async_computation.1 | async-start | bytes 786432 | tf_op jit(solution)/shard_map/all_to_all | solution.py:170
  144.0 1.9 collective-permute-done.18
  145.9 7.7 %collective-permute-done.22 = bf16[384,1024]{1,0:T(8,128)(2,1)} collective-permute-done((bf16[384,1024]{1,0:T(8,128)(2,1)S(1)}, bf16[384,1024]{1,0:T(8,128)(2,1)}, u32[]{:S(2)}, u32[]{:S(2)}) %collective-permute-start.22) | collective-permute-done | bytes 786464 | tf_op jit(solution)/shard_map/ppermute | solution.py:20
  153.6 1.6 convert_add_fusion
  155.7 8.2 %collective-permute-done.23 = bf16[192,1024]{1,0:T(8,128)(2,1)S(1)} collective-permute-done((bf16[192,1024]{1,0:T(8,128)(2,1)S(1)}, bf16[192,1024]{1,0:T(8,128)(2,1)S(1)}, u32[]{:S(2)}, u32[]{:S(2)}) %collective-permute-start.23) | collective-permute-done | bytes 393248 | tf_op jit(solution)/shard_map/ppermute | solution.py:24
  163.8 0.9 add_convert_fusion.2
  164.7 6.1 %all-to-all-start.2 = ((bf16[8,24,1024]{2,1,0:T(8,128)(2,1)}), bf16[8,24,1024]{2,1,0:T(8,128)(2,1)S(1)}, u32[]{:S(2)}, u32[]{:S(2)}) async-start(bf16[8,24,1024]{2,1,0:T(8,128)(2,1)} %bitcast.10), calls=%async_computation.2 | async-start | bytes 786432 | tf_op jit(solution)/shard_map/all_to_all | solution.py:170
  170.8 8.9 %all-to-all-done.2 = bf16[8,24,1024]{2,1,0:T(8,128)(2,1)S(1)} async-done(((bf16[8,24,1024]{2,1,0:T(8,128)(2,1)}), bf16[8,24,1024]{2,1,0:T(8,128)(2,1)S(1)}, u32[]{:S(2)}, u32[]{:S(2)}) %all-to-all-start.2) | async-done | bytes 393248 | tf_op jit(solution)/shard_map/all_to_all | solution.py:170
  179.7 2.0 fusion.47
  182.9 2.7 %collective-permute-start.25 = (bf16[64,2048]{1,0:T(8,128)(2,1)S(1)}, bf16[64,2048]{1,0:T(8,128)(2,1)S(1)}, u32[]{:S(2)}, u32[]{:S(2)}) collective-permute-start(bf16[64,2048]{1,0:T(8,128)(2,1)S(1)} %get-tuple-element.127), channel_id=1, source_target_pairs={{0,96},{32,0},{64,32},{96,64},{1,97},{33,1},{65,33},{97,65},{2,98}... | collective-permute-start | bytes 786440 | tf_op jit(solution)/shard_map/ppermute | solution.py:20
  185.6 5.8 %collective-permute-done.24 = bf16[64,2048]{1,0:T(8,128)(2,1)S(1)} collective-permute-done((bf16[64,2048]{1,0:T(8,128)(2,1)S(1)}, bf16[64,2048]{1,0:T(8,128)(2,1)S(1)}, u32[]{:S(2)}, u32[]{:S(2)}) %collective-permute-start.24) | collective-permute-done | bytes 262176 | tf_op jit(solution)/shard_map/ppermute | solution.py:20
  191.4 3.2 %collective-permute-start.27 = (bf16[64,2048]{1,0:T(8,128)(2,1)S(1)}, bf16[64,2048]{1,0:T(8,128)(2,1)S(1)}, u32[]{:S(2)}, u32[]{:S(2)}) collective-permute-start(bf16[64,2048]{1,0:T(8,128)(2,1)S(1)} %get-tuple-element.82), channel_id=1, source_target_pairs={{0,96},{32,0},{64,32},{96,64},{1,97},{33,1},{65,33},{97,65},{2,98}... | collective-permute-start | bytes 786440 | tf_op jit(solution)/shard_map/ppermute | solution.py:20
  194.6 4.9 %collective-permute-done.26 = bf16[64,2048]{1,0:T(8,128)(2,1)S(1)} collective-permute-done((bf16[64,2048]{1,0:T(8,128)(2,1)S(1)}, bf16[64,2048]{1,0:T(8,128)(2,1)S(1)}, u32[]{:S(2)}, u32[]{:S(2)}) %collective-permute-start.26) | collective-permute-done | bytes 262176 | tf_op jit(solution)/shard_map/ppermute | solution.py:20
  199.5 1.3 fusion.17
  200.8 1.3 fusion.18
  203.0 1.3 fusion.48
  204.5 1.3 fusion.1
  205.8 2.3 collective-permute-start.29
  208.2 2.0 collective-permute-start.31
  210.2 4.5 %collective-permute-done.29 = bf16[64,2048]{1,0:T(8,128)(2,1)S(1)} collective-permute-done((bf16[64,2048]{1,0:T(8,128)(2,1)S(1)}, bf16[64,2048]{1,0:T(8,128)(2,1)S(1)}, u32[]{:S(2)}, u32[]{:S(2)}) %collective-permute-start.29) | collective-permute-done | bytes 262176 | tf_op jit(solution)/shard_map/ppermute | solution.py:20
  214.7 1.3 fusion.20
  216.0 1.3 fusion.19
  217.6 1.3 fusion.49
  218.9 1.3 fusion.2
  220.3 3.2 %collective-permute-start.32 = (bf16[64,2048]{1,0:T(8,128)(2,1)S(1)}, bf16[64,2048]{1,0:T(8,128)(2,1)S(1)}, u32[]{:S(2)}, u32[]{:S(2)}) collective-permute-start(bf16[64,2048]{1,0:T(8,128)(2,1)S(1)} %add_convert_fusion.4), channel_id=1, source_target_pairs={{0,96},{32,0},{64,32},{96,64},{1,97},{33,1},{65,33},{97,65},{2,98}... | collective-permute-start | bytes 786440 | tf_op jit(solution)/shard_map/ppermute | solution.py:20
  223.5 1.9 collective-permute-start.33
  225.5 2.7 %collective-permute-done.34 = bf16[64,2048]{1,0:T(8,128)(2,1)S(1)} collective-permute-done((bf16[64,2048]{1,0:T(8,128)(2,1)S(1)}, bf16[64,2048]{1,0:T(8,128)(2,1)S(1)}, u32[]{:S(2)}, u32[]{:S(2)}) %collective-permute-start.34) | collective-permute-done | bytes 262176 | tf_op jit(solution)/shard_map/ppermute | solution.py:20
  228.8 2.7 %collective-permute-done.33 = bf16[64,2048]{1,0:T(8,128)(2,1)S(1)} collective-permute-done((bf16[64,2048]{1,0:T(8,128)(2,1)S(1)}, bf16[64,2048]{1,0:T(8,128)(2,1)S(1)}, u32[]{:S(2)}, u32[]{:S(2)}) %collective-permute-start.33) | collective-permute-done | bytes 262176 | tf_op jit(solution)/shard_map/ppermute | solution.py:20
  231.5 4.6 %collective-permute-done.35 = bf16[64,2048]{1,0:T(8,128)(2,1)S(1)} collective-permute-done((bf16[64,2048]{1,0:T(8,128)(2,1)S(1)}, bf16[64,2048]{1,0:T(8,128)(2,1)S(1)}, u32[]{:S(2)}, u32[]{:S(2)}) %collective-permute-start.35) | collective-permute-done | bytes 262176 | tf_op jit(solution)/shard_map/ppermute | solution.py:20
  236.2 0.9 fusion.25
  (103 shorter events, 13.6 us)
Async XLA Ops:
  0.0 12.3 %copy-start.15 = (f32[1024]{0:T(1024)S(1)}, f32[1024]{0:T(1024)}, u32[]{:S(2)}) copy-start(f32[1024]{0:T(1024)} %param.23) | copy-start | bytes 12292
  0.0 25.4 %collective-permute-start.1 = (bf16[2048,1024]{1,0:T(8,128)(2,1)}, bf16[2048,1024]{1,0:T(8,128)(2,1)}, u32[]{:S(2)}, u32[]{:S(2)}) collective-permute-start(bf16[2048,1024]{1,0:T(8,128)(2,1)} %param.22), channel_id=1, source_target_pairs={{0,16},{16,0},{1,17},{17,1},{2,18},{18,2},{3,19},{19,3},{4,20},{20... | collective-permute-start | bytes 12582920 | tf_op jit(solution)/shard_map/ppermute | solution.py:32
  0.0 25.4 %collective-permute-start.2 = (bf16[1024,2048]{1,0:T(8,128)(2,1)}, bf16[1024,2048]{1,0:T(8,128)(2,1)}, u32[]{:S(2)}, u32[]{:S(2)}) collective-permute-start(bf16[1024,2048]{1,0:T(8,128)(2,1)} %param.24), channel_id=1, source_target_pairs={{0,16},{16,0},{1,17},{17,1},{2,18},{18,2},{3,19},{19,3},{4,20},{20... | collective-permute-start | bytes 12582920 | tf_op jit(solution)/shard_map/ppermute | solution.py:32
  0.5 7.3 %collective-permute-start = (f32[512]{0:T(512)}, f32[512]{0:T(512)S(1)}, u32[]{:S(2)}, u32[]{:S(2)}) collective-permute-start(f32[512]{0:T(512)} %bitcast.48), channel_id=1, source_target_pairs={{0,3},{3,0},{1,2},{2,1},{4,7},{7,4},{5,6},{6,5},{8,11},{11,8},{9,1... | collective-permute-start | bytes 6152 | tf_op jit(solution)/shard_map/ppermute | solution.py:28
  4.1 1.0 copy-start.4
  5.2 0.8 copy-start.6
  6.0 23.9 %copy-start.7 = (bf16[1,512,2048]{2,1,0:T(8,128)(2,1)S(1)}, bf16[1,512,2048]{2,1,0:T(8,128)(2,1)}, u32[]{:S(2)}) copy-start(bf16[1,512,2048]{2,1,0:T(8,128)(2,1)} %param.19) | copy-start | bytes 6291460
  7.8 17.6 %all-to-all-start = ((bf16[8,24,2048]{2,1,0:T(8,128)(2,1)}), bf16[8,24,2048]{2,1,0:T(8,128)(2,1)S(1)}, u32[]{:S(2)}, u32[]{:S(2)}) async-start(bf16[8,24,2048]{2,1,0:T(8,128)(2,1)} %bitcast.4), calls=%async_computation | async-start | bytes 1572864 | tf_op jit(solution)/shard_map/all_to_all | solution.py:170
  12.3 1.3 collective-permute-start.3
  12.8 53.7 %collective-permute-start.10 = (bf16[2048,512]{1,0:T(8,128)(2,1)}, bf16[2048,512]{1,0:T(8,128)(2,1)}, u32[]{:S(2)}, u32[]{:S(2)}) collective-permute-start(bf16[2048,512]{1,0:T(8,128)(2,1)} %bitcast.50), channel_id=1, source_target_pairs={{0,3},{3,0},{1,2},{2,1},{4,7},{7,4},{5,6},{6,5},{8,11},{11,8},{9,1... | collective-permute-start | bytes 6291464 | tf_op jit(solution)/shard_map/ppermute | solution.py:28
  25.5 13.0 %collective-permute-start.4 = (bf16[96,2048]{1,0:T(8,128)(2,1)S(1)}, bf16[96,2048]{1,0:T(8,128)(2,1)S(1)}, u32[]{:S(2)}, u32[]{:S(2)}) collective-permute-start(bf16[96,2048]{1,0:T(8,128)(2,1)S(1)} %get-tuple-element.126), channel_id=1, source_target_pairs={{0,4},{4,8},{8,12},{12,0},{1,5},{5,9},{9,13},{13,1},{2,6},{6,10},{... | collective-permute-start | bytes 1179656 | tf_op jit(solution)/shard_map/ppermute | solution.py:20
  27.5 11.0 %collective-permute-start.5 = (bf16[96,2048]{1,0:T(8,128)(2,1)S(1)}, bf16[96,2048]{1,0:T(8,128)(2,1)S(1)}, u32[]{:S(2)}, u32[]{:S(2)}) collective-permute-start(bf16[96,2048]{1,0:T(8,128)(2,1)S(1)} %get-tuple-element.126), channel_id=1, source_target_pairs={{0,12},{4,0},{8,4},{12,8},{1,13},{5,1},{9,5},{13,9},{2,14},{6,2},{... | collective-permute-start | bytes 1179656 | tf_op jit(solution)/shard_map/ppermute | solution.py:20
  29.7 10.4 %collective-permute-start.6 = (bf16[96,2048]{1,0:T(8,128)(2,1)S(1)}, bf16[96,2048]{1,0:T(8,128)(2,1)S(1)}, u32[]{:S(2)}, u32[]{:S(2)}) collective-permute-start(bf16[96,2048]{1,0:T(8,128)(2,1)S(1)} %get-tuple-element.125), channel_id=1, source_target_pairs={{0,1},{1,0},{2,3},{3,2},{4,5},{5,4},{6,7},{7,6},{8,9},{9,8},{10,11... | collective-permute-start | bytes 1179656 | tf_op jit(solution)/shard_map/ppermute | solution.py:24
  30.1 12.2 %copy-start.11 = (f32[1,512]{1,0:T(1,128)S(1)}, f32[1,512]{1,0:T(1,128)}, u32[]{:S(2)}) copy-start(f32[1,512]{1,0:T(1,128)} %param.18) | copy-start | bytes 6148
  38.5 11.4 %collective-permute-start.7 = (bf16[96,2048]{1,0:T(8,128)(2,1)S(1)}, bf16[96,2048]{1,0:T(8,128)(2,1)S(1)}, u32[]{:S(2)}, u32[]{:S(2)}) collective-permute-start(bf16[96,2048]{1,0:T(8,128)(2,1)S(1)} %collective-permute-done.4), channel_id=1, source_target_pairs={{0,4},{4,8},{8,12},{12,0},{1,5},{5,9},{9,13},{13,1},{2,6},{6,10},{... | collective-permute-start | bytes 1179656 | tf_op jit(solution)/shard_map/ppermute | solution.py:20
  40.1 26.4 %collective-permute-start.11 = (bf16[288,2048]{1,0:T(8,128)(2,1)S(1)}, bf16[288,2048]{1,0:T(8,128)(2,1)S(1)}, u32[]{:S(2)}, u32[]{:S(2)}) collective-permute-start(bf16[288,2048]{1,0:T(8,128)(2,1)S(1)} %pad_maximum_fusion.10), channel_id=1, source_target_pairs={{0,1},{1,0},{2,3},{3,2},{4,5},{5,4},{6,7},{7,6},{8,9},{9,8},{10,11... | collective-permute-start | bytes 3538952 | tf_op jit(solution)/shard_map/ppermute | solution.py:24
  40.4 18.7 %collective-permute-start.8 = (bf16[192,2048]{1,0:T(8,128)(2,1)S(1)}, bf16[192,2048]{1,0:T(8,128)(2,1)S(1)}, u32[]{:S(2)}, u32[]{:S(2)}) collective-permute-start(bf16[192,2048]{1,0:T(8,128)(2,1)S(1)} %pad_maximum_fusion.13), channel_id=1, source_target_pairs={{0,12},{4,0},{8,4},{12,8},{1,13},{5,1},{9,5},{13,9},{2,14},{6,2},{... | collective-permute-start | bytes 2359304 | tf_op jit(solution)/shard_map/ppermute | solution.py:20
  49.9 19.0 %collective-permute-start.9 = (bf16[192,2048]{1,0:T(8,128)(2,1)S(1)}, bf16[192,2048]{1,0:T(8,128)(2,1)S(1)}, u32[]{:S(2)}, u32[]{:S(2)}) collective-permute-start(bf16[192,2048]{1,0:T(8,128)(2,1)S(1)} %pad_maximum_fusion.13), channel_id=1, source_target_pairs={{0,4},{4,8},{8,12},{12,0},{1,5},{5,9},{9,13},{13,1},{2,6},{6,10},{... | collective-permute-start | bytes 2359304 | tf_op jit(solution)/shard_map/ppermute | solution.py:20
  52.2 2.0 copy-start.2
  56.4 2.0 copy-start
  58.4 27.3 %collective-permute-start.14 = (bf16[512,1024]{1,0:T(8,128)(2,1)S(1)}, bf16[512,1024]{1,0:T(8,128)(2,1)S(1)}, u32[]{:S(2)}, u32[]{:S(2)}) collective-permute-start(bf16[512,1024]{1,0:T(8,128)(2,1)S(1)} %get-tuple-element.65), channel_id=1, source_target_pairs={{0,3},{3,0},{1,2},{2,1},{4,7},{7,4},{5,6},{6,5},{8,11},{11,8},{9,1... | collective-permute-start | bytes 3145736 | tf_op jit(solution)/shard_map/ppermute | solution.py:28
  59.1 18.1 %collective-permute-start.13 = (bf16[192,2048]{1,0:T(8,128)(2,1)S(1)}, bf16[192,2048]{1,0:T(8,128)(2,1)S(1)}, u32[]{:S(2)}, u32[]{:S(2)}) collective-permute-start(bf16[192,2048]{1,0:T(8,128)(2,1)S(1)} %collective-permute-done.8), channel_id=1, source_target_pairs={{0,12},{4,0},{8,4},{12,8},{1,13},{5,1},{9,5},{13,9},{2,14},{6,2},{... | collective-permute-start | bytes 2359304 | tf_op jit(solution)/shard_map/ppermute | solution.py:20
  62.5 7.2 %copy-start.14 = (bf16[1,2048,512]{2,1,0:T(8,128)(2,1)S(1)}, bf16[1,2048,512]{2,1,0:T(8,128)(2,1)}, u32[]{:S(2)}) copy-start(bf16[1,2048,512]{2,1,0:T(8,128)(2,1)} %param.17) | copy-start | bytes 6291460
  66.5 10.7 %collective-permute-start.12 = (bf16[96,2048]{1,0:T(8,128)(2,1)S(1)}, bf16[96,2048]{1,0:T(8,128)(2,1)S(1)}, u32[]{:S(2)}, u32[]{:S(2)}) collective-permute-start(bf16[96,2048]{1,0:T(8,128)(2,1)S(1)} %collective-permute-done.7), channel_id=1, source_target_pairs={{0,1},{1,0},{2,3},{3,2},{4,5},{5,4},{6,7},{7,6},{8,9},{9,8},{10,11... | collective-permute-start | bytes 1179656 | tf_op jit(solution)/shard_map/ppermute | solution.py:24
  68.9 37.8 %collective-permute-start.17 = (bf16[512,1024]{1,0:T(8,128)(2,1)S(1)}, bf16[512,1024]{1,0:T(8,128)(2,1)S(1)}, u32[]{:S(2)}, u32[]{:S(2)}) collective-permute-start(bf16[512,1024]{1,0:T(8,128)(2,1)S(1)} %get-tuple-element.66), channel_id=1, source_target_pairs={{0,3},{3,0},{1,2},{2,1},{4,7},{7,4},{5,6},{6,5},{8,11},{11,8},{9,1... | collective-permute-start | bytes 3145736 | tf_op jit(solution)/shard_map/ppermute | solution.py:28
  90.5 19.6 %collective-permute-start.16 = (bf16[384,1024]{1,0:T(8,128)(2,1)S(1)}, bf16[384,1024]{1,0:T(8,128)(2,1)S(1)}, u32[]{:S(2)}, u32[]{:S(2)}) collective-permute-start(bf16[384,1024]{1,0:T(8,128)(2,1)S(1)} %pad_maximum_fusion.15), channel_id=1, source_target_pairs={{0,4},{4,8},{8,12},{12,0},{1,5},{5,9},{9,13},{13,1},{2,6},{6,10},{... | collective-permute-start | bytes 2359304 | tf_op jit(solution)/shard_map/ppermute | solution.py:20
  92.0 18.2 %collective-permute-start.15 = (bf16[384,1024]{1,0:T(8,128)(2,1)S(1)}, bf16[384,1024]{1,0:T(8,128)(2,1)S(1)}, u32[]{:S(2)}, u32[]{:S(2)}) collective-permute-start(bf16[384,1024]{1,0:T(8,128)(2,1)S(1)} %pad_maximum_fusion.14), channel_id=1, source_target_pairs={{0,12},{4,0},{8,4},{12,8},{1,13},{5,1},{9,5},{13,9},{2,14},{6,2},{... | collective-permute-start | bytes 2359304 | tf_op jit(solution)/shard_map/ppermute | solution.py:20
  110.4 17.6 %collective-permute-start.20 = (bf16[384,1024]{1,0:T(8,128)(2,1)S(1)}, bf16[384,1024]{1,0:T(8,128)(2,1)S(1)}, u32[]{:S(2)}, u32[]{:S(2)}) collective-permute-start(bf16[384,1024]{1,0:T(8,128)(2,1)S(1)} %add_convert_fusion.1), channel_id=1, source_target_pairs={{0,12},{4,0},{8,4},{12,8},{1,13},{5,1},{9,5},{13,9},{2,14},{6,2},{... | collective-permute-start | bytes 2359304 | tf_op jit(solution)/shard_map/ppermute | solution.py:20
  117.8 17.9 %collective-permute-start.19 = (bf16[384,1024]{1,0:T(8,128)(2,1)S(1)}, bf16[384,1024]{1,0:T(8,128)(2,1)S(1)}, u32[]{:S(2)}, u32[]{:S(2)}) collective-permute-start(bf16[384,1024]{1,0:T(8,128)(2,1)S(1)} %pad_maximum_fusion.17), channel_id=1, source_target_pairs={{0,4},{4,8},{8,12},{12,0},{1,5},{5,9},{9,13},{13,1},{2,6},{6,10},{... | collective-permute-start | bytes 2359304 | tf_op jit(solution)/shard_map/ppermute | solution.py:20
  128.5 7.9 %collective-permute-start.21 = (bf16[192,1024]{1,0:T(8,128)(2,1)S(1)}, bf16[192,1024]{1,0:T(8,128)(2,1)S(1)}, u32[]{:S(2)}, u32[]{:S(2)}) collective-permute-start(bf16[192,1024]{1,0:T(8,128)(2,1)S(1)} %slice.248), channel_id=1, source_target_pairs={{0,1},{1,0},{2,3},{3,2},{4,5},{5,4},{6,7},{7,6},{8,9},{9,8},{10,11... | collective-permute-start | bytes 1179656 | tf_op jit(solution)/shard_map/ppermute | solution.py:24
  128.7 17.3 %collective-permute-start.18 = (bf16[384,1024]{1,0:T(8,128)(2,1)S(1)}, bf16[384,1024]{1,0:T(8,128)(2,1)S(1)}, u32[]{:S(2)}, u32[]{:S(2)}) collective-permute-start(bf16[384,1024]{1,0:T(8,128)(2,1)S(1)} %pad_maximum_fusion.16), channel_id=1, source_target_pairs={{0,12},{4,0},{8,4},{12,8},{1,13},{5,1},{9,5},{13,9},{2,14},{6,2},{... | collective-permute-start | bytes 2359304 | tf_op jit(solution)/shard_map/ppermute | solution.py:20
  136.7 17.0 %collective-permute-start.22 = (bf16[384,1024]{1,0:T(8,128)(2,1)S(1)}, bf16[384,1024]{1,0:T(8,128)(2,1)}, u32[]{:S(2)}, u32[]{:S(2)}) collective-permute-start(bf16[384,1024]{1,0:T(8,128)(2,1)S(1)} %add_convert_fusion), channel_id=1, source_target_pairs={{0,4},{4,8},{8,12},{12,0},{1,5},{5,9},{9,13},{13,1},{2,6},{6,10},{... | collective-permute-start | bytes 2359304 | tf_op jit(solution)/shard_map/ppermute | solution.py:20
  138.4 16.8 %all-to-all-start.1 = ((bf16[8,24,1024]{2,1,0:T(8,128)(2,1)}), bf16[8,24,1024]{2,1,0:T(8,128)(2,1)}, u32[]{:S(2)}, u32[]{:S(2)}) async-start(bf16[8,24,1024]{2,1,0:T(8,128)(2,1)} %bitcast.8), calls=%async_computation.1 | async-start | bytes 786432 | tf_op jit(solution)/shard_map/all_to_all | solution.py:170
  155.2 15.6 %copy-start.8 = (f32[8,2048]{1,0:T(8,128)S(1)}, f32[8,2048]{1,0:T(8,128)}, u32[]{:S(2)}) copy-start(f32[8,2048]{1,0:T(8,128)} %param.20) | copy-start | bytes 196612
  155.2 24.5 %copy-start.5 = (bf16[128,2048]{1,0:T(8,128)(2,1)S(1)}, bf16[128,2048]{1,0:T(8,128)(2,1)}, u32[]{:S(2)}) copy-start(bf16[128,2048]{1,0:T(8,128)(2,1)} %tokens_ref.1) | copy-start | bytes 1572868
  155.3 8.5 %collective-permute-start.23 = (bf16[192,1024]{1,0:T(8,128)(2,1)S(1)}, bf16[192,1024]{1,0:T(8,128)(2,1)S(1)}, u32[]{:S(2)}, u32[]{:S(2)}) collective-permute-start(bf16[192,1024]{1,0:T(8,128)(2,1)S(1)} %slice.247), channel_id=1, source_target_pairs={{0,1},{1,0},{2,3},{3,2},{4,5},{5,4},{6,7},{7,6},{8,9},{9,8},{10,11... | collective-permute-start | bytes 1179656 | tf_op jit(solution)/shard_map/ppermute | solution.py:24
  164.7 15.0 %all-to-all-start.2 = ((bf16[8,24,1024]{2,1,0:T(8,128)(2,1)}), bf16[8,24,1024]{2,1,0:T(8,128)(2,1)S(1)}, u32[]{:S(2)}, u32[]{:S(2)}) async-start(bf16[8,24,1024]{2,1,0:T(8,128)(2,1)} %bitcast.10), calls=%async_computation.2 | async-start | bytes 786432 | tf_op jit(solution)/shard_map/all_to_all | solution.py:170
  179.7 2.3 copy-start.9
  179.7 19.8 %copy-start.12 = (bf16[2048,1024]{1,0:T(8,128)(2,1)S(1)}, bf16[2048,1024]{1,0:T(8,128)(2,1)}, u32[]{:S(2)}) copy-start(bf16[2048,1024]{1,0:T(8,128)(2,1)} %param.22) | copy-start | bytes 12582916
  182.2 9.1 %collective-permute-start.24 = (bf16[64,2048]{1,0:T(8,128)(2,1)S(1)}, bf16[64,2048]{1,0:T(8,128)(2,1)S(1)}, u32[]{:S(2)}, u32[]{:S(2)}) collective-permute-start(bf16[64,2048]{1,0:T(8,128)(2,1)S(1)} %get-tuple-element.127), channel_id=1, source_target_pairs={{0,32},{32,64},{64,96},{96,0},{1,33},{33,65},{65,97},{97,1},{2,34}... | collective-permute-start | bytes 786440 | tf_op jit(solution)/shard_map/ppermute | solution.py:20
  182.9 8.5 %collective-permute-start.25 = (bf16[64,2048]{1,0:T(8,128)(2,1)S(1)}, bf16[64,2048]{1,0:T(8,128)(2,1)S(1)}, u32[]{:S(2)}, u32[]{:S(2)}) collective-permute-start(bf16[64,2048]{1,0:T(8,128)(2,1)S(1)} %get-tuple-element.127), channel_id=1, source_target_pairs={{0,96},{32,0},{64,32},{96,64},{1,97},{33,1},{65,33},{97,65},{2,98}... | collective-permute-start | bytes 786440 | tf_op jit(solution)/shard_map/ppermute | solution.py:20
  191.4 8.2 %collective-permute-start.26 = (bf16[64,2048]{1,0:T(8,128)(2,1)S(1)}, bf16[64,2048]{1,0:T(8,128)(2,1)S(1)}, u32[]{:S(2)}, u32[]{:S(2)}) collective-permute-start(bf16[64,2048]{1,0:T(8,128)(2,1)S(1)} %collective-permute-done.24), channel_id=1, source_target_pairs={{0,32},{32,64},{64,96},{96,0},{1,33},{33,65},{65,97},{97,1},{2,34}... | collective-permute-start | bytes 786440 | tf_op jit(solution)/shard_map/ppermute | solution.py:20
  191.4 9.4 %copy-start.3 = (bf16[2048,1024]{1,0:T(8,128)(2,1)S(1)}, bf16[2048,1024]{1,0:T(8,128)(2,1)}, u32[]{:S(2)}) copy-start(bf16[2048,1024]{1,0:T(8,128)(2,1)} %copy-done.2) | copy-start | bytes 12582916
  191.4 10.7 %collective-permute-start.27 = (bf16[64,2048]{1,0:T(8,128)(2,1)S(1)}, bf16[64,2048]{1,0:T(8,128)(2,1)S(1)}, u32[]{:S(2)}, u32[]{:S(2)}) collective-permute-start(bf16[64,2048]{1,0:T(8,128)(2,1)S(1)} %get-tuple-element.82), channel_id=1, source_target_pairs={{0,96},{32,0},{64,32},{96,64},{1,97},{33,1},{65,33},{97,65},{2,98}... | collective-permute-start | bytes 786440 | tf_op jit(solution)/shard_map/ppermute | solution.py:20
  200.8 2.2 copy-start.1
  202.1 2.4 %copy-start.13 = (bf16[1024,2048]{1,0:T(8,128)(2,1)S(1)}, bf16[1024,2048]{1,0:T(8,128)(2,1)}, u32[]{:S(2)}) copy-start(bf16[1024,2048]{1,0:T(8,128)(2,1)} %param.24) | copy-start | bytes 12582916
  202.1 8.1 %collective-permute-start.28 = (bf16[64,2048]{1,0:T(8,128)(2,1)S(1)}, bf16[64,2048]{1,0:T(8,128)(2,1)S(1)}, u32[]{:S(2)}, u32[]{:S(2)}) collective-permute-start(bf16[64,2048]{1,0:T(8,128)(2,1)S(1)} %get-tuple-element.82), channel_id=1, source_target_pairs={{0,32},{32,64},{64,96},{96,0},{1,33},{33,65},{65,97},{97,1},{2,34}... | collective-permute-start | bytes 786440 | tf_op jit(solution)/shard_map/ppermute | solution.py:20
  205.8 8.9 %collective-permute-start.29 = (bf16[64,2048]{1,0:T(8,128)(2,1)S(1)}, bf16[64,2048]{1,0:T(8,128)(2,1)S(1)}, u32[]{:S(2)}, u32[]{:S(2)}) collective-permute-start(bf16[64,2048]{1,0:T(8,128)(2,1)S(1)} %collective-permute-done.27), channel_id=1, source_target_pairs={{0,96},{32,0},{64,32},{96,64},{1,97},{33,1},{65,33},{97,65},{2,98}... | collective-permute-start | bytes 786440 | tf_op jit(solution)/shard_map/ppermute | solution.py:20
  208.1 9.4 %collective-permute-start.30 = (bf16[64,2048]{1,0:T(8,128)(2,1)S(1)}, bf16[64,2048]{1,0:T(8,128)(2,1)S(1)}, u32[]{:S(2)}, u32[]{:S(2)}) collective-permute-start(bf16[64,2048]{1,0:T(8,128)(2,1)S(1)} %get-tuple-element.124), channel_id=1, source_target_pairs={{0,96},{32,0},{64,32},{96,64},{1,97},{33,1},{65,33},{97,65},{2,98}... | collective-permute-start | bytes 786440 | tf_op jit(solution)/shard_map/ppermute | solution.py:20
  208.2 9.4 %collective-permute-start.31 = (bf16[64,2048]{1,0:T(8,128)(2,1)S(1)}, bf16[64,2048]{1,0:T(8,128)(2,1)S(1)}, u32[]{:S(2)}, u32[]{:S(2)}) collective-permute-start(bf16[64,2048]{1,0:T(8,128)(2,1)S(1)} %get-tuple-element.123), channel_id=1, source_target_pairs={{0,32},{32,64},{64,96},{96,0},{1,33},{33,65},{65,97},{97,1},{2,34}... | collective-permute-start | bytes 786440 | tf_op jit(solution)/shard_map/ppermute | solution.py:20
  220.2 16.0 %copy-start.10 = (f32[2048]{0:T(1024)S(1)}, f32[2048]{0:T(1024)}, u32[]{:S(2)}) copy-start(f32[2048]{0:T(1024)} %param.25) | copy-start | bytes 24580
  220.2 7.9 %collective-permute-start.34 = (bf16[64,2048]{1,0:T(8,128)(2,1)S(1)}, bf16[64,2048]{1,0:T(8,128)(2,1)S(1)}, u32[]{:S(2)}, u32[]{:S(2)}) collective-permute-start(bf16[64,2048]{1,0:T(8,128)(2,1)S(1)} %get-tuple-element.122), channel_id=1, source_target_pairs={{0,32},{32,64},{64,96},{96,0},{1,33},{33,65},{65,97},{97,1},{2,34}... | collective-permute-start | bytes 786440 | tf_op jit(solution)/shard_map/ppermute | solution.py:20
  220.3 8.4 %collective-permute-start.32 = (bf16[64,2048]{1,0:T(8,128)(2,1)S(1)}, bf16[64,2048]{1,0:T(8,128)(2,1)S(1)}, u32[]{:S(2)}, u32[]{:S(2)}) collective-permute-start(bf16[64,2048]{1,0:T(8,128)(2,1)S(1)} %add_convert_fusion.4), channel_id=1, source_target_pairs={{0,96},{32,0},{64,32},{96,64},{1,97},{33,1},{65,33},{97,65},{2,98}... | collective-permute-start | bytes 786440 | tf_op jit(solution)/shard_map/ppermute | solution.py:20
  223.5 8.0 %collective-permute-start.33 = (bf16[64,2048]{1,0:T(8,128)(2,1)S(1)}, bf16[64,2048]{1,0:T(8,128)(2,1)S(1)}, u32[]{:S(2)}, u32[]{:S(2)}) collective-permute-start(bf16[64,2048]{1,0:T(8,128)(2,1)S(1)} %get-tuple-element.121), channel_id=1, source_target_pairs={{0,96},{32,0},{64,32},{96,64},{1,97},{33,1},{65,33},{97,65},{2,98}... | collective-permute-start | bytes 786440 | tf_op jit(solution)/shard_map/ppermute | solution.py:20
  228.2 7.9 %collective-permute-start.35 = (bf16[64,2048]{1,0:T(8,128)(2,1)S(1)}, bf16[64,2048]{1,0:T(8,128)(2,1)S(1)}, u32[]{:S(2)}, u32[]{:S(2)}) collective-permute-start(bf16[64,2048]{1,0:T(8,128)(2,1)S(1)} %add_convert_fusion.3), channel_id=1, source_target_pairs={{0,32},{32,64},{64,96},{96,0},{1,33},{33,65},{65,97},{97,1},{2,34}... | collective-permute-start | bytes 786440 | tf_op jit(solution)/shard_map/ppermute | solution.py:20

commit v7 on v5

--- a/solution.py
+++ b/solution.py
@@ -211,6 +211,8 @@
         at = {"own": (0, 4, 10, 5), "prev": (1, 8, 11, 9), "foll": (2, 6, 12, 7), "far": (3, 14, 13, 15)}
         return jnp.concatenate([part[i * count : (i + 1) * count] for i in at[step]], axis=0)
 
+    wide = 4 * count
+
     def ring(weight, weight_pair, hidden, way, after):
         part = second(hidden, weight, weight_pair)
         own, prev, foll = (block(part, step) for step in ("own", "prev", "foll"))
@@ -233,11 +235,22 @@
     sum_l, hidden, right_pair = ring(left, left_pair, hidden, 1, right_pair)
     out_l = down(sum_l[2 * count :])
     back_l = swap_column(out_l)
-    sum_r, _, back_l = ring(right, right_pair, hidden, -1, back_l)
+    part = second(hidden, right, right_pair)
+    back = swap_column(part[10 * count : 14 * count])
+    via = shift(part[14 * count :], "z", 1)
+    prev = shift(part[8 * count : 10 * count], "z", -1)
+    foll = shift(down(up(part[6 * count : 8 * count]) + up(via)), "z", 1)
+    sum_b = up(part[4 * count : 6 * count]) + up(prev) + up(foll)
+    sum_b = sum_b[:count] + up(swap_column(down(sum_b[count:])))
+    own, prev, foll, far = jnp.split(down(up(part[:wide]) + up(back)), 4)
+    via = shift(far, "z", -1)
+    foll = shift(foll, "z", 1)
+    via, foll, back_l = hold(via, foll, back_l)
     return_l = finish(sum_l, back_l)
-    sum_r, return_l = hold(sum_r, return_l)
-    back_r = swap_column(down(sum_r[2 * count :]))
-    return_r = finish(sum_r, back_r)
+    prev = shift(down(up(prev) + up(via)), "z", -1)
+    sum_b, return_l = hold(sum_b, return_l)
+    sum_a = up(own) + up(prev) + up(foll)
+    return_r = exchange(down(jnp.concatenate([sum_a, sum_b], axis=0)))
     returned = jnp.concatenate([return_l, return_r], axis=1)
     group_out = lax.dot_general(
         dispatch_map, returned, (((0,), (0,)), ((), ())), preferred_element_type=jnp.float32

time: 235 us -> 234 us (level)
    all_to_all x3, waiting for transfers between devices: 13.9 us -> 22.7 us  [exchange(): lax.all_to_all(value, ('y', 'core'), split_axis=0, concat_axis=0, tiled=T...]
    ppermute x24 -> x27, waiting for transfers between devices: 65.1 us -> 60.5 us  [shift(): lax.ppermute(value, axis, [(i, (i + step) % size) for i in range(size)])]
    ppermute x5 -> x6, waiting for transfers between devices: 13.6 us -> 9.04 us  [swap_column(): return lax.ppermute(value, 'xl', [(0, 1), (1, 0)])]
    ppermute x24 -> x27, starting transfers between devices: 38.7 us -> 39.6 us  [shift(): lax.ppermute(value, axis, [(i, (i + step) % size) for i in range(size)])]
    unnamed x37 -> x43, local copies, waits for them, and re-layouts: 7.29 us -> 7.25 us
  transfers between devices with their start and end apart: 39 -> 43, of which waited for: 28 -> 28; matrix products, arithmetic and copies ran while one was open for 13% -> 13% of each run, Pallas kernels for 3% -> 3%
where the time goes in v7:
time: 234 us
  waiting for transfers between devices  114 us (49%)
  starting transfers between devices  68.8 us (29%)
  matrix products  29 us (12%)
  local copies, waits for them, and re-layouts  8.36 us (4%)
  other arithmetic  6.78 us (3%)
  Pallas kernels  6.14 us (3%)
    ppermute x27, waiting for transfers between devices, shift(): lax.ppermute(value, axis, [(i, (i + step) % size) for i in range(size)])  60.5 us
    ppermute x27, starting transfers between devices, shift(): lax.ppermute(value, axis, [(i, (i + step) % size) for i in range(size)])  39.6 us
    all_to_all x3, waiting for transfers between devices, exchange(): lax.all_to_all(value, ('y', 'core'), split_axis=0, concat_axis=0, tiled=T...  22.7 us
    ppermute x4, waiting for transfers between devices, swap_blocks(): return lax.ppermute(value, X, [(0, 3), (3, 0), (1, 2), (2, 1)])  22 us
    all_to_all x3, starting transfers between devices, exchange(): lax.all_to_all(value, ('y', 'core'), split_axis=0, concat_axis=0, tiled=T...  13.3 us
    ppermute x4, starting transfers between devices, swap_blocks(): return lax.ppermute(value, X, [(0, 3), (3, 0), (1, 2), (2, 1)])  11 us
    ppermute x6, waiting for transfers between devices, swap_column(): return lax.ppermute(value, 'xl', [(0, 1), (1, 0)])  9.04 us
    dot_general x2, matrix products, first(): jnp.dot(rows, w1, preferred_element_type=jnp.float32) + b1  9.02 us
  transfers between devices with their start and end apart: 43, of which 28 were waited for; matrix products, arithmetic and copies ran while one was open for 13% of the time, Pallas kernels for 3%

profile of v7, /device:TPU:0, one launch (start us, length us, event | category | flops | bytes accessed | tf_op | source)
XLA Modules:
  0.0 233.8 jit_solution(8881830593464942973)
XLA Ops:
  3.2 1.8 dispatch.1
  4.9 4.6 %all-to-all-start = ((bf16[8,24,2048]{2,1,0:T(8,128)(2,1)}), bf16[8,24,2048]{2,1,0:T(8,128)(2,1)S(1)}, u32[]{:S(2)}, u32[]{:S(2)}) async-start(bf16[8,24,2048]{2,1,0:T(8,128)(2,1)} %bitcast.2), calls=%async_computation | async-start | bytes 1572864 | tf_op jit(solution)/shard_map/all_to_all | solution.py:169
  10.0 2.8 %collective-permute-start.9 = (f32[512]{0:T(512)S(1)}, f32[512]{0:T(512)S(1)}, u32[]{:S(2)}, u32[]{:S(2)}) collective-permute-start(f32[512]{0:T(512)S(1)} %bitcast.49), channel_id=1, source_target_pairs={{0,3},{3,0},{1,2},{2,1},{4,7},{7,4},{5,6},{6,5},{8,11},{11,8},{9,1... | collective-permute-start | bytes 6152 | tf_op jit(solution)/shard_map/ppermute | solution.py:28
  12.8 2.0 collective-permute-done.9
  14.8 2.8 %collective-permute-start.10 = (bf16[2048,512]{1,0:T(8,128)(2,1)}, bf16[2048,512]{1,0:T(8,128)(2,1)}, u32[]{:S(2)}, u32[]{:S(2)}) collective-permute-start(bf16[2048,512]{1,0:T(8,128)(2,1)} %bitcast.51), channel_id=1, source_target_pairs={{0,3},{3,0},{1,2},{2,1},{4,7},{7,4},{5,6},{6,5},{8,11},{11,8},{9,1... | collective-permute-start | bytes 6291464 | tf_op jit(solution)/shard_map/ppermute | solution.py:28
  17.6 5.1 %all-to-all-done = bf16[8,24,2048]{2,1,0:T(8,128)(2,1)S(1)} async-done(((bf16[8,24,2048]{2,1,0:T(8,128)(2,1)}), bf16[8,24,2048]{2,1,0:T(8,128)(2,1)S(1)}, u32[]{:S(2)}, u32[]{:S(2)}) %all-to-all-start) | async-done | bytes 786464 | tf_op jit(solution)/shard_map/all_to_all | solution.py:169
  22.7 2.0 collective-permute-start.3
  24.7 2.2 collective-permute-start.4
  26.9 1.5 collective-permute-start.5
  28.6 7.1 %collective-permute-done.3 = bf16[96,2048]{1,0:T(8,128)(2,1)S(1)} collective-permute-done((bf16[96,2048]{1,0:T(8,128)(2,1)S(1)}, bf16[96,2048]{1,0:T(8,128)(2,1)S(1)}, u32[]{:S(2)}, u32[]{:S(2)}) %collective-permute-start.3) | collective-permute-done | bytes 393248 | tf_op jit(solution)/shard_map/ppermute | solution.py:20
  35.8 1.5 collective-permute-done.5
  37.3 1.5 collective-permute-start.11
  38.9 1.9 collective-permute-start.7
  40.8 6.3 %collective-permute-done.6 = bf16[96,2048]{1,0:T(8,128)(2,1)S(1)} collective-permute-done((bf16[96,2048]{1,0:T(8,128)(2,1)S(1)}, bf16[96,2048]{1,0:T(8,128)(2,1)S(1)}, u32[]{:S(2)}, u32[]{:S(2)}) %collective-permute-start.6) | collective-permute-done | bytes 393248 | tf_op jit(solution)/shard_map/ppermute | solution.py:20
  47.2 2.2 on_chip.2
  49.4 2.0 copy-done.2
  51.4 2.2 on_chip.3
  53.6 2.0 copy-done
  55.6 2.8 %collective-permute-start.14 = (bf16[512,1024]{1,0:T(8,128)(2,1)S(1)}, bf16[512,1024]{1,0:T(8,128)(2,1)S(1)}, u32[]{:S(2)}, u32[]{:S(2)}) collective-permute-start(bf16[512,1024]{1,0:T(8,128)(2,1)S(1)} %get-tuple-element.62), channel_id=1, source_target_pairs={{0,3},{3,0},{1,2},{2,1},{4,7},{7,4},{5,6},{6,5},{8,11},{11,8},{9,1... | collective-permute-start | bytes 3145736 | tf_op jit(solution)/shard_map/ppermute | solution.py:28
  58.5 3.3 %collective-permute-start.13 = (bf16[192,2048]{1,0:T(8,128)(2,1)S(1)}, bf16[192,2048]{1,0:T(8,128)(2,1)S(1)}, u32[]{:S(2)}, u32[]{:S(2)}) collective-permute-start(bf16[192,2048]{1,0:T(8,128)(2,1)S(1)} %collective-permute-done.7), channel_id=1, source_target_pairs={{0,12},{4,0},{8,4},{12,8},{1,13},{5,1},{9,5},{13,9},{2,14},{6,2},{... | collective-permute-start | bytes 2359304 | tf_op jit(solution)/shard_map/ppermute | solution.py:20
  61.9 1.8 collective-permute-done.11
  66.1 2.8 %collective-permute-start.17 = (bf16[512,1024]{1,0:T(8,128)(2,1)S(1)}, bf16[512,1024]{1,0:T(8,128)(2,1)S(1)}, u32[]{:S(2)}, u32[]{:S(2)}) collective-permute-start(bf16[512,1024]{1,0:T(8,128)(2,1)S(1)} %get-tuple-element.63), channel_id=1, source_target_pairs={{0,3},{3,0},{1,2},{2,1},{4,7},{7,4},{5,6},{6,5},{8,11},{11,8},{9,1... | collective-permute-start | bytes 3145736 | tf_op jit(solution)/shard_map/ppermute | solution.py:28
  69.1 6.0 %maximum_convert_fusion = bf16[1248,1024]{1,0:T(8,128)(2,1)S(1)} fusion(bf16[1248,2048]{1,0:T(8,128)(2,1)S(1)} %constant_dynamic-update-slice_fusion, bf16[2048,512]{1,0:T(8,128)(2,1)} %collective-permute-done.10, bf16[2048,512]{1,0:T(8,128)(2,1)S(1)} %bitcast.52, f32[1024]{0:T(1024)S(1)} %pad_maximum_fusion.21), kind=kOutput, calls=%fused_computation | convolution fusion | flops 5246713856 | bytes 11866112 | tf_op jit(solution)/shard_map/dot_general | solution.py:202
  75.1 1.4 collective-permute-done.13
  76.5 3.0 %fusion.12 = bf16[288,1024]{1,0:T(8,128)(2,1)S(1)} fusion(bf16[2048,512]{1,0:T(8,128)(2,1)} %collective-permute-done.10, bf16[2048,512]{1,0:T(8,128)(2,1)S(1)} %bitcast.53, bf16[192,2048]{1,0:T(8,128)(2,1)S(1)} %collective-permute-done.13, bf16[96,2048]{1,0:T(8,128)(2,1)S(1)} %collective-permute-done.12, f32[1024]{0:T(1024)S(1)} %pad_maximum_fusion.21), kind=kOutput, calls=%fused_computation.23 | convolution fusion | flops 1219592192 | bytes 5967872 | tf_op jit(solution)/shard_map/dot_general | solution.py:202
  79.5 7.7 %collective-permute-done.14 = bf16[512,1024]{1,0:T(8,128)(2,1)S(1)} collective-permute-done((bf16[512,1024]{1,0:T(8,128)(2,1)S(1)}, bf16[512,1024]{1,0:T(8,128)(2,1)S(1)}, u32[]{:S(2)}, u32[]{:S(2)}) %collective-permute-start.14) | collective-permute-done | bytes 1048608 | tf_op jit(solution)/shard_map/ppermute | solution.py:28
  87.3 4.3 %convolution_convert_fusion.1 = bf16[1536,1024]{1,0:T(8,128)(2,1)S(1)} fusion(bf16[512,1024]{1,0:T(8,128)(2,1)S(1)} %collective-permute-done.14, bf16[512,1024]{1,0:T(8,128)(2,1)S(1)} %get-tuple-element.62, bf16[288,1024]{1,0:T(8,128)(2,1)S(1)} %fusion.12, bf16[1248,1024]{1,0:T(8,128)(2,1)S(1)} %maximum_convert_fusion), kind=kOutput, calls=%fused_computation.3 | convolution fusion | flops 3233284096 | bytes 8388608 | tf_op jit(solution)/shard_map/dot_general | solution.py:208
  92.0 2.0 collective-permute-start.16
  94.1 2.2 collective-permute-start.15
  96.6 11.0 %collective-permute-done.17 = bf16[512,1024]{1,0:T(8,128)(2,1)S(1)} collective-permute-done((bf16[512,1024]{1,0:T(8,128)(2,1)S(1)}, bf16[512,1024]{1,0:T(8,128)(2,1)S(1)}, u32[]{:S(2)}, u32[]{:S(2)}) %collective-permute-start.17) | collective-permute-done | bytes 1048608 | tf_op jit(solution)/shard_map/ppermute | solution.py:28
  107.6 2.1 collective-permute-done.16
  110.3 2.9 %collective-permute-start.22 = (bf16[384,1024]{1,0:T(8,128)(2,1)S(1)}, bf16[384,1024]{1,0:T(8,128)(2,1)S(1)}, u32[]{:S(2)}, u32[]{:S(2)}) collective-permute-start(bf16[384,1024]{1,0:T(8,128)(2,1)S(1)} %add_convert_fusion.1), channel_id=1, source_target_pairs={{0,12},{4,0},{8,4},{12,8},{1,13},{5,1},{9,5},{13,9},{2,14},{6,2},{... | collective-permute-start | bytes 2359304 | tf_op jit(solution)/shard_map/ppermute | solution.py:20
  113.2 3.8 %convolution_convert_fusion = bf16[1536,1024]{1,0:T(8,128)(2,1)S(1)} fusion(bf16[1536,1024]{1,0:T(8,128)(2,1)S(1)} %pad_maximum_fusion.1, bf16[512,1024]{1,0:T(8,128)(2,1)S(1)} %collective-permute-done.17, bf16[512,1024]{1,0:T(8,128)(2,1)S(1)} %get-tuple-element.63), kind=kOutput, calls=%fused_computation.2 | convolution fusion | flops 3226992640 | bytes 8388608 | tf_op jit(solution)/shard_map/dot_general | solution.py:208
  117.9 3.2 %collective-permute-start.18 = (bf16[192,1024]{1,0:T(8,128)(2,1)S(1)}, bf16[192,1024]{1,0:T(8,128)(2,1)S(1)}, u32[]{:S(2)}, u32[]{:S(2)}) collective-permute-start(bf16[192,1024]{1,0:T(8,128)(2,1)S(1)} %get-tuple-element.101), channel_id=1, source_target_pairs={{0,12},{4,0},{8,4},{12,8},{1,13},{5,1},{9,5},{13,9},{2,14},{6,2},{... | collective-permute-start | bytes 1179656 | tf_op jit(solution)/shard_map/ppermute | solution.py:20
  121.1 5.5 %collective-permute-done.19 = bf16[192,1024]{1,0:T(8,128)(2,1)S(1)} collective-permute-done((bf16[192,1024]{1,0:T(8,128)(2,1)S(1)}, bf16[192,1024]{1,0:T(8,128)(2,1)S(1)}, u32[]{:S(2)}, u32[]{:S(2)}) %collective-permute-start.19) | collective-permute-done | bytes 393248 | tf_op jit(solution)/shard_map/ppermute | solution.py:20
  126.9 4.4 %collective-permute-done.22 = bf16[384,1024]{1,0:T(8,128)(2,1)S(1)} collective-permute-done((bf16[384,1024]{1,0:T(8,128)(2,1)S(1)}, bf16[384,1024]{1,0:T(8,128)(2,1)S(1)}, u32[]{:S(2)}, u32[]{:S(2)}) %collective-permute-start.22) | collective-permute-done | bytes 786464 | tf_op jit(solution)/shard_map/ppermute | solution.py:20
  132.0 5.7 %collective-permute-done.23 = bf16[384,1024]{1,0:T(8,128)(2,1)S(1)} collective-permute-done((bf16[384,1024]{1,0:T(8,128)(2,1)S(1)}, bf16[384,1024]{1,0:T(8,128)(2,1)S(1)}, u32[]{:S(2)}, u32[]{:S(2)}) %collective-permute-start.23) | collective-permute-done | bytes 786464 | tf_op jit(solution)/shard_map/ppermute | solution.py:24
  138.1 3.3 %collective-permute-start.24 = (bf16[96,1024]{1,0:T(8,128)(2,1)S(1)}, bf16[96,1024]{1,0:T(8,128)(2,1)S(1)}, u32[]{:S(2)}, u32[]{:S(2)}) collective-permute-start(bf16[96,1024]{1,0:T(8,128)(2,1)S(1)} %get-tuple-element.110), channel_id=1, source_target_pairs={{0,12},{4,0},{8,4},{12,8},{1,13},{5,1},{9,5},{13,9},{2,14},{6,2},{... | collective-permute-start | bytes 589832 | tf_op jit(solution)/shard_map/ppermute | solution.py:20
  141.7 3.0 %collective-permute-done.24 = bf16[96,1024]{1,0:T(8,128)(2,1)S(1)} collective-permute-done((bf16[96,1024]{1,0:T(8,128)(2,1)S(1)}, bf16[96,1024]{1,0:T(8,128)(2,1)S(1)}, u32[]{:S(2)}, u32[]{:S(2)}) %collective-permute-start.24) | collective-permute-done | bytes 196640 | tf_op jit(solution)/shard_map/ppermute | solution.py:20
  144.7 3.6 %collective-permute-done.25 = bf16[96,1024]{1,0:T(8,128)(2,1)S(1)} collective-permute-done((bf16[96,1024]{1,0:T(8,128)(2,1)S(1)}, bf16[96,1024]{1,0:T(8,128)(2,1)S(1)}, u32[]{:S(2)}, u32[]{:S(2)}) %collective-permute-start.25) | collective-permute-done | bytes 196640 | tf_op jit(solution)/shard_map/ppermute | solution.py:20
  149.3 5.3 %all-to-all-start.1 = ((bf16[8,24,1024]{2,1,0:T(8,128)(2,1)}), bf16[8,24,1024]{2,1,0:T(8,128)(2,1)S(1)}, u32[]{:S(2)}, u32[]{:S(2)}) async-start(bf16[8,24,1024]{2,1,0:T(8,128)(2,1)} %bitcast.8), calls=%async_computation.1 | async-start | bytes 786432 | tf_op jit(solution)/shard_map/all_to_all | solution.py:169
  154.8 8.8 %all-to-all-done.1 = bf16[8,24,1024]{2,1,0:T(8,128)(2,1)S(1)} async-done(((bf16[8,24,1024]{2,1,0:T(8,128)(2,1)}), bf16[8,24,1024]{2,1,0:T(8,128)(2,1)S(1)}, u32[]{:S(2)}, u32[]{:S(2)}) %all-to-all-start.1) | async-done | bytes 393248 | tf_op jit(solution)/shard_map/all_to_all | solution.py:169
  164.3 3.5 %all-to-all-start.2 = ((bf16[8,24,1024]{2,1,0:T(8,128)(2,1)}), bf16[8,24,1024]{2,1,0:T(8,128)(2,1)S(1)}, u32[]{:S(2)}, u32[]{:S(2)}) async-start(bf16[8,24,1024]{2,1,0:T(8,128)(2,1)} %bitcast.10), calls=%async_computation.2 | async-start | bytes 786432 | tf_op jit(solution)/shard_map/all_to_all | solution.py:169
  167.9 8.8 %all-to-all-done.2 = bf16[8,24,1024]{2,1,0:T(8,128)(2,1)S(1)} async-done(((bf16[8,24,1024]{2,1,0:T(8,128)(2,1)}), bf16[8,24,1024]{2,1,0:T(8,128)(2,1)S(1)}, u32[]{:S(2)}, u32[]{:S(2)}) %all-to-all-start.2) | async-done | bytes 393248 | tf_op jit(solution)/shard_map/all_to_all | solution.py:169
  176.7 1.6 fusion.48
  179.5 2.7 %collective-permute-start.29 = (bf16[64,2048]{1,0:T(8,128)(2,1)S(1)}, bf16[64,2048]{1,0:T(8,128)(2,1)S(1)}, u32[]{:S(2)}, u32[]{:S(2)}) collective-permute-start(bf16[64,2048]{1,0:T(8,128)(2,1)S(1)} %get-tuple-element.113), channel_id=1, source_target_pairs={{0,96},{32,0},{64,32},{96,64},{1,97},{33,1},{65,33},{97,65},{2,98}... | collective-permute-start | bytes 786440 | tf_op jit(solution)/shard_map/ppermute | solution.py:20
  182.2 5.8 %collective-permute-done.28 = bf16[64,2048]{1,0:T(8,128)(2,1)S(1)} collective-permute-done((bf16[64,2048]{1,0:T(8,128)(2,1)S(1)}, bf16[64,2048]{1,0:T(8,128)(2,1)S(1)}, u32[]{:S(2)}, u32[]{:S(2)}) %collective-permute-start.28) | collective-permute-done | bytes 262176 | tf_op jit(solution)/shard_map/ppermute | solution.py:20
  188.0 3.2 %collective-permute-start.31 = (bf16[64,2048]{1,0:T(8,128)(2,1)S(1)}, bf16[64,2048]{1,0:T(8,128)(2,1)S(1)}, u32[]{:S(2)}, u32[]{:S(2)}) collective-permute-start(bf16[64,2048]{1,0:T(8,128)(2,1)S(1)} %get-tuple-element.80), channel_id=1, source_target_pairs={{0,96},{32,0},{64,32},{96,64},{1,97},{33,1},{65,33},{97,65},{2,98}... | collective-permute-start | bytes 786440 | tf_op jit(solution)/shard_map/ppermute | solution.py:20
  191.2 4.9 %collective-permute-done.30 = bf16[64,2048]{1,0:T(8,128)(2,1)S(1)} collective-permute-done((bf16[64,2048]{1,0:T(8,128)(2,1)S(1)}, bf16[64,2048]{1,0:T(8,128)(2,1)S(1)}, u32[]{:S(2)}, u32[]{:S(2)}) %collective-permute-start.30) | collective-permute-done | bytes 262176 | tf_op jit(solution)/shard_map/ppermute | solution.py:20
  196.2 1.3 fusion.17
  197.5 1.3 fusion.18
  199.6 1.3 fusion.49
  201.1 1.3 fusion.1
  202.5 2.3 collective-permute-start.33
  204.9 2.0 collective-permute-start.35
  206.9 4.5 %collective-permute-done.33 = bf16[64,2048]{1,0:T(8,128)(2,1)S(1)} collective-permute-done((bf16[64,2048]{1,0:T(8,128)(2,1)S(1)}, bf16[64,2048]{1,0:T(8,128)(2,1)S(1)}, u32[]{:S(2)}, u32[]{:S(2)}) %collective-permute-start.33) | collective-permute-done | bytes 262176 | tf_op jit(solution)/shard_map/ppermute | solution.py:20
  212.7 1.3 fusion.19
  214.3 1.3 fusion.50
  215.5 1.3 fusion.2
  217.0 3.2 %collective-permute-start.36 = (bf16[64,2048]{1,0:T(8,128)(2,1)S(1)}, bf16[64,2048]{1,0:T(8,128)(2,1)S(1)}, u32[]{:S(2)}, u32[]{:S(2)}) collective-permute-start(bf16[64,2048]{1,0:T(8,128)(2,1)S(1)} %add_convert_fusion.4), channel_id=1, source_target_pairs={{0,96},{32,0},{64,32},{96,64},{1,97},{33,1},{65,33},{97,65},{2,98}... | collective-permute-start | bytes 786440 | tf_op jit(solution)/shard_map/ppermute | solution.py:20
  220.2 1.9 collective-permute-start.37
  222.1 2.7 %collective-permute-done.38 = bf16[64,2048]{1,0:T(8,128)(2,1)S(1)} collective-permute-done((bf16[64,2048]{1,0:T(8,128)(2,1)S(1)}, bf16[64,2048]{1,0:T(8,128)(2,1)S(1)}, u32[]{:S(2)}, u32[]{:S(2)}) %collective-permute-start.38) | collective-permute-done | bytes 262176 | tf_op jit(solution)/shard_map/ppermute | solution.py:20
  225.5 2.7 %collective-permute-done.37 = bf16[64,2048]{1,0:T(8,128)(2,1)S(1)} collective-permute-done((bf16[64,2048]{1,0:T(8,128)(2,1)S(1)}, bf16[64,2048]{1,0:T(8,128)(2,1)S(1)}, u32[]{:S(2)}, u32[]{:S(2)}) %collective-permute-start.37) | collective-permute-done | bytes 262176 | tf_op jit(solution)/shard_map/ppermute | solution.py:20
  228.2 4.6 %collective-permute-done.39 = bf16[64,2048]{1,0:T(8,128)(2,1)S(1)} collective-permute-done((bf16[64,2048]{1,0:T(8,128)(2,1)S(1)}, bf16[64,2048]{1,0:T(8,128)(2,1)S(1)}, u32[]{:S(2)}, u32[]{:S(2)}) %collective-permute-start.39) | collective-permute-done | bytes 262176 | tf_op jit(solution)/shard_map/ppermute | solution.py:20
  (121 shorter events, 18.5 us)
Async XLA Ops:
  0.0 10.0 %copy-start.11 = (f32[1,512]{1,0:T(1,128)S(1)}, f32[1,512]{1,0:T(1,128)}, u32[]{:S(2)}) copy-start(f32[1,512]{1,0:T(1,128)} %param.18) | copy-start | bytes 6148
  0.0 22.6 %collective-permute-start = (bf16[2048,1024]{1,0:T(8,128)(2,1)}, bf16[2048,1024]{1,0:T(8,128)(2,1)}, u32[]{:S(2)}, u32[]{:S(2)}) collective-permute-start(bf16[2048,1024]{1,0:T(8,128)(2,1)} %param.22), channel_id=1, source_target_pairs={{0,16},{16,0},{1,17},{17,1},{2,18},{18,2},{3,19},{19,3},{4,20},{20... | collective-permute-start | bytes 12582920 | tf_op jit(solution)/shard_map/ppermute | solution.py:32
  0.0 22.6 %collective-permute-start.1 = (bf16[1024,2048]{1,0:T(8,128)(2,1)}, bf16[1024,2048]{1,0:T(8,128)(2,1)}, u32[]{:S(2)}, u32[]{:S(2)}) collective-permute-start(bf16[1024,2048]{1,0:T(8,128)(2,1)} %param.24), channel_id=1, source_target_pairs={{0,16},{16,0},{1,17},{17,1},{2,18},{18,2},{3,19},{19,3},{4,20},{20... | collective-permute-start | bytes 12582920 | tf_op jit(solution)/shard_map/ppermute | solution.py:32
  1.3 1.0 copy-start.4
  2.3 0.8 copy-start.6
  3.2 6.3 %copy-start.15 = (f32[1024]{0:T(1024)S(1)}, f32[1024]{0:T(1024)}, u32[]{:S(2)}) copy-start(f32[1024]{0:T(1024)} %param.23) | copy-start | bytes 12292
  3.2 25.3 %copy-start.7 = (bf16[1,512,2048]{2,1,0:T(8,128)(2,1)S(1)}, bf16[1,512,2048]{2,1,0:T(8,128)(2,1)}, u32[]{:S(2)}) copy-start(bf16[1,512,2048]{2,1,0:T(8,128)(2,1)} %param.19) | copy-start | bytes 6291460
  4.9 17.7 %all-to-all-start = ((bf16[8,24,2048]{2,1,0:T(8,128)(2,1)}), bf16[8,24,2048]{2,1,0:T(8,128)(2,1)S(1)}, u32[]{:S(2)}, u32[]{:S(2)}) async-start(bf16[8,24,2048]{2,1,0:T(8,128)(2,1)} %bitcast.2), calls=%async_computation | async-start | bytes 1572864 | tf_op jit(solution)/shard_map/all_to_all | solution.py:169
  9.5 8.1 %collective-permute-start.2 = (f32[1024]{0:T(1024)S(1)}, f32[1024]{0:T(1024)S(1)}, u32[]{:S(2)}, u32[]{:S(2)}) collective-permute-start(f32[1024]{0:T(1024)S(1)} %copy-done.15), channel_id=1, source_target_pairs={{0,16},{16,0},{1,17},{17,1},{2,18},{18,2},{3,19},{19,3},{4,20},{20... | collective-permute-start | bytes 12296 | tf_op jit(solution)/shard_map/ppermute | solution.py:32
  10.0 4.8 %collective-permute-start.9 = (f32[512]{0:T(512)S(1)}, f32[512]{0:T(512)S(1)}, u32[]{:S(2)}, u32[]{:S(2)}) collective-permute-start(f32[512]{0:T(512)S(1)} %bitcast.49), channel_id=1, source_target_pairs={{0,3},{3,0},{1,2},{2,1},{4,7},{7,4},{5,6},{6,5},{8,11},{11,8},{9,1... | collective-permute-start | bytes 6152 | tf_op jit(solution)/shard_map/ppermute | solution.py:28
  14.8 50.1 %collective-permute-start.10 = (bf16[2048,512]{1,0:T(8,128)(2,1)}, bf16[2048,512]{1,0:T(8,128)(2,1)}, u32[]{:S(2)}, u32[]{:S(2)}) collective-permute-start(bf16[2048,512]{1,0:T(8,128)(2,1)} %bitcast.51), channel_id=1, source_target_pairs={{0,3},{3,0},{1,2},{2,1},{4,7},{7,4},{5,6},{6,5},{8,11},{11,8},{9,1... | collective-permute-start | bytes 6291464 | tf_op jit(solution)/shard_map/ppermute | solution.py:28
  17.6 11.1 %copy-start.17 = (f32[1024]{0:T(1024)}, f32[1024]{0:T(1024)S(1)}, u32[]{:S(2)}) copy-start(f32[1024]{0:T(1024)S(1)} %collective-permute-done.2) | copy-start | bytes 12292
  22.7 13.0 %collective-permute-start.3 = (bf16[96,2048]{1,0:T(8,128)(2,1)S(1)}, bf16[96,2048]{1,0:T(8,128)(2,1)S(1)}, u32[]{:S(2)}, u32[]{:S(2)}) collective-permute-start(bf16[96,2048]{1,0:T(8,128)(2,1)S(1)} %get-tuple-element.112), channel_id=1, source_target_pairs={{0,4},{4,8},{8,12},{12,0},{1,5},{5,9},{9,13},{13,1},{2,6},{6,10},{... | collective-permute-start | bytes 1179656 | tf_op jit(solution)/shard_map/ppermute | solution.py:20
  24.7 11.0 %collective-permute-start.4 = (bf16[96,2048]{1,0:T(8,128)(2,1)S(1)}, bf16[96,2048]{1,0:T(8,128)(2,1)S(1)}, u32[]{:S(2)}, u32[]{:S(2)}) collective-permute-start(bf16[96,2048]{1,0:T(8,128)(2,1)S(1)} %get-tuple-element.112), channel_id=1, source_target_pairs={{0,12},{4,0},{8,4},{12,8},{1,13},{5,1},{9,5},{13,9},{2,14},{6,2},{... | collective-permute-start | bytes 1179656 | tf_op jit(solution)/shard_map/ppermute | solution.py:20
  26.9 10.4 %collective-permute-start.5 = (bf16[96,2048]{1,0:T(8,128)(2,1)S(1)}, bf16[96,2048]{1,0:T(8,128)(2,1)S(1)}, u32[]{:S(2)}, u32[]{:S(2)}) collective-permute-start(bf16[96,2048]{1,0:T(8,128)(2,1)S(1)} %get-tuple-element.111), channel_id=1, source_target_pairs={{0,1},{1,0},{2,3},{3,2},{4,5},{5,4},{6,7},{7,6},{8,9},{9,8},{10,11... | collective-permute-start | bytes 1179656 | tf_op jit(solution)/shard_map/ppermute | solution.py:24
  35.8 11.4 %collective-permute-start.6 = (bf16[96,2048]{1,0:T(8,128)(2,1)S(1)}, bf16[96,2048]{1,0:T(8,128)(2,1)S(1)}, u32[]{:S(2)}, u32[]{:S(2)}) collective-permute-start(bf16[96,2048]{1,0:T(8,128)(2,1)S(1)} %collective-permute-done.3), channel_id=1, source_target_pairs={{0,4},{4,8},{8,12},{12,0},{1,5},{5,9},{9,13},{13,1},{2,6},{6,10},{... | collective-permute-start | bytes 1179656 | tf_op jit(solution)/shard_map/ppermute | solution.py:20
  37.3 26.4 %collective-permute-start.11 = (bf16[288,2048]{1,0:T(8,128)(2,1)S(1)}, bf16[288,2048]{1,0:T(8,128)(2,1)S(1)}, u32[]{:S(2)}, u32[]{:S(2)}) collective-permute-start(bf16[288,2048]{1,0:T(8,128)(2,1)S(1)} %pad_maximum_fusion.10), channel_id=1, source_target_pairs={{0,1},{1,0},{2,3},{3,2},{4,5},{5,4},{6,7},{7,6},{8,9},{9,8},{10,11... | collective-permute-start | bytes 3538952 | tf_op jit(solution)/shard_map/ppermute | solution.py:24
  38.9 19.6 %collective-permute-start.7 = (bf16[192,2048]{1,0:T(8,128)(2,1)S(1)}, bf16[192,2048]{1,0:T(8,128)(2,1)S(1)}, u32[]{:S(2)}, u32[]{:S(2)}) collective-permute-start(bf16[192,2048]{1,0:T(8,128)(2,1)S(1)} %pad_maximum_fusion.13), channel_id=1, source_target_pairs={{0,12},{4,0},{8,4},{12,8},{1,13},{5,1},{9,5},{13,9},{2,14},{6,2},{... | collective-permute-start | bytes 2359304 | tf_op jit(solution)/shard_map/ppermute | solution.py:20
  47.1 19.0 %collective-permute-start.8 = (bf16[192,2048]{1,0:T(8,128)(2,1)S(1)}, bf16[192,2048]{1,0:T(8,128)(2,1)S(1)}, u32[]{:S(2)}, u32[]{:S(2)}) collective-permute-start(bf16[192,2048]{1,0:T(8,128)(2,1)S(1)} %pad_maximum_fusion.13), channel_id=1, source_target_pairs={{0,4},{4,8},{8,12},{12,0},{1,5},{5,9},{9,13},{13,1},{2,6},{6,10},{... | collective-permute-start | bytes 2359304 | tf_op jit(solution)/shard_map/ppermute | solution.py:20
  49.4 2.0 copy-start.2
  53.6 2.0 copy-start
  55.6 31.7 %collective-permute-start.14 = (bf16[512,1024]{1,0:T(8,128)(2,1)S(1)}, bf16[512,1024]{1,0:T(8,128)(2,1)S(1)}, u32[]{:S(2)}, u32[]{:S(2)}) collective-permute-start(bf16[512,1024]{1,0:T(8,128)(2,1)S(1)} %get-tuple-element.62), channel_id=1, source_target_pairs={{0,3},{3,0},{1,2},{2,1},{4,7},{7,4},{5,6},{6,5},{8,11},{11,8},{9,1... | collective-permute-start | bytes 3145736 | tf_op jit(solution)/shard_map/ppermute | solution.py:28
  58.5 18.1 %collective-permute-start.13 = (bf16[192,2048]{1,0:T(8,128)(2,1)S(1)}, bf16[192,2048]{1,0:T(8,128)(2,1)S(1)}, u32[]{:S(2)}, u32[]{:S(2)}) collective-permute-start(bf16[192,2048]{1,0:T(8,128)(2,1)S(1)} %collective-permute-done.7), channel_id=1, source_target_pairs={{0,12},{4,0},{8,4},{12,8},{1,13},{5,1},{9,5},{13,9},{2,14},{6,2},{... | collective-permute-start | bytes 2359304 | tf_op jit(solution)/shard_map/ppermute | solution.py:20
  61.9 7.2 %copy-start.14 = (bf16[1,2048,512]{2,1,0:T(8,128)(2,1)S(1)}, bf16[1,2048,512]{2,1,0:T(8,128)(2,1)}, u32[]{:S(2)}) copy-start(bf16[1,2048,512]{2,1,0:T(8,128)(2,1)} %param.17) | copy-start | bytes 6291460
  64.9 11.6 %collective-permute-start.12 = (bf16[96,2048]{1,0:T(8,128)(2,1)S(1)}, bf16[96,2048]{1,0:T(8,128)(2,1)S(1)}, u32[]{:S(2)}, u32[]{:S(2)}) collective-permute-start(bf16[96,2048]{1,0:T(8,128)(2,1)S(1)} %collective-permute-done.6), channel_id=1, source_target_pairs={{0,1},{1,0},{2,3},{3,2},{4,5},{5,4},{6,7},{7,6},{8,9},{9,8},{10,11... | collective-permute-start | bytes 1179656 | tf_op jit(solution)/shard_map/ppermute | solution.py:24
  66.1 41.5 %collective-permute-start.17 = (bf16[512,1024]{1,0:T(8,128)(2,1)S(1)}, bf16[512,1024]{1,0:T(8,128)(2,1)S(1)}, u32[]{:S(2)}, u32[]{:S(2)}) collective-permute-start(bf16[512,1024]{1,0:T(8,128)(2,1)S(1)} %get-tuple-element.63), channel_id=1, source_target_pairs={{0,3},{3,0},{1,2},{2,1},{4,7},{7,4},{5,6},{6,5},{8,11},{11,8},{9,1... | collective-permute-start | bytes 3145736 | tf_op jit(solution)/shard_map/ppermute | solution.py:28
  92.0 17.7 %collective-permute-start.16 = (bf16[384,1024]{1,0:T(8,128)(2,1)S(1)}, bf16[384,1024]{1,0:T(8,128)(2,1)S(1)}, u32[]{:S(2)}, u32[]{:S(2)}) collective-permute-start(bf16[384,1024]{1,0:T(8,128)(2,1)S(1)} %pad_maximum_fusion.15), channel_id=1, source_target_pairs={{0,4},{4,8},{8,12},{12,0},{1,5},{5,9},{9,13},{13,1},{2,6},{6,10},{... | collective-permute-start | bytes 2359304 | tf_op jit(solution)/shard_map/ppermute | solution.py:20
  94.1 15.9 %collective-permute-start.15 = (bf16[384,1024]{1,0:T(8,128)(2,1)S(1)}, bf16[384,1024]{1,0:T(8,128)(2,1)S(1)}, u32[]{:S(2)}, u32[]{:S(2)}) collective-permute-start(bf16[384,1024]{1,0:T(8,128)(2,1)S(1)} %pad_maximum_fusion.14), channel_id=1, source_target_pairs={{0,12},{4,0},{8,4},{12,8},{1,13},{5,1},{9,5},{13,9},{2,14},{6,2},{... | collective-permute-start | bytes 2359304 | tf_op jit(solution)/shard_map/ppermute | solution.py:20
  110.3 20.9 %collective-permute-start.22 = (bf16[384,1024]{1,0:T(8,128)(2,1)S(1)}, bf16[384,1024]{1,0:T(8,128)(2,1)S(1)}, u32[]{:S(2)}, u32[]{:S(2)}) collective-permute-start(bf16[384,1024]{1,0:T(8,128)(2,1)S(1)} %add_convert_fusion.1), channel_id=1, source_target_pairs={{0,12},{4,0},{8,4},{12,8},{1,13},{5,1},{9,5},{13,9},{2,14},{6,2},{... | collective-permute-start | bytes 2359304 | tf_op jit(solution)/shard_map/ppermute | solution.py:20
  117.1 9.6 %collective-permute-start.19 = (bf16[192,1024]{1,0:T(8,128)(2,1)S(1)}, bf16[192,1024]{1,0:T(8,128)(2,1)S(1)}, u32[]{:S(2)}, u32[]{:S(2)}) collective-permute-start(bf16[192,1024]{1,0:T(8,128)(2,1)S(1)} %get-tuple-element.102), channel_id=1, source_target_pairs={{0,4},{4,8},{8,12},{12,0},{1,5},{5,9},{9,13},{13,1},{2,6},{6,10},{... | collective-permute-start | bytes 1179656 | tf_op jit(solution)/shard_map/ppermute | solution.py:20
  117.2 20.6 %collective-permute-start.23 = (bf16[384,1024]{1,0:T(8,128)(2,1)S(1)}, bf16[384,1024]{1,0:T(8,128)(2,1)S(1)}, u32[]{:S(2)}, u32[]{:S(2)}) collective-permute-start(bf16[384,1024]{1,0:T(8,128)(2,1)S(1)} %slice.186), channel_id=1, source_target_pairs={{0,1},{1,0},{2,3},{3,2},{4,5},{5,4},{6,7},{7,6},{8,9},{9,8},{10,11... | collective-permute-start | bytes 2359304 | tf_op jit(solution)/shard_map/ppermute | solution.py:24
  117.9 23.5 %collective-permute-start.18 = (bf16[192,1024]{1,0:T(8,128)(2,1)S(1)}, bf16[192,1024]{1,0:T(8,128)(2,1)S(1)}, u32[]{:S(2)}, u32[]{:S(2)}) collective-permute-start(bf16[192,1024]{1,0:T(8,128)(2,1)S(1)} %get-tuple-element.101), channel_id=1, source_target_pairs={{0,12},{4,0},{8,4},{12,8},{1,13},{5,1},{9,5},{13,9},{2,14},{6,2},{... | collective-permute-start | bytes 1179656 | tf_op jit(solution)/shard_map/ppermute | solution.py:20
  126.8 14.6 %collective-permute-start.20 = (bf16[192,1024]{1,0:T(8,128)(2,1)S(1)}, bf16[192,1024]{1,0:T(8,128)(2,1)S(1)}, u32[]{:S(2)}, u32[]{:S(2)}) collective-permute-start(bf16[192,1024]{1,0:T(8,128)(2,1)S(1)} %add_convert_fusion.2), channel_id=1, source_target_pairs={{0,4},{4,8},{8,12},{12,0},{1,5},{5,9},{9,13},{13,1},{2,6},{6,10},{... | collective-permute-start | bytes 1179656 | tf_op jit(solution)/shard_map/ppermute | solution.py:20
  131.7 16.6 %collective-permute-start.26 = (bf16[192,1024]{1,0:T(8,128)(2,1)S(1)}, bf16[192,1024]{1,0:T(8,128)(2,1)S(1)}, u32[]{:S(2)}, u32[]{:S(2)}) collective-permute-start(bf16[192,1024]{1,0:T(8,128)(2,1)S(1)} %slice.201), channel_id=1, source_target_pairs={{0,1},{1,0},{2,3},{3,2},{4,5},{5,4},{6,7},{7,6},{8,9},{9,8},{10,11... | collective-permute-start | bytes 1179656 | tf_op jit(solution)/shard_map/ppermute | solution.py:24
  138.1 6.6 %collective-permute-start.24 = (bf16[96,1024]{1,0:T(8,128)(2,1)S(1)}, bf16[96,1024]{1,0:T(8,128)(2,1)S(1)}, u32[]{:S(2)}, u32[]{:S(2)}) collective-permute-start(bf16[96,1024]{1,0:T(8,128)(2,1)S(1)} %get-tuple-element.110), channel_id=1, source_target_pairs={{0,12},{4,0},{8,4},{12,8},{1,13},{5,1},{9,5},{13,9},{2,14},{6,2},{... | collective-permute-start | bytes 589832 | tf_op jit(solution)/shard_map/ppermute | solution.py:20
  141.4 6.9 %collective-permute-start.25 = (bf16[96,1024]{1,0:T(8,128)(2,1)S(1)}, bf16[96,1024]{1,0:T(8,128)(2,1)S(1)}, u32[]{:S(2)}, u32[]{:S(2)}) collective-permute-start(bf16[96,1024]{1,0:T(8,128)(2,1)S(1)} %get-tuple-element.109), channel_id=1, source_target_pairs={{0,4},{4,8},{8,12},{12,0},{1,5},{5,9},{9,13},{13,1},{2,6},{6,10},{... | collective-permute-start | bytes 589832 | tf_op jit(solution)/shard_map/ppermute | solution.py:20
  141.6 13.0 %collective-permute-start.21 = (bf16[96,1024]{1,0:T(8,128)(2,1)S(1)}, bf16[96,1024]{1,0:T(8,128)(2,1)S(1)}, u32[]{:S(2)}, u32[]{:S(2)}) collective-permute-start(bf16[96,1024]{1,0:T(8,128)(2,1)S(1)} %slice.202), channel_id=1, source_target_pairs={{0,1},{1,0},{2,3},{3,2},{4,5},{5,4},{6,7},{7,6},{8,9},{9,8},{10,11... | collective-permute-start | bytes 589832 | tf_op jit(solution)/shard_map/ppermute | solution.py:24
  148.3 6.3 %collective-permute-start.27 = (bf16[96,1024]{1,0:T(8,128)(2,1)S(1)}, bf16[96,1024]{1,0:T(8,128)(2,1)S(1)}, u32[]{:S(2)}, u32[]{:S(2)}) collective-permute-start(bf16[96,1024]{1,0:T(8,128)(2,1)S(1)} %add_convert_fusion.6), channel_id=1, source_target_pairs={{0,12},{4,0},{8,4},{12,8},{1,13},{5,1},{9,5},{13,9},{2,14},{6,2},{... | collective-permute-start | bytes 589832 | tf_op jit(solution)/shard_map/ppermute | solution.py:20
  149.3 18.5 %copy-start.8 = (f32[8,2048]{1,0:T(8,128)S(1)}, f32[8,2048]{1,0:T(8,128)}, u32[]{:S(2)}) copy-start(f32[8,2048]{1,0:T(8,128)} %param.20) | copy-start | bytes 196612
  149.3 27.3 %copy-start.5 = (bf16[128,2048]{1,0:T(8,128)(2,1)S(1)}, bf16[128,2048]{1,0:T(8,128)(2,1)}, u32[]{:S(2)}) copy-start(bf16[128,2048]{1,0:T(8,128)(2,1)} %tokens_ref.1) | copy-start | bytes 1572868
  149.3 14.2 %all-to-all-start.1 = ((bf16[8,24,1024]{2,1,0:T(8,128)(2,1)}), bf16[8,24,1024]{2,1,0:T(8,128)(2,1)S(1)}, u32[]{:S(2)}, u32[]{:S(2)}) async-start(bf16[8,24,1024]{2,1,0:T(8,128)(2,1)} %bitcast.8), calls=%async_computation.1 | async-start | bytes 786432 | tf_op jit(solution)/shard_map/all_to_all | solution.py:169
  164.3 12.3 %all-to-all-start.2 = ((bf16[8,24,1024]{2,1,0:T(8,128)(2,1)}), bf16[8,24,1024]{2,1,0:T(8,128)(2,1)S(1)}, u32[]{:S(2)}, u32[]{:S(2)}) async-start(bf16[8,24,1024]{2,1,0:T(8,128)(2,1)} %bitcast.10), calls=%async_computation.2 | async-start | bytes 786432 | tf_op jit(solution)/shard_map/all_to_all | solution.py:169
  176.7 1.9 copy-start.9
  176.7 19.5 %copy-start.12 = (bf16[2048,1024]{1,0:T(8,128)(2,1)S(1)}, bf16[2048,1024]{1,0:T(8,128)(2,1)}, u32[]{:S(2)}) copy-start(bf16[2048,1024]{1,0:T(8,128)(2,1)} %param.22) | copy-start | bytes 12582916
  178.3 17.8 %copy-start.16 = (f32[1024]{0:T(1024)S(1)}, f32[1024]{0:T(1024)}, u32[]{:S(2)}) copy-start(f32[1024]{0:T(1024)} %param.23) | copy-start | bytes 12292
  178.9 9.1 %collective-permute-start.28 = (bf16[64,2048]{1,0:T(8,128)(2,1)S(1)}, bf16[64,2048]{1,0:T(8,128)(2,1)S(1)}, u32[]{:S(2)}, u32[]{:S(2)}) collective-permute-start(bf16[64,2048]{1,0:T(8,128)(2,1)S(1)} %get-tuple-element.113), channel_id=1, source_target_pairs={{0,32},{32,64},{64,96},{96,0},{1,33},{33,65},{65,97},{97,1},{2,34}... | collective-permute-start | bytes 786440 | tf_op jit(solution)/shard_map/ppermute | solution.py:20
  179.5 8.5 %collective-permute-start.29 = (bf16[64,2048]{1,0:T(8,128)(2,1)S(1)}, bf16[64,2048]{1,0:T(8,128)(2,1)S(1)}, u32[]{:S(2)}, u32[]{:S(2)}) collective-permute-start(bf16[64,2048]{1,0:T(8,128)(2,1)S(1)} %get-tuple-element.113), channel_id=1, source_target_pairs={{0,96},{32,0},{64,32},{96,64},{1,97},{33,1},{65,33},{97,65},{2,98}... | collective-permute-start | bytes 786440 | tf_op jit(solution)/shard_map/ppermute | solution.py:20
  188.0 8.2 %collective-permute-start.30 = (bf16[64,2048]{1,0:T(8,128)(2,1)S(1)}, bf16[64,2048]{1,0:T(8,128)(2,1)S(1)}, u32[]{:S(2)}, u32[]{:S(2)}) collective-permute-start(bf16[64,2048]{1,0:T(8,128)(2,1)S(1)} %collective-permute-done.28), channel_id=1, source_target_pairs={{0,32},{32,64},{64,96},{96,0},{1,33},{33,65},{65,97},{97,1},{2,34}... | collective-permute-start | bytes 786440 | tf_op jit(solution)/shard_map/ppermute | solution.py:20
  188.0 9.4 %copy-start.3 = (bf16[2048,1024]{1,0:T(8,128)(2,1)S(1)}, bf16[2048,1024]{1,0:T(8,128)(2,1)}, u32[]{:S(2)}) copy-start(bf16[2048,1024]{1,0:T(8,128)(2,1)} %copy-done.2) | copy-start | bytes 12582916
  188.0 9.4 %copy-start.18 = (f32[1024]{0:T(1024)S(1)}, f32[1024]{0:T(1024)}, u32[]{:S(2)}) copy-start(f32[1024]{0:T(1024)} %copy-done.17) | copy-start | bytes 12292
  188.0 10.7 %collective-permute-start.31 = (bf16[64,2048]{1,0:T(8,128)(2,1)S(1)}, bf16[64,2048]{1,0:T(8,128)(2,1)S(1)}, u32[]{:S(2)}, u32[]{:S(2)}) collective-permute-start(bf16[64,2048]{1,0:T(8,128)(2,1)S(1)} %get-tuple-element.80), channel_id=1, source_target_pairs={{0,96},{32,0},{64,32},{96,64},{1,97},{33,1},{65,33},{97,65},{2,98}... | collective-permute-start | bytes 786440 | tf_op jit(solution)/shard_map/ppermute | solution.py:20
  197.4 2.2 copy-start.1
  198.7 2.4 %copy-start.13 = (bf16[1024,2048]{1,0:T(8,128)(2,1)S(1)}, bf16[1024,2048]{1,0:T(8,128)(2,1)}, u32[]{:S(2)}) copy-start(bf16[1024,2048]{1,0:T(8,128)(2,1)} %param.24) | copy-start | bytes 12582916
  198.8 8.1 %collective-permute-start.32 = (bf16[64,2048]{1,0:T(8,128)(2,1)S(1)}, bf16[64,2048]{1,0:T(8,128)(2,1)S(1)}, u32[]{:S(2)}, u32[]{:S(2)}) collective-permute-start(bf16[64,2048]{1,0:T(8,128)(2,1)S(1)} %get-tuple-element.80), channel_id=1, source_target_pairs={{0,32},{32,64},{64,96},{96,0},{1,33},{33,65},{65,97},{97,1},{2,34}... | collective-permute-start | bytes 786440 | tf_op jit(solution)/shard_map/ppermute | solution.py:20
  202.5 8.9 %collective-permute-start.33 = (bf16[64,2048]{1,0:T(8,128)(2,1)S(1)}, bf16[64,2048]{1,0:T(8,128)(2,1)S(1)}, u32[]{:S(2)}, u32[]{:S(2)}) collective-permute-start(bf16[64,2048]{1,0:T(8,128)(2,1)S(1)} %collective-permute-done.31), channel_id=1, source_target_pairs={{0,96},{32,0},{64,32},{96,64},{1,97},{33,1},{65,33},{97,65},{2,98}... | collective-permute-start | bytes 786440 | tf_op jit(solution)/shard_map/ppermute | solution.py:20
  204.8 9.4 %collective-permute-start.34 = (bf16[64,2048]{1,0:T(8,128)(2,1)S(1)}, bf16[64,2048]{1,0:T(8,128)(2,1)S(1)}, u32[]{:S(2)}, u32[]{:S(2)}) collective-permute-start(bf16[64,2048]{1,0:T(8,128)(2,1)S(1)} %get-tuple-element.108), channel_id=1, source_target_pairs={{0,96},{32,0},{64,32},{96,64},{1,97},{33,1},{65,33},{97,65},{2,98}... | collective-permute-start | bytes 786440 | tf_op jit(solution)/shard_map/ppermute | solution.py:20
  204.9 9.4 %collective-permute-start.35 = (bf16[64,2048]{1,0:T(8,128)(2,1)S(1)}, bf16[64,2048]{1,0:T(8,128)(2,1)S(1)}, u32[]{:S(2)}, u32[]{:S(2)}) collective-permute-start(bf16[64,2048]{1,0:T(8,128)(2,1)S(1)} %get-tuple-element.107), channel_id=1, source_target_pairs={{0,32},{32,64},{64,96},{96,0},{1,33},{33,65},{65,97},{97,1},{2,34}... | collective-permute-start | bytes 786440 | tf_op jit(solution)/shard_map/ppermute | solution.py:20
  216.8 16.0 %copy-start.10 = (f32[2048]{0:T(1024)S(1)}, f32[2048]{0:T(1024)}, u32[]{:S(2)}) copy-start(f32[2048]{0:T(1024)} %param.25) | copy-start | bytes 24580
  216.9 7.9 %collective-permute-start.38 = (bf16[64,2048]{1,0:T(8,128)(2,1)S(1)}, bf16[64,2048]{1,0:T(8,128)(2,1)S(1)}, u32[]{:S(2)}, u32[]{:S(2)}) collective-permute-start(bf16[64,2048]{1,0:T(8,128)(2,1)S(1)} %get-tuple-element.106), channel_id=1, source_target_pairs={{0,32},{32,64},{64,96},{96,0},{1,33},{33,65},{65,97},{97,1},{2,34}... | collective-permute-start | bytes 786440 | tf_op jit(solution)/shard_map/ppermute | solution.py:20
  217.0 8.4 %collective-permute-start.36 = (bf16[64,2048]{1,0:T(8,128)(2,1)S(1)}, bf16[64,2048]{1,0:T(8,128)(2,1)S(1)}, u32[]{:S(2)}, u32[]{:S(2)}) collective-permute-start(bf16[64,2048]{1,0:T(8,128)(2,1)S(1)} %add_convert_fusion.4), channel_id=1, source_target_pairs={{0,96},{32,0},{64,32},{96,64},{1,97},{33,1},{65,33},{97,65},{2,98}... | collective-permute-start | bytes 786440 | tf_op jit(solution)/shard_map/ppermute | solution.py:20
  220.2 8.0 %collective-permute-start.37 = (bf16[64,2048]{1,0:T(8,128)(2,1)S(1)}, bf16[64,2048]{1,0:T(8,128)(2,1)S(1)}, u32[]{:S(2)}, u32[]{:S(2)}) collective-permute-start(bf16[64,2048]{1,0:T(8,128)(2,1)S(1)} %get-tuple-element.105), channel_id=1, source_target_pairs={{0,96},{32,0},{64,32},{96,64},{1,97},{33,1},{65,33},{97,65},{2,98}... | collective-permute-start | bytes 786440 | tf_op jit(solution)/shard_map/ppermute | solution.py:20
  224.9 7.9 %collective-permute-start.39 = (bf16[64,2048]{1,0:T(8,128)(2,1)S(1)}, bf16[64,2048]{1,0:T(8,128)(2,1)S(1)}, u32[]{:S(2)}, u32[]{:S(2)}) collective-permute-start(bf16[64,2048]{1,0:T(8,128)(2,1)S(1)} %add_convert_fusion.3), channel_id=1, source_target_pairs={{0,32},{32,64},{64,96},{96,0},{1,33},{33,65},{65,97},{97,1},{2,34}... | collective-permute-start | bytes 786440 | tf_op jit(solution)/shard_map/ppermute | solution.py:20

commit v8 on v5

--- a/solution.py
+++ b/solution.py
@@ -81,14 +81,19 @@
             tokens_ref[...],
             preferred_element_type=jnp.float32,
         )
-        for start in range(0, num_slots, 16):
-            rows = rows_ref[start : start + 16]
-            gains = [
-                jnp.broadcast_to(gain_ref[at // capacity : at // capacity + 1], (8, width))
-                for at in (start, start + 8)
-            ]
-            normed = layer_norm(rows, jnp.concatenate(gains, axis=0))
-            out_ref[start : start + 16] = normed.astype(jnp.bfloat16)
+
+        def two_groups(pair, carry):
+            for start in range(0, 2 * capacity, 16):
+                at = pl.ds(pl.multiple_of(pair * 2 * capacity + start, 16), 16)
+                gains = [
+                    jnp.broadcast_to(gain_ref[pl.ds(2 * pair + row // capacity, 1)], (8, width))
+                    for row in (start, start + 8)
+                ]
+                normed = layer_norm(rows_ref[at], jnp.concatenate(gains, axis=0))
+                out_ref[at] = normed.astype(jnp.bfloat16)
+            return carry
+
+        lax.fori_loop(0, num_groups // 2, two_groups, 0)
 
     outgoing, position = pl.pallas_call(
         body,
@@ -195,49 +200,46 @@
     right_pair = swap_blocks(right_out)
     w1 = jnp.concatenate([group_w1[0], w1_pair], axis=1)
     b1 = jnp.concatenate([group_b1[0], b1_pair])
-    early = jnp.concatenate([a_near, a_far, b_own, b_foll, b_prev, near_pair], axis=0)
-    late = jnp.concatenate([far_pair, b_far], axis=0)
-
-    def first(rows):
-        return down(jax.nn.relu(jnp.dot(rows, w1, preferred_element_type=jnp.float32) + b1))
-
-    hidden = jnp.concatenate([first(early), first(late)], axis=0)
+    rows = jnp.concatenate(
+        [a_near, a_far, b_own, b_foll, b_prev, near_pair, far_pair, b_far], axis=0
+    )
+    hidden = down(jax.nn.relu(jnp.dot(rows, w1, preferred_element_type=jnp.float32) + b1))
 
     def second(hidden, weight, weight_pair):
         weight = jnp.concatenate([weight, weight_pair], axis=0)
         return down(jnp.dot(hidden, weight, preferred_element_type=jnp.float32))
 
-    def block(part, step):
-        at = {"own": (0, 4, 10, 5), "prev": (1, 8, 11, 9), "foll": (2, 6, 12, 7), "far": (3, 14, 13, 15)}
-        return jnp.concatenate([part[i * count : (i + 1) * count] for i in at[step]], axis=0)
-
-    def ring(weight, weight_pair, hidden, way, after):
+    wide = 4 * count
+
+    def open_half(weight, weight_pair, hidden):
         part = second(hidden, weight, weight_pair)
-        own, prev, foll = (block(part, step) for step in ("own", "prev", "foll"))
-        via = shift(block(part, "far"), "z", -way)
-        if way == 1:
-            foll = shift(foll, "z", 1)
-            via, foll, after = hold(via, foll, after)
-            prev = down(up(prev) + up(via))
-            hidden, prev = hold(hidden, prev)
-            prev = shift(prev, "z", -1)
-        else:
-            prev = shift(prev, "z", -1)
-            via, after = hold(via, after)
-            foll = shift(down(up(foll) + up(via)), "z", 1)
-        return up(own) + up(prev) + up(foll), hidden, after
-
-    def finish(summed, back):
-        return exchange(down(summed[: 2 * count] + up(back)))
-
-    sum_l, hidden, right_pair = ring(left, left_pair, hidden, 1, right_pair)
-    out_l = down(sum_l[2 * count :])
-    back_l = swap_column(out_l)
-    sum_r, _, back_l = ring(right, right_pair, hidden, -1, back_l)
-    return_l = finish(sum_l, back_l)
-    sum_r, return_l = hold(sum_r, return_l)
-    back_r = swap_column(down(sum_r[2 * count :]))
-    return_r = finish(sum_r, back_r)
+        back = swap_column(part[10 * count : 14 * count])
+        via = shift(part[14 * count :], "z", 1)
+        prev = shift(part[8 * count : 10 * count], "z", -1)
+        foll = shift(down(up(part[6 * count : 8 * count]) + up(via)), "z", 1)
+        sum_b = up(part[4 * count : 6 * count]) + up(prev) + up(foll)
+        return part, back, sum_b[:count] + up(swap_column(down(sum_b[count:])))
+
+    def close_half(rows, after):
+        own, prev, foll, far = jnp.split(rows, 4)
+        via = shift(far, "z", -1)
+        foll = shift(foll, "z", 1)
+        via, foll, after = hold(via, foll, after)
+        prev = shift(down(up(prev) + up(via)), "z", -1)
+        return up(own) + up(prev) + up(foll), after
+
+    def finish(sum_a, sum_b):
+        return exchange(down(jnp.concatenate([sum_a, sum_b], axis=0)))
+
+    part, back, sum_b = open_half(left, left_pair, hidden)
+    back, right_pair = hold(back, right_pair)
+    rows = down(up(part[:wide]) + up(back))
+    hidden, rows = hold(hidden, rows)
+    sum_a, _ = close_half(rows, b1)
+    return_l = finish(sum_a, sum_b)
+    part, back, sum_b = open_half(right, right_pair, hidden)
+    sum_a, return_l = close_half(down(up(part[:wide]) + up(back)), return_l)
+    return_r = finish(sum_a, sum_b)
     returned = jnp.concatenate([return_l, return_r], axis=1)
     group_out = lax.dot_general(
         dispatch_map, returned, (((0,), (0,)), ((), ())), preferred_element_type=jnp.float32

time: 235 us -> 239 us (1.017)
  starting transfers between devices: 67.7 us -> 78.7 us
  waiting for transfers between devices: 115 us -> 104 us
  other arithmetic: 7.46 us -> 11.4 us
  matrix products: 29.3 us -> 25.5 us
  local copies, waits for them, and re-layouts: 8.59 us -> 11.3 us
    ppermute x4, waiting for transfers between devices: 22 us -> 12 us  [swap_blocks(): return lax.ppermute(value, X, [(0, 3), (3, 0), (1, 2), (2, 1)])]
    ppermute x24 -> x30, starting transfers between devices: 38.7 us -> 45.8 us  [shift(): lax.ppermute(value, axis, [(i, (i + step) % size) for i in range(size)])]
    ppermute x5 -> x7, waiting for transfers between devices: 13.6 us -> 8.24 us  [swap_column(): return lax.ppermute(value, 'xl', [(0, 1), (1, 0)])]
    ppermute x24 -> x30, waiting for transfers between devices: 65.1 us -> 69.9 us  [shift(): lax.ppermute(value, axis, [(i, (i + step) % size) for i in range(size)])]
    ppermute x5 -> x7, starting transfers between devices: 3.58 us -> 6.71 us  [swap_column(): return lax.ppermute(value, 'xl', [(0, 1), (1, 0)])]
    dot_general x2 -> x1, matrix products: 9 us -> 7.12 us  [on_device(): jnp.dot(rows, w1, preferred_element_type=jnp.float32) + b1]
    unnamed x37 -> x55, local copies, waits for them, and re-layouts: 7.29 us -> 7.65 us
  transfers between devices with their start and end apart: 39 -> 47, of which waited for: 28 -> 27; matrix products, arithmetic and copies ran while one was open for 13% -> 14% of each run, Pallas kernels for 3% -> 3%
where the time goes in v8:
time: 239 us; the launch traced here: 238 us
  waiting for transfers between devices  104 us (44%)
  starting transfers between devices  78.7 us (33%)
  matrix products  25.5 us (11%)
  other arithmetic  11.4 us (5%)
  local copies, waits for them, and re-layouts  11.3 us (5%)
  Pallas kernels  6.73 us (3%)
    ppermute x30, waiting for transfers between devices, shift(): lax.ppermute(value, axis, [(i, (i + step) % size) for i in range(size)])  69.9 us
    ppermute x30, starting transfers between devices, shift(): lax.ppermute(value, axis, [(i, (i + step) % size) for i in range(size)])  45.8 us
    all_to_all x3, starting transfers between devices, exchange(): lax.all_to_all(value, ('y', 'core'), split_axis=0, concat_axis=0, tiled=T...  14.2 us
    all_to_all x3, waiting for transfers between devices, exchange(): lax.all_to_all(value, ('y', 'core'), split_axis=0, concat_axis=0, tiled=T...  13.8 us
    ppermute x4, waiting for transfers between devices, swap_blocks(): return lax.ppermute(value, X, [(0, 3), (3, 0), (1, 2), (2, 1)])  12 us
    ppermute x4, starting transfers between devices, swap_blocks(): return lax.ppermute(value, X, [(0, 3), (3, 0), (1, 2), (2, 1)])  11 us
    ppermute x7, waiting for transfers between devices, swap_column(): return lax.ppermute(value, 'xl', [(0, 1), (1, 0)])  8.24 us
    unnamed x55, local copies, waits for them, and re-layouts  7.65 us
  transfers between devices with their start and end apart: 47, of which 27 were waited for; matrix products, arithmetic and copies ran while one was open for 14% of the time, Pallas kernels for 3%

profile of v8, /device:TPU:0, one launch (start us, length us, event | category | flops | bytes accessed | tf_op | source)
XLA Modules:
  0.0 238.1 jit_solution(1550379274826614154)
XLA Ops:
  3.2 2.4 dispatch.1
  5.5 4.6 %all-to-all-start = ((bf16[8,24,2048]{2,1,0:T(8,128)(2,1)}), bf16[8,24,2048]{2,1,0:T(8,128)(2,1)S(1)}, u32[]{:S(2)}, u32[]{:S(2)}) async-start(bf16[8,24,2048]{2,1,0:T(8,128)(2,1)} %bitcast.2), calls=%async_computation | async-start | bytes 1572864 | tf_op jit(solution)/shard_map/all_to_all | solution.py:174
  10.6 2.8 %collective-permute-start.9 = (f32[512]{0:T(512)}, f32[512]{0:T(512)S(1)}, u32[]{:S(2)}, u32[]{:S(2)}) collective-permute-start(f32[512]{0:T(512)} %bitcast.50), channel_id=1, source_target_pairs={{0,3},{3,0},{1,2},{2,1},{4,7},{7,4},{5,6},{6,5},{8,11},{11,8},{9,1... | collective-permute-start | bytes 6152 | tf_op jit(solution)/shard_map/ppermute | solution.py:28
  13.3 2.3 collective-permute-done.9
  15.6 2.8 %collective-permute-start.10 = (bf16[2048,512]{1,0:T(8,128)(2,1)}, bf16[2048,512]{1,0:T(8,128)(2,1)}, u32[]{:S(2)}, u32[]{:S(2)}) collective-permute-start(bf16[2048,512]{1,0:T(8,128)(2,1)} %bitcast.52), channel_id=1, source_target_pairs={{0,3},{3,0},{1,2},{2,1},{4,7},{7,4},{5,6},{6,5},{8,11},{11,8},{9,1... | collective-permute-start | bytes 6291464 | tf_op jit(solution)/shard_map/ppermute | solution.py:28
  18.4 4.9 %all-to-all-done = bf16[8,24,2048]{2,1,0:T(8,128)(2,1)S(1)} async-done(((bf16[8,24,2048]{2,1,0:T(8,128)(2,1)}), bf16[8,24,2048]{2,1,0:T(8,128)(2,1)S(1)}, u32[]{:S(2)}, u32[]{:S(2)}) %all-to-all-start) | async-done | bytes 786464 | tf_op jit(solution)/shard_map/all_to_all | solution.py:174
  23.3 2.0 collective-permute-start.3
  25.3 2.2 collective-permute-start.4
  27.5 1.5 collective-permute-start.5
  29.2 7.2 %collective-permute-done.3 = bf16[96,2048]{1,0:T(8,128)(2,1)S(1)} collective-permute-done((bf16[96,2048]{1,0:T(8,128)(2,1)S(1)}, bf16[96,2048]{1,0:T(8,128)(2,1)S(1)}, u32[]{:S(2)}, u32[]{:S(2)}) %collective-permute-start.3) | collective-permute-done | bytes 393248 | tf_op jit(solution)/shard_map/ppermute | solution.py:20
  36.5 1.4 collective-permute-done.5
  37.9 1.5 collective-permute-start.11
  39.4 2.0 collective-permute-start.7
  41.4 6.3 %collective-permute-done.6 = bf16[96,2048]{1,0:T(8,128)(2,1)S(1)} collective-permute-done((bf16[96,2048]{1,0:T(8,128)(2,1)S(1)}, bf16[96,2048]{1,0:T(8,128)(2,1)S(1)}, u32[]{:S(2)}, u32[]{:S(2)}) %collective-permute-start.6) | collective-permute-done | bytes 393248 | tf_op jit(solution)/shard_map/ppermute | solution.py:20
  47.8 2.2 on_chip.2
  50.0 2.0 copy-done.2
  52.0 2.2 on_chip.3
  54.2 2.0 copy-done
  56.2 2.8 %collective-permute-start.14 = (bf16[512,1024]{1,0:T(8,128)(2,1)S(1)}, bf16[512,1024]{1,0:T(8,128)(2,1)S(1)}, u32[]{:S(2)}, u32[]{:S(2)}) collective-permute-start(bf16[512,1024]{1,0:T(8,128)(2,1)S(1)} %get-tuple-element.61), channel_id=1, source_target_pairs={{0,3},{3,0},{1,2},{2,1},{4,7},{7,4},{5,6},{6,5},{8,11},{11,8},{9,1... | collective-permute-start | bytes 3145736 | tf_op jit(solution)/shard_map/ppermute | solution.py:28
  59.1 3.3 %collective-permute-start.13 = (bf16[192,2048]{1,0:T(8,128)(2,1)S(1)}, bf16[192,2048]{1,0:T(8,128)(2,1)S(1)}, u32[]{:S(2)}, u32[]{:S(2)}) collective-permute-start(bf16[192,2048]{1,0:T(8,128)(2,1)S(1)} %collective-permute-done.7), channel_id=1, source_target_pairs={{0,12},{4,0},{8,4},{12,8},{1,13},{5,1},{9,5},{13,9},{2,14},{6,2},{... | collective-permute-start | bytes 2359304 | tf_op jit(solution)/shard_map/ppermute | solution.py:20
  62.5 1.8 collective-permute-done.11
  64.3 1.4 collective-permute-done.10
  66.7 2.8 %collective-permute-start.16 = (bf16[512,1024]{1,0:T(8,128)(2,1)S(1)}, bf16[512,1024]{1,0:T(8,128)(2,1)S(1)}, u32[]{:S(2)}, u32[]{:S(2)}) collective-permute-start(bf16[512,1024]{1,0:T(8,128)(2,1)S(1)} %get-tuple-element.62), channel_id=1, source_target_pairs={{0,3},{3,0},{1,2},{2,1},{4,7},{7,4},{5,6},{6,5},{8,11},{11,8},{9,1... | collective-permute-start | bytes 3145736 | tf_op jit(solution)/shard_map/ppermute | solution.py:28
  69.6 3.8 %collective-permute-done.12 = bf16[96,2048]{1,0:T(8,128)(2,1)S(1)} collective-permute-done((bf16[96,2048]{1,0:T(8,128)(2,1)S(1)}, bf16[96,2048]{1,0:T(8,128)(2,1)S(1)}, u32[]{:S(2)}, u32[]{:S(2)}) %collective-permute-start.12) | collective-permute-done | bytes 393248 | tf_op jit(solution)/shard_map/ppermute | solution.py:24
  73.5 3.6 %collective-permute-done.13 = bf16[192,2048]{1,0:T(8,128)(2,1)S(1)} collective-permute-done((bf16[192,2048]{1,0:T(8,128)(2,1)S(1)}, bf16[192,2048]{1,0:T(8,128)(2,1)S(1)}, u32[]{:S(2)}, u32[]{:S(2)}) %collective-permute-start.13) | collective-permute-done | bytes 786464 | tf_op jit(solution)/shard_map/ppermute | solution.py:20
  77.2 7.1 %maximum_convert_fusion = bf16[1536,1024]{1,0:T(8,128)(2,1)S(1)} fusion(bf16[1536,2048]{1,0:T(8,128)(2,1)S(1)} %constant_dynamic-update-slice_fusion, bf16[2048,512]{1,0:T(8,128)(2,1)} %collective-permute-done.10, bf16[2048,512]{1,0:T(8,128)(2,1)S(1)} %bitcast.53, f32[1024]{0:T(1024)S(1)} %pad_maximum_fusion.10), kind=kOutput, calls=%fused_computation | convolution fusion | flops 6455558144 | bytes 13635584 | tf_op jit(solution)/shard_map/dot_general | solution.py:206
  84.3 3.7 %collective-permute-done.14 = bf16[512,1024]{1,0:T(8,128)(2,1)S(1)} collective-permute-done((bf16[512,1024]{1,0:T(8,128)(2,1)S(1)}, bf16[512,1024]{1,0:T(8,128)(2,1)S(1)}, u32[]{:S(2)}, u32[]{:S(2)}) %collective-permute-start.14) | collective-permute-done | bytes 1048608 | tf_op jit(solution)/shard_map/ppermute | solution.py:28
  88.1 3.6 %convolution_convert_fusion.1 = bf16[1536,1024]{1,0:T(8,128)(2,1)S(1)} fusion(bf16[1536,1024]{1,0:T(8,128)(2,1)S(1)} %maximum_convert_fusion, bf16[512,1024]{1,0:T(8,128)(2,1)S(1)} %collective-permute-done.14, bf16[512,1024]{1,0:T(8,128)(2,1)S(1)} %get-tuple-element.61), kind=kOutput, calls=%fused_computation.5 | convolution fusion | flops 3226992640 | bytes 8388608 | tf_op jit(solution)/shard_map/dot_general | solution.py:210
  92.1 2.0 collective-permute-start.24
  94.7 2.1 collective-permute-start.23
  96.8 5.9 %collective-permute-done.24 = bf16[192,1024]{1,0:T(8,128)(2,1)S(1)} collective-permute-done((bf16[192,1024]{1,0:T(8,128)(2,1)S(1)}, bf16[192,1024]{1,0:T(8,128)(2,1)S(1)}, u32[]{:S(2)}, u32[]{:S(2)}) %collective-permute-start.24) | collective-permute-done | bytes 393248 | tf_op jit(solution)/shard_map/ppermute | solution.py:20
  103.7 4.6 %collective-permute-done.16 = bf16[512,1024]{1,0:T(8,128)(2,1)S(1)} collective-permute-done((bf16[512,1024]{1,0:T(8,128)(2,1)S(1)}, bf16[512,1024]{1,0:T(8,128)(2,1)S(1)}, u32[]{:S(2)}, u32[]{:S(2)}) %collective-permute-start.16) | collective-permute-done | bytes 1048608 | tf_op jit(solution)/shard_map/ppermute | solution.py:28
  108.7 4.1 %collective-permute-start.20 = (bf16[96,1024]{1,0:T(8,128)(2,1)S(1)}, bf16[96,1024]{1,0:T(8,128)(2,1)S(1)}, u32[]{:S(2)}, u32[]{:S(2)}) collective-permute-start(bf16[96,1024]{1,0:T(8,128)(2,1)S(1)} %get-tuple-element.94), channel_id=1, source_target_pairs={{0,12},{4,0},{8,4},{12,8},{1,13},{5,1},{9,5},{13,9},{2,14},{6,2},{... | collective-permute-start | bytes 589832 | tf_op jit(solution)/shard_map/ppermute | solution.py:20
  113.0 2.8 %collective-permute-start.26 = (bf16[96,1024]{1,0:T(8,128)(2,1)S(1)}, bf16[96,1024]{1,0:T(8,128)(2,1)S(1)}, u32[]{:S(2)}, u32[]{:S(2)}) collective-permute-start(bf16[96,1024]{1,0:T(8,128)(2,1)S(1)} %slice.157), channel_id=1, source_target_pairs={{0,1},{1,0},{2,3},{3,2},{4,5},{5,4},{6,7},{7,6},{8,9},{9,8},{10,11... | collective-permute-start | bytes 589832 | tf_op jit(solution)/shard_map/ppermute | solution.py:24
  115.9 3.6 %convolution_convert_fusion = bf16[1536,1024]{1,0:T(8,128)(2,1)S(1)} fusion(bf16[1536,1024]{1,0:T(8,128)(2,1)S(1)} %maximum_convert_fusion, bf16[512,1024]{1,0:T(8,128)(2,1)S(1)} %collective-permute-done.16, bf16[512,1024]{1,0:T(8,128)(2,1)S(1)} %get-tuple-element.62), kind=kOutput, calls=%fused_computation.4 | convolution fusion | flops 3226992640 | bytes 8388608 | tf_op jit(solution)/shard_map/dot_general | solution.py:210
  122.0 2.9 %collective-permute-start.28 = (bf16[192,1024]{1,0:T(8,128)(2,1)}, bf16[192,1024]{1,0:T(8,128)(2,1)}, u32[]{:S(2)}, u32[]{:S(2)}) collective-permute-start(bf16[192,1024]{1,0:T(8,128)(2,1)} %get-tuple-element.85), channel_id=1, source_target_pairs={{0,12},{4,0},{8,4},{12,8},{1,13},{5,1},{9,5},{13,9},{2,14},{6,2},{... | collective-permute-start | bytes 1179656 | tf_op jit(solution)/shard_map/ppermute | solution.py:20
  125.0 1.9 collective-permute-start.22
  126.9 6.9 %collective-permute-done.22 = bf16[96,1024]{1,0:T(8,128)(2,1)S(1)} collective-permute-done((bf16[96,1024]{1,0:T(8,128)(2,1)S(1)}, bf16[96,1024]{1,0:T(8,128)(2,1)S(1)}, u32[]{:S(2)}, u32[]{:S(2)}) %collective-permute-start.22) | collective-permute-done | bytes 196640 | tf_op jit(solution)/shard_map/ppermute | solution.py:20
  134.7 5.4 %all-to-all-start.1 = ((bf16[8,24,1024]{2,1,0:T(8,128)(2,1)}), bf16[8,24,1024]{2,1,0:T(8,128)(2,1)S(1)}, u32[]{:S(2)}, u32[]{:S(2)}) async-start(bf16[8,24,1024]{2,1,0:T(8,128)(2,1)} %bitcast.8), calls=%async_computation.1 | async-start | bytes 786432 | tf_op jit(solution)/shard_map/all_to_all | solution.py:174
  141.3 1.9 collective-permute-start.30
  143.2 1.4 add_convert_fusion
  145.7 1.9 collective-permute-start.18
  147.8 7.2 %collective-permute-done.30 = bf16[192,1024]{1,0:T(8,128)(2,1)S(1)} collective-permute-done((bf16[192,1024]{1,0:T(8,128)(2,1)S(1)}, bf16[192,1024]{1,0:T(8,128)(2,1)S(1)}, u32[]{:S(2)}, u32[]{:S(2)}) %collective-permute-start.30) | collective-permute-done | bytes 393248 | tf_op jit(solution)/shard_map/ppermute | solution.py:20
  155.0 1.3 convert_add_fusion
  156.9 2.2 collective-permute-done.19
  160.0 1.8 collective-permute-start.27
  163.0 3.8 %collective-permute-done.27 = bf16[96,1024]{1,0:T(8,128)(2,1)S(1)} collective-permute-done((bf16[96,1024]{1,0:T(8,128)(2,1)S(1)}, bf16[96,1024]{1,0:T(8,128)(2,1)S(1)}, u32[]{:S(2)}, u32[]{:S(2)}) %collective-permute-start.27) | collective-permute-done | bytes 196640 | tf_op jit(solution)/shard_map/ppermute | solution.py:20
  168.6 4.2 %all-to-all-start.2 = ((bf16[8,24,1024]{2,1,0:T(8,128)(2,1)}), bf16[8,24,1024]{2,1,0:T(8,128)(2,1)S(1)}, u32[]{:S(2)}, u32[]{:S(2)}) async-start(bf16[8,24,1024]{2,1,0:T(8,128)(2,1)} %bitcast.10), calls=%async_computation.2 | async-start | bytes 786432 | tf_op jit(solution)/shard_map/all_to_all | solution.py:174
  172.8 8.9 %all-to-all-done.2 = bf16[8,24,1024]{2,1,0:T(8,128)(2,1)S(1)} async-done(((bf16[8,24,1024]{2,1,0:T(8,128)(2,1)}), bf16[8,24,1024]{2,1,0:T(8,128)(2,1)S(1)}, u32[]{:S(2)}, u32[]{:S(2)}) %all-to-all-start.2) | async-done | bytes 393248 | tf_op jit(solution)/shard_map/all_to_all | solution.py:174
  183.7 2.7 %collective-permute-start.33 = (bf16[64,2048]{1,0:T(8,128)(2,1)S(1)}, bf16[64,2048]{1,0:T(8,128)(2,1)S(1)}, u32[]{:S(2)}, u32[]{:S(2)}) collective-permute-start(bf16[64,2048]{1,0:T(8,128)(2,1)S(1)} %get-tuple-element.99), channel_id=1, source_target_pairs={{0,96},{32,0},{64,32},{96,64},{1,97},{33,1},{65,33},{97,65},{2,98}... | collective-permute-start | bytes 786440 | tf_op jit(solution)/shard_map/ppermute | solution.py:20
  186.4 5.8 %collective-permute-done.32 = bf16[64,2048]{1,0:T(8,128)(2,1)S(1)} collective-permute-done((bf16[64,2048]{1,0:T(8,128)(2,1)S(1)}, bf16[64,2048]{1,0:T(8,128)(2,1)S(1)}, u32[]{:S(2)}, u32[]{:S(2)}) %collective-permute-start.32) | collective-permute-done | bytes 262176 | tf_op jit(solution)/shard_map/ppermute | solution.py:20
  192.3 3.2 %collective-permute-start.35 = (bf16[64,2048]{1,0:T(8,128)(2,1)S(1)}, bf16[64,2048]{1,0:T(8,128)(2,1)S(1)}, u32[]{:S(2)}, u32[]{:S(2)}) collective-permute-start(bf16[64,2048]{1,0:T(8,128)(2,1)S(1)} %get-tuple-element.78), channel_id=1, source_target_pairs={{0,96},{32,0},{64,32},{96,64},{1,97},{33,1},{65,33},{97,65},{2,98}... | collective-permute-start | bytes 786440 | tf_op jit(solution)/shard_map/ppermute | solution.py:20
  195.5 4.9 %collective-permute-done.34 = bf16[64,2048]{1,0:T(8,128)(2,1)S(1)} collective-permute-done((bf16[64,2048]{1,0:T(8,128)(2,1)S(1)}, bf16[64,2048]{1,0:T(8,128)(2,1)S(1)}, u32[]{:S(2)}, u32[]{:S(2)}) %collective-permute-start.34) | collective-permute-done | bytes 262176 | tf_op jit(solution)/shard_map/ppermute | solution.py:20
  205.4 1.3 fusion.3
  206.7 2.3 collective-permute-start.37
  209.1 2.0 collective-permute-start.39
  211.1 4.5 %collective-permute-done.37 = bf16[64,2048]{1,0:T(8,128)(2,1)S(1)} collective-permute-done((bf16[64,2048]{1,0:T(8,128)(2,1)S(1)}, bf16[64,2048]{1,0:T(8,128)(2,1)S(1)}, u32[]{:S(2)}, u32[]{:S(2)}) %collective-permute-start.37) | collective-permute-done | bytes 262176 | tf_op jit(solution)/shard_map/ppermute | solution.py:20
  216.9 1.3 fusion.18
  219.8 1.3 fusion.4
  221.2 3.2 %collective-permute-start.40 = (bf16[64,2048]{1,0:T(8,128)(2,1)S(1)}, bf16[64,2048]{1,0:T(8,128)(2,1)S(1)}, u32[]{:S(2)}, u32[]{:S(2)}) collective-permute-start(bf16[64,2048]{1,0:T(8,128)(2,1)S(1)} %add_convert_fusion.5), channel_id=1, source_target_pairs={{0,96},{32,0},{64,32},{96,64},{1,97},{33,1},{65,33},{97,65},{2,98}... | collective-permute-start | bytes 786440 | tf_op jit(solution)/shard_map/ppermute | solution.py:20
  224.5 1.9 collective-permute-start.41
  226.4 2.7 %collective-permute-done.42 = bf16[64,2048]{1,0:T(8,128)(2,1)S(1)} collective-permute-done((bf16[64,2048]{1,0:T(8,128)(2,1)S(1)}, bf16[64,2048]{1,0:T(8,128)(2,1)S(1)}, u32[]{:S(2)}, u32[]{:S(2)}) %collective-permute-start.42) | collective-permute-done | bytes 262176 | tf_op jit(solution)/shard_map/ppermute | solution.py:20
  229.7 2.7 %collective-permute-done.41 = bf16[64,2048]{1,0:T(8,128)(2,1)S(1)} collective-permute-done((bf16[64,2048]{1,0:T(8,128)(2,1)S(1)}, bf16[64,2048]{1,0:T(8,128)(2,1)S(1)}, u32[]{:S(2)}, u32[]{:S(2)}) %collective-permute-start.41) | collective-permute-done | bytes 262176 | tf_op jit(solution)/shard_map/ppermute | solution.py:20
  232.4 4.6 %collective-permute-done.43 = bf16[64,2048]{1,0:T(8,128)(2,1)S(1)} collective-permute-done((bf16[64,2048]{1,0:T(8,128)(2,1)S(1)}, bf16[64,2048]{1,0:T(8,128)(2,1)S(1)}, u32[]{:S(2)}, u32[]{:S(2)}) %collective-permute-start.43) | collective-permute-done | bytes 262176 | tf_op jit(solution)/shard_map/ppermute | solution.py:20
  (143 shorter events, 30.2 us)
Async XLA Ops:
  0.0 23.2 %collective-permute-start = (bf16[2048,1024]{1,0:T(8,128)(2,1)}, bf16[2048,1024]{1,0:T(8,128)(2,1)}, u32[]{:S(2)}, u32[]{:S(2)}) collective-permute-start(bf16[2048,1024]{1,0:T(8,128)(2,1)} %param.22), channel_id=1, source_target_pairs={{0,16},{16,0},{1,17},{17,1},{2,18},{18,2},{3,19},{19,3},{4,20},{20... | collective-permute-start | bytes 12582920 | tf_op jit(solution)/shard_map/ppermute | solution.py:32
  0.0 23.2 %collective-permute-start.1 = (bf16[1024,2048]{1,0:T(8,128)(2,1)}, bf16[1024,2048]{1,0:T(8,128)(2,1)}, u32[]{:S(2)}, u32[]{:S(2)}) collective-permute-start(bf16[1024,2048]{1,0:T(8,128)(2,1)} %param.24), channel_id=1, source_target_pairs={{0,16},{16,0},{1,17},{17,1},{2,18},{18,2},{3,19},{19,3},{4,20},{20... | collective-permute-start | bytes 12582920 | tf_op jit(solution)/shard_map/ppermute | solution.py:32
  3.2 25.8 %copy-start.9 = (bf16[1,512,2048]{2,1,0:T(8,128)(2,1)S(1)}, bf16[1,512,2048]{2,1,0:T(8,128)(2,1)}, u32[]{:S(2)}) copy-start(bf16[1,512,2048]{2,1,0:T(8,128)(2,1)} %param.19) | copy-start | bytes 6291460
  5.5 17.7 %all-to-all-start = ((bf16[8,24,2048]{2,1,0:T(8,128)(2,1)}), bf16[8,24,2048]{2,1,0:T(8,128)(2,1)S(1)}, u32[]{:S(2)}, u32[]{:S(2)}) async-start(bf16[8,24,2048]{2,1,0:T(8,128)(2,1)} %bitcast.2), calls=%async_computation | async-start | bytes 1572864 | tf_op jit(solution)/shard_map/all_to_all | solution.py:174
  10.1 8.3 %collective-permute-start.2 = (f32[1024]{0:T(1024)}, f32[1024]{0:T(1024)S(1)}, u32[]{:S(2)}, u32[]{:S(2)}) collective-permute-start(f32[1024]{0:T(1024)} %param.23), channel_id=1, source_target_pairs={{0,16},{16,0},{1,17},{17,1},{2,18},{18,2},{3,19},{19,3},{4,20},{20... | collective-permute-start | bytes 12296 | tf_op jit(solution)/shard_map/ppermute | solution.py:32
  10.6 5.0 %collective-permute-start.9 = (f32[512]{0:T(512)}, f32[512]{0:T(512)S(1)}, u32[]{:S(2)}, u32[]{:S(2)}) collective-permute-start(f32[512]{0:T(512)} %bitcast.50), channel_id=1, source_target_pairs={{0,3},{3,0},{1,2},{2,1},{4,7},{7,4},{5,6},{6,5},{8,11},{11,8},{9,1... | collective-permute-start | bytes 6152 | tf_op jit(solution)/shard_map/ppermute | solution.py:28
  15.6 50.1 %collective-permute-start.10 = (bf16[2048,512]{1,0:T(8,128)(2,1)}, bf16[2048,512]{1,0:T(8,128)(2,1)}, u32[]{:S(2)}, u32[]{:S(2)}) collective-permute-start(bf16[2048,512]{1,0:T(8,128)(2,1)} %bitcast.52), channel_id=1, source_target_pairs={{0,3},{3,0},{1,2},{2,1},{4,7},{7,4},{5,6},{6,5},{8,11},{11,8},{9,1... | collective-permute-start | bytes 6291464 | tf_op jit(solution)/shard_map/ppermute | solution.py:28
  18.3 9.1 %copy-start.22 = (f32[1024]{0:T(1024)}, f32[1024]{0:T(1024)S(1)}, u32[]{:S(2)}) copy-start(f32[1024]{0:T(1024)S(1)} %collective-permute-done.2) | copy-start | bytes 12292
  23.3 13.0 %collective-permute-start.3 = (bf16[96,2048]{1,0:T(8,128)(2,1)S(1)}, bf16[96,2048]{1,0:T(8,128)(2,1)S(1)}, u32[]{:S(2)}, u32[]{:S(2)}) collective-permute-start(bf16[96,2048]{1,0:T(8,128)(2,1)S(1)} %get-tuple-element.98), channel_id=1, source_target_pairs={{0,4},{4,8},{8,12},{12,0},{1,5},{5,9},{9,13},{13,1},{2,6},{6,10},{... | collective-permute-start | bytes 1179656 | tf_op jit(solution)/shard_map/ppermute | solution.py:20
  25.3 11.0 %collective-permute-start.4 = (bf16[96,2048]{1,0:T(8,128)(2,1)S(1)}, bf16[96,2048]{1,0:T(8,128)(2,1)S(1)}, u32[]{:S(2)}, u32[]{:S(2)}) collective-permute-start(bf16[96,2048]{1,0:T(8,128)(2,1)S(1)} %get-tuple-element.98), channel_id=1, source_target_pairs={{0,12},{4,0},{8,4},{12,8},{1,13},{5,1},{9,5},{13,9},{2,14},{6,2},{... | collective-permute-start | bytes 1179656 | tf_op jit(solution)/shard_map/ppermute | solution.py:20
  27.5 13.9 %copy-start.13 = (f32[1,512]{1,0:T(1,128)S(1)}, f32[1,512]{1,0:T(1,128)}, u32[]{:S(2)}) copy-start(f32[1,512]{1,0:T(1,128)} %param.18) | copy-start | bytes 6148
  27.5 10.4 %collective-permute-start.5 = (bf16[96,2048]{1,0:T(8,128)(2,1)S(1)}, bf16[96,2048]{1,0:T(8,128)(2,1)S(1)}, u32[]{:S(2)}, u32[]{:S(2)}) collective-permute-start(bf16[96,2048]{1,0:T(8,128)(2,1)S(1)} %get-tuple-element.97), channel_id=1, source_target_pairs={{0,1},{1,0},{2,3},{3,2},{4,5},{5,4},{6,7},{7,6},{8,9},{9,8},{10,11... | collective-permute-start | bytes 1179656 | tf_op jit(solution)/shard_map/ppermute | solution.py:24
  36.3 11.4 %collective-permute-start.6 = (bf16[96,2048]{1,0:T(8,128)(2,1)S(1)}, bf16[96,2048]{1,0:T(8,128)(2,1)S(1)}, u32[]{:S(2)}, u32[]{:S(2)}) collective-permute-start(bf16[96,2048]{1,0:T(8,128)(2,1)S(1)} %collective-permute-done.3), channel_id=1, source_target_pairs={{0,4},{4,8},{8,12},{12,0},{1,5},{5,9},{9,13},{13,1},{2,6},{6,10},{... | collective-permute-start | bytes 1179656 | tf_op jit(solution)/shard_map/ppermute | solution.py:20
  37.9 26.4 %collective-permute-start.11 = (bf16[288,2048]{1,0:T(8,128)(2,1)S(1)}, bf16[288,2048]{1,0:T(8,128)(2,1)S(1)}, u32[]{:S(2)}, u32[]{:S(2)}) collective-permute-start(bf16[288,2048]{1,0:T(8,128)(2,1)S(1)} %pad_maximum_fusion), channel_id=1, source_target_pairs={{0,1},{1,0},{2,3},{3,2},{4,5},{5,4},{6,7},{7,6},{8,9},{9,8},{10,11... | collective-permute-start | bytes 3538952 | tf_op jit(solution)/shard_map/ppermute | solution.py:24
  39.4 19.7 %collective-permute-start.7 = (bf16[192,2048]{1,0:T(8,128)(2,1)S(1)}, bf16[192,2048]{1,0:T(8,128)(2,1)S(1)}, u32[]{:S(2)}, u32[]{:S(2)}) collective-permute-start(bf16[192,2048]{1,0:T(8,128)(2,1)S(1)} %pad_maximum_fusion.3), channel_id=1, source_target_pairs={{0,12},{4,0},{8,4},{12,8},{1,13},{5,1},{9,5},{13,9},{2,14},{6,2},{... | collective-permute-start | bytes 2359304 | tf_op jit(solution)/shard_map/ppermute | solution.py:20
  47.7 19.0 %collective-permute-start.8 = (bf16[192,2048]{1,0:T(8,128)(2,1)S(1)}, bf16[192,2048]{1,0:T(8,128)(2,1)S(1)}, u32[]{:S(2)}, u32[]{:S(2)}) collective-permute-start(bf16[192,2048]{1,0:T(8,128)(2,1)S(1)} %pad_maximum_fusion.3), channel_id=1, source_target_pairs={{0,4},{4,8},{8,12},{12,0},{1,5},{5,9},{9,13},{13,1},{2,6},{6,10},{... | collective-permute-start | bytes 2359304 | tf_op jit(solution)/shard_map/ppermute | solution.py:20
  56.2 31.8 %collective-permute-start.14 = (bf16[512,1024]{1,0:T(8,128)(2,1)S(1)}, bf16[512,1024]{1,0:T(8,128)(2,1)S(1)}, u32[]{:S(2)}, u32[]{:S(2)}) collective-permute-start(bf16[512,1024]{1,0:T(8,128)(2,1)S(1)} %get-tuple-element.61), channel_id=1, source_target_pairs={{0,3},{3,0},{1,2},{2,1},{4,7},{7,4},{5,6},{6,5},{8,11},{11,8},{9,1... | collective-permute-start | bytes 3145736 | tf_op jit(solution)/shard_map/ppermute | solution.py:28
  59.1 18.1 %collective-permute-start.13 = (bf16[192,2048]{1,0:T(8,128)(2,1)S(1)}, bf16[192,2048]{1,0:T(8,128)(2,1)S(1)}, u32[]{:S(2)}, u32[]{:S(2)}) collective-permute-start(bf16[192,2048]{1,0:T(8,128)(2,1)S(1)} %collective-permute-done.7), channel_id=1, source_target_pairs={{0,12},{4,0},{8,4},{12,8},{1,13},{5,1},{9,5},{13,9},{2,14},{6,2},{... | collective-permute-start | bytes 2359304 | tf_op jit(solution)/shard_map/ppermute | solution.py:20
  65.7 7.8 %collective-permute-start.12 = (bf16[96,2048]{1,0:T(8,128)(2,1)S(1)}, bf16[96,2048]{1,0:T(8,128)(2,1)S(1)}, u32[]{:S(2)}, u32[]{:S(2)}) collective-permute-start(bf16[96,2048]{1,0:T(8,128)(2,1)S(1)} %collective-permute-done.6), channel_id=1, source_target_pairs={{0,1},{1,0},{2,3},{3,2},{4,5},{5,4},{6,7},{7,6},{8,9},{9,8},{10,11... | collective-permute-start | bytes 1179656 | tf_op jit(solution)/shard_map/ppermute | solution.py:24
  66.7 10.5 %copy-start.20 = (bf16[1,2048,512]{2,1,0:T(8,128)(2,1)S(1)}, bf16[1,2048,512]{2,1,0:T(8,128)(2,1)}, u32[]{:S(2)}) copy-start(bf16[1,2048,512]{2,1,0:T(8,128)(2,1)} %param.17) | copy-start | bytes 6291460
  66.7 41.6 %collective-permute-start.16 = (bf16[512,1024]{1,0:T(8,128)(2,1)S(1)}, bf16[512,1024]{1,0:T(8,128)(2,1)S(1)}, u32[]{:S(2)}, u32[]{:S(2)}) collective-permute-start(bf16[512,1024]{1,0:T(8,128)(2,1)S(1)} %get-tuple-element.62), channel_id=1, source_target_pairs={{0,3},{3,0},{1,2},{2,1},{4,7},{7,4},{5,6},{6,5},{8,11},{11,8},{9,1... | collective-permute-start | bytes 3145736 | tf_op jit(solution)/shard_map/ppermute | solution.py:28
  91.8 16.6 %collective-permute-start.15 = (bf16[384,1024]{1,0:T(8,128)(2,1)S(1)}, bf16[384,1024]{1,0:T(8,128)(2,1)S(1)}, u32[]{:S(2)}, u32[]{:S(2)}) collective-permute-start(bf16[384,1024]{1,0:T(8,128)(2,1)S(1)} %slice.123), channel_id=1, source_target_pairs={{0,1},{1,0},{2,3},{3,2},{4,5},{5,4},{6,7},{7,6},{8,9},{9,8},{10,11... | collective-permute-start | bytes 2359304 | tf_op jit(solution)/shard_map/ppermute | solution.py:24
  92.1 10.6 %collective-permute-start.24 = (bf16[192,1024]{1,0:T(8,128)(2,1)S(1)}, bf16[192,1024]{1,0:T(8,128)(2,1)S(1)}, u32[]{:S(2)}, u32[]{:S(2)}) collective-permute-start(bf16[192,1024]{1,0:T(8,128)(2,1)S(1)} %get-tuple-element.84), channel_id=1, source_target_pairs={{0,4},{4,8},{8,12},{12,0},{1,5},{5,9},{9,13},{13,1},{2,6},{6,10},{... | collective-permute-start | bytes 1179656 | tf_op jit(solution)/shard_map/ppermute | solution.py:20
  94.7 18.1 %collective-permute-start.23 = (bf16[192,1024]{1,0:T(8,128)(2,1)S(1)}, bf16[192,1024]{1,0:T(8,128)(2,1)S(1)}, u32[]{:S(2)}, u32[]{:S(2)}) collective-permute-start(bf16[192,1024]{1,0:T(8,128)(2,1)S(1)} %get-tuple-element.83), channel_id=1, source_target_pairs={{0,12},{4,0},{8,4},{12,8},{1,13},{5,1},{9,5},{13,9},{2,14},{6,2},{... | collective-permute-start | bytes 1179656 | tf_op jit(solution)/shard_map/ppermute | solution.py:20
  102.8 10.0 %collective-permute-start.25 = (bf16[192,1024]{1,0:T(8,128)(2,1)S(1)}, bf16[192,1024]{1,0:T(8,128)(2,1)S(1)}, u32[]{:S(2)}, u32[]{:S(2)}) collective-permute-start(bf16[192,1024]{1,0:T(8,128)(2,1)S(1)} %add_convert_fusion.3), channel_id=1, source_target_pairs={{0,4},{4,8},{8,12},{12,0},{1,5},{5,9},{9,13},{13,1},{2,6},{6,10},{... | collective-permute-start | bytes 1179656 | tf_op jit(solution)/shard_map/ppermute | solution.py:20
  108.7 13.3 %collective-permute-start.20 = (bf16[96,1024]{1,0:T(8,128)(2,1)S(1)}, bf16[96,1024]{1,0:T(8,128)(2,1)S(1)}, u32[]{:S(2)}, u32[]{:S(2)}) collective-permute-start(bf16[96,1024]{1,0:T(8,128)(2,1)S(1)} %get-tuple-element.94), channel_id=1, source_target_pairs={{0,12},{4,0},{8,4},{12,8},{1,13},{5,1},{9,5},{13,9},{2,14},{6,2},{... | collective-permute-start | bytes 589832 | tf_op jit(solution)/shard_map/ppermute | solution.py:20
  112.8 12.1 %collective-permute-start.21 = (bf16[96,1024]{1,0:T(8,128)(2,1)S(1)}, bf16[96,1024]{1,0:T(8,128)(2,1)S(1)}, u32[]{:S(2)}, u32[]{:S(2)}) collective-permute-start(bf16[96,1024]{1,0:T(8,128)(2,1)S(1)} %get-tuple-element.93), channel_id=1, source_target_pairs={{0,4},{4,8},{8,12},{12,0},{1,5},{5,9},{9,13},{13,1},{2,6},{6,10},{... | collective-permute-start | bytes 589832 | tf_op jit(solution)/shard_map/ppermute | solution.py:20
  113.0 13.9 %collective-permute-start.26 = (bf16[96,1024]{1,0:T(8,128)(2,1)S(1)}, bf16[96,1024]{1,0:T(8,128)(2,1)S(1)}, u32[]{:S(2)}, u32[]{:S(2)}) collective-permute-start(bf16[96,1024]{1,0:T(8,128)(2,1)S(1)} %slice.157), channel_id=1, source_target_pairs={{0,1},{1,0},{2,3},{3,2},{4,5},{5,4},{6,7},{7,6},{8,9},{9,8},{10,11... | collective-permute-start | bytes 589832 | tf_op jit(solution)/shard_map/ppermute | solution.py:24
  119.5 25.1 %copy-start.7 = (bf16[1536,1024]{1,0:T(8,128)(2,1)}, bf16[1536,1024]{1,0:T(8,128)(2,1)S(1)}, u32[]{:S(2)}) copy-start(bf16[1536,1024]{1,0:T(8,128)(2,1)S(1)} %convolution_convert_fusion) | copy-start | bytes 9437188
  120.6 22.6 %collective-permute-start.17 = (bf16[384,1024]{1,0:T(8,128)(2,1)}, bf16[384,1024]{1,0:T(8,128)(2,1)}, u32[]{:S(2)}, u32[]{:S(2)}) collective-permute-start(bf16[384,1024]{1,0:T(8,128)(2,1)} %slice.125), channel_id=1, source_target_pairs={{0,1},{1,0},{2,3},{3,2},{4,5},{5,4},{6,7},{7,6},{8,9},{9,8},{10,11... | collective-permute-start | bytes 2359304 | tf_op jit(solution)/shard_map/ppermute | solution.py:24
  121.7 18.5 %collective-permute-start.29 = (bf16[192,1024]{1,0:T(8,128)(2,1)}, bf16[192,1024]{1,0:T(8,128)(2,1)}, u32[]{:S(2)}, u32[]{:S(2)}) collective-permute-start(bf16[192,1024]{1,0:T(8,128)(2,1)} %get-tuple-element.86), channel_id=1, source_target_pairs={{0,4},{4,8},{8,12},{12,0},{1,5},{5,9},{9,13},{13,1},{2,6},{6,10},{... | collective-permute-start | bytes 1179656 | tf_op jit(solution)/shard_map/ppermute | solution.py:20
  122.0 25.8 %collective-permute-start.28 = (bf16[192,1024]{1,0:T(8,128)(2,1)}, bf16[192,1024]{1,0:T(8,128)(2,1)}, u32[]{:S(2)}, u32[]{:S(2)}) collective-permute-start(bf16[192,1024]{1,0:T(8,128)(2,1)} %get-tuple-element.85), channel_id=1, source_target_pairs={{0,12},{4,0},{8,4},{12,8},{1,13},{5,1},{9,5},{13,9},{2,14},{6,2},{... | collective-permute-start | bytes 1179656 | tf_op jit(solution)/shard_map/ppermute | solution.py:20
  125.0 8.8 %collective-permute-start.22 = (bf16[96,1024]{1,0:T(8,128)(2,1)S(1)}, bf16[96,1024]{1,0:T(8,128)(2,1)S(1)}, u32[]{:S(2)}, u32[]{:S(2)}) collective-permute-start(bf16[96,1024]{1,0:T(8,128)(2,1)S(1)} %add_convert_fusion.9), channel_id=1, source_target_pairs={{0,12},{4,0},{8,4},{12,8},{1,13},{5,1},{9,5},{13,9},{2,14},{6,2},{... | collective-permute-start | bytes 589832 | tf_op jit(solution)/shard_map/ppermute | solution.py:20
  134.7 22.1 %all-to-all-start.1 = ((bf16[8,24,1024]{2,1,0:T(8,128)(2,1)}), bf16[8,24,1024]{2,1,0:T(8,128)(2,1)S(1)}, u32[]{:S(2)}, u32[]{:S(2)}) async-start(bf16[8,24,1024]{2,1,0:T(8,128)(2,1)} %bitcast.8), calls=%async_computation.1 | async-start | bytes 786432 | tf_op jit(solution)/shard_map/all_to_all | solution.py:174
  141.3 13.7 %collective-permute-start.30 = (bf16[192,1024]{1,0:T(8,128)(2,1)S(1)}, bf16[192,1024]{1,0:T(8,128)(2,1)S(1)}, u32[]{:S(2)}, u32[]{:S(2)}) collective-permute-start(bf16[192,1024]{1,0:T(8,128)(2,1)S(1)} %add_convert_fusion.2), channel_id=1, source_target_pairs={{0,4},{4,8},{8,12},{12,0},{1,5},{5,9},{9,13},{13,1},{2,6},{6,10},{... | collective-permute-start | bytes 1179656 | tf_op jit(solution)/shard_map/ppermute | solution.py:20
  145.7 27.1 %copy-start.10 = (f32[8,2048]{1,0:T(8,128)S(1)}, f32[8,2048]{1,0:T(8,128)}, u32[]{:S(2)}) copy-start(f32[8,2048]{1,0:T(8,128)} %param.20) | copy-start | bytes 196612
  145.7 36.0 %copy-start.5 = (bf16[128,2048]{1,0:T(8,128)(2,1)S(1)}, bf16[128,2048]{1,0:T(8,128)(2,1)}, u32[]{:S(2)}) copy-start(bf16[128,2048]{1,0:T(8,128)(2,1)} %tokens_ref.1) | copy-start | bytes 1572868
  145.7 36.0 %copy-start.14 = (pred[128]{0:T(512)(128)(4,1)S(1)}, pred[128]{0:T(512)(128)(4,1)}, u32[]{:S(2)}) copy-start(pred[128]{0:T(512)(128)(4,1)} %get-tuple-element.112) | copy-start | bytes 388
  145.7 36.0 %copy-start.15 = (pred[128]{0:T(512)(128)(4,1)S(1)}, pred[128]{0:T(512)(128)(4,1)}, u32[]{:S(2)}) copy-start(pred[128]{0:T(512)(128)(4,1)} %get-tuple-element.113) | copy-start | bytes 388
  145.7 36.0 %copy-start.16 = (pred[128]{0:T(512)(128)(4,1)S(1)}, pred[128]{0:T(512)(128)(4,1)}, u32[]{:S(2)}) copy-start(pred[128]{0:T(512)(128)(4,1)} %get-tuple-element.114) | copy-start | bytes 388
  145.7 36.0 %copy-start.17 = (pred[128]{0:T(512)(128)(4,1)S(1)}, pred[128]{0:T(512)(128)(4,1)}, u32[]{:S(2)}) copy-start(pred[128]{0:T(512)(128)(4,1)} %get-tuple-element.115) | copy-start | bytes 388
  145.7 11.2 %collective-permute-start.18 = (bf16[96,1024]{1,0:T(8,128)(2,1)}, bf16[96,1024]{1,0:T(8,128)(2,1)S(1)}, u32[]{:S(2)}, u32[]{:S(2)}) collective-permute-start(bf16[96,1024]{1,0:T(8,128)(2,1)} %get-tuple-element.96), channel_id=1, source_target_pairs={{0,12},{4,0},{8,4},{12,8},{1,13},{5,1},{9,5},{13,9},{2,14},{6,2},{... | collective-permute-start | bytes 589832 | tf_op jit(solution)/shard_map/ppermute | solution.py:20
  147.6 11.4 %collective-permute-start.19 = (bf16[96,1024]{1,0:T(8,128)(2,1)}, bf16[96,1024]{1,0:T(8,128)(2,1)S(1)}, u32[]{:S(2)}, u32[]{:S(2)}) collective-permute-start(bf16[96,1024]{1,0:T(8,128)(2,1)} %get-tuple-element.95), channel_id=1, source_target_pairs={{0,4},{4,8},{8,12},{12,0},{1,5},{5,9},{9,13},{13,1},{2,6},{6,10},{... | collective-permute-start | bytes 589832 | tf_op jit(solution)/shard_map/ppermute | solution.py:20
  156.3 6.6 %collective-permute-start.31 = (bf16[96,1024]{1,0:T(8,128)(2,1)S(1)}, bf16[96,1024]{1,0:T(8,128)(2,1)S(1)}, u32[]{:S(2)}, u32[]{:S(2)}) collective-permute-start(bf16[96,1024]{1,0:T(8,128)(2,1)S(1)} %slice.156), channel_id=1, source_target_pairs={{0,1},{1,0},{2,3},{3,2},{4,5},{5,4},{6,7},{7,6},{8,9},{9,8},{10,11... | collective-permute-start | bytes 589832 | tf_op jit(solution)/shard_map/ppermute | solution.py:24
  160.0 6.8 %collective-permute-start.27 = (bf16[96,1024]{1,0:T(8,128)(2,1)S(1)}, bf16[96,1024]{1,0:T(8,128)(2,1)S(1)}, u32[]{:S(2)}, u32[]{:S(2)}) collective-permute-start(bf16[96,1024]{1,0:T(8,128)(2,1)S(1)} %add_convert_fusion.7), channel_id=1, source_target_pairs={{0,12},{4,0},{8,4},{12,8},{1,13},{5,1},{9,5},{13,9},{2,14},{6,2},{... | collective-permute-start | bytes 589832 | tf_op jit(solution)/shard_map/ppermute | solution.py:20
  168.6 13.1 %all-to-all-start.2 = ((bf16[8,24,1024]{2,1,0:T(8,128)(2,1)}), bf16[8,24,1024]{2,1,0:T(8,128)(2,1)S(1)}, u32[]{:S(2)}, u32[]{:S(2)}) async-start(bf16[8,24,1024]{2,1,0:T(8,128)(2,1)} %bitcast.10), calls=%async_computation.2 | async-start | bytes 786432 | tf_op jit(solution)/shard_map/all_to_all | solution.py:174
  181.7 18.7 %copy-start.18 = (bf16[2048,1024]{1,0:T(8,128)(2,1)S(1)}, bf16[2048,1024]{1,0:T(8,128)(2,1)}, u32[]{:S(2)}) copy-start(bf16[2048,1024]{1,0:T(8,128)(2,1)} %param.22) | copy-start | bytes 12582916
  182.5 17.8 %copy-start.21 = (f32[1024]{0:T(1024)S(1)}, f32[1024]{0:T(1024)}, u32[]{:S(2)}) copy-start(f32[1024]{0:T(1024)} %param.23) | copy-start | bytes 12292
  183.1 9.1 %collective-permute-start.32 = (bf16[64,2048]{1,0:T(8,128)(2,1)S(1)}, bf16[64,2048]{1,0:T(8,128)(2,1)S(1)}, u32[]{:S(2)}, u32[]{:S(2)}) collective-permute-start(bf16[64,2048]{1,0:T(8,128)(2,1)S(1)} %get-tuple-element.99), channel_id=1, source_target_pairs={{0,32},{32,64},{64,96},{96,0},{1,33},{33,65},{65,97},{97,1},{2,34}... | collective-permute-start | bytes 786440 | tf_op jit(solution)/shard_map/ppermute | solution.py:20
  183.7 8.5 %collective-permute-start.33 = (bf16[64,2048]{1,0:T(8,128)(2,1)S(1)}, bf16[64,2048]{1,0:T(8,128)(2,1)S(1)}, u32[]{:S(2)}, u32[]{:S(2)}) collective-permute-start(bf16[64,2048]{1,0:T(8,128)(2,1)S(1)} %get-tuple-element.99), channel_id=1, source_target_pairs={{0,96},{32,0},{64,32},{96,64},{1,97},{33,1},{65,33},{97,65},{2,98}... | collective-permute-start | bytes 786440 | tf_op jit(solution)/shard_map/ppermute | solution.py:20
  192.2 8.2 %collective-permute-start.34 = (bf16[64,2048]{1,0:T(8,128)(2,1)S(1)}, bf16[64,2048]{1,0:T(8,128)(2,1)S(1)}, u32[]{:S(2)}, u32[]{:S(2)}) collective-permute-start(bf16[64,2048]{1,0:T(8,128)(2,1)S(1)} %collective-permute-done.32), channel_id=1, source_target_pairs={{0,32},{32,64},{64,96},{96,0},{1,33},{33,65},{65,97},{97,1},{2,34}... | collective-permute-start | bytes 786440 | tf_op jit(solution)/shard_map/ppermute | solution.py:20
  192.2 9.4 %copy-start.3 = (bf16[2048,1024]{1,0:T(8,128)(2,1)S(1)}, bf16[2048,1024]{1,0:T(8,128)(2,1)}, u32[]{:S(2)}) copy-start(bf16[2048,1024]{1,0:T(8,128)(2,1)} %copy-done.2) | copy-start | bytes 12582916
  192.2 9.4 %copy-start.23 = (f32[1024]{0:T(1024)S(1)}, f32[1024]{0:T(1024)}, u32[]{:S(2)}) copy-start(f32[1024]{0:T(1024)} %copy-done.22) | copy-start | bytes 12292
  192.3 10.7 %collective-permute-start.35 = (bf16[64,2048]{1,0:T(8,128)(2,1)S(1)}, bf16[64,2048]{1,0:T(8,128)(2,1)S(1)}, u32[]{:S(2)}, u32[]{:S(2)}) collective-permute-start(bf16[64,2048]{1,0:T(8,128)(2,1)S(1)} %get-tuple-element.78), channel_id=1, source_target_pairs={{0,96},{32,0},{64,32},{96,64},{1,97},{33,1},{65,33},{97,65},{2,98}... | collective-permute-start | bytes 786440 | tf_op jit(solution)/shard_map/ppermute | solution.py:20
  203.0 2.4 %copy-start.19 = (bf16[1024,2048]{1,0:T(8,128)(2,1)S(1)}, bf16[1024,2048]{1,0:T(8,128)(2,1)}, u32[]{:S(2)}) copy-start(bf16[1024,2048]{1,0:T(8,128)(2,1)} %param.24) | copy-start | bytes 12582916
  203.0 8.1 %collective-permute-start.36 = (bf16[64,2048]{1,0:T(8,128)(2,1)S(1)}, bf16[64,2048]{1,0:T(8,128)(2,1)S(1)}, u32[]{:S(2)}, u32[]{:S(2)}) collective-permute-start(bf16[64,2048]{1,0:T(8,128)(2,1)S(1)} %get-tuple-element.78), channel_id=1, source_target_pairs={{0,32},{32,64},{64,96},{96,0},{1,33},{33,65},{65,97},{97,1},{2,34}... | collective-permute-start | bytes 786440 | tf_op jit(solution)/shard_map/ppermute | solution.py:20
  206.7 8.9 %collective-permute-start.37 = (bf16[64,2048]{1,0:T(8,128)(2,1)S(1)}, bf16[64,2048]{1,0:T(8,128)(2,1)S(1)}, u32[]{:S(2)}, u32[]{:S(2)}) collective-permute-start(bf16[64,2048]{1,0:T(8,128)(2,1)S(1)} %collective-permute-done.35), channel_id=1, source_target_pairs={{0,96},{32,0},{64,32},{96,64},{1,97},{33,1},{65,33},{97,65},{2,98}... | collective-permute-start | bytes 786440 | tf_op jit(solution)/shard_map/ppermute | solution.py:20
  209.0 9.4 %collective-permute-start.38 = (bf16[64,2048]{1,0:T(8,128)(2,1)S(1)}, bf16[64,2048]{1,0:T(8,128)(2,1)S(1)}, u32[]{:S(2)}, u32[]{:S(2)}) collective-permute-start(bf16[64,2048]{1,0:T(8,128)(2,1)S(1)} %get-tuple-element.92), channel_id=1, source_target_pairs={{0,96},{32,0},{64,32},{96,64},{1,97},{33,1},{65,33},{97,65},{2,98}... | collective-permute-start | bytes 786440 | tf_op jit(solution)/shard_map/ppermute | solution.py:20
  209.1 9.4 %collective-permute-start.39 = (bf16[64,2048]{1,0:T(8,128)(2,1)S(1)}, bf16[64,2048]{1,0:T(8,128)(2,1)S(1)}, u32[]{:S(2)}, u32[]{:S(2)}) collective-permute-start(bf16[64,2048]{1,0:T(8,128)(2,1)S(1)} %get-tuple-element.91), channel_id=1, source_target_pairs={{0,32},{32,64},{64,96},{96,0},{1,33},{33,65},{65,97},{97,1},{2,34}... | collective-permute-start | bytes 786440 | tf_op jit(solution)/shard_map/ppermute | solution.py:20
  221.1 16.0 %copy-start.12 = (f32[2048]{0:T(1024)S(1)}, f32[2048]{0:T(1024)}, u32[]{:S(2)}) copy-start(f32[2048]{0:T(1024)} %param.25) | copy-start | bytes 24580
  221.2 7.9 %collective-permute-start.42 = (bf16[64,2048]{1,0:T(8,128)(2,1)S(1)}, bf16[64,2048]{1,0:T(8,128)(2,1)S(1)}, u32[]{:S(2)}, u32[]{:S(2)}) collective-permute-start(bf16[64,2048]{1,0:T(8,128)(2,1)S(1)} %get-tuple-element.90), channel_id=1, source_target_pairs={{0,32},{32,64},{64,96},{96,0},{1,33},{33,65},{65,97},{97,1},{2,34}... | collective-permute-start | bytes 786440 | tf_op jit(solution)/shard_map/ppermute | solution.py:20
  221.2 8.4 %collective-permute-start.40 = (bf16[64,2048]{1,0:T(8,128)(2,1)S(1)}, bf16[64,2048]{1,0:T(8,128)(2,1)S(1)}, u32[]{:S(2)}, u32[]{:S(2)}) collective-permute-start(bf16[64,2048]{1,0:T(8,128)(2,1)S(1)} %add_convert_fusion.5), channel_id=1, source_target_pairs={{0,96},{32,0},{64,32},{96,64},{1,97},{33,1},{65,33},{97,65},{2,98}... | collective-permute-start | bytes 786440 | tf_op jit(solution)/shard_map/ppermute | solution.py:20
  224.5 8.0 %collective-permute-start.41 = (bf16[64,2048]{1,0:T(8,128)(2,1)S(1)}, bf16[64,2048]{1,0:T(8,128)(2,1)S(1)}, u32[]{:S(2)}, u32[]{:S(2)}) collective-permute-start(bf16[64,2048]{1,0:T(8,128)(2,1)S(1)} %get-tuple-element.89), channel_id=1, source_target_pairs={{0,96},{32,0},{64,32},{96,64},{1,97},{33,1},{65,33},{97,65},{2,98}... | collective-permute-start | bytes 786440 | tf_op jit(solution)/shard_map/ppermute | solution.py:20
  229.1 7.9 %collective-permute-start.43 = (bf16[64,2048]{1,0:T(8,128)(2,1)S(1)}, bf16[64,2048]{1,0:T(8,128)(2,1)S(1)}, u32[]{:S(2)}, u32[]{:S(2)}) collective-permute-start(bf16[64,2048]{1,0:T(8,128)(2,1)S(1)} %add_convert_fusion.4), channel_id=1, source_target_pairs={{0,32},{32,64},{64,96},{96,0},{1,33},{33,65},{65,97},{97,1},{2,34}... | collective-permute-start | bytes 786440 | tf_op jit(solution)/shard_map/ppermute | solution.py:20
  (7 other events, 10.3 us)

commit v9 on v7

--- a/solution.py
+++ b/solution.py
@@ -229,9 +229,6 @@
             foll = shift(down(up(foll) + up(via)), "z", 1)
         return up(own) + up(prev) + up(foll), hidden, after
 
-    def finish(summed, back):
-        return exchange(down(summed[: 2 * count] + up(back)))
-
     sum_l, hidden, right_pair = ring(left, left_pair, hidden, 1, right_pair)
     out_l = down(sum_l[2 * count :])
     back_l = swap_column(out_l)
@@ -241,17 +238,18 @@
     prev = shift(part[8 * count : 10 * count], "z", -1)
     foll = shift(down(up(part[6 * count : 8 * count]) + up(via)), "z", 1)
     sum_b = up(part[4 * count : 6 * count]) + up(prev) + up(foll)
-    sum_b = sum_b[:count] + up(swap_column(down(sum_b[count:])))
+    back_b = swap_column(down(sum_b[count:]))
     own, prev, foll, far = jnp.split(down(up(part[:wide]) + up(back)), 4)
     via = shift(far, "z", -1)
     foll = shift(foll, "z", 1)
-    via, foll, back_l = hold(via, foll, back_l)
-    return_l = finish(sum_l, back_l)
+    via, foll = hold(via, foll)
     prev = shift(down(up(prev) + up(via)), "z", -1)
-    sum_b, return_l = hold(sum_b, return_l)
+    prev, back_b, back_l = hold(prev, back_b, back_l)
+    sum_b = sum_b[:count] + up(back_b)
+    sum_l = down(sum_l[: 2 * count] + up(back_l))
     sum_a = up(own) + up(prev) + up(foll)
-    return_r = exchange(down(jnp.concatenate([sum_a, sum_b], axis=0)))
-    returned = jnp.concatenate([return_l, return_r], axis=1)
+    sum_r = down(jnp.concatenate([sum_a, sum_b], axis=0))
+    returned = exchange(jnp.concatenate([sum_l, sum_r], axis=1))
     group_out = lax.dot_general(
         dispatch_map, returned, (((0,), (0,)), ((), ())), preferred_element_type=jnp.float32
     )

time: 234 us -> 231 us (0.987)
  starting transfers between devices: 68.8 us -> 65.4 us
    ppermute x27, waiting for transfers between devices: 60.5 us -> 66.6 us  [shift(): lax.ppermute(value, axis, [(i, (i + step) % size) for i in range(size)])]
    all_to_all x3 -> x2, waiting for transfers between devices: 22.7 us -> 18.2 us  [exchange(): lax.all_to_all(value, ('y', 'core'), split_axis=0, concat_axis=0, tiled=T...]
    all_to_all x3 -> x2, starting transfers between devices: 13.3 us -> 9.72 us  [exchange(): lax.all_to_all(value, ('y', 'core'), split_axis=0, concat_axis=0, tiled=T...]
    unnamed x43 -> x37, local copies, waits for them, and re-layouts: 7.25 us -> 7.31 us
  transfers between devices with their start and end apart: 43 -> 42, of which waited for: 28 -> 28; matrix products, arithmetic and copies ran while one was open for 13% -> 12% of each run, Pallas kernels for 3% -> 3%
where the time goes in v9:
time: 231 us; the launch traced here: 230 us
  waiting for transfers between devices  116 us (50%)
  starting transfers between devices  65.4 us (28%)
  matrix products  28.1 us (12%)
  local copies, waits for them, and re-layouts  8.36 us (4%)
  Pallas kernels  6.17 us (3%)
  other arithmetic  5.65 us (2%)
    ppermute x27, waiting for transfers between devices, shift(): lax.ppermute(value, axis, [(i, (i + step) % size) for i in range(size)])  66.6 us
    ppermute x27, starting transfers between devices, shift(): lax.ppermute(value, axis, [(i, (i + step) % size) for i in range(size)])  40 us
    ppermute x4, waiting for transfers between devices, swap_blocks(): return lax.ppermute(value, X, [(0, 3), (3, 0), (1, 2), (2, 1)])  22 us
    all_to_all x2, waiting for transfers between devices, exchange(): lax.all_to_all(value, ('y', 'core'), split_axis=0, concat_axis=0, tiled=T...  18.2 us
    ppermute x4, starting transfers between devices, swap_blocks(): return lax.ppermute(value, X, [(0, 3), (3, 0), (1, 2), (2, 1)])  11 us
    all_to_all x2, starting transfers between devices, exchange(): lax.all_to_all(value, ('y', 'core'), split_axis=0, concat_axis=0, tiled=T...  9.72 us
    ppermute x6, waiting for transfers between devices, swap_column(): return lax.ppermute(value, 'xl', [(0, 1), (1, 0)])  9.16 us
    dot_general x2, matrix products, first(): jnp.dot(rows, w1, preferred_element_type=jnp.float32) + b1  9 us
  transfers between devices with their start and end apart: 42, of which 28 were waited for; matrix products, arithmetic and copies ran while one was open for 12% of the time, Pallas kernels for 3%

profile of v9, /device:TPU:0, one launch (start us, length us, event | category | flops | bytes accessed | tf_op | source)
XLA Modules:
  0.0 230.1 jit_solution(13277461841838747289)
XLA Ops:
  3.2 1.8 dispatch.1
  5.0 4.6 %all-to-all-start = ((bf16[8,24,2048]{2,1,0:T(8,128)(2,1)}), bf16[8,24,2048]{2,1,0:T(8,128)(2,1)S(1)}, u32[]{:S(2)}, u32[]{:S(2)}) async-start(bf16[8,24,2048]{2,1,0:T(8,128)(2,1)} %bitcast.2), calls=%async_computation | async-start | bytes 1572864 | tf_op jit(solution)/shard_map/all_to_all | solution.py:169
  10.0 2.8 %collective-permute-start.9 = (f32[512]{0:T(512)S(1)}, f32[512]{0:T(512)S(1)}, u32[]{:S(2)}, u32[]{:S(2)}) collective-permute-start(f32[512]{0:T(512)S(1)} %bitcast.47), channel_id=1, source_target_pairs={{0,3},{3,0},{1,2},{2,1},{4,7},{7,4},{5,6},{6,5},{8,11},{11,8},{9,1... | collective-permute-start | bytes 6152 | tf_op jit(solution)/shard_map/ppermute | solution.py:28
  12.8 2.0 collective-permute-done.9
  14.8 2.8 %collective-permute-start.10 = (bf16[2048,512]{1,0:T(8,128)(2,1)}, bf16[2048,512]{1,0:T(8,128)(2,1)}, u32[]{:S(2)}, u32[]{:S(2)}) collective-permute-start(bf16[2048,512]{1,0:T(8,128)(2,1)} %bitcast.49), channel_id=1, source_target_pairs={{0,3},{3,0},{1,2},{2,1},{4,7},{7,4},{5,6},{6,5},{8,11},{11,8},{9,1... | collective-permute-start | bytes 6291464 | tf_op jit(solution)/shard_map/ppermute | solution.py:28
  17.6 5.1 %all-to-all-done = bf16[8,24,2048]{2,1,0:T(8,128)(2,1)S(1)} async-done(((bf16[8,24,2048]{2,1,0:T(8,128)(2,1)}), bf16[8,24,2048]{2,1,0:T(8,128)(2,1)S(1)}, u32[]{:S(2)}, u32[]{:S(2)}) %all-to-all-start) | async-done | bytes 786464 | tf_op jit(solution)/shard_map/all_to_all | solution.py:169
  22.7 2.0 collective-permute-start.3
  24.7 2.2 collective-permute-start.4
  26.9 1.5 collective-permute-start.5
  28.6 7.2 %collective-permute-done.3 = bf16[96,2048]{1,0:T(8,128)(2,1)S(1)} collective-permute-done((bf16[96,2048]{1,0:T(8,128)(2,1)S(1)}, bf16[96,2048]{1,0:T(8,128)(2,1)S(1)}, u32[]{:S(2)}, u32[]{:S(2)}) %collective-permute-start.3) | collective-permute-done | bytes 393248 | tf_op jit(solution)/shard_map/ppermute | solution.py:20
  35.9 1.4 collective-permute-done.5
  37.3 1.5 collective-permute-start.11
  38.9 2.0 collective-permute-start.7
  40.9 6.3 %collective-permute-done.6 = bf16[96,2048]{1,0:T(8,128)(2,1)S(1)} collective-permute-done((bf16[96,2048]{1,0:T(8,128)(2,1)S(1)}, bf16[96,2048]{1,0:T(8,128)(2,1)S(1)}, u32[]{:S(2)}, u32[]{:S(2)}) %collective-permute-start.6) | collective-permute-done | bytes 393248 | tf_op jit(solution)/shard_map/ppermute | solution.py:20
  47.3 2.2 on_chip.2
  49.5 2.0 copy-done.2
  51.5 2.2 on_chip.3
  53.7 2.0 copy-done
  55.7 2.8 %collective-permute-start.14 = (bf16[512,1024]{1,0:T(8,128)(2,1)S(1)}, bf16[512,1024]{1,0:T(8,128)(2,1)S(1)}, u32[]{:S(2)}, u32[]{:S(2)}) collective-permute-start(bf16[512,1024]{1,0:T(8,128)(2,1)S(1)} %get-tuple-element.62), channel_id=1, source_target_pairs={{0,3},{3,0},{1,2},{2,1},{4,7},{7,4},{5,6},{6,5},{8,11},{11,8},{9,1... | collective-permute-start | bytes 3145736 | tf_op jit(solution)/shard_map/ppermute | solution.py:28
  58.5 3.3 %collective-permute-start.13 = (bf16[192,2048]{1,0:T(8,128)(2,1)S(1)}, bf16[192,2048]{1,0:T(8,128)(2,1)S(1)}, u32[]{:S(2)}, u32[]{:S(2)}) collective-permute-start(bf16[192,2048]{1,0:T(8,128)(2,1)S(1)} %collective-permute-done.7), channel_id=1, source_target_pairs={{0,12},{4,0},{8,4},{12,8},{1,13},{5,1},{9,5},{13,9},{2,14},{6,2},{... | collective-permute-start | bytes 2359304 | tf_op jit(solution)/shard_map/ppermute | solution.py:20
  61.9 1.8 collective-permute-done.11
  63.7 1.2 collective-permute-done.10
  66.2 2.8 %collective-permute-start.17 = (bf16[512,1024]{1,0:T(8,128)(2,1)S(1)}, bf16[512,1024]{1,0:T(8,128)(2,1)S(1)}, u32[]{:S(2)}, u32[]{:S(2)}) collective-permute-start(bf16[512,1024]{1,0:T(8,128)(2,1)S(1)} %get-tuple-element.63), channel_id=1, source_target_pairs={{0,3},{3,0},{1,2},{2,1},{4,7},{7,4},{5,6},{6,5},{8,11},{11,8},{9,1... | collective-permute-start | bytes 3145736 | tf_op jit(solution)/shard_map/ppermute | solution.py:28
  69.1 6.0 %maximum_convert_fusion = bf16[1248,1024]{1,0:T(8,128)(2,1)S(1)} fusion(bf16[1248,2048]{1,0:T(8,128)(2,1)S(1)} %constant_dynamic-update-slice_fusion, bf16[2048,512]{1,0:T(8,128)(2,1)} %collective-permute-done.10, bf16[2048,512]{1,0:T(8,128)(2,1)S(1)} %bitcast.50, f32[1024]{0:T(1024)S(1)} %pad_maximum_fusion.20), kind=kOutput, calls=%fused_computation | convolution fusion | flops 5246713856 | bytes 11866112 | tf_op jit(solution)/shard_map/dot_general | solution.py:202
  75.2 1.4 collective-permute-done.13
  76.6 3.0 %fusion.12 = bf16[288,1024]{1,0:T(8,128)(2,1)S(1)} fusion(bf16[2048,512]{1,0:T(8,128)(2,1)} %collective-permute-done.10, bf16[2048,512]{1,0:T(8,128)(2,1)S(1)} %bitcast.51, bf16[192,2048]{1,0:T(8,128)(2,1)S(1)} %collective-permute-done.13, bf16[96,2048]{1,0:T(8,128)(2,1)S(1)} %collective-permute-done.12, f32[1024]{0:T(1024)S(1)} %pad_maximum_fusion.20), kind=kOutput, calls=%fused_computation.23 | convolution fusion | flops 1219592192 | bytes 5967872 | tf_op jit(solution)/shard_map/dot_general | solution.py:202
  79.6 7.7 %collective-permute-done.14 = bf16[512,1024]{1,0:T(8,128)(2,1)S(1)} collective-permute-done((bf16[512,1024]{1,0:T(8,128)(2,1)S(1)}, bf16[512,1024]{1,0:T(8,128)(2,1)S(1)}, u32[]{:S(2)}, u32[]{:S(2)}) %collective-permute-start.14) | collective-permute-done | bytes 1048608 | tf_op jit(solution)/shard_map/ppermute | solution.py:28
  87.3 4.3 %convolution_convert_fusion.1 = bf16[1536,1024]{1,0:T(8,128)(2,1)S(1)} fusion(bf16[512,1024]{1,0:T(8,128)(2,1)S(1)} %collective-permute-done.14, bf16[512,1024]{1,0:T(8,128)(2,1)S(1)} %get-tuple-element.62, bf16[288,1024]{1,0:T(8,128)(2,1)S(1)} %fusion.12, bf16[1248,1024]{1,0:T(8,128)(2,1)S(1)} %maximum_convert_fusion), kind=kOutput, calls=%fused_computation.3 | convolution fusion | flops 3233284096 | bytes 8388608 | tf_op jit(solution)/shard_map/dot_general | solution.py:208
  92.0 2.0 collective-permute-start.16
  94.1 2.2 collective-permute-start.15
  96.6 11.1 %collective-permute-done.17 = bf16[512,1024]{1,0:T(8,128)(2,1)S(1)} collective-permute-done((bf16[512,1024]{1,0:T(8,128)(2,1)S(1)}, bf16[512,1024]{1,0:T(8,128)(2,1)S(1)}, u32[]{:S(2)}, u32[]{:S(2)}) %collective-permute-start.17) | collective-permute-done | bytes 1048608 | tf_op jit(solution)/shard_map/ppermute | solution.py:28
  107.7 2.1 collective-permute-done.16
  110.3 3.0 %collective-permute-start.18 = (bf16[384,1024]{1,0:T(8,128)(2,1)S(1)}, bf16[384,1024]{1,0:T(8,128)(2,1)S(1)}, u32[]{:S(2)}, u32[]{:S(2)}) collective-permute-start(bf16[384,1024]{1,0:T(8,128)(2,1)S(1)} %add_convert_fusion.1), channel_id=1, source_target_pairs={{0,12},{4,0},{8,4},{12,8},{1,13},{5,1},{9,5},{13,9},{2,14},{6,2},{... | collective-permute-start | bytes 2359304 | tf_op jit(solution)/shard_map/ppermute | solution.py:20
  113.2 3.8 %convolution_convert_fusion = bf16[1536,1024]{1,0:T(8,128)(2,1)S(1)} fusion(bf16[1536,1024]{1,0:T(8,128)(2,1)S(1)} %pad_maximum_fusion.1, bf16[512,1024]{1,0:T(8,128)(2,1)S(1)} %collective-permute-done.17, bf16[512,1024]{1,0:T(8,128)(2,1)S(1)} %get-tuple-element.63), kind=kOutput, calls=%fused_computation.2 | convolution fusion | flops 3226992640 | bytes 8388608 | tf_op jit(solution)/shard_map/dot_general | solution.py:208
  117.3 3.3 %collective-permute-start.23 = (bf16[192,1024]{1,0:T(8,128)(2,1)S(1)}, bf16[192,1024]{1,0:T(8,128)(2,1)S(1)}, u32[]{:S(2)}, u32[]{:S(2)}) collective-permute-start(bf16[192,1024]{1,0:T(8,128)(2,1)S(1)} %get-tuple-element.101), channel_id=1, source_target_pairs={{0,12},{4,0},{8,4},{12,8},{1,13},{5,1},{9,5},{13,9},{2,14},{6,2},{... | collective-permute-start | bytes 1179656 | tf_op jit(solution)/shard_map/ppermute | solution.py:20
  120.6 6.0 %collective-permute-done.24 = bf16[192,1024]{1,0:T(8,128)(2,1)S(1)} collective-permute-done((bf16[192,1024]{1,0:T(8,128)(2,1)S(1)}, bf16[192,1024]{1,0:T(8,128)(2,1)S(1)}, u32[]{:S(2)}, u32[]{:S(2)}) %collective-permute-start.24) | collective-permute-done | bytes 393248 | tf_op jit(solution)/shard_map/ppermute | solution.py:20
  126.8 4.4 %collective-permute-done.18 = bf16[384,1024]{1,0:T(8,128)(2,1)S(1)} collective-permute-done((bf16[384,1024]{1,0:T(8,128)(2,1)S(1)}, bf16[384,1024]{1,0:T(8,128)(2,1)S(1)}, u32[]{:S(2)}, u32[]{:S(2)}) %collective-permute-start.18) | collective-permute-done | bytes 786464 | tf_op jit(solution)/shard_map/ppermute | solution.py:20
  131.8 5.9 %collective-permute-done.19 = bf16[384,1024]{1,0:T(8,128)(2,1)S(1)} collective-permute-done((bf16[384,1024]{1,0:T(8,128)(2,1)S(1)}, bf16[384,1024]{1,0:T(8,128)(2,1)S(1)}, u32[]{:S(2)}, u32[]{:S(2)}) %collective-permute-start.19) | collective-permute-done | bytes 786464 | tf_op jit(solution)/shard_map/ppermute | solution.py:24
  138.1 3.5 %collective-permute-start.20 = (bf16[96,1024]{1,0:T(8,128)(2,1)S(1)}, bf16[96,1024]{1,0:T(8,128)(2,1)S(1)}, u32[]{:S(2)}, u32[]{:S(2)}) collective-permute-start(bf16[96,1024]{1,0:T(8,128)(2,1)S(1)} %get-tuple-element.110), channel_id=1, source_target_pairs={{0,12},{4,0},{8,4},{12,8},{1,13},{5,1},{9,5},{13,9},{2,14},{6,2},{... | collective-permute-start | bytes 589832 | tf_op jit(solution)/shard_map/ppermute | solution.py:20
  141.9 2.9 %collective-permute-done.20 = bf16[96,1024]{1,0:T(8,128)(2,1)S(1)} collective-permute-done((bf16[96,1024]{1,0:T(8,128)(2,1)S(1)}, bf16[96,1024]{1,0:T(8,128)(2,1)S(1)}, u32[]{:S(2)}, u32[]{:S(2)}) %collective-permute-start.20) | collective-permute-done | bytes 196640 | tf_op jit(solution)/shard_map/ppermute | solution.py:20
  144.9 3.6 %collective-permute-done.21 = bf16[96,1024]{1,0:T(8,128)(2,1)S(1)} collective-permute-done((bf16[96,1024]{1,0:T(8,128)(2,1)S(1)}, bf16[96,1024]{1,0:T(8,128)(2,1)S(1)}, u32[]{:S(2)}, u32[]{:S(2)}) %collective-permute-start.21) | collective-permute-done | bytes 196640 | tf_op jit(solution)/shard_map/ppermute | solution.py:20
  148.7 5.6 %collective-permute-done.22 = bf16[96,1024]{1,0:T(8,128)(2,1)S(1)} collective-permute-done((bf16[96,1024]{1,0:T(8,128)(2,1)S(1)}, bf16[96,1024]{1,0:T(8,128)(2,1)S(1)}, u32[]{:S(2)}, u32[]{:S(2)}) %collective-permute-start.22) | collective-permute-done | bytes 196640 | tf_op jit(solution)/shard_map/ppermute | solution.py:20
  155.5 5.2 %all-to-all-start.1 = ((bf16[8,24,2048]{2,1,0:T(8,128)(2,1)}), bf16[8,24,2048]{2,1,0:T(8,128)(2,1)S(1)}, u32[]{:S(2)}, u32[]{:S(2)}) async-start(bf16[8,24,2048]{2,1,0:T(8,128)(2,1)} %bitcast.8), calls=%async_computation.1 | async-start | bytes 1572864 | tf_op jit(solution)/shard_map/all_to_all | solution.py:169
  160.8 13.1 %all-to-all-done.1 = bf16[8,24,2048]{2,1,0:T(8,128)(2,1)S(1)} async-done(((bf16[8,24,2048]{2,1,0:T(8,128)(2,1)}), bf16[8,24,2048]{2,1,0:T(8,128)(2,1)S(1)}, u32[]{:S(2)}, u32[]{:S(2)}) %all-to-all-start.1) | async-done | bytes 786464 | tf_op jit(solution)/shard_map/all_to_all | solution.py:169
  175.9 2.7 %collective-permute-start.29 = (bf16[64,2048]{1,0:T(8,128)(2,1)S(1)}, bf16[64,2048]{1,0:T(8,128)(2,1)S(1)}, u32[]{:S(2)}, u32[]{:S(2)}) collective-permute-start(bf16[64,2048]{1,0:T(8,128)(2,1)S(1)} %get-tuple-element.113), channel_id=1, source_target_pairs={{0,96},{32,0},{64,32},{96,64},{1,97},{33,1},{65,33},{97,65},{2,98}... | collective-permute-start | bytes 786440 | tf_op jit(solution)/shard_map/ppermute | solution.py:20
  178.6 5.8 %collective-permute-done.28 = bf16[64,2048]{1,0:T(8,128)(2,1)S(1)} collective-permute-done((bf16[64,2048]{1,0:T(8,128)(2,1)S(1)}, bf16[64,2048]{1,0:T(8,128)(2,1)S(1)}, u32[]{:S(2)}, u32[]{:S(2)}) %collective-permute-start.28) | collective-permute-done | bytes 262176 | tf_op jit(solution)/shard_map/ppermute | solution.py:20
  184.4 3.2 %collective-permute-start.31 = (bf16[64,2048]{1,0:T(8,128)(2,1)S(1)}, bf16[64,2048]{1,0:T(8,128)(2,1)S(1)}, u32[]{:S(2)}, u32[]{:S(2)}) collective-permute-start(bf16[64,2048]{1,0:T(8,128)(2,1)S(1)} %get-tuple-element.80), channel_id=1, source_target_pairs={{0,96},{32,0},{64,32},{96,64},{1,97},{33,1},{65,33},{97,65},{2,98}... | collective-permute-start | bytes 786440 | tf_op jit(solution)/shard_map/ppermute | solution.py:20
  187.6 4.9 %collective-permute-done.30 = bf16[64,2048]{1,0:T(8,128)(2,1)S(1)} collective-permute-done((bf16[64,2048]{1,0:T(8,128)(2,1)S(1)}, bf16[64,2048]{1,0:T(8,128)(2,1)S(1)}, u32[]{:S(2)}, u32[]{:S(2)}) %collective-permute-start.30) | collective-permute-done | bytes 262176 | tf_op jit(solution)/shard_map/ppermute | solution.py:20
  192.5 1.3 fusion.17
  193.8 1.3 fusion.18
  196.0 1.3 fusion.46
  197.5 1.3 fusion.1
  198.8 2.3 collective-permute-start.33
  201.2 2.0 collective-permute-start.35
  203.2 4.5 %collective-permute-done.33 = bf16[64,2048]{1,0:T(8,128)(2,1)S(1)} collective-permute-done((bf16[64,2048]{1,0:T(8,128)(2,1)S(1)}, bf16[64,2048]{1,0:T(8,128)(2,1)S(1)}, u32[]{:S(2)}, u32[]{:S(2)}) %collective-permute-start.33) | collective-permute-done | bytes 262176 | tf_op jit(solution)/shard_map/ppermute | solution.py:20
  207.7 1.3 fusion.20
  209.0 1.3 fusion.19
  210.6 1.3 fusion.47
  211.9 1.3 fusion.2
  213.3 3.2 %collective-permute-start.36 = (bf16[64,2048]{1,0:T(8,128)(2,1)S(1)}, bf16[64,2048]{1,0:T(8,128)(2,1)S(1)}, u32[]{:S(2)}, u32[]{:S(2)}) collective-permute-start(bf16[64,2048]{1,0:T(8,128)(2,1)S(1)} %add_convert_fusion.4), channel_id=1, source_target_pairs={{0,96},{32,0},{64,32},{96,64},{1,97},{33,1},{65,33},{97,65},{2,98}... | collective-permute-start | bytes 786440 | tf_op jit(solution)/shard_map/ppermute | solution.py:20
  216.5 1.9 collective-permute-start.37
  218.5 2.7 %collective-permute-done.38 = bf16[64,2048]{1,0:T(8,128)(2,1)S(1)} collective-permute-done((bf16[64,2048]{1,0:T(8,128)(2,1)S(1)}, bf16[64,2048]{1,0:T(8,128)(2,1)S(1)}, u32[]{:S(2)}, u32[]{:S(2)}) %collective-permute-start.38) | collective-permute-done | bytes 262176 | tf_op jit(solution)/shard_map/ppermute | solution.py:20
  221.8 2.7 %collective-permute-done.37 = bf16[64,2048]{1,0:T(8,128)(2,1)S(1)} collective-permute-done((bf16[64,2048]{1,0:T(8,128)(2,1)S(1)}, bf16[64,2048]{1,0:T(8,128)(2,1)S(1)}, u32[]{:S(2)}, u32[]{:S(2)}) %collective-permute-start.37) | collective-permute-done | bytes 262176 | tf_op jit(solution)/shard_map/ppermute | solution.py:20
  224.5 4.6 %collective-permute-done.39 = bf16[64,2048]{1,0:T(8,128)(2,1)S(1)} collective-permute-done((bf16[64,2048]{1,0:T(8,128)(2,1)S(1)}, bf16[64,2048]{1,0:T(8,128)(2,1)S(1)}, u32[]{:S(2)}, u32[]{:S(2)}) %collective-permute-start.39) | collective-permute-done | bytes 262176 | tf_op jit(solution)/shard_map/ppermute | solution.py:20
  (112 shorter events, 15.5 us)
Async XLA Ops:
  0.0 10.0 %copy-start.11 = (f32[1,512]{1,0:T(1,128)S(1)}, f32[1,512]{1,0:T(1,128)}, u32[]{:S(2)}) copy-start(f32[1,512]{1,0:T(1,128)} %param.18) | copy-start | bytes 6148
  0.0 22.7 %collective-permute-start = (bf16[2048,1024]{1,0:T(8,128)(2,1)}, bf16[2048,1024]{1,0:T(8,128)(2,1)}, u32[]{:S(2)}, u32[]{:S(2)}) collective-permute-start(bf16[2048,1024]{1,0:T(8,128)(2,1)} %param.22), channel_id=1, source_target_pairs={{0,16},{16,0},{1,17},{17,1},{2,18},{18,2},{3,19},{19,3},{4,20},{20... | collective-permute-start | bytes 12582920 | tf_op jit(solution)/shard_map/ppermute | solution.py:32
  0.0 22.7 %collective-permute-start.1 = (bf16[1024,2048]{1,0:T(8,128)(2,1)}, bf16[1024,2048]{1,0:T(8,128)(2,1)}, u32[]{:S(2)}, u32[]{:S(2)}) collective-permute-start(bf16[1024,2048]{1,0:T(8,128)(2,1)} %param.24), channel_id=1, source_target_pairs={{0,16},{16,0},{1,17},{17,1},{2,18},{18,2},{3,19},{19,3},{4,20},{20... | collective-permute-start | bytes 12582920 | tf_op jit(solution)/shard_map/ppermute | solution.py:32
  1.3 1.0 copy-start.4
  2.3 0.8 copy-start.6
  3.2 6.3 %copy-start.15 = (f32[1024]{0:T(1024)S(1)}, f32[1024]{0:T(1024)}, u32[]{:S(2)}) copy-start(f32[1024]{0:T(1024)} %param.23) | copy-start | bytes 12292
  3.2 25.3 %copy-start.7 = (bf16[1,512,2048]{2,1,0:T(8,128)(2,1)S(1)}, bf16[1,512,2048]{2,1,0:T(8,128)(2,1)}, u32[]{:S(2)}) copy-start(bf16[1,512,2048]{2,1,0:T(8,128)(2,1)} %param.19) | copy-start | bytes 6291460
  5.0 17.7 %all-to-all-start = ((bf16[8,24,2048]{2,1,0:T(8,128)(2,1)}), bf16[8,24,2048]{2,1,0:T(8,128)(2,1)S(1)}, u32[]{:S(2)}, u32[]{:S(2)}) async-start(bf16[8,24,2048]{2,1,0:T(8,128)(2,1)} %bitcast.2), calls=%async_computation | async-start | bytes 1572864 | tf_op jit(solution)/shard_map/all_to_all | solution.py:169
  9.5 8.1 %collective-permute-start.2 = (f32[1024]{0:T(1024)S(1)}, f32[1024]{0:T(1024)S(1)}, u32[]{:S(2)}, u32[]{:S(2)}) collective-permute-start(f32[1024]{0:T(1024)S(1)} %copy-done.15), channel_id=1, source_target_pairs={{0,16},{16,0},{1,17},{17,1},{2,18},{18,2},{3,19},{19,3},{4,20},{20... | collective-permute-start | bytes 12296 | tf_op jit(solution)/shard_map/ppermute | solution.py:32
  10.0 4.8 %collective-permute-start.9 = (f32[512]{0:T(512)S(1)}, f32[512]{0:T(512)S(1)}, u32[]{:S(2)}, u32[]{:S(2)}) collective-permute-start(f32[512]{0:T(512)S(1)} %bitcast.47), channel_id=1, source_target_pairs={{0,3},{3,0},{1,2},{2,1},{4,7},{7,4},{5,6},{6,5},{8,11},{11,8},{9,1... | collective-permute-start | bytes 6152 | tf_op jit(solution)/shard_map/ppermute | solution.py:28
  14.8 50.1 %collective-permute-start.10 = (bf16[2048,512]{1,0:T(8,128)(2,1)}, bf16[2048,512]{1,0:T(8,128)(2,1)}, u32[]{:S(2)}, u32[]{:S(2)}) collective-permute-start(bf16[2048,512]{1,0:T(8,128)(2,1)} %bitcast.49), channel_id=1, source_target_pairs={{0,3},{3,0},{1,2},{2,1},{4,7},{7,4},{5,6},{6,5},{8,11},{11,8},{9,1... | collective-permute-start | bytes 6291464 | tf_op jit(solution)/shard_map/ppermute | solution.py:28
  22.7 13.0 %collective-permute-start.3 = (bf16[96,2048]{1,0:T(8,128)(2,1)S(1)}, bf16[96,2048]{1,0:T(8,128)(2,1)S(1)}, u32[]{:S(2)}, u32[]{:S(2)}) collective-permute-start(bf16[96,2048]{1,0:T(8,128)(2,1)S(1)} %get-tuple-element.112), channel_id=1, source_target_pairs={{0,4},{4,8},{8,12},{12,0},{1,5},{5,9},{9,13},{13,1},{2,6},{6,10},{... | collective-permute-start | bytes 1179656 | tf_op jit(solution)/shard_map/ppermute | solution.py:20
  24.7 11.0 %collective-permute-start.4 = (bf16[96,2048]{1,0:T(8,128)(2,1)S(1)}, bf16[96,2048]{1,0:T(8,128)(2,1)S(1)}, u32[]{:S(2)}, u32[]{:S(2)}) collective-permute-start(bf16[96,2048]{1,0:T(8,128)(2,1)S(1)} %get-tuple-element.112), channel_id=1, source_target_pairs={{0,12},{4,0},{8,4},{12,8},{1,13},{5,1},{9,5},{13,9},{2,14},{6,2},{... | collective-permute-start | bytes 1179656 | tf_op jit(solution)/shard_map/ppermute | solution.py:20
  26.9 10.4 %collective-permute-start.5 = (bf16[96,2048]{1,0:T(8,128)(2,1)S(1)}, bf16[96,2048]{1,0:T(8,128)(2,1)S(1)}, u32[]{:S(2)}, u32[]{:S(2)}) collective-permute-start(bf16[96,2048]{1,0:T(8,128)(2,1)S(1)} %get-tuple-element.111), channel_id=1, source_target_pairs={{0,1},{1,0},{2,3},{3,2},{4,5},{5,4},{6,7},{7,6},{8,9},{9,8},{10,11... | collective-permute-start | bytes 1179656 | tf_op jit(solution)/shard_map/ppermute | solution.py:24
  35.8 11.4 %collective-permute-start.6 = (bf16[96,2048]{1,0:T(8,128)(2,1)S(1)}, bf16[96,2048]{1,0:T(8,128)(2,1)S(1)}, u32[]{:S(2)}, u32[]{:S(2)}) collective-permute-start(bf16[96,2048]{1,0:T(8,128)(2,1)S(1)} %collective-permute-done.3), channel_id=1, source_target_pairs={{0,4},{4,8},{8,12},{12,0},{1,5},{5,9},{9,13},{13,1},{2,6},{6,10},{... | collective-permute-start | bytes 1179656 | tf_op jit(solution)/shard_map/ppermute | solution.py:20
  37.3 26.4 %collective-permute-start.11 = (bf16[288,2048]{1,0:T(8,128)(2,1)S(1)}, bf16[288,2048]{1,0:T(8,128)(2,1)S(1)}, u32[]{:S(2)}, u32[]{:S(2)}) collective-permute-start(bf16[288,2048]{1,0:T(8,128)(2,1)S(1)} %pad_maximum_fusion.10), channel_id=1, source_target_pairs={{0,1},{1,0},{2,3},{3,2},{4,5},{5,4},{6,7},{7,6},{8,9},{9,8},{10,11... | collective-permute-start | bytes 3538952 | tf_op jit(solution)/shard_map/ppermute | solution.py:24
  38.9 19.7 %collective-permute-start.7 = (bf16[192,2048]{1,0:T(8,128)(2,1)S(1)}, bf16[192,2048]{1,0:T(8,128)(2,1)S(1)}, u32[]{:S(2)}, u32[]{:S(2)}) collective-permute-start(bf16[192,2048]{1,0:T(8,128)(2,1)S(1)} %pad_maximum_fusion.13), channel_id=1, source_target_pairs={{0,12},{4,0},{8,4},{12,8},{1,13},{5,1},{9,5},{13,9},{2,14},{6,2},{... | collective-permute-start | bytes 2359304 | tf_op jit(solution)/shard_map/ppermute | solution.py:20
  47.1 19.0 %collective-permute-start.8 = (bf16[192,2048]{1,0:T(8,128)(2,1)S(1)}, bf16[192,2048]{1,0:T(8,128)(2,1)S(1)}, u32[]{:S(2)}, u32[]{:S(2)}) collective-permute-start(bf16[192,2048]{1,0:T(8,128)(2,1)S(1)} %pad_maximum_fusion.13), channel_id=1, source_target_pairs={{0,4},{4,8},{8,12},{12,0},{1,5},{5,9},{9,13},{13,1},{2,6},{6,10},{... | collective-permute-start | bytes 2359304 | tf_op jit(solution)/shard_map/ppermute | solution.py:20
  49.5 2.0 copy-start.2
  53.6 2.0 copy-start
  55.7 31.6 %collective-permute-start.14 = (bf16[512,1024]{1,0:T(8,128)(2,1)S(1)}, bf16[512,1024]{1,0:T(8,128)(2,1)S(1)}, u32[]{:S(2)}, u32[]{:S(2)}) collective-permute-start(bf16[512,1024]{1,0:T(8,128)(2,1)S(1)} %get-tuple-element.62), channel_id=1, source_target_pairs={{0,3},{3,0},{1,2},{2,1},{4,7},{7,4},{5,6},{6,5},{8,11},{11,8},{9,1... | collective-permute-start | bytes 3145736 | tf_op jit(solution)/shard_map/ppermute | solution.py:28
  58.5 18.1 %collective-permute-start.13 = (bf16[192,2048]{1,0:T(8,128)(2,1)S(1)}, bf16[192,2048]{1,0:T(8,128)(2,1)S(1)}, u32[]{:S(2)}, u32[]{:S(2)}) collective-permute-start(bf16[192,2048]{1,0:T(8,128)(2,1)S(1)} %collective-permute-done.7), channel_id=1, source_target_pairs={{0,12},{4,0},{8,4},{12,8},{1,13},{5,1},{9,5},{13,9},{2,14},{6,2},{... | collective-permute-start | bytes 2359304 | tf_op jit(solution)/shard_map/ppermute | solution.py:20
  61.9 7.2 %copy-start.14 = (bf16[1,2048,512]{2,1,0:T(8,128)(2,1)S(1)}, bf16[1,2048,512]{2,1,0:T(8,128)(2,1)}, u32[]{:S(2)}) copy-start(bf16[1,2048,512]{2,1,0:T(8,128)(2,1)} %param.17) | copy-start | bytes 6291460
  64.9 11.7 %collective-permute-start.12 = (bf16[96,2048]{1,0:T(8,128)(2,1)S(1)}, bf16[96,2048]{1,0:T(8,128)(2,1)S(1)}, u32[]{:S(2)}, u32[]{:S(2)}) collective-permute-start(bf16[96,2048]{1,0:T(8,128)(2,1)S(1)} %collective-permute-done.6), channel_id=1, source_target_pairs={{0,1},{1,0},{2,3},{3,2},{4,5},{5,4},{6,7},{7,6},{8,9},{9,8},{10,11... | collective-permute-start | bytes 1179656 | tf_op jit(solution)/shard_map/ppermute | solution.py:24
  66.2 41.5 %collective-permute-start.17 = (bf16[512,1024]{1,0:T(8,128)(2,1)S(1)}, bf16[512,1024]{1,0:T(8,128)(2,1)S(1)}, u32[]{:S(2)}, u32[]{:S(2)}) collective-permute-start(bf16[512,1024]{1,0:T(8,128)(2,1)S(1)} %get-tuple-element.63), channel_id=1, source_target_pairs={{0,3},{3,0},{1,2},{2,1},{4,7},{7,4},{5,6},{6,5},{8,11},{11,8},{9,1... | collective-permute-start | bytes 3145736 | tf_op jit(solution)/shard_map/ppermute | solution.py:28
  92.0 17.7 %collective-permute-start.16 = (bf16[384,1024]{1,0:T(8,128)(2,1)S(1)}, bf16[384,1024]{1,0:T(8,128)(2,1)S(1)}, u32[]{:S(2)}, u32[]{:S(2)}) collective-permute-start(bf16[384,1024]{1,0:T(8,128)(2,1)S(1)} %pad_maximum_fusion.15), channel_id=1, source_target_pairs={{0,4},{4,8},{8,12},{12,0},{1,5},{5,9},{9,13},{13,1},{2,6},{6,10},{... | collective-permute-start | bytes 2359304 | tf_op jit(solution)/shard_map/ppermute | solution.py:20
  94.1 15.9 %collective-permute-start.15 = (bf16[384,1024]{1,0:T(8,128)(2,1)S(1)}, bf16[384,1024]{1,0:T(8,128)(2,1)S(1)}, u32[]{:S(2)}, u32[]{:S(2)}) collective-permute-start(bf16[384,1024]{1,0:T(8,128)(2,1)S(1)} %pad_maximum_fusion.14), channel_id=1, source_target_pairs={{0,12},{4,0},{8,4},{12,8},{1,13},{5,1},{9,5},{13,9},{2,14},{6,2},{... | collective-permute-start | bytes 2359304 | tf_op jit(solution)/shard_map/ppermute | solution.py:20
  110.3 21.0 %collective-permute-start.18 = (bf16[384,1024]{1,0:T(8,128)(2,1)S(1)}, bf16[384,1024]{1,0:T(8,128)(2,1)S(1)}, u32[]{:S(2)}, u32[]{:S(2)}) collective-permute-start(bf16[384,1024]{1,0:T(8,128)(2,1)S(1)} %add_convert_fusion.1), channel_id=1, source_target_pairs={{0,12},{4,0},{8,4},{12,8},{1,13},{5,1},{9,5},{13,9},{2,14},{6,2},{... | collective-permute-start | bytes 2359304 | tf_op jit(solution)/shard_map/ppermute | solution.py:20
  117.1 9.6 %collective-permute-start.24 = (bf16[192,1024]{1,0:T(8,128)(2,1)S(1)}, bf16[192,1024]{1,0:T(8,128)(2,1)S(1)}, u32[]{:S(2)}, u32[]{:S(2)}) collective-permute-start(bf16[192,1024]{1,0:T(8,128)(2,1)S(1)} %get-tuple-element.102), channel_id=1, source_target_pairs={{0,4},{4,8},{8,12},{12,0},{1,5},{5,9},{9,13},{13,1},{2,6},{6,10},{... | collective-permute-start | bytes 1179656 | tf_op jit(solution)/shard_map/ppermute | solution.py:20
  117.2 20.6 %collective-permute-start.19 = (bf16[384,1024]{1,0:T(8,128)(2,1)S(1)}, bf16[384,1024]{1,0:T(8,128)(2,1)S(1)}, u32[]{:S(2)}, u32[]{:S(2)}) collective-permute-start(bf16[384,1024]{1,0:T(8,128)(2,1)S(1)} %slice.180), channel_id=1, source_target_pairs={{0,1},{1,0},{2,3},{3,2},{4,5},{5,4},{6,7},{7,6},{8,9},{9,8},{10,11... | collective-permute-start | bytes 2359304 | tf_op jit(solution)/shard_map/ppermute | solution.py:24
  117.3 24.3 %collective-permute-start.23 = (bf16[192,1024]{1,0:T(8,128)(2,1)S(1)}, bf16[192,1024]{1,0:T(8,128)(2,1)S(1)}, u32[]{:S(2)}, u32[]{:S(2)}) collective-permute-start(bf16[192,1024]{1,0:T(8,128)(2,1)S(1)} %get-tuple-element.101), channel_id=1, source_target_pairs={{0,12},{4,0},{8,4},{12,8},{1,13},{5,1},{9,5},{13,9},{2,14},{6,2},{... | collective-permute-start | bytes 1179656 | tf_op jit(solution)/shard_map/ppermute | solution.py:20
  126.8 14.9 %collective-permute-start.25 = (bf16[192,1024]{1,0:T(8,128)(2,1)S(1)}, bf16[192,1024]{1,0:T(8,128)(2,1)S(1)}, u32[]{:S(2)}, u32[]{:S(2)}) collective-permute-start(bf16[192,1024]{1,0:T(8,128)(2,1)S(1)} %add_convert_fusion.2), channel_id=1, source_target_pairs={{0,4},{4,8},{8,12},{12,0},{1,5},{5,9},{9,13},{13,1},{2,6},{6,10},{... | collective-permute-start | bytes 1179656 | tf_op jit(solution)/shard_map/ppermute | solution.py:20
  131.7 17.0 %collective-permute-start.27 = (bf16[192,1024]{1,0:T(8,128)(2,1)S(1)}, bf16[192,1024]{1,0:T(8,128)(2,1)S(1)}, u32[]{:S(2)}, u32[]{:S(2)}) collective-permute-start(bf16[192,1024]{1,0:T(8,128)(2,1)S(1)} %slice.203), channel_id=1, source_target_pairs={{0,1},{1,0},{2,3},{3,2},{4,5},{5,4},{6,7},{7,6},{8,9},{9,8},{10,11... | collective-permute-start | bytes 1179656 | tf_op jit(solution)/shard_map/ppermute | solution.py:24
  138.1 6.8 %collective-permute-start.20 = (bf16[96,1024]{1,0:T(8,128)(2,1)S(1)}, bf16[96,1024]{1,0:T(8,128)(2,1)S(1)}, u32[]{:S(2)}, u32[]{:S(2)}) collective-permute-start(bf16[96,1024]{1,0:T(8,128)(2,1)S(1)} %get-tuple-element.110), channel_id=1, source_target_pairs={{0,12},{4,0},{8,4},{12,8},{1,13},{5,1},{9,5},{13,9},{2,14},{6,2},{... | collective-permute-start | bytes 589832 | tf_op jit(solution)/shard_map/ppermute | solution.py:20
  141.6 6.9 %collective-permute-start.21 = (bf16[96,1024]{1,0:T(8,128)(2,1)S(1)}, bf16[96,1024]{1,0:T(8,128)(2,1)S(1)}, u32[]{:S(2)}, u32[]{:S(2)}) collective-permute-start(bf16[96,1024]{1,0:T(8,128)(2,1)S(1)} %get-tuple-element.109), channel_id=1, source_target_pairs={{0,4},{4,8},{8,12},{12,0},{1,5},{5,9},{9,13},{13,1},{2,6},{6,10},{... | collective-permute-start | bytes 589832 | tf_op jit(solution)/shard_map/ppermute | solution.py:20
  141.9 6.9 %collective-permute-start.26 = (bf16[96,1024]{1,0:T(8,128)(2,1)S(1)}, bf16[96,1024]{1,0:T(8,128)(2,1)S(1)}, u32[]{:S(2)}, u32[]{:S(2)}) collective-permute-start(bf16[96,1024]{1,0:T(8,128)(2,1)S(1)} %slice.204), channel_id=1, source_target_pairs={{0,1},{1,0},{2,3},{3,2},{4,5},{5,4},{6,7},{7,6},{8,9},{9,8},{10,11... | collective-permute-start | bytes 589832 | tf_op jit(solution)/shard_map/ppermute | solution.py:24
  148.6 5.7 %collective-permute-start.22 = (bf16[96,1024]{1,0:T(8,128)(2,1)S(1)}, bf16[96,1024]{1,0:T(8,128)(2,1)S(1)}, u32[]{:S(2)}, u32[]{:S(2)}) collective-permute-start(bf16[96,1024]{1,0:T(8,128)(2,1)S(1)} %add_convert_fusion.6), channel_id=1, source_target_pairs={{0,12},{4,0},{8,4},{12,8},{1,13},{5,1},{9,5},{13,9},{2,14},{6,2},{... | collective-permute-start | bytes 589832 | tf_op jit(solution)/shard_map/ppermute | solution.py:20
  154.4 6.3 %copy-start.8 = (f32[8,2048]{1,0:T(8,128)S(1)}, f32[8,2048]{1,0:T(8,128)}, u32[]{:S(2)}) copy-start(f32[8,2048]{1,0:T(8,128)} %param.20) | copy-start | bytes 196612
  154.4 19.5 %copy-start.5 = (bf16[128,2048]{1,0:T(8,128)(2,1)S(1)}, bf16[128,2048]{1,0:T(8,128)(2,1)}, u32[]{:S(2)}) copy-start(bf16[128,2048]{1,0:T(8,128)(2,1)} %tokens_ref.1) | copy-start | bytes 1572868
  155.5 18.3 %all-to-all-start.1 = ((bf16[8,24,2048]{2,1,0:T(8,128)(2,1)}), bf16[8,24,2048]{2,1,0:T(8,128)(2,1)S(1)}, u32[]{:S(2)}, u32[]{:S(2)}) async-start(bf16[8,24,2048]{2,1,0:T(8,128)(2,1)} %bitcast.8), calls=%async_computation.1 | async-start | bytes 1572864 | tf_op jit(solution)/shard_map/all_to_all | solution.py:169
  173.9 1.1 copy-start.9
  173.9 18.7 %copy-start.12 = (bf16[2048,1024]{1,0:T(8,128)(2,1)S(1)}, bf16[2048,1024]{1,0:T(8,128)(2,1)}, u32[]{:S(2)}) copy-start(bf16[2048,1024]{1,0:T(8,128)(2,1)} %param.22) | copy-start | bytes 12582916
  175.2 9.1 %collective-permute-start.28 = (bf16[64,2048]{1,0:T(8,128)(2,1)S(1)}, bf16[64,2048]{1,0:T(8,128)(2,1)S(1)}, u32[]{:S(2)}, u32[]{:S(2)}) collective-permute-start(bf16[64,2048]{1,0:T(8,128)(2,1)S(1)} %get-tuple-element.113), channel_id=1, source_target_pairs={{0,32},{32,64},{64,96},{96,0},{1,33},{33,65},{65,97},{97,1},{2,34}... | collective-permute-start | bytes 786440 | tf_op jit(solution)/shard_map/ppermute | solution.py:20
  175.9 8.5 %collective-permute-start.29 = (bf16[64,2048]{1,0:T(8,128)(2,1)S(1)}, bf16[64,2048]{1,0:T(8,128)(2,1)S(1)}, u32[]{:S(2)}, u32[]{:S(2)}) collective-permute-start(bf16[64,2048]{1,0:T(8,128)(2,1)S(1)} %get-tuple-element.113), channel_id=1, source_target_pairs={{0,96},{32,0},{64,32},{96,64},{1,97},{33,1},{65,33},{97,65},{2,98}... | collective-permute-start | bytes 786440 | tf_op jit(solution)/shard_map/ppermute | solution.py:20
  184.4 8.2 %collective-permute-start.30 = (bf16[64,2048]{1,0:T(8,128)(2,1)S(1)}, bf16[64,2048]{1,0:T(8,128)(2,1)S(1)}, u32[]{:S(2)}, u32[]{:S(2)}) collective-permute-start(bf16[64,2048]{1,0:T(8,128)(2,1)S(1)} %collective-permute-done.28), channel_id=1, source_target_pairs={{0,32},{32,64},{64,96},{96,0},{1,33},{33,65},{65,97},{97,1},{2,34}... | collective-permute-start | bytes 786440 | tf_op jit(solution)/shard_map/ppermute | solution.py:20
  184.4 9.4 %copy-start.3 = (bf16[2048,1024]{1,0:T(8,128)(2,1)S(1)}, bf16[2048,1024]{1,0:T(8,128)(2,1)}, u32[]{:S(2)}) copy-start(bf16[2048,1024]{1,0:T(8,128)(2,1)} %copy-done.2) | copy-start | bytes 12582916
  184.4 10.7 %collective-permute-start.31 = (bf16[64,2048]{1,0:T(8,128)(2,1)S(1)}, bf16[64,2048]{1,0:T(8,128)(2,1)S(1)}, u32[]{:S(2)}, u32[]{:S(2)}) collective-permute-start(bf16[64,2048]{1,0:T(8,128)(2,1)S(1)} %get-tuple-element.80), channel_id=1, source_target_pairs={{0,96},{32,0},{64,32},{96,64},{1,97},{33,1},{65,33},{97,65},{2,98}... | collective-permute-start | bytes 786440 | tf_op jit(solution)/shard_map/ppermute | solution.py:20
  193.8 2.2 copy-start.1
  195.1 2.4 %copy-start.13 = (bf16[1024,2048]{1,0:T(8,128)(2,1)S(1)}, bf16[1024,2048]{1,0:T(8,128)(2,1)}, u32[]{:S(2)}) copy-start(bf16[1024,2048]{1,0:T(8,128)(2,1)} %param.24) | copy-start | bytes 12582916
  195.1 8.1 %collective-permute-start.32 = (bf16[64,2048]{1,0:T(8,128)(2,1)S(1)}, bf16[64,2048]{1,0:T(8,128)(2,1)S(1)}, u32[]{:S(2)}, u32[]{:S(2)}) collective-permute-start(bf16[64,2048]{1,0:T(8,128)(2,1)S(1)} %get-tuple-element.80), channel_id=1, source_target_pairs={{0,32},{32,64},{64,96},{96,0},{1,33},{33,65},{65,97},{97,1},{2,34}... | collective-permute-start | bytes 786440 | tf_op jit(solution)/shard_map/ppermute | solution.py:20
  198.8 8.9 %collective-permute-start.33 = (bf16[64,2048]{1,0:T(8,128)(2,1)S(1)}, bf16[64,2048]{1,0:T(8,128)(2,1)S(1)}, u32[]{:S(2)}, u32[]{:S(2)}) collective-permute-start(bf16[64,2048]{1,0:T(8,128)(2,1)S(1)} %collective-permute-done.31), channel_id=1, source_target_pairs={{0,96},{32,0},{64,32},{96,64},{1,97},{33,1},{65,33},{97,65},{2,98}... | collective-permute-start | bytes 786440 | tf_op jit(solution)/shard_map/ppermute | solution.py:20
  201.1 9.4 %collective-permute-start.34 = (bf16[64,2048]{1,0:T(8,128)(2,1)S(1)}, bf16[64,2048]{1,0:T(8,128)(2,1)S(1)}, u32[]{:S(2)}, u32[]{:S(2)}) collective-permute-start(bf16[64,2048]{1,0:T(8,128)(2,1)S(1)} %get-tuple-element.108), channel_id=1, source_target_pairs={{0,96},{32,0},{64,32},{96,64},{1,97},{33,1},{65,33},{97,65},{2,98}... | collective-permute-start | bytes 786440 | tf_op jit(solution)/shard_map/ppermute | solution.py:20
  201.2 9.4 %collective-permute-start.35 = (bf16[64,2048]{1,0:T(8,128)(2,1)S(1)}, bf16[64,2048]{1,0:T(8,128)(2,1)S(1)}, u32[]{:S(2)}, u32[]{:S(2)}) collective-permute-start(bf16[64,2048]{1,0:T(8,128)(2,1)S(1)} %get-tuple-element.107), channel_id=1, source_target_pairs={{0,32},{32,64},{64,96},{96,0},{1,33},{33,65},{65,97},{97,1},{2,34}... | collective-permute-start | bytes 786440 | tf_op jit(solution)/shard_map/ppermute | solution.py:20
  213.2 16.0 %copy-start.10 = (f32[2048]{0:T(1024)S(1)}, f32[2048]{0:T(1024)}, u32[]{:S(2)}) copy-start(f32[2048]{0:T(1024)} %param.25) | copy-start | bytes 24580
  213.2 7.9 %collective-permute-start.38 = (bf16[64,2048]{1,0:T(8,128)(2,1)S(1)}, bf16[64,2048]{1,0:T(8,128)(2,1)S(1)}, u32[]{:S(2)}, u32[]{:S(2)}) collective-permute-start(bf16[64,2048]{1,0:T(8,128)(2,1)S(1)} %get-tuple-element.106), channel_id=1, source_target_pairs={{0,32},{32,64},{64,96},{96,0},{1,33},{33,65},{65,97},{97,1},{2,34}... | collective-permute-start | bytes 786440 | tf_op jit(solution)/shard_map/ppermute | solution.py:20
  213.3 8.4 %collective-permute-start.36 = (bf16[64,2048]{1,0:T(8,128)(2,1)S(1)}, bf16[64,2048]{1,0:T(8,128)(2,1)S(1)}, u32[]{:S(2)}, u32[]{:S(2)}) collective-permute-start(bf16[64,2048]{1,0:T(8,128)(2,1)S(1)} %add_convert_fusion.4), channel_id=1, source_target_pairs={{0,96},{32,0},{64,32},{96,64},{1,97},{33,1},{65,33},{97,65},{2,98}... | collective-permute-start | bytes 786440 | tf_op jit(solution)/shard_map/ppermute | solution.py:20
  216.5 8.0 %collective-permute-start.37 = (bf16[64,2048]{1,0:T(8,128)(2,1)S(1)}, bf16[64,2048]{1,0:T(8,128)(2,1)S(1)}, u32[]{:S(2)}, u32[]{:S(2)}) collective-permute-start(bf16[64,2048]{1,0:T(8,128)(2,1)S(1)} %get-tuple-element.105), channel_id=1, source_target_pairs={{0,96},{32,0},{64,32},{96,64},{1,97},{33,1},{65,33},{97,65},{2,98}... | collective-permute-start | bytes 786440 | tf_op jit(solution)/shard_map/ppermute | solution.py:20
  221.2 7.9 %collective-permute-start.39 = (bf16[64,2048]{1,0:T(8,128)(2,1)S(1)}, bf16[64,2048]{1,0:T(8,128)(2,1)S(1)}, u32[]{:S(2)}, u32[]{:S(2)}) collective-permute-start(bf16[64,2048]{1,0:T(8,128)(2,1)S(1)} %add_convert_fusion.3), channel_id=1, source_target_pairs={{0,32},{32,64},{64,96},{96,0},{1,33},{33,65},{65,97},{97,1},{2,34}... | collective-permute-start | bytes 786440 | tf_op jit(solution)/shard_map/ppermute | solution.py:20

commit v10 on v9

--- a/solution.py
+++ b/solution.py
@@ -213,26 +213,16 @@
 
     wide = 4 * count
 
-    def ring(weight, weight_pair, hidden, way, after):
-        part = second(hidden, weight, weight_pair)
-        own, prev, foll = (block(part, step) for step in ("own", "prev", "foll"))
-        via = shift(block(part, "far"), "z", -way)
-        if way == 1:
-            foll = shift(foll, "z", 1)
-            via, foll, after = hold(via, foll, after)
-            prev = down(up(prev) + up(via))
-            hidden, prev = hold(hidden, prev)
-            prev = shift(prev, "z", -1)
-        else:
-            prev = shift(prev, "z", -1)
-            via, after = hold(via, after)
-            foll = shift(down(up(foll) + up(via)), "z", 1)
-        return up(own) + up(prev) + up(foll), hidden, after
-
-    sum_l, hidden, right_pair = ring(left, left_pair, hidden, 1, right_pair)
-    out_l = down(sum_l[2 * count :])
-    back_l = swap_column(out_l)
+    part = second(hidden, left, left_pair)
+    own, prev, foll = (block(part, step) for step in ("own", "prev", "foll"))
+    via = shift(block(part, "far"), "z", -1)
+    foll = shift(foll, "z", 1)
     part = second(hidden, right, right_pair)
+    via, foll, _ = hold(via, foll, part)
+    prev = shift(down(up(prev) + up(via)), "z", -1)
+    sum_l = up(own) + up(prev) + up(foll)
+    back_l = swap_column(down(sum_l[2 * count :]))
+
     back = swap_column(part[10 * count : 14 * count])
     via = shift(part[14 * count :], "z", 1)
     prev = shift(part[8 * count : 10 * count], "z", -1)
@@ -242,9 +232,8 @@
     own, prev, foll, far = jnp.split(down(up(part[:wide]) + up(back)), 4)
     via = shift(far, "z", -1)
     foll = shift(foll, "z", 1)
-    via, foll = hold(via, foll)
     prev = shift(down(up(prev) + up(via)), "z", -1)
-    prev, back_b, back_l = hold(prev, back_b, back_l)
+    prev, foll, back_b, back_l = hold(prev, foll, back_b, back_l)
     sum_b = sum_b[:count] + up(back_b)
     sum_l = down(sum_l[: 2 * count] + up(back_l))
     sum_a = up(own) + up(prev) + up(foll)

time: 231 us -> 228 us (0.987)
  waiting for transfers between devices: 116 us -> 106 us
  starting transfers between devices: 65.4 us -> 71.7 us
    ppermute x27, waiting for transfers between devices: 66.6 us -> 57 us  [shift(): lax.ppermute(value, axis, [(i, (i + step) % size) for i in range(size)])]
    ppermute x27, starting transfers between devices: 40 us -> 43.8 us  [shift(): lax.ppermute(value, axis, [(i, (i + step) % size) for i in range(size)])]
    ppermute x6, starting transfers between devices: 3.56 us -> 6.12 us  [swap_column(): return lax.ppermute(value, 'xl', [(0, 1), (1, 0)])]
  transfers between devices with their start and end apart: 42 -> 42, of which waited for: 28 -> 24; matrix products, arithmetic and copies ran while one was open for 12% -> 13% of each run, Pallas kernels for 3% -> 3%
where the time goes in v10:
time: 228 us; the launch traced here: 227 us
  waiting for transfers between devices  106 us (46%)
  starting transfers between devices  71.7 us (31%)
  matrix products  28.3 us (12%)
  local copies, waits for them, and re-layouts  8.45 us (4%)
  Pallas kernels  6.17 us (3%)
  other arithmetic  5.35 us (2%)
    ppermute x27, waiting for transfers between devices, shift(): lax.ppermute(value, axis, [(i, (i + step) % size) for i in range(size)])  57 us
    ppermute x27, starting transfers between devices, shift(): lax.ppermute(value, axis, [(i, (i + step) % size) for i in range(size)])  43.8 us
    ppermute x4, waiting for transfers between devices, swap_blocks(): return lax.ppermute(value, X, [(0, 3), (3, 0), (1, 2), (2, 1)])  22.3 us
    all_to_all x2, waiting for transfers between devices, exchange(): lax.all_to_all(value, ('y', 'core'), split_axis=0, concat_axis=0, tiled=T...  18.2 us
    ppermute x4, starting transfers between devices, swap_blocks(): return lax.ppermute(value, X, [(0, 3), (3, 0), (1, 2), (2, 1)])  11 us
    all_to_all x2, starting transfers between devices, exchange(): lax.all_to_all(value, ('y', 'core'), split_axis=0, concat_axis=0, tiled=T...  9.72 us
    ppermute x6, waiting for transfers between devices, swap_column(): return lax.ppermute(value, 'xl', [(0, 1), (1, 0)])  9.03 us
    dot_general x2, matrix products, first(): jnp.dot(rows, w1, preferred_element_type=jnp.float32) + b1  8.84 us
  transfers between devices with their start and end apart: 42, of which 24 were waited for; matrix products, arithmetic and copies ran while one was open for 13% of the time, Pallas kernels for 3%

profile of v10, /device:TPU:0, one launch (start us, length us, event | category | flops | bytes accessed | tf_op | source)
XLA Modules:
  0.0 226.9 jit_solution(12875265727622499508)
XLA Ops:
  3.2 1.8 dispatch.1
  5.0 4.6 %all-to-all-start = ((bf16[8,24,2048]{2,1,0:T(8,128)(2,1)}), bf16[8,24,2048]{2,1,0:T(8,128)(2,1)S(1)}, u32[]{:S(2)}, u32[]{:S(2)}) async-start(bf16[8,24,2048]{2,1,0:T(8,128)(2,1)} %bitcast.2), calls=%async_computation | async-start | bytes 1572864 | tf_op jit(solution)/shard_map/all_to_all | solution.py:169
  10.0 2.8 %collective-permute-start.9 = (f32[512]{0:T(512)S(1)}, f32[512]{0:T(512)S(1)}, u32[]{:S(2)}, u32[]{:S(2)}) collective-permute-start(f32[512]{0:T(512)S(1)} %bitcast.46), channel_id=1, source_target_pairs={{0,3},{3,0},{1,2},{2,1},{4,7},{7,4},{5,6},{6,5},{8,11},{11,8},{9,1... | collective-permute-start | bytes 6152 | tf_op jit(solution)/shard_map/ppermute | solution.py:28
  12.8 2.0 collective-permute-done.9
  14.8 2.8 %collective-permute-start.10 = (bf16[2048,512]{1,0:T(8,128)(2,1)}, bf16[2048,512]{1,0:T(8,128)(2,1)}, u32[]{:S(2)}, u32[]{:S(2)}) collective-permute-start(bf16[2048,512]{1,0:T(8,128)(2,1)} %bitcast.48), channel_id=1, source_target_pairs={{0,3},{3,0},{1,2},{2,1},{4,7},{7,4},{5,6},{6,5},{8,11},{11,8},{9,1... | collective-permute-start | bytes 6291464 | tf_op jit(solution)/shard_map/ppermute | solution.py:28
  17.6 5.1 %all-to-all-done = bf16[8,24,2048]{2,1,0:T(8,128)(2,1)S(1)} async-done(((bf16[8,24,2048]{2,1,0:T(8,128)(2,1)}), bf16[8,24,2048]{2,1,0:T(8,128)(2,1)S(1)}, u32[]{:S(2)}, u32[]{:S(2)}) %all-to-all-start) | async-done | bytes 786464 | tf_op jit(solution)/shard_map/all_to_all | solution.py:169
  22.8 2.0 collective-permute-start.3
  24.7 2.2 collective-permute-start.4
  26.9 1.5 collective-permute-start.5
  28.7 7.1 %collective-permute-done.3 = bf16[96,2048]{1,0:T(8,128)(2,1)S(1)} collective-permute-done((bf16[96,2048]{1,0:T(8,128)(2,1)S(1)}, bf16[96,2048]{1,0:T(8,128)(2,1)S(1)}, u32[]{:S(2)}, u32[]{:S(2)}) %collective-permute-start.3) | collective-permute-done | bytes 393248 | tf_op jit(solution)/shard_map/ppermute | solution.py:20
  35.9 1.5 collective-permute-done.5
  37.3 1.5 collective-permute-start.11
  38.9 1.9 collective-permute-start.7
  40.8 6.3 %collective-permute-done.6 = bf16[96,2048]{1,0:T(8,128)(2,1)S(1)} collective-permute-done((bf16[96,2048]{1,0:T(8,128)(2,1)S(1)}, bf16[96,2048]{1,0:T(8,128)(2,1)S(1)}, u32[]{:S(2)}, u32[]{:S(2)}) %collective-permute-start.6) | collective-permute-done | bytes 393248 | tf_op jit(solution)/shard_map/ppermute | solution.py:20
  47.3 2.2 on_chip.2
  49.5 2.0 copy-done.2
  51.5 2.2 on_chip.3
  53.7 2.0 copy-done
  55.7 2.8 %collective-permute-start.14 = (bf16[512,1024]{1,0:T(8,128)(2,1)S(1)}, bf16[512,1024]{1,0:T(8,128)(2,1)S(1)}, u32[]{:S(2)}, u32[]{:S(2)}) collective-permute-start(bf16[512,1024]{1,0:T(8,128)(2,1)S(1)} %get-tuple-element.58), channel_id=1, source_target_pairs={{0,3},{3,0},{1,2},{2,1},{4,7},{7,4},{5,6},{6,5},{8,11},{11,8},{9,1... | collective-permute-start | bytes 3145736 | tf_op jit(solution)/shard_map/ppermute | solution.py:28
  58.5 3.3 %collective-permute-start.13 = (bf16[192,2048]{1,0:T(8,128)(2,1)S(1)}, bf16[192,2048]{1,0:T(8,128)(2,1)S(1)}, u32[]{:S(2)}, u32[]{:S(2)}) collective-permute-start(bf16[192,2048]{1,0:T(8,128)(2,1)S(1)} %collective-permute-done.7), channel_id=1, source_target_pairs={{0,12},{4,0},{8,4},{12,8},{1,13},{5,1},{9,5},{13,9},{2,14},{6,2},{... | collective-permute-start | bytes 2359304 | tf_op jit(solution)/shard_map/ppermute | solution.py:20
  61.9 1.8 collective-permute-done.11
  63.7 1.2 collective-permute-done.10
  66.2 2.8 %collective-permute-start.17 = (bf16[512,1024]{1,0:T(8,128)(2,1)S(1)}, bf16[512,1024]{1,0:T(8,128)(2,1)S(1)}, u32[]{:S(2)}, u32[]{:S(2)}) collective-permute-start(bf16[512,1024]{1,0:T(8,128)(2,1)S(1)} %get-tuple-element.59), channel_id=1, source_target_pairs={{0,3},{3,0},{1,2},{2,1},{4,7},{7,4},{5,6},{6,5},{8,11},{11,8},{9,1... | collective-permute-start | bytes 3145736 | tf_op jit(solution)/shard_map/ppermute | solution.py:28
  69.1 5.9 %maximum_convert_fusion = bf16[1248,1024]{1,0:T(8,128)(2,1)S(1)} fusion(bf16[1248,2048]{1,0:T(8,128)(2,1)S(1)} %constant_dynamic-update-slice_fusion, bf16[2048,512]{1,0:T(8,128)(2,1)} %collective-permute-done.10, bf16[2048,512]{1,0:T(8,128)(2,1)S(1)} %bitcast.49, f32[1024]{0:T(1024)S(1)} %pad_maximum_fusion.22), kind=kOutput, calls=%fused_computation | convolution fusion | flops 5246713856 | bytes 11866112 | tf_op jit(solution)/shard_map/dot_general | solution.py:202
  75.0 1.6 collective-permute-done.13
  76.6 3.0 %fusion.12 = bf16[288,1024]{1,0:T(8,128)(2,1)S(1)} fusion(bf16[2048,512]{1,0:T(8,128)(2,1)} %collective-permute-done.10, bf16[2048,512]{1,0:T(8,128)(2,1)S(1)} %bitcast.50, bf16[192,2048]{1,0:T(8,128)(2,1)S(1)} %collective-permute-done.13, bf16[96,2048]{1,0:T(8,128)(2,1)S(1)} %collective-permute-done.12, f32[1024]{0:T(1024)S(1)} %pad_maximum_fusion.22), kind=kOutput, calls=%fused_computation.23 | convolution fusion | flops 1219592192 | bytes 5967872 | tf_op jit(solution)/shard_map/dot_general | solution.py:202
  79.6 7.7 %collective-permute-done.14 = bf16[512,1024]{1,0:T(8,128)(2,1)S(1)} collective-permute-done((bf16[512,1024]{1,0:T(8,128)(2,1)S(1)}, bf16[512,1024]{1,0:T(8,128)(2,1)S(1)}, u32[]{:S(2)}, u32[]{:S(2)}) %collective-permute-start.14) | collective-permute-done | bytes 1048608 | tf_op jit(solution)/shard_map/ppermute | solution.py:28
  87.3 4.3 %convolution_convert_fusion.1 = bf16[1536,1024]{1,0:T(8,128)(2,1)S(1)} fusion(bf16[512,1024]{1,0:T(8,128)(2,1)S(1)} %collective-permute-done.14, bf16[512,1024]{1,0:T(8,128)(2,1)S(1)} %get-tuple-element.58, bf16[288,1024]{1,0:T(8,128)(2,1)S(1)} %fusion.12, bf16[1248,1024]{1,0:T(8,128)(2,1)S(1)} %maximum_convert_fusion), kind=kOutput, calls=%fused_computation.3 | convolution fusion | flops 3233284096 | bytes 8388608 | tf_op jit(solution)/shard_map/dot_general | solution.py:208
  92.1 2.0 collective-permute-start.16
  94.1 2.2 collective-permute-start.15
  96.3 11.3 %collective-permute-done.17 = bf16[512,1024]{1,0:T(8,128)(2,1)S(1)} collective-permute-done((bf16[512,1024]{1,0:T(8,128)(2,1)S(1)}, bf16[512,1024]{1,0:T(8,128)(2,1)S(1)}, u32[]{:S(2)}, u32[]{:S(2)}) %collective-permute-start.17) | collective-permute-done | bytes 1048608 | tf_op jit(solution)/shard_map/ppermute | solution.py:28
  107.7 4.3 %convolution_convert_fusion = bf16[1536,1024]{1,0:T(8,128)(2,1)S(1)} fusion(bf16[512,1024]{1,0:T(8,128)(2,1)S(1)} %collective-permute-done.17, bf16[512,1024]{1,0:T(8,128)(2,1)S(1)} %get-tuple-element.59, bf16[288,1024]{1,0:T(8,128)(2,1)S(1)} %fusion.12, bf16[1248,1024]{1,0:T(8,128)(2,1)S(1)} %maximum_convert_fusion), kind=kOutput, calls=%fused_computation.2 | convolution fusion | flops 3233284096 | bytes 8388608 | tf_op jit(solution)/shard_map/dot_general | solution.py:208
  112.2 2.0 collective-permute-start.24
  114.2 2.2 collective-permute-start.23
  116.7 2.0 collective-permute-start.18
  118.7 4.9 %collective-permute-done.24 = bf16[192,1024]{1,0:T(8,128)(2,1)S(1)} collective-permute-done((bf16[192,1024]{1,0:T(8,128)(2,1)S(1)}, bf16[192,1024]{1,0:T(8,128)(2,1)S(1)}, u32[]{:S(2)}, u32[]{:S(2)}) %collective-permute-start.24) | collective-permute-done | bytes 393248 | tf_op jit(solution)/shard_map/ppermute | solution.py:20
  123.8 5.8 %collective-permute-done.19 = bf16[384,1024]{1,0:T(8,128)(2,1)S(1)} collective-permute-done((bf16[384,1024]{1,0:T(8,128)(2,1)S(1)}, bf16[384,1024]{1,0:T(8,128)(2,1)S(1)}, u32[]{:S(2)}, u32[]{:S(2)}) %collective-permute-start.19) | collective-permute-done | bytes 786464 | tf_op jit(solution)/shard_map/ppermute | solution.py:24
  129.9 4.1 %collective-permute-start.20 = (bf16[96,1024]{1,0:T(8,128)(2,1)S(1)}, bf16[96,1024]{1,0:T(8,128)(2,1)S(1)}, u32[]{:S(2)}, u32[]{:S(2)}) collective-permute-start(bf16[96,1024]{1,0:T(8,128)(2,1)S(1)} %get-tuple-element.102), channel_id=1, source_target_pairs={{0,12},{4,0},{8,4},{12,8},{1,13},{5,1},{9,5},{13,9},{2,14},{6,2},{... | collective-permute-start | bytes 589832 | tf_op jit(solution)/shard_map/ppermute | solution.py:20
  135.2 6.9 %collective-permute-done.18 = bf16[384,1024]{1,0:T(8,128)(2,1)S(1)} collective-permute-done((bf16[384,1024]{1,0:T(8,128)(2,1)S(1)}, bf16[384,1024]{1,0:T(8,128)(2,1)S(1)}, u32[]{:S(2)}, u32[]{:S(2)}) %collective-permute-start.18) | collective-permute-done | bytes 786464 | tf_op jit(solution)/shard_map/ppermute | solution.py:20
  142.5 1.8 collective-permute-start.27
  144.4 3.6 %collective-permute-start.21 = (bf16[96,1024]{1,0:T(8,128)(2,1)S(1)}, bf16[96,1024]{1,0:T(8,128)(2,1)S(1)}, u32[]{:S(2)}, u32[]{:S(2)}) collective-permute-start(bf16[96,1024]{1,0:T(8,128)(2,1)S(1)} %add_convert_fusion.6), channel_id=1, source_target_pairs={{0,12},{4,0},{8,4},{12,8},{1,13},{5,1},{9,5},{13,9},{2,14},{6,2},{... | collective-permute-start | bytes 589832 | tf_op jit(solution)/shard_map/ppermute | solution.py:20
  148.0 3.2 %collective-permute-done.21 = bf16[96,1024]{1,0:T(8,128)(2,1)S(1)} collective-permute-done((bf16[96,1024]{1,0:T(8,128)(2,1)S(1)}, bf16[96,1024]{1,0:T(8,128)(2,1)S(1)}, u32[]{:S(2)}, u32[]{:S(2)}) %collective-permute-start.21) | collective-permute-done | bytes 196640 | tf_op jit(solution)/shard_map/ppermute | solution.py:20
  152.4 5.2 %all-to-all-start.1 = ((bf16[8,24,2048]{2,1,0:T(8,128)(2,1)}), bf16[8,24,2048]{2,1,0:T(8,128)(2,1)S(1)}, u32[]{:S(2)}, u32[]{:S(2)}) async-start(bf16[8,24,2048]{2,1,0:T(8,128)(2,1)} %bitcast.8), calls=%async_computation.1 | async-start | bytes 1572864 | tf_op jit(solution)/shard_map/all_to_all | solution.py:169
  157.7 13.1 %all-to-all-done.1 = bf16[8,24,2048]{2,1,0:T(8,128)(2,1)S(1)} async-done(((bf16[8,24,2048]{2,1,0:T(8,128)(2,1)}), bf16[8,24,2048]{2,1,0:T(8,128)(2,1)S(1)}, u32[]{:S(2)}, u32[]{:S(2)}) %all-to-all-start.1) | async-done | bytes 786464 | tf_op jit(solution)/shard_map/all_to_all | solution.py:169
  172.8 2.7 %collective-permute-start.29 = (bf16[64,2048]{1,0:T(8,128)(2,1)S(1)}, bf16[64,2048]{1,0:T(8,128)(2,1)S(1)}, u32[]{:S(2)}, u32[]{:S(2)}) collective-permute-start(bf16[64,2048]{1,0:T(8,128)(2,1)S(1)} %get-tuple-element.105), channel_id=1, source_target_pairs={{0,96},{32,0},{64,32},{96,64},{1,97},{33,1},{65,33},{97,65},{2,98}... | collective-permute-start | bytes 786440 | tf_op jit(solution)/shard_map/ppermute | solution.py:20
  175.4 5.8 %collective-permute-done.28 = bf16[64,2048]{1,0:T(8,128)(2,1)S(1)} collective-permute-done((bf16[64,2048]{1,0:T(8,128)(2,1)S(1)}, bf16[64,2048]{1,0:T(8,128)(2,1)S(1)}, u32[]{:S(2)}, u32[]{:S(2)}) %collective-permute-start.28) | collective-permute-done | bytes 262176 | tf_op jit(solution)/shard_map/ppermute | solution.py:20
  181.3 3.2 %collective-permute-start.31 = (bf16[64,2048]{1,0:T(8,128)(2,1)S(1)}, bf16[64,2048]{1,0:T(8,128)(2,1)S(1)}, u32[]{:S(2)}, u32[]{:S(2)}) collective-permute-start(bf16[64,2048]{1,0:T(8,128)(2,1)S(1)} %get-tuple-element.72), channel_id=1, source_target_pairs={{0,96},{32,0},{64,32},{96,64},{1,97},{33,1},{65,33},{97,65},{2,98}... | collective-permute-start | bytes 786440 | tf_op jit(solution)/shard_map/ppermute | solution.py:20
  184.5 4.9 %collective-permute-done.30 = bf16[64,2048]{1,0:T(8,128)(2,1)S(1)} collective-permute-done((bf16[64,2048]{1,0:T(8,128)(2,1)S(1)}, bf16[64,2048]{1,0:T(8,128)(2,1)S(1)}, u32[]{:S(2)}, u32[]{:S(2)}) %collective-permute-start.30) | collective-permute-done | bytes 262176 | tf_op jit(solution)/shard_map/ppermute | solution.py:20
  189.4 1.2 fusion.17
  190.7 1.3 fusion.18
  192.9 1.2 fusion.46
  194.4 1.3 fusion.1
  195.6 2.2 collective-permute-start.33
  198.0 2.0 collective-permute-start.35
  200.0 4.5 %collective-permute-done.33 = bf16[64,2048]{1,0:T(8,128)(2,1)S(1)} collective-permute-done((bf16[64,2048]{1,0:T(8,128)(2,1)S(1)}, bf16[64,2048]{1,0:T(8,128)(2,1)S(1)}, u32[]{:S(2)}, u32[]{:S(2)}) %collective-permute-start.33) | collective-permute-done | bytes 262176 | tf_op jit(solution)/shard_map/ppermute | solution.py:20
  204.5 1.2 fusion.20
  205.8 1.3 fusion.19
  207.4 1.2 fusion.47
  208.7 1.3 fusion.2
  210.1 3.2 %collective-permute-start.36 = (bf16[64,2048]{1,0:T(8,128)(2,1)S(1)}, bf16[64,2048]{1,0:T(8,128)(2,1)S(1)}, u32[]{:S(2)}, u32[]{:S(2)}) collective-permute-start(bf16[64,2048]{1,0:T(8,128)(2,1)S(1)} %add_convert_fusion.4), channel_id=1, source_target_pairs={{0,96},{32,0},{64,32},{96,64},{1,97},{33,1},{65,33},{97,65},{2,98}... | collective-permute-start | bytes 786440 | tf_op jit(solution)/shard_map/ppermute | solution.py:20
  213.3 1.9 collective-permute-start.37
  215.2 2.7 %collective-permute-done.38 = bf16[64,2048]{1,0:T(8,128)(2,1)S(1)} collective-permute-done((bf16[64,2048]{1,0:T(8,128)(2,1)S(1)}, bf16[64,2048]{1,0:T(8,128)(2,1)S(1)}, u32[]{:S(2)}, u32[]{:S(2)}) %collective-permute-start.38) | collective-permute-done | bytes 262176 | tf_op jit(solution)/shard_map/ppermute | solution.py:20
  218.5 2.7 %collective-permute-done.37 = bf16[64,2048]{1,0:T(8,128)(2,1)S(1)} collective-permute-done((bf16[64,2048]{1,0:T(8,128)(2,1)S(1)}, bf16[64,2048]{1,0:T(8,128)(2,1)S(1)}, u32[]{:S(2)}, u32[]{:S(2)}) %collective-permute-start.37) | collective-permute-done | bytes 262176 | tf_op jit(solution)/shard_map/ppermute | solution.py:20
  221.3 4.6 %collective-permute-done.39 = bf16[64,2048]{1,0:T(8,128)(2,1)S(1)} collective-permute-done((bf16[64,2048]{1,0:T(8,128)(2,1)S(1)}, bf16[64,2048]{1,0:T(8,128)(2,1)S(1)}, u32[]{:S(2)}, u32[]{:S(2)}) %collective-permute-start.39) | collective-permute-done | bytes 262176 | tf_op jit(solution)/shard_map/ppermute | solution.py:20
  (111 shorter events, 15.7 us)
Async XLA Ops:
  0.0 10.0 %copy-start.11 = (f32[1,512]{1,0:T(1,128)S(1)}, f32[1,512]{1,0:T(1,128)}, u32[]{:S(2)}) copy-start(f32[1,512]{1,0:T(1,128)} %param.18) | copy-start | bytes 6148
  0.0 22.7 %collective-permute-start = (bf16[2048,1024]{1,0:T(8,128)(2,1)}, bf16[2048,1024]{1,0:T(8,128)(2,1)}, u32[]{:S(2)}, u32[]{:S(2)}) collective-permute-start(bf16[2048,1024]{1,0:T(8,128)(2,1)} %param.22), channel_id=1, source_target_pairs={{0,16},{16,0},{1,17},{17,1},{2,18},{18,2},{3,19},{19,3},{4,20},{20... | collective-permute-start | bytes 12582920 | tf_op jit(solution)/shard_map/ppermute | solution.py:32
  0.0 22.7 %collective-permute-start.1 = (bf16[1024,2048]{1,0:T(8,128)(2,1)}, bf16[1024,2048]{1,0:T(8,128)(2,1)}, u32[]{:S(2)}, u32[]{:S(2)}) collective-permute-start(bf16[1024,2048]{1,0:T(8,128)(2,1)} %param.24), channel_id=1, source_target_pairs={{0,16},{16,0},{1,17},{17,1},{2,18},{18,2},{3,19},{19,3},{4,20},{20... | collective-permute-start | bytes 12582920 | tf_op jit(solution)/shard_map/ppermute | solution.py:32
  1.3 1.0 copy-start.4
  2.3 0.8 copy-start.6
  3.2 6.3 %copy-start.15 = (f32[1024]{0:T(1024)S(1)}, f32[1024]{0:T(1024)}, u32[]{:S(2)}) copy-start(f32[1024]{0:T(1024)} %param.23) | copy-start | bytes 12292
  3.2 25.3 %copy-start.7 = (bf16[1,512,2048]{2,1,0:T(8,128)(2,1)S(1)}, bf16[1,512,2048]{2,1,0:T(8,128)(2,1)}, u32[]{:S(2)}) copy-start(bf16[1,512,2048]{2,1,0:T(8,128)(2,1)} %param.19) | copy-start | bytes 6291460
  5.0 17.7 %all-to-all-start = ((bf16[8,24,2048]{2,1,0:T(8,128)(2,1)}), bf16[8,24,2048]{2,1,0:T(8,128)(2,1)S(1)}, u32[]{:S(2)}, u32[]{:S(2)}) async-start(bf16[8,24,2048]{2,1,0:T(8,128)(2,1)} %bitcast.2), calls=%async_computation | async-start | bytes 1572864 | tf_op jit(solution)/shard_map/all_to_all | solution.py:169
  9.5 8.1 %collective-permute-start.2 = (f32[1024]{0:T(1024)S(1)}, f32[1024]{0:T(1024)S(1)}, u32[]{:S(2)}, u32[]{:S(2)}) collective-permute-start(f32[1024]{0:T(1024)S(1)} %copy-done.15), channel_id=1, source_target_pairs={{0,16},{16,0},{1,17},{17,1},{2,18},{18,2},{3,19},{19,3},{4,20},{20... | collective-permute-start | bytes 12296 | tf_op jit(solution)/shard_map/ppermute | solution.py:32
  10.0 4.8 %collective-permute-start.9 = (f32[512]{0:T(512)S(1)}, f32[512]{0:T(512)S(1)}, u32[]{:S(2)}, u32[]{:S(2)}) collective-permute-start(f32[512]{0:T(512)S(1)} %bitcast.46), channel_id=1, source_target_pairs={{0,3},{3,0},{1,2},{2,1},{4,7},{7,4},{5,6},{6,5},{8,11},{11,8},{9,1... | collective-permute-start | bytes 6152 | tf_op jit(solution)/shard_map/ppermute | solution.py:28
  14.8 50.1 %collective-permute-start.10 = (bf16[2048,512]{1,0:T(8,128)(2,1)}, bf16[2048,512]{1,0:T(8,128)(2,1)}, u32[]{:S(2)}, u32[]{:S(2)}) collective-permute-start(bf16[2048,512]{1,0:T(8,128)(2,1)} %bitcast.48), channel_id=1, source_target_pairs={{0,3},{3,0},{1,2},{2,1},{4,7},{7,4},{5,6},{6,5},{8,11},{11,8},{9,1... | collective-permute-start | bytes 6291464 | tf_op jit(solution)/shard_map/ppermute | solution.py:28
  22.8 13.0 %collective-permute-start.3 = (bf16[96,2048]{1,0:T(8,128)(2,1)S(1)}, bf16[96,2048]{1,0:T(8,128)(2,1)S(1)}, u32[]{:S(2)}, u32[]{:S(2)}) collective-permute-start(bf16[96,2048]{1,0:T(8,128)(2,1)S(1)} %get-tuple-element.104), channel_id=1, source_target_pairs={{0,4},{4,8},{8,12},{12,0},{1,5},{5,9},{9,13},{13,1},{2,6},{6,10},{... | collective-permute-start | bytes 1179656 | tf_op jit(solution)/shard_map/ppermute | solution.py:20
  24.7 11.0 %collective-permute-start.4 = (bf16[96,2048]{1,0:T(8,128)(2,1)S(1)}, bf16[96,2048]{1,0:T(8,128)(2,1)S(1)}, u32[]{:S(2)}, u32[]{:S(2)}) collective-permute-start(bf16[96,2048]{1,0:T(8,128)(2,1)S(1)} %get-tuple-element.104), channel_id=1, source_target_pairs={{0,12},{4,0},{8,4},{12,8},{1,13},{5,1},{9,5},{13,9},{2,14},{6,2},{... | collective-permute-start | bytes 1179656 | tf_op jit(solution)/shard_map/ppermute | solution.py:20
  26.9 10.4 %collective-permute-start.5 = (bf16[96,2048]{1,0:T(8,128)(2,1)S(1)}, bf16[96,2048]{1,0:T(8,128)(2,1)S(1)}, u32[]{:S(2)}, u32[]{:S(2)}) collective-permute-start(bf16[96,2048]{1,0:T(8,128)(2,1)S(1)} %get-tuple-element.103), channel_id=1, source_target_pairs={{0,1},{1,0},{2,3},{3,2},{4,5},{5,4},{6,7},{7,6},{8,9},{9,8},{10,11... | collective-permute-start | bytes 1179656 | tf_op jit(solution)/shard_map/ppermute | solution.py:24
  35.8 11.4 %collective-permute-start.6 = (bf16[96,2048]{1,0:T(8,128)(2,1)S(1)}, bf16[96,2048]{1,0:T(8,128)(2,1)S(1)}, u32[]{:S(2)}, u32[]{:S(2)}) collective-permute-start(bf16[96,2048]{1,0:T(8,128)(2,1)S(1)} %collective-permute-done.3), channel_id=1, source_target_pairs={{0,4},{4,8},{8,12},{12,0},{1,5},{5,9},{9,13},{13,1},{2,6},{6,10},{... | collective-permute-start | bytes 1179656 | tf_op jit(solution)/shard_map/ppermute | solution.py:20
  37.3 26.4 %collective-permute-start.11 = (bf16[288,2048]{1,0:T(8,128)(2,1)S(1)}, bf16[288,2048]{1,0:T(8,128)(2,1)S(1)}, u32[]{:S(2)}, u32[]{:S(2)}) collective-permute-start(bf16[288,2048]{1,0:T(8,128)(2,1)S(1)} %pad_maximum_fusion.12), channel_id=1, source_target_pairs={{0,1},{1,0},{2,3},{3,2},{4,5},{5,4},{6,7},{7,6},{8,9},{9,8},{10,11... | collective-permute-start | bytes 3538952 | tf_op jit(solution)/shard_map/ppermute | solution.py:24
  38.9 19.6 %collective-permute-start.7 = (bf16[192,2048]{1,0:T(8,128)(2,1)S(1)}, bf16[192,2048]{1,0:T(8,128)(2,1)S(1)}, u32[]{:S(2)}, u32[]{:S(2)}) collective-permute-start(bf16[192,2048]{1,0:T(8,128)(2,1)S(1)} %pad_maximum_fusion.15), channel_id=1, source_target_pairs={{0,12},{4,0},{8,4},{12,8},{1,13},{5,1},{9,5},{13,9},{2,14},{6,2},{... | collective-permute-start | bytes 2359304 | tf_op jit(solution)/shard_map/ppermute | solution.py:20
  47.2 19.0 %collective-permute-start.8 = (bf16[192,2048]{1,0:T(8,128)(2,1)S(1)}, bf16[192,2048]{1,0:T(8,128)(2,1)S(1)}, u32[]{:S(2)}, u32[]{:S(2)}) collective-permute-start(bf16[192,2048]{1,0:T(8,128)(2,1)S(1)} %pad_maximum_fusion.15), channel_id=1, source_target_pairs={{0,4},{4,8},{8,12},{12,0},{1,5},{5,9},{9,13},{13,1},{2,6},{6,10},{... | collective-permute-start | bytes 2359304 | tf_op jit(solution)/shard_map/ppermute | solution.py:20
  49.5 2.0 copy-start.2
  53.7 2.0 copy-start
  55.7 31.6 %collective-permute-start.14 = (bf16[512,1024]{1,0:T(8,128)(2,1)S(1)}, bf16[512,1024]{1,0:T(8,128)(2,1)S(1)}, u32[]{:S(2)}, u32[]{:S(2)}) collective-permute-start(bf16[512,1024]{1,0:T(8,128)(2,1)S(1)} %get-tuple-element.58), channel_id=1, source_target_pairs={{0,3},{3,0},{1,2},{2,1},{4,7},{7,4},{5,6},{6,5},{8,11},{11,8},{9,1... | collective-permute-start | bytes 3145736 | tf_op jit(solution)/shard_map/ppermute | solution.py:28
  58.5 18.1 %collective-permute-start.13 = (bf16[192,2048]{1,0:T(8,128)(2,1)S(1)}, bf16[192,2048]{1,0:T(8,128)(2,1)S(1)}, u32[]{:S(2)}, u32[]{:S(2)}) collective-permute-start(bf16[192,2048]{1,0:T(8,128)(2,1)S(1)} %collective-permute-done.7), channel_id=1, source_target_pairs={{0,12},{4,0},{8,4},{12,8},{1,13},{5,1},{9,5},{13,9},{2,14},{6,2},{... | collective-permute-start | bytes 2359304 | tf_op jit(solution)/shard_map/ppermute | solution.py:20
  61.9 7.2 %copy-start.14 = (bf16[1,2048,512]{2,1,0:T(8,128)(2,1)S(1)}, bf16[1,2048,512]{2,1,0:T(8,128)(2,1)}, u32[]{:S(2)}) copy-start(bf16[1,2048,512]{2,1,0:T(8,128)(2,1)} %param.17) | copy-start | bytes 6291460
  64.9 11.7 %collective-permute-start.12 = (bf16[96,2048]{1,0:T(8,128)(2,1)S(1)}, bf16[96,2048]{1,0:T(8,128)(2,1)S(1)}, u32[]{:S(2)}, u32[]{:S(2)}) collective-permute-start(bf16[96,2048]{1,0:T(8,128)(2,1)S(1)} %collective-permute-done.6), channel_id=1, source_target_pairs={{0,1},{1,0},{2,3},{3,2},{4,5},{5,4},{6,7},{7,6},{8,9},{9,8},{10,11... | collective-permute-start | bytes 1179656 | tf_op jit(solution)/shard_map/ppermute | solution.py:24
  66.2 41.5 %collective-permute-start.17 = (bf16[512,1024]{1,0:T(8,128)(2,1)S(1)}, bf16[512,1024]{1,0:T(8,128)(2,1)S(1)}, u32[]{:S(2)}, u32[]{:S(2)}) collective-permute-start(bf16[512,1024]{1,0:T(8,128)(2,1)S(1)} %get-tuple-element.59), channel_id=1, source_target_pairs={{0,3},{3,0},{1,2},{2,1},{4,7},{7,4},{5,6},{6,5},{8,11},{11,8},{9,1... | collective-permute-start | bytes 3145736 | tf_op jit(solution)/shard_map/ppermute | solution.py:28
  92.1 24.3 %collective-permute-start.16 = (bf16[384,1024]{1,0:T(8,128)(2,1)S(1)}, bf16[384,1024]{1,0:T(8,128)(2,1)S(1)}, u32[]{:S(2)}, u32[]{:S(2)}) collective-permute-start(bf16[384,1024]{1,0:T(8,128)(2,1)S(1)} %pad_maximum_fusion.17), channel_id=1, source_target_pairs={{0,4},{4,8},{8,12},{12,0},{1,5},{5,9},{9,13},{13,1},{2,6},{6,10},{... | collective-permute-start | bytes 2359304 | tf_op jit(solution)/shard_map/ppermute | solution.py:20
  94.1 22.3 %collective-permute-start.15 = (bf16[384,1024]{1,0:T(8,128)(2,1)S(1)}, bf16[384,1024]{1,0:T(8,128)(2,1)S(1)}, u32[]{:S(2)}, u32[]{:S(2)}) collective-permute-start(bf16[384,1024]{1,0:T(8,128)(2,1)S(1)} %pad_maximum_fusion.16), channel_id=1, source_target_pairs={{0,12},{4,0},{8,4},{12,8},{1,13},{5,1},{9,5},{13,9},{2,14},{6,2},{... | collective-permute-start | bytes 2359304 | tf_op jit(solution)/shard_map/ppermute | solution.py:20
  112.0 17.5 %collective-permute-start.19 = (bf16[384,1024]{1,0:T(8,128)(2,1)S(1)}, bf16[384,1024]{1,0:T(8,128)(2,1)S(1)}, u32[]{:S(2)}, u32[]{:S(2)}) collective-permute-start(bf16[384,1024]{1,0:T(8,128)(2,1)S(1)} %slice.180), channel_id=1, source_target_pairs={{0,1},{1,0},{2,3},{3,2},{4,5},{5,4},{6,7},{7,6},{8,9},{9,8},{10,11... | collective-permute-start | bytes 2359304 | tf_op jit(solution)/shard_map/ppermute | solution.py:24
  112.2 11.4 %collective-permute-start.24 = (bf16[192,1024]{1,0:T(8,128)(2,1)S(1)}, bf16[192,1024]{1,0:T(8,128)(2,1)S(1)}, u32[]{:S(2)}, u32[]{:S(2)}) collective-permute-start(bf16[192,1024]{1,0:T(8,128)(2,1)S(1)} %get-tuple-element.94), channel_id=1, source_target_pairs={{0,4},{4,8},{8,12},{12,0},{1,5},{5,9},{9,13},{13,1},{2,6},{6,10},{... | collective-permute-start | bytes 1179656 | tf_op jit(solution)/shard_map/ppermute | solution.py:20
  114.2 19.9 %collective-permute-start.23 = (bf16[192,1024]{1,0:T(8,128)(2,1)S(1)}, bf16[192,1024]{1,0:T(8,128)(2,1)S(1)}, u32[]{:S(2)}, u32[]{:S(2)}) collective-permute-start(bf16[192,1024]{1,0:T(8,128)(2,1)S(1)} %get-tuple-element.93), channel_id=1, source_target_pairs={{0,12},{4,0},{8,4},{12,8},{1,13},{5,1},{9,5},{13,9},{2,14},{6,2},{... | collective-permute-start | bytes 1179656 | tf_op jit(solution)/shard_map/ppermute | solution.py:20
  116.7 25.4 %collective-permute-start.18 = (bf16[384,1024]{1,0:T(8,128)(2,1)S(1)}, bf16[384,1024]{1,0:T(8,128)(2,1)S(1)}, u32[]{:S(2)}, u32[]{:S(2)}) collective-permute-start(bf16[384,1024]{1,0:T(8,128)(2,1)S(1)} %add_convert_fusion.1), channel_id=1, source_target_pairs={{0,12},{4,0},{8,4},{12,8},{1,13},{5,1},{9,5},{13,9},{2,14},{6,2},{... | collective-permute-start | bytes 2359304 | tf_op jit(solution)/shard_map/ppermute | solution.py:20
  123.7 10.3 %collective-permute-start.25 = (bf16[192,1024]{1,0:T(8,128)(2,1)S(1)}, bf16[192,1024]{1,0:T(8,128)(2,1)S(1)}, u32[]{:S(2)}, u32[]{:S(2)}) collective-permute-start(bf16[192,1024]{1,0:T(8,128)(2,1)S(1)} %add_convert_fusion.2), channel_id=1, source_target_pairs={{0,4},{4,8},{8,12},{12,0},{1,5},{5,9},{9,13},{13,1},{2,6},{6,10},{... | collective-permute-start | bytes 1179656 | tf_op jit(solution)/shard_map/ppermute | solution.py:20
  129.9 14.5 %collective-permute-start.20 = (bf16[96,1024]{1,0:T(8,128)(2,1)S(1)}, bf16[96,1024]{1,0:T(8,128)(2,1)S(1)}, u32[]{:S(2)}, u32[]{:S(2)}) collective-permute-start(bf16[96,1024]{1,0:T(8,128)(2,1)S(1)} %get-tuple-element.102), channel_id=1, source_target_pairs={{0,12},{4,0},{8,4},{12,8},{1,13},{5,1},{9,5},{13,9},{2,14},{6,2},{... | collective-permute-start | bytes 589832 | tf_op jit(solution)/shard_map/ppermute | solution.py:20
  134.0 14.0 %collective-permute-start.22 = (bf16[96,1024]{1,0:T(8,128)(2,1)S(1)}, bf16[96,1024]{1,0:T(8,128)(2,1)S(1)}, u32[]{:S(2)}, u32[]{:S(2)}) collective-permute-start(bf16[96,1024]{1,0:T(8,128)(2,1)S(1)} %get-tuple-element.101), channel_id=1, source_target_pairs={{0,4},{4,8},{8,12},{12,0},{1,5},{5,9},{9,13},{13,1},{2,6},{6,10},{... | collective-permute-start | bytes 589832 | tf_op jit(solution)/shard_map/ppermute | solution.py:20
  134.3 13.7 %collective-permute-start.26 = (bf16[96,1024]{1,0:T(8,128)(2,1)S(1)}, bf16[96,1024]{1,0:T(8,128)(2,1)S(1)}, u32[]{:S(2)}, u32[]{:S(2)}) collective-permute-start(bf16[96,1024]{1,0:T(8,128)(2,1)S(1)} %slice.204), channel_id=1, source_target_pairs={{0,1},{1,0},{2,3},{3,2},{4,5},{5,4},{6,7},{7,6},{8,9},{9,8},{10,11... | collective-permute-start | bytes 589832 | tf_op jit(solution)/shard_map/ppermute | solution.py:24
  142.5 8.7 %collective-permute-start.27 = (bf16[192,1024]{1,0:T(8,128)(2,1)S(1)}, bf16[192,1024]{1,0:T(8,128)(2,1)S(1)}, u32[]{:S(2)}, u32[]{:S(2)}) collective-permute-start(bf16[192,1024]{1,0:T(8,128)(2,1)S(1)} %slice.203), channel_id=1, source_target_pairs={{0,1},{1,0},{2,3},{3,2},{4,5},{5,4},{6,7},{7,6},{8,9},{9,8},{10,11... | collective-permute-start | bytes 1179656 | tf_op jit(solution)/shard_map/ppermute | solution.py:24
  144.4 6.8 %collective-permute-start.21 = (bf16[96,1024]{1,0:T(8,128)(2,1)S(1)}, bf16[96,1024]{1,0:T(8,128)(2,1)S(1)}, u32[]{:S(2)}, u32[]{:S(2)}) collective-permute-start(bf16[96,1024]{1,0:T(8,128)(2,1)S(1)} %add_convert_fusion.6), channel_id=1, source_target_pairs={{0,12},{4,0},{8,4},{12,8},{1,13},{5,1},{9,5},{13,9},{2,14},{6,2},{... | collective-permute-start | bytes 589832 | tf_op jit(solution)/shard_map/ppermute | solution.py:20
  151.3 6.3 %copy-start.8 = (f32[8,2048]{1,0:T(8,128)S(1)}, f32[8,2048]{1,0:T(8,128)}, u32[]{:S(2)}) copy-start(f32[8,2048]{1,0:T(8,128)} %param.20) | copy-start | bytes 196612
  151.3 19.4 %copy-start.5 = (bf16[128,2048]{1,0:T(8,128)(2,1)S(1)}, bf16[128,2048]{1,0:T(8,128)(2,1)}, u32[]{:S(2)}) copy-start(bf16[128,2048]{1,0:T(8,128)(2,1)} %tokens_ref.1) | copy-start | bytes 1572868
  152.4 18.3 %all-to-all-start.1 = ((bf16[8,24,2048]{2,1,0:T(8,128)(2,1)}), bf16[8,24,2048]{2,1,0:T(8,128)(2,1)S(1)}, u32[]{:S(2)}, u32[]{:S(2)}) async-start(bf16[8,24,2048]{2,1,0:T(8,128)(2,1)} %bitcast.8), calls=%async_computation.1 | async-start | bytes 1572864 | tf_op jit(solution)/shard_map/all_to_all | solution.py:169
  170.7 1.1 copy-start.9
  170.7 18.7 %copy-start.12 = (bf16[2048,1024]{1,0:T(8,128)(2,1)S(1)}, bf16[2048,1024]{1,0:T(8,128)(2,1)}, u32[]{:S(2)}) copy-start(bf16[2048,1024]{1,0:T(8,128)(2,1)} %param.22) | copy-start | bytes 12582916
  172.1 9.1 %collective-permute-start.28 = (bf16[64,2048]{1,0:T(8,128)(2,1)S(1)}, bf16[64,2048]{1,0:T(8,128)(2,1)S(1)}, u32[]{:S(2)}, u32[]{:S(2)}) collective-permute-start(bf16[64,2048]{1,0:T(8,128)(2,1)S(1)} %get-tuple-element.105), channel_id=1, source_target_pairs={{0,32},{32,64},{64,96},{96,0},{1,33},{33,65},{65,97},{97,1},{2,34}... | collective-permute-start | bytes 786440 | tf_op jit(solution)/shard_map/ppermute | solution.py:20
  172.8 8.5 %collective-permute-start.29 = (bf16[64,2048]{1,0:T(8,128)(2,1)S(1)}, bf16[64,2048]{1,0:T(8,128)(2,1)S(1)}, u32[]{:S(2)}, u32[]{:S(2)}) collective-permute-start(bf16[64,2048]{1,0:T(8,128)(2,1)S(1)} %get-tuple-element.105), channel_id=1, source_target_pairs={{0,96},{32,0},{64,32},{96,64},{1,97},{33,1},{65,33},{97,65},{2,98}... | collective-permute-start | bytes 786440 | tf_op jit(solution)/shard_map/ppermute | solution.py:20
  181.2 8.2 %collective-permute-start.30 = (bf16[64,2048]{1,0:T(8,128)(2,1)S(1)}, bf16[64,2048]{1,0:T(8,128)(2,1)S(1)}, u32[]{:S(2)}, u32[]{:S(2)}) collective-permute-start(bf16[64,2048]{1,0:T(8,128)(2,1)S(1)} %collective-permute-done.28), channel_id=1, source_target_pairs={{0,32},{32,64},{64,96},{96,0},{1,33},{33,65},{65,97},{97,1},{2,34}... | collective-permute-start | bytes 786440 | tf_op jit(solution)/shard_map/ppermute | solution.py:20
  181.3 9.4 %copy-start.3 = (bf16[2048,1024]{1,0:T(8,128)(2,1)S(1)}, bf16[2048,1024]{1,0:T(8,128)(2,1)}, u32[]{:S(2)}) copy-start(bf16[2048,1024]{1,0:T(8,128)(2,1)} %copy-done.2) | copy-start | bytes 12582916
  181.3 10.7 %collective-permute-start.31 = (bf16[64,2048]{1,0:T(8,128)(2,1)S(1)}, bf16[64,2048]{1,0:T(8,128)(2,1)S(1)}, u32[]{:S(2)}, u32[]{:S(2)}) collective-permute-start(bf16[64,2048]{1,0:T(8,128)(2,1)S(1)} %get-tuple-element.72), channel_id=1, source_target_pairs={{0,96},{32,0},{64,32},{96,64},{1,97},{33,1},{65,33},{97,65},{2,98}... | collective-permute-start | bytes 786440 | tf_op jit(solution)/shard_map/ppermute | solution.py:20
  190.7 2.2 copy-start.1
  191.9 2.4 %copy-start.13 = (bf16[1024,2048]{1,0:T(8,128)(2,1)S(1)}, bf16[1024,2048]{1,0:T(8,128)(2,1)}, u32[]{:S(2)}) copy-start(bf16[1024,2048]{1,0:T(8,128)(2,1)} %param.24) | copy-start | bytes 12582916
  192.0 8.0 %collective-permute-start.32 = (bf16[64,2048]{1,0:T(8,128)(2,1)S(1)}, bf16[64,2048]{1,0:T(8,128)(2,1)S(1)}, u32[]{:S(2)}, u32[]{:S(2)}) collective-permute-start(bf16[64,2048]{1,0:T(8,128)(2,1)S(1)} %get-tuple-element.72), channel_id=1, source_target_pairs={{0,32},{32,64},{64,96},{96,0},{1,33},{33,65},{65,97},{97,1},{2,34}... | collective-permute-start | bytes 786440 | tf_op jit(solution)/shard_map/ppermute | solution.py:20
  195.6 8.9 %collective-permute-start.33 = (bf16[64,2048]{1,0:T(8,128)(2,1)S(1)}, bf16[64,2048]{1,0:T(8,128)(2,1)S(1)}, u32[]{:S(2)}, u32[]{:S(2)}) collective-permute-start(bf16[64,2048]{1,0:T(8,128)(2,1)S(1)} %collective-permute-done.31), channel_id=1, source_target_pairs={{0,96},{32,0},{64,32},{96,64},{1,97},{33,1},{65,33},{97,65},{2,98}... | collective-permute-start | bytes 786440 | tf_op jit(solution)/shard_map/ppermute | solution.py:20
  197.9 9.4 %collective-permute-start.34 = (bf16[64,2048]{1,0:T(8,128)(2,1)S(1)}, bf16[64,2048]{1,0:T(8,128)(2,1)S(1)}, u32[]{:S(2)}, u32[]{:S(2)}) collective-permute-start(bf16[64,2048]{1,0:T(8,128)(2,1)S(1)} %get-tuple-element.100), channel_id=1, source_target_pairs={{0,96},{32,0},{64,32},{96,64},{1,97},{33,1},{65,33},{97,65},{2,98}... | collective-permute-start | bytes 786440 | tf_op jit(solution)/shard_map/ppermute | solution.py:20
  198.0 9.4 %collective-permute-start.35 = (bf16[64,2048]{1,0:T(8,128)(2,1)S(1)}, bf16[64,2048]{1,0:T(8,128)(2,1)S(1)}, u32[]{:S(2)}, u32[]{:S(2)}) collective-permute-start(bf16[64,2048]{1,0:T(8,128)(2,1)S(1)} %get-tuple-element.99), channel_id=1, source_target_pairs={{0,32},{32,64},{64,96},{96,0},{1,33},{33,65},{65,97},{97,1},{2,34}... | collective-permute-start | bytes 786440 | tf_op jit(solution)/shard_map/ppermute | solution.py:20
  209.9 16.0 %copy-start.10 = (f32[2048]{0:T(1024)S(1)}, f32[2048]{0:T(1024)}, u32[]{:S(2)}) copy-start(f32[2048]{0:T(1024)} %param.25) | copy-start | bytes 24580
  210.0 7.9 %collective-permute-start.38 = (bf16[64,2048]{1,0:T(8,128)(2,1)S(1)}, bf16[64,2048]{1,0:T(8,128)(2,1)S(1)}, u32[]{:S(2)}, u32[]{:S(2)}) collective-permute-start(bf16[64,2048]{1,0:T(8,128)(2,1)S(1)} %get-tuple-element.98), channel_id=1, source_target_pairs={{0,32},{32,64},{64,96},{96,0},{1,33},{33,65},{65,97},{97,1},{2,34}... | collective-permute-start | bytes 786440 | tf_op jit(solution)/shard_map/ppermute | solution.py:20
  210.1 8.4 %collective-permute-start.36 = (bf16[64,2048]{1,0:T(8,128)(2,1)S(1)}, bf16[64,2048]{1,0:T(8,128)(2,1)S(1)}, u32[]{:S(2)}, u32[]{:S(2)}) collective-permute-start(bf16[64,2048]{1,0:T(8,128)(2,1)S(1)} %add_convert_fusion.4), channel_id=1, source_target_pairs={{0,96},{32,0},{64,32},{96,64},{1,97},{33,1},{65,33},{97,65},{2,98}... | collective-permute-start | bytes 786440 | tf_op jit(solution)/shard_map/ppermute | solution.py:20
  213.3 8.0 %collective-permute-start.37 = (bf16[64,2048]{1,0:T(8,128)(2,1)S(1)}, bf16[64,2048]{1,0:T(8,128)(2,1)S(1)}, u32[]{:S(2)}, u32[]{:S(2)}) collective-permute-start(bf16[64,2048]{1,0:T(8,128)(2,1)S(1)} %get-tuple-element.97), channel_id=1, source_target_pairs={{0,96},{32,0},{64,32},{96,64},{1,97},{33,1},{65,33},{97,65},{2,98}... | collective-permute-start | bytes 786440 | tf_op jit(solution)/shard_map/ppermute | solution.py:20
  218.0 7.9 %collective-permute-start.39 = (bf16[64,2048]{1,0:T(8,128)(2,1)S(1)}, bf16[64,2048]{1,0:T(8,128)(2,1)S(1)}, u32[]{:S(2)}, u32[]{:S(2)}) collective-permute-start(bf16[64,2048]{1,0:T(8,128)(2,1)S(1)} %add_convert_fusion.3), channel_id=1, source_target_pairs={{0,32},{32,64},{64,96},{96,0},{1,33},{33,65},{65,97},{97,1},{2,34}... | collective-permute-start | bytes 786440 | tf_op jit(solution)/shard_map/ppermute | solution.py:20

commit v11 on v10

--- a/solution.py
+++ b/solution.py
@@ -230,9 +230,9 @@
     sum_b = up(part[4 * count : 6 * count]) + up(prev) + up(foll)
     back_b = swap_column(down(sum_b[count:]))
     own, prev, foll, far = jnp.split(down(up(part[:wide]) + up(back)), 4)
-    via = shift(far, "z", -1)
-    foll = shift(foll, "z", 1)
-    prev = shift(down(up(prev) + up(via)), "z", -1)
+    via = shift(far, "z", 1)
+    prev = shift(prev, "z", -1)
+    foll = shift(down(up(foll) + up(via)), "z", 1)
     prev, foll, back_b, back_l = hold(prev, foll, back_b, back_l)
     sum_b = sum_b[:count] + up(back_b)
     sum_l = down(sum_l[: 2 * count] + up(back_l))

time: 228 us -> 228 us (level)
  transfers between devices with their start and end apart: 42 -> 42, of which waited for: 24 -> 25; matrix products, arithmetic and copies ran while one was open for 13% -> 13% of each run, Pallas kernels for 3% -> 3%
where the time goes in v11:
time: 228 us; the launch traced here: 227 us
  waiting for transfers between devices  107 us (47%)
  starting transfers between devices  71.6 us (31%)
  matrix products  28.3 us (12%)
  local copies, waits for them, and re-layouts  8.44 us (4%)
  Pallas kernels  6.17 us (3%)
  other arithmetic  5.35 us (2%)
    ppermute x27, waiting for transfers between devices, shift(): lax.ppermute(value, axis, [(i, (i + step) % size) for i in range(size)])  57.5 us
    ppermute x27, starting transfers between devices, shift(): lax.ppermute(value, axis, [(i, (i + step) % size) for i in range(size)])  42.3 us
    ppermute x4, waiting for transfers between devices, swap_blocks(): return lax.ppermute(value, X, [(0, 3), (3, 0), (1, 2), (2, 1)])  22.3 us
    all_to_all x2, waiting for transfers between devices, exchange(): lax.all_to_all(value, ('y', 'core'), split_axis=0, concat_axis=0, tiled=T...  18.2 us
    ppermute x4, starting transfers between devices, swap_blocks(): return lax.ppermute(value, X, [(0, 3), (3, 0), (1, 2), (2, 1)])  11 us
    all_to_all x2, starting transfers between devices, exchange(): lax.all_to_all(value, ('y', 'core'), split_axis=0, concat_axis=0, tiled=T...  9.72 us
    ppermute x6, waiting for transfers between devices, swap_column(): return lax.ppermute(value, 'xl', [(0, 1), (1, 0)])  9.03 us
    dot_general x2, matrix products, first(): jnp.dot(rows, w1, preferred_element_type=jnp.float32) + b1  8.84 us
  transfers between devices with their start and end apart: 42, of which 25 were waited for; matrix products, arithmetic and copies ran while one was open for 13% of the time, Pallas kernels for 3%

profile of v11, /device:TPU:0, one launch (start us, length us, event | category | flops | bytes accessed | tf_op | source)
XLA Modules:
  0.0 227.4 jit_solution(1749778300327295079)
XLA Ops:
  3.2 1.8 dispatch.1
  5.0 4.6 %all-to-all-start = ((bf16[8,24,2048]{2,1,0:T(8,128)(2,1)}), bf16[8,24,2048]{2,1,0:T(8,128)(2,1)S(1)}, u32[]{:S(2)}, u32[]{:S(2)}) async-start(bf16[8,24,2048]{2,1,0:T(8,128)(2,1)} %bitcast.2), calls=%async_computation | async-start | bytes 1572864 | tf_op jit(solution)/shard_map/all_to_all | solution.py:169
  10.0 2.8 %collective-permute-start.9 = (f32[512]{0:T(512)S(1)}, f32[512]{0:T(512)S(1)}, u32[]{:S(2)}, u32[]{:S(2)}) collective-permute-start(f32[512]{0:T(512)S(1)} %bitcast.46), channel_id=1, source_target_pairs={{0,3},{3,0},{1,2},{2,1},{4,7},{7,4},{5,6},{6,5},{8,11},{11,8},{9,1... | collective-permute-start | bytes 6152 | tf_op jit(solution)/shard_map/ppermute | solution.py:28
  12.8 2.0 collective-permute-done.9
  14.8 2.8 %collective-permute-start.10 = (bf16[2048,512]{1,0:T(8,128)(2,1)}, bf16[2048,512]{1,0:T(8,128)(2,1)}, u32[]{:S(2)}, u32[]{:S(2)}) collective-permute-start(bf16[2048,512]{1,0:T(8,128)(2,1)} %bitcast.48), channel_id=1, source_target_pairs={{0,3},{3,0},{1,2},{2,1},{4,7},{7,4},{5,6},{6,5},{8,11},{11,8},{9,1... | collective-permute-start | bytes 6291464 | tf_op jit(solution)/shard_map/ppermute | solution.py:28
  17.6 5.1 %all-to-all-done = bf16[8,24,2048]{2,1,0:T(8,128)(2,1)S(1)} async-done(((bf16[8,24,2048]{2,1,0:T(8,128)(2,1)}), bf16[8,24,2048]{2,1,0:T(8,128)(2,1)S(1)}, u32[]{:S(2)}, u32[]{:S(2)}) %all-to-all-start) | async-done | bytes 786464 | tf_op jit(solution)/shard_map/all_to_all | solution.py:169
  22.8 2.0 collective-permute-start.3
  24.7 2.2 collective-permute-start.4
  26.9 1.5 collective-permute-start.5
  28.7 7.1 %collective-permute-done.3 = bf16[96,2048]{1,0:T(8,128)(2,1)S(1)} collective-permute-done((bf16[96,2048]{1,0:T(8,128)(2,1)S(1)}, bf16[96,2048]{1,0:T(8,128)(2,1)S(1)}, u32[]{:S(2)}, u32[]{:S(2)}) %collective-permute-start.3) | collective-permute-done | bytes 393248 | tf_op jit(solution)/shard_map/ppermute | solution.py:20
  35.9 1.5 collective-permute-done.5
  37.3 1.5 collective-permute-start.11
  38.9 1.9 collective-permute-start.7
  40.8 6.3 %collective-permute-done.6 = bf16[96,2048]{1,0:T(8,128)(2,1)S(1)} collective-permute-done((bf16[96,2048]{1,0:T(8,128)(2,1)S(1)}, bf16[96,2048]{1,0:T(8,128)(2,1)S(1)}, u32[]{:S(2)}, u32[]{:S(2)}) %collective-permute-start.6) | collective-permute-done | bytes 393248 | tf_op jit(solution)/shard_map/ppermute | solution.py:20
  47.3 2.2 on_chip.2
  49.5 2.0 copy-done.2
  51.5 2.2 on_chip.3
  53.7 2.0 copy-done
  55.7 2.8 %collective-permute-start.14 = (bf16[512,1024]{1,0:T(8,128)(2,1)S(1)}, bf16[512,1024]{1,0:T(8,128)(2,1)S(1)}, u32[]{:S(2)}, u32[]{:S(2)}) collective-permute-start(bf16[512,1024]{1,0:T(8,128)(2,1)S(1)} %get-tuple-element.58), channel_id=1, source_target_pairs={{0,3},{3,0},{1,2},{2,1},{4,7},{7,4},{5,6},{6,5},{8,11},{11,8},{9,1... | collective-permute-start | bytes 3145736 | tf_op jit(solution)/shard_map/ppermute | solution.py:28
  58.5 3.3 %collective-permute-start.13 = (bf16[192,2048]{1,0:T(8,128)(2,1)S(1)}, bf16[192,2048]{1,0:T(8,128)(2,1)S(1)}, u32[]{:S(2)}, u32[]{:S(2)}) collective-permute-start(bf16[192,2048]{1,0:T(8,128)(2,1)S(1)} %collective-permute-done.7), channel_id=1, source_target_pairs={{0,12},{4,0},{8,4},{12,8},{1,13},{5,1},{9,5},{13,9},{2,14},{6,2},{... | collective-permute-start | bytes 2359304 | tf_op jit(solution)/shard_map/ppermute | solution.py:20
  61.9 1.8 collective-permute-done.11
  66.2 2.8 %collective-permute-start.17 = (bf16[512,1024]{1,0:T(8,128)(2,1)S(1)}, bf16[512,1024]{1,0:T(8,128)(2,1)S(1)}, u32[]{:S(2)}, u32[]{:S(2)}) collective-permute-start(bf16[512,1024]{1,0:T(8,128)(2,1)S(1)} %get-tuple-element.59), channel_id=1, source_target_pairs={{0,3},{3,0},{1,2},{2,1},{4,7},{7,4},{5,6},{6,5},{8,11},{11,8},{9,1... | collective-permute-start | bytes 3145736 | tf_op jit(solution)/shard_map/ppermute | solution.py:28
  69.1 5.9 %maximum_convert_fusion = bf16[1248,1024]{1,0:T(8,128)(2,1)S(1)} fusion(bf16[1248,2048]{1,0:T(8,128)(2,1)S(1)} %constant_dynamic-update-slice_fusion, bf16[2048,512]{1,0:T(8,128)(2,1)} %collective-permute-done.10, bf16[2048,512]{1,0:T(8,128)(2,1)S(1)} %bitcast.49, f32[1024]{0:T(1024)S(1)} %pad_maximum_fusion.22), kind=kOutput, calls=%fused_computation | convolution fusion | flops 5246713856 | bytes 11866112 | tf_op jit(solution)/shard_map/dot_general | solution.py:202
  75.0 1.6 collective-permute-done.13
  76.6 3.0 %fusion.12 = bf16[288,1024]{1,0:T(8,128)(2,1)S(1)} fusion(bf16[2048,512]{1,0:T(8,128)(2,1)} %collective-permute-done.10, bf16[2048,512]{1,0:T(8,128)(2,1)S(1)} %bitcast.50, bf16[192,2048]{1,0:T(8,128)(2,1)S(1)} %collective-permute-done.13, bf16[96,2048]{1,0:T(8,128)(2,1)S(1)} %collective-permute-done.12, f32[1024]{0:T(1024)S(1)} %pad_maximum_fusion.22), kind=kOutput, calls=%fused_computation.23 | convolution fusion | flops 1219592192 | bytes 5967872 | tf_op jit(solution)/shard_map/dot_general | solution.py:202
  79.6 7.7 %collective-permute-done.14 = bf16[512,1024]{1,0:T(8,128)(2,1)S(1)} collective-permute-done((bf16[512,1024]{1,0:T(8,128)(2,1)S(1)}, bf16[512,1024]{1,0:T(8,128)(2,1)S(1)}, u32[]{:S(2)}, u32[]{:S(2)}) %collective-permute-start.14) | collective-permute-done | bytes 1048608 | tf_op jit(solution)/shard_map/ppermute | solution.py:28
  87.3 4.3 %convolution_convert_fusion.1 = bf16[1536,1024]{1,0:T(8,128)(2,1)S(1)} fusion(bf16[512,1024]{1,0:T(8,128)(2,1)S(1)} %collective-permute-done.14, bf16[512,1024]{1,0:T(8,128)(2,1)S(1)} %get-tuple-element.58, bf16[288,1024]{1,0:T(8,128)(2,1)S(1)} %fusion.12, bf16[1248,1024]{1,0:T(8,128)(2,1)S(1)} %maximum_convert_fusion), kind=kOutput, calls=%fused_computation.3 | convolution fusion | flops 3233284096 | bytes 8388608 | tf_op jit(solution)/shard_map/dot_general | solution.py:208
  92.1 2.0 collective-permute-start.16
  94.1 2.2 collective-permute-start.15
  96.3 11.3 %collective-permute-done.17 = bf16[512,1024]{1,0:T(8,128)(2,1)S(1)} collective-permute-done((bf16[512,1024]{1,0:T(8,128)(2,1)S(1)}, bf16[512,1024]{1,0:T(8,128)(2,1)S(1)}, u32[]{:S(2)}, u32[]{:S(2)}) %collective-permute-start.17) | collective-permute-done | bytes 1048608 | tf_op jit(solution)/shard_map/ppermute | solution.py:28
  107.7 4.3 %convolution_convert_fusion = bf16[1536,1024]{1,0:T(8,128)(2,1)S(1)} fusion(bf16[512,1024]{1,0:T(8,128)(2,1)S(1)} %collective-permute-done.17, bf16[512,1024]{1,0:T(8,128)(2,1)S(1)} %get-tuple-element.59, bf16[288,1024]{1,0:T(8,128)(2,1)S(1)} %fusion.12, bf16[1248,1024]{1,0:T(8,128)(2,1)S(1)} %maximum_convert_fusion), kind=kOutput, calls=%fused_computation.2 | convolution fusion | flops 3233284096 | bytes 8388608 | tf_op jit(solution)/shard_map/dot_general | solution.py:208
  112.2 2.0 collective-permute-start.24
  114.2 2.2 collective-permute-start.23
  116.7 2.0 collective-permute-start.18
  118.7 4.9 %collective-permute-done.24 = bf16[192,1024]{1,0:T(8,128)(2,1)S(1)} collective-permute-done((bf16[192,1024]{1,0:T(8,128)(2,1)S(1)}, bf16[192,1024]{1,0:T(8,128)(2,1)S(1)}, u32[]{:S(2)}, u32[]{:S(2)}) %collective-permute-start.24) | collective-permute-done | bytes 393248 | tf_op jit(solution)/shard_map/ppermute | solution.py:20
  123.8 5.8 %collective-permute-done.19 = bf16[384,1024]{1,0:T(8,128)(2,1)S(1)} collective-permute-done((bf16[384,1024]{1,0:T(8,128)(2,1)S(1)}, bf16[384,1024]{1,0:T(8,128)(2,1)S(1)}, u32[]{:S(2)}, u32[]{:S(2)}) %collective-permute-start.19) | collective-permute-done | bytes 786464 | tf_op jit(solution)/shard_map/ppermute | solution.py:24
  129.9 2.0 collective-permute-start.21
  131.9 2.4 %collective-permute-start.20 = (bf16[96,1024]{1,0:T(8,128)(2,1)S(1)}, bf16[96,1024]{1,0:T(8,128)(2,1)S(1)}, u32[]{:S(2)}, u32[]{:S(2)}) collective-permute-start(bf16[96,1024]{1,0:T(8,128)(2,1)S(1)} %get-tuple-element.102), channel_id=1, source_target_pairs={{0,12},{4,0},{8,4},{12,8},{1,13},{5,1},{9,5},{13,9},{2,14},{6,2},{... | collective-permute-start | bytes 589832 | tf_op jit(solution)/shard_map/ppermute | solution.py:20
  135.0 2.3 collective-permute-start.26
  137.3 4.8 %collective-permute-done.18 = bf16[384,1024]{1,0:T(8,128)(2,1)S(1)} collective-permute-done((bf16[384,1024]{1,0:T(8,128)(2,1)S(1)}, bf16[384,1024]{1,0:T(8,128)(2,1)S(1)}, u32[]{:S(2)}, u32[]{:S(2)}) %collective-permute-start.18) | collective-permute-done | bytes 786464 | tf_op jit(solution)/shard_map/ppermute | solution.py:20
  142.5 1.8 collective-permute-start.27
  144.4 1.8 collective-permute-start.22
  146.2 5.4 %collective-permute-done.22 = bf16[96,1024]{1,0:T(8,128)(2,1)S(1)} collective-permute-done((bf16[96,1024]{1,0:T(8,128)(2,1)S(1)}, bf16[96,1024]{1,0:T(8,128)(2,1)S(1)}, u32[]{:S(2)}, u32[]{:S(2)}) %collective-permute-start.22) | collective-permute-done | bytes 196640 | tf_op jit(solution)/shard_map/ppermute | solution.py:20
  152.9 5.2 %all-to-all-start.1 = ((bf16[8,24,2048]{2,1,0:T(8,128)(2,1)}), bf16[8,24,2048]{2,1,0:T(8,128)(2,1)S(1)}, u32[]{:S(2)}, u32[]{:S(2)}) async-start(bf16[8,24,2048]{2,1,0:T(8,128)(2,1)} %bitcast.8), calls=%async_computation.1 | async-start | bytes 1572864 | tf_op jit(solution)/shard_map/all_to_all | solution.py:169
  158.1 13.1 %all-to-all-done.1 = bf16[8,24,2048]{2,1,0:T(8,128)(2,1)S(1)} async-done(((bf16[8,24,2048]{2,1,0:T(8,128)(2,1)}), bf16[8,24,2048]{2,1,0:T(8,128)(2,1)S(1)}, u32[]{:S(2)}, u32[]{:S(2)}) %all-to-all-start.1) | async-done | bytes 786464 | tf_op jit(solution)/shard_map/all_to_all | solution.py:169
  173.2 2.7 %collective-permute-start.29 = (bf16[64,2048]{1,0:T(8,128)(2,1)S(1)}, bf16[64,2048]{1,0:T(8,128)(2,1)S(1)}, u32[]{:S(2)}, u32[]{:S(2)}) collective-permute-start(bf16[64,2048]{1,0:T(8,128)(2,1)S(1)} %get-tuple-element.105), channel_id=1, source_target_pairs={{0,96},{32,0},{64,32},{96,64},{1,97},{33,1},{65,33},{97,65},{2,98}... | collective-permute-start | bytes 786440 | tf_op jit(solution)/shard_map/ppermute | solution.py:20
  175.9 5.8 %collective-permute-done.28 = bf16[64,2048]{1,0:T(8,128)(2,1)S(1)} collective-permute-done((bf16[64,2048]{1,0:T(8,128)(2,1)S(1)}, bf16[64,2048]{1,0:T(8,128)(2,1)S(1)}, u32[]{:S(2)}, u32[]{:S(2)}) %collective-permute-start.28) | collective-permute-done | bytes 262176 | tf_op jit(solution)/shard_map/ppermute | solution.py:20
  181.7 3.2 %collective-permute-start.31 = (bf16[64,2048]{1,0:T(8,128)(2,1)S(1)}, bf16[64,2048]{1,0:T(8,128)(2,1)S(1)}, u32[]{:S(2)}, u32[]{:S(2)}) collective-permute-start(bf16[64,2048]{1,0:T(8,128)(2,1)S(1)} %get-tuple-element.72), channel_id=1, source_target_pairs={{0,96},{32,0},{64,32},{96,64},{1,97},{33,1},{65,33},{97,65},{2,98}... | collective-permute-start | bytes 786440 | tf_op jit(solution)/shard_map/ppermute | solution.py:20
  185.0 4.9 %collective-permute-done.30 = bf16[64,2048]{1,0:T(8,128)(2,1)S(1)} collective-permute-done((bf16[64,2048]{1,0:T(8,128)(2,1)S(1)}, bf16[64,2048]{1,0:T(8,128)(2,1)S(1)}, u32[]{:S(2)}, u32[]{:S(2)}) %collective-permute-start.30) | collective-permute-done | bytes 262176 | tf_op jit(solution)/shard_map/ppermute | solution.py:20
  189.9 1.2 fusion.17
  191.2 1.3 fusion.18
  194.8 1.3 fusion.1
  196.1 2.2 collective-permute-start.33
  198.5 2.0 collective-permute-start.35
  200.5 4.5 %collective-permute-done.33 = bf16[64,2048]{1,0:T(8,128)(2,1)S(1)} collective-permute-done((bf16[64,2048]{1,0:T(8,128)(2,1)S(1)}, bf16[64,2048]{1,0:T(8,128)(2,1)S(1)}, u32[]{:S(2)}, u32[]{:S(2)}) %collective-permute-start.33) | collective-permute-done | bytes 262176 | tf_op jit(solution)/shard_map/ppermute | solution.py:20
  205.0 1.2 fusion.20
  206.3 1.3 fusion.19
  207.9 1.2 fusion.47
  209.1 1.3 fusion.2
  210.6 3.2 %collective-permute-start.36 = (bf16[64,2048]{1,0:T(8,128)(2,1)S(1)}, bf16[64,2048]{1,0:T(8,128)(2,1)S(1)}, u32[]{:S(2)}, u32[]{:S(2)}) collective-permute-start(bf16[64,2048]{1,0:T(8,128)(2,1)S(1)} %add_convert_fusion.4), channel_id=1, source_target_pairs={{0,96},{32,0},{64,32},{96,64},{1,97},{33,1},{65,33},{97,65},{2,98}... | collective-permute-start | bytes 786440 | tf_op jit(solution)/shard_map/ppermute | solution.py:20
  213.8 1.9 collective-permute-start.37
  215.7 2.7 %collective-permute-done.38 = bf16[64,2048]{1,0:T(8,128)(2,1)S(1)} collective-permute-done((bf16[64,2048]{1,0:T(8,128)(2,1)S(1)}, bf16[64,2048]{1,0:T(8,128)(2,1)S(1)}, u32[]{:S(2)}, u32[]{:S(2)}) %collective-permute-start.38) | collective-permute-done | bytes 262176 | tf_op jit(solution)/shard_map/ppermute | solution.py:20
  219.0 2.7 %collective-permute-done.37 = bf16[64,2048]{1,0:T(8,128)(2,1)S(1)} collective-permute-done((bf16[64,2048]{1,0:T(8,128)(2,1)S(1)}, bf16[64,2048]{1,0:T(8,128)(2,1)S(1)}, u32[]{:S(2)}, u32[]{:S(2)}) %collective-permute-start.37) | collective-permute-done | bytes 262176 | tf_op jit(solution)/shard_map/ppermute | solution.py:20
  221.7 4.6 %collective-permute-done.39 = bf16[64,2048]{1,0:T(8,128)(2,1)S(1)} collective-permute-done((bf16[64,2048]{1,0:T(8,128)(2,1)S(1)}, bf16[64,2048]{1,0:T(8,128)(2,1)S(1)}, u32[]{:S(2)}, u32[]{:S(2)}) %collective-permute-start.39) | collective-permute-done | bytes 262176 | tf_op jit(solution)/shard_map/ppermute | solution.py:20
  (111 shorter events, 17.6 us)
Async XLA Ops:
  0.0 10.0 %copy-start.11 = (f32[1,512]{1,0:T(1,128)S(1)}, f32[1,512]{1,0:T(1,128)}, u32[]{:S(2)}) copy-start(f32[1,512]{1,0:T(1,128)} %param.18) | copy-start | bytes 6148
  0.0 22.7 %collective-permute-start = (bf16[2048,1024]{1,0:T(8,128)(2,1)}, bf16[2048,1024]{1,0:T(8,128)(2,1)}, u32[]{:S(2)}, u32[]{:S(2)}) collective-permute-start(bf16[2048,1024]{1,0:T(8,128)(2,1)} %param.22), channel_id=1, source_target_pairs={{0,16},{16,0},{1,17},{17,1},{2,18},{18,2},{3,19},{19,3},{4,20},{20... | collective-permute-start | bytes 12582920 | tf_op jit(solution)/shard_map/ppermute | solution.py:32
  0.0 22.7 %collective-permute-start.1 = (bf16[1024,2048]{1,0:T(8,128)(2,1)}, bf16[1024,2048]{1,0:T(8,128)(2,1)}, u32[]{:S(2)}, u32[]{:S(2)}) collective-permute-start(bf16[1024,2048]{1,0:T(8,128)(2,1)} %param.24), channel_id=1, source_target_pairs={{0,16},{16,0},{1,17},{17,1},{2,18},{18,2},{3,19},{19,3},{4,20},{20... | collective-permute-start | bytes 12582920 | tf_op jit(solution)/shard_map/ppermute | solution.py:32
  1.3 1.0 copy-start.4
  2.3 0.8 copy-start.6
  3.2 6.3 %copy-start.15 = (f32[1024]{0:T(1024)S(1)}, f32[1024]{0:T(1024)}, u32[]{:S(2)}) copy-start(f32[1024]{0:T(1024)} %param.23) | copy-start | bytes 12292
  3.2 25.3 %copy-start.7 = (bf16[1,512,2048]{2,1,0:T(8,128)(2,1)S(1)}, bf16[1,512,2048]{2,1,0:T(8,128)(2,1)}, u32[]{:S(2)}) copy-start(bf16[1,512,2048]{2,1,0:T(8,128)(2,1)} %param.19) | copy-start | bytes 6291460
  5.0 17.7 %all-to-all-start = ((bf16[8,24,2048]{2,1,0:T(8,128)(2,1)}), bf16[8,24,2048]{2,1,0:T(8,128)(2,1)S(1)}, u32[]{:S(2)}, u32[]{:S(2)}) async-start(bf16[8,24,2048]{2,1,0:T(8,128)(2,1)} %bitcast.2), calls=%async_computation | async-start | bytes 1572864 | tf_op jit(solution)/shard_map/all_to_all | solution.py:169
  9.5 8.1 %collective-permute-start.2 = (f32[1024]{0:T(1024)S(1)}, f32[1024]{0:T(1024)S(1)}, u32[]{:S(2)}, u32[]{:S(2)}) collective-permute-start(f32[1024]{0:T(1024)S(1)} %copy-done.15), channel_id=1, source_target_pairs={{0,16},{16,0},{1,17},{17,1},{2,18},{18,2},{3,19},{19,3},{4,20},{20... | collective-permute-start | bytes 12296 | tf_op jit(solution)/shard_map/ppermute | solution.py:32
  10.0 4.8 %collective-permute-start.9 = (f32[512]{0:T(512)S(1)}, f32[512]{0:T(512)S(1)}, u32[]{:S(2)}, u32[]{:S(2)}) collective-permute-start(f32[512]{0:T(512)S(1)} %bitcast.46), channel_id=1, source_target_pairs={{0,3},{3,0},{1,2},{2,1},{4,7},{7,4},{5,6},{6,5},{8,11},{11,8},{9,1... | collective-permute-start | bytes 6152 | tf_op jit(solution)/shard_map/ppermute | solution.py:28
  14.8 50.1 %collective-permute-start.10 = (bf16[2048,512]{1,0:T(8,128)(2,1)}, bf16[2048,512]{1,0:T(8,128)(2,1)}, u32[]{:S(2)}, u32[]{:S(2)}) collective-permute-start(bf16[2048,512]{1,0:T(8,128)(2,1)} %bitcast.48), channel_id=1, source_target_pairs={{0,3},{3,0},{1,2},{2,1},{4,7},{7,4},{5,6},{6,5},{8,11},{11,8},{9,1... | collective-permute-start | bytes 6291464 | tf_op jit(solution)/shard_map/ppermute | solution.py:28
  22.8 13.0 %collective-permute-start.3 = (bf16[96,2048]{1,0:T(8,128)(2,1)S(1)}, bf16[96,2048]{1,0:T(8,128)(2,1)S(1)}, u32[]{:S(2)}, u32[]{:S(2)}) collective-permute-start(bf16[96,2048]{1,0:T(8,128)(2,1)S(1)} %get-tuple-element.104), channel_id=1, source_target_pairs={{0,4},{4,8},{8,12},{12,0},{1,5},{5,9},{9,13},{13,1},{2,6},{6,10},{... | collective-permute-start | bytes 1179656 | tf_op jit(solution)/shard_map/ppermute | solution.py:20
  24.7 11.0 %collective-permute-start.4 = (bf16[96,2048]{1,0:T(8,128)(2,1)S(1)}, bf16[96,2048]{1,0:T(8,128)(2,1)S(1)}, u32[]{:S(2)}, u32[]{:S(2)}) collective-permute-start(bf16[96,2048]{1,0:T(8,128)(2,1)S(1)} %get-tuple-element.104), channel_id=1, source_target_pairs={{0,12},{4,0},{8,4},{12,8},{1,13},{5,1},{9,5},{13,9},{2,14},{6,2},{... | collective-permute-start | bytes 1179656 | tf_op jit(solution)/shard_map/ppermute | solution.py:20
  26.9 10.4 %collective-permute-start.5 = (bf16[96,2048]{1,0:T(8,128)(2,1)S(1)}, bf16[96,2048]{1,0:T(8,128)(2,1)S(1)}, u32[]{:S(2)}, u32[]{:S(2)}) collective-permute-start(bf16[96,2048]{1,0:T(8,128)(2,1)S(1)} %get-tuple-element.103), channel_id=1, source_target_pairs={{0,1},{1,0},{2,3},{3,2},{4,5},{5,4},{6,7},{7,6},{8,9},{9,8},{10,11... | collective-permute-start | bytes 1179656 | tf_op jit(solution)/shard_map/ppermute | solution.py:24
  35.8 11.4 %collective-permute-start.6 = (bf16[96,2048]{1,0:T(8,128)(2,1)S(1)}, bf16[96,2048]{1,0:T(8,128)(2,1)S(1)}, u32[]{:S(2)}, u32[]{:S(2)}) collective-permute-start(bf16[96,2048]{1,0:T(8,128)(2,1)S(1)} %collective-permute-done.3), channel_id=1, source_target_pairs={{0,4},{4,8},{8,12},{12,0},{1,5},{5,9},{9,13},{13,1},{2,6},{6,10},{... | collective-permute-start | bytes 1179656 | tf_op jit(solution)/shard_map/ppermute | solution.py:20
  37.3 26.4 %collective-permute-start.11 = (bf16[288,2048]{1,0:T(8,128)(2,1)S(1)}, bf16[288,2048]{1,0:T(8,128)(2,1)S(1)}, u32[]{:S(2)}, u32[]{:S(2)}) collective-permute-start(bf16[288,2048]{1,0:T(8,128)(2,1)S(1)} %pad_maximum_fusion.12), channel_id=1, source_target_pairs={{0,1},{1,0},{2,3},{3,2},{4,5},{5,4},{6,7},{7,6},{8,9},{9,8},{10,11... | collective-permute-start | bytes 3538952 | tf_op jit(solution)/shard_map/ppermute | solution.py:24
  38.9 19.6 %collective-permute-start.7 = (bf16[192,2048]{1,0:T(8,128)(2,1)S(1)}, bf16[192,2048]{1,0:T(8,128)(2,1)S(1)}, u32[]{:S(2)}, u32[]{:S(2)}) collective-permute-start(bf16[192,2048]{1,0:T(8,128)(2,1)S(1)} %pad_maximum_fusion.15), channel_id=1, source_target_pairs={{0,12},{4,0},{8,4},{12,8},{1,13},{5,1},{9,5},{13,9},{2,14},{6,2},{... | collective-permute-start | bytes 2359304 | tf_op jit(solution)/shard_map/ppermute | solution.py:20
  47.2 19.0 %collective-permute-start.8 = (bf16[192,2048]{1,0:T(8,128)(2,1)S(1)}, bf16[192,2048]{1,0:T(8,128)(2,1)S(1)}, u32[]{:S(2)}, u32[]{:S(2)}) collective-permute-start(bf16[192,2048]{1,0:T(8,128)(2,1)S(1)} %pad_maximum_fusion.15), channel_id=1, source_target_pairs={{0,4},{4,8},{8,12},{12,0},{1,5},{5,9},{9,13},{13,1},{2,6},{6,10},{... | collective-permute-start | bytes 2359304 | tf_op jit(solution)/shard_map/ppermute | solution.py:20
  49.5 2.0 copy-start.2
  53.7 2.0 copy-start
  55.7 31.6 %collective-permute-start.14 = (bf16[512,1024]{1,0:T(8,128)(2,1)S(1)}, bf16[512,1024]{1,0:T(8,128)(2,1)S(1)}, u32[]{:S(2)}, u32[]{:S(2)}) collective-permute-start(bf16[512,1024]{1,0:T(8,128)(2,1)S(1)} %get-tuple-element.58), channel_id=1, source_target_pairs={{0,3},{3,0},{1,2},{2,1},{4,7},{7,4},{5,6},{6,5},{8,11},{11,8},{9,1... | collective-permute-start | bytes 3145736 | tf_op jit(solution)/shard_map/ppermute | solution.py:28
  58.5 18.1 %collective-permute-start.13 = (bf16[192,2048]{1,0:T(8,128)(2,1)S(1)}, bf16[192,2048]{1,0:T(8,128)(2,1)S(1)}, u32[]{:S(2)}, u32[]{:S(2)}) collective-permute-start(bf16[192,2048]{1,0:T(8,128)(2,1)S(1)} %collective-permute-done.7), channel_id=1, source_target_pairs={{0,12},{4,0},{8,4},{12,8},{1,13},{5,1},{9,5},{13,9},{2,14},{6,2},{... | collective-permute-start | bytes 2359304 | tf_op jit(solution)/shard_map/ppermute | solution.py:20
  61.9 7.2 %copy-start.14 = (bf16[1,2048,512]{2,1,0:T(8,128)(2,1)S(1)}, bf16[1,2048,512]{2,1,0:T(8,128)(2,1)}, u32[]{:S(2)}) copy-start(bf16[1,2048,512]{2,1,0:T(8,128)(2,1)} %param.17) | copy-start | bytes 6291460
  64.9 11.7 %collective-permute-start.12 = (bf16[96,2048]{1,0:T(8,128)(2,1)S(1)}, bf16[96,2048]{1,0:T(8,128)(2,1)S(1)}, u32[]{:S(2)}, u32[]{:S(2)}) collective-permute-start(bf16[96,2048]{1,0:T(8,128)(2,1)S(1)} %collective-permute-done.6), channel_id=1, source_target_pairs={{0,1},{1,0},{2,3},{3,2},{4,5},{5,4},{6,7},{7,6},{8,9},{9,8},{10,11... | collective-permute-start | bytes 1179656 | tf_op jit(solution)/shard_map/ppermute | solution.py:24
  66.2 41.5 %collective-permute-start.17 = (bf16[512,1024]{1,0:T(8,128)(2,1)S(1)}, bf16[512,1024]{1,0:T(8,128)(2,1)S(1)}, u32[]{:S(2)}, u32[]{:S(2)}) collective-permute-start(bf16[512,1024]{1,0:T(8,128)(2,1)S(1)} %get-tuple-element.59), channel_id=1, source_target_pairs={{0,3},{3,0},{1,2},{2,1},{4,7},{7,4},{5,6},{6,5},{8,11},{11,8},{9,1... | collective-permute-start | bytes 3145736 | tf_op jit(solution)/shard_map/ppermute | solution.py:28
  92.1 24.3 %collective-permute-start.16 = (bf16[384,1024]{1,0:T(8,128)(2,1)S(1)}, bf16[384,1024]{1,0:T(8,128)(2,1)S(1)}, u32[]{:S(2)}, u32[]{:S(2)}) collective-permute-start(bf16[384,1024]{1,0:T(8,128)(2,1)S(1)} %pad_maximum_fusion.17), channel_id=1, source_target_pairs={{0,4},{4,8},{8,12},{12,0},{1,5},{5,9},{9,13},{13,1},{2,6},{6,10},{... | collective-permute-start | bytes 2359304 | tf_op jit(solution)/shard_map/ppermute | solution.py:20
  94.1 22.3 %collective-permute-start.15 = (bf16[384,1024]{1,0:T(8,128)(2,1)S(1)}, bf16[384,1024]{1,0:T(8,128)(2,1)S(1)}, u32[]{:S(2)}, u32[]{:S(2)}) collective-permute-start(bf16[384,1024]{1,0:T(8,128)(2,1)S(1)} %pad_maximum_fusion.16), channel_id=1, source_target_pairs={{0,12},{4,0},{8,4},{12,8},{1,13},{5,1},{9,5},{13,9},{2,14},{6,2},{... | collective-permute-start | bytes 2359304 | tf_op jit(solution)/shard_map/ppermute | solution.py:20
  112.0 17.5 %collective-permute-start.19 = (bf16[384,1024]{1,0:T(8,128)(2,1)S(1)}, bf16[384,1024]{1,0:T(8,128)(2,1)S(1)}, u32[]{:S(2)}, u32[]{:S(2)}) collective-permute-start(bf16[384,1024]{1,0:T(8,128)(2,1)S(1)} %slice.180), channel_id=1, source_target_pairs={{0,1},{1,0},{2,3},{3,2},{4,5},{5,4},{6,7},{7,6},{8,9},{9,8},{10,11... | collective-permute-start | bytes 2359304 | tf_op jit(solution)/shard_map/ppermute | solution.py:24
  112.2 11.4 %collective-permute-start.24 = (bf16[192,1024]{1,0:T(8,128)(2,1)S(1)}, bf16[192,1024]{1,0:T(8,128)(2,1)S(1)}, u32[]{:S(2)}, u32[]{:S(2)}) collective-permute-start(bf16[192,1024]{1,0:T(8,128)(2,1)S(1)} %get-tuple-element.94), channel_id=1, source_target_pairs={{0,4},{4,8},{8,12},{12,0},{1,5},{5,9},{9,13},{13,1},{2,6},{6,10},{... | collective-permute-start | bytes 1179656 | tf_op jit(solution)/shard_map/ppermute | solution.py:20
  114.2 20.2 %collective-permute-start.23 = (bf16[192,1024]{1,0:T(8,128)(2,1)S(1)}, bf16[192,1024]{1,0:T(8,128)(2,1)S(1)}, u32[]{:S(2)}, u32[]{:S(2)}) collective-permute-start(bf16[192,1024]{1,0:T(8,128)(2,1)S(1)} %get-tuple-element.93), channel_id=1, source_target_pairs={{0,12},{4,0},{8,4},{12,8},{1,13},{5,1},{9,5},{13,9},{2,14},{6,2},{... | collective-permute-start | bytes 1179656 | tf_op jit(solution)/shard_map/ppermute | solution.py:20
  116.7 25.4 %collective-permute-start.18 = (bf16[384,1024]{1,0:T(8,128)(2,1)S(1)}, bf16[384,1024]{1,0:T(8,128)(2,1)S(1)}, u32[]{:S(2)}, u32[]{:S(2)}) collective-permute-start(bf16[384,1024]{1,0:T(8,128)(2,1)S(1)} %add_convert_fusion.1), channel_id=1, source_target_pairs={{0,12},{4,0},{8,4},{12,8},{1,13},{5,1},{9,5},{13,9},{2,14},{6,2},{... | collective-permute-start | bytes 2359304 | tf_op jit(solution)/shard_map/ppermute | solution.py:20
  123.7 11.0 %collective-permute-start.25 = (bf16[192,1024]{1,0:T(8,128)(2,1)S(1)}, bf16[192,1024]{1,0:T(8,128)(2,1)S(1)}, u32[]{:S(2)}, u32[]{:S(2)}) collective-permute-start(bf16[192,1024]{1,0:T(8,128)(2,1)S(1)} %add_convert_fusion.2), channel_id=1, source_target_pairs={{0,4},{4,8},{8,12},{12,0},{1,5},{5,9},{9,13},{13,1},{2,6},{6,10},{... | collective-permute-start | bytes 1179656 | tf_op jit(solution)/shard_map/ppermute | solution.py:20
  129.9 14.4 %collective-permute-start.21 = (bf16[96,1024]{1,0:T(8,128)(2,1)S(1)}, bf16[96,1024]{1,0:T(8,128)(2,1)S(1)}, u32[]{:S(2)}, u32[]{:S(2)}) collective-permute-start(bf16[96,1024]{1,0:T(8,128)(2,1)S(1)} %get-tuple-element.101), channel_id=1, source_target_pairs={{0,4},{4,8},{8,12},{12,0},{1,5},{5,9},{9,13},{13,1},{2,6},{6,10},{... | collective-permute-start | bytes 589832 | tf_op jit(solution)/shard_map/ppermute | solution.py:20
  131.9 14.3 %collective-permute-start.20 = (bf16[96,1024]{1,0:T(8,128)(2,1)S(1)}, bf16[96,1024]{1,0:T(8,128)(2,1)S(1)}, u32[]{:S(2)}, u32[]{:S(2)}) collective-permute-start(bf16[96,1024]{1,0:T(8,128)(2,1)S(1)} %get-tuple-element.102), channel_id=1, source_target_pairs={{0,12},{4,0},{8,4},{12,8},{1,13},{5,1},{9,5},{13,9},{2,14},{6,2},{... | collective-permute-start | bytes 589832 | tf_op jit(solution)/shard_map/ppermute | solution.py:20
  135.0 11.2 %collective-permute-start.26 = (bf16[96,1024]{1,0:T(8,128)(2,1)S(1)}, bf16[96,1024]{1,0:T(8,128)(2,1)S(1)}, u32[]{:S(2)}, u32[]{:S(2)}) collective-permute-start(bf16[96,1024]{1,0:T(8,128)(2,1)S(1)} %slice.204), channel_id=1, source_target_pairs={{0,1},{1,0},{2,3},{3,2},{4,5},{5,4},{6,7},{7,6},{8,9},{9,8},{10,11... | collective-permute-start | bytes 589832 | tf_op jit(solution)/shard_map/ppermute | solution.py:24
  142.5 9.1 %collective-permute-start.27 = (bf16[192,1024]{1,0:T(8,128)(2,1)S(1)}, bf16[192,1024]{1,0:T(8,128)(2,1)S(1)}, u32[]{:S(2)}, u32[]{:S(2)}) collective-permute-start(bf16[192,1024]{1,0:T(8,128)(2,1)S(1)} %slice.203), channel_id=1, source_target_pairs={{0,1},{1,0},{2,3},{3,2},{4,5},{5,4},{6,7},{7,6},{8,9},{9,8},{10,11... | collective-permute-start | bytes 1179656 | tf_op jit(solution)/shard_map/ppermute | solution.py:24
  144.4 7.2 %collective-permute-start.22 = (bf16[96,1024]{1,0:T(8,128)(2,1)S(1)}, bf16[96,1024]{1,0:T(8,128)(2,1)S(1)}, u32[]{:S(2)}, u32[]{:S(2)}) collective-permute-start(bf16[96,1024]{1,0:T(8,128)(2,1)S(1)} %add_convert_fusion.6), channel_id=1, source_target_pairs={{0,4},{4,8},{8,12},{12,0},{1,5},{5,9},{9,13},{13,1},{2,6},{6,10},{... | collective-permute-start | bytes 589832 | tf_op jit(solution)/shard_map/ppermute | solution.py:20
  151.7 6.3 %copy-start.8 = (f32[8,2048]{1,0:T(8,128)S(1)}, f32[8,2048]{1,0:T(8,128)}, u32[]{:S(2)}) copy-start(f32[8,2048]{1,0:T(8,128)} %param.20) | copy-start | bytes 196612
  151.8 19.4 %copy-start.5 = (bf16[128,2048]{1,0:T(8,128)(2,1)S(1)}, bf16[128,2048]{1,0:T(8,128)(2,1)}, u32[]{:S(2)}) copy-start(bf16[128,2048]{1,0:T(8,128)(2,1)} %tokens_ref.1) | copy-start | bytes 1572868
  152.9 18.3 %all-to-all-start.1 = ((bf16[8,24,2048]{2,1,0:T(8,128)(2,1)}), bf16[8,24,2048]{2,1,0:T(8,128)(2,1)S(1)}, u32[]{:S(2)}, u32[]{:S(2)}) async-start(bf16[8,24,2048]{2,1,0:T(8,128)(2,1)} %bitcast.8), calls=%async_computation.1 | async-start | bytes 1572864 | tf_op jit(solution)/shard_map/all_to_all | solution.py:169
  171.2 1.1 copy-start.9
  171.2 18.7 %copy-start.12 = (bf16[2048,1024]{1,0:T(8,128)(2,1)S(1)}, bf16[2048,1024]{1,0:T(8,128)(2,1)}, u32[]{:S(2)}) copy-start(bf16[2048,1024]{1,0:T(8,128)(2,1)} %param.22) | copy-start | bytes 12582916
  172.6 9.1 %collective-permute-start.28 = (bf16[64,2048]{1,0:T(8,128)(2,1)S(1)}, bf16[64,2048]{1,0:T(8,128)(2,1)S(1)}, u32[]{:S(2)}, u32[]{:S(2)}) collective-permute-start(bf16[64,2048]{1,0:T(8,128)(2,1)S(1)} %get-tuple-element.105), channel_id=1, source_target_pairs={{0,32},{32,64},{64,96},{96,0},{1,33},{33,65},{65,97},{97,1},{2,34}... | collective-permute-start | bytes 786440 | tf_op jit(solution)/shard_map/ppermute | solution.py:20
  173.2 8.5 %collective-permute-start.29 = (bf16[64,2048]{1,0:T(8,128)(2,1)S(1)}, bf16[64,2048]{1,0:T(8,128)(2,1)S(1)}, u32[]{:S(2)}, u32[]{:S(2)}) collective-permute-start(bf16[64,2048]{1,0:T(8,128)(2,1)S(1)} %get-tuple-element.105), channel_id=1, source_target_pairs={{0,96},{32,0},{64,32},{96,64},{1,97},{33,1},{65,33},{97,65},{2,98}... | collective-permute-start | bytes 786440 | tf_op jit(solution)/shard_map/ppermute | solution.py:20
  181.7 8.2 %collective-permute-start.30 = (bf16[64,2048]{1,0:T(8,128)(2,1)S(1)}, bf16[64,2048]{1,0:T(8,128)(2,1)S(1)}, u32[]{:S(2)}, u32[]{:S(2)}) collective-permute-start(bf16[64,2048]{1,0:T(8,128)(2,1)S(1)} %collective-permute-done.28), channel_id=1, source_target_pairs={{0,32},{32,64},{64,96},{96,0},{1,33},{33,65},{65,97},{97,1},{2,34}... | collective-permute-start | bytes 786440 | tf_op jit(solution)/shard_map/ppermute | solution.py:20
  181.7 9.4 %copy-start.3 = (bf16[2048,1024]{1,0:T(8,128)(2,1)S(1)}, bf16[2048,1024]{1,0:T(8,128)(2,1)}, u32[]{:S(2)}) copy-start(bf16[2048,1024]{1,0:T(8,128)(2,1)} %copy-done.2) | copy-start | bytes 12582916
  181.7 10.7 %collective-permute-start.31 = (bf16[64,2048]{1,0:T(8,128)(2,1)S(1)}, bf16[64,2048]{1,0:T(8,128)(2,1)S(1)}, u32[]{:S(2)}, u32[]{:S(2)}) collective-permute-start(bf16[64,2048]{1,0:T(8,128)(2,1)S(1)} %get-tuple-element.72), channel_id=1, source_target_pairs={{0,96},{32,0},{64,32},{96,64},{1,97},{33,1},{65,33},{97,65},{2,98}... | collective-permute-start | bytes 786440 | tf_op jit(solution)/shard_map/ppermute | solution.py:20
  191.1 2.2 copy-start.1
  192.4 2.4 %copy-start.13 = (bf16[1024,2048]{1,0:T(8,128)(2,1)S(1)}, bf16[1024,2048]{1,0:T(8,128)(2,1)}, u32[]{:S(2)}) copy-start(bf16[1024,2048]{1,0:T(8,128)(2,1)} %param.24) | copy-start | bytes 12582916
  192.4 8.0 %collective-permute-start.32 = (bf16[64,2048]{1,0:T(8,128)(2,1)S(1)}, bf16[64,2048]{1,0:T(8,128)(2,1)S(1)}, u32[]{:S(2)}, u32[]{:S(2)}) collective-permute-start(bf16[64,2048]{1,0:T(8,128)(2,1)S(1)} %get-tuple-element.72), channel_id=1, source_target_pairs={{0,32},{32,64},{64,96},{96,0},{1,33},{33,65},{65,97},{97,1},{2,34}... | collective-permute-start | bytes 786440 | tf_op jit(solution)/shard_map/ppermute | solution.py:20
  196.1 8.9 %collective-permute-start.33 = (bf16[64,2048]{1,0:T(8,128)(2,1)S(1)}, bf16[64,2048]{1,0:T(8,128)(2,1)S(1)}, u32[]{:S(2)}, u32[]{:S(2)}) collective-permute-start(bf16[64,2048]{1,0:T(8,128)(2,1)S(1)} %collective-permute-done.31), channel_id=1, source_target_pairs={{0,96},{32,0},{64,32},{96,64},{1,97},{33,1},{65,33},{97,65},{2,98}... | collective-permute-start | bytes 786440 | tf_op jit(solution)/shard_map/ppermute | solution.py:20
  198.4 9.4 %collective-permute-start.34 = (bf16[64,2048]{1,0:T(8,128)(2,1)S(1)}, bf16[64,2048]{1,0:T(8,128)(2,1)S(1)}, u32[]{:S(2)}, u32[]{:S(2)}) collective-permute-start(bf16[64,2048]{1,0:T(8,128)(2,1)S(1)} %get-tuple-element.100), channel_id=1, source_target_pairs={{0,96},{32,0},{64,32},{96,64},{1,97},{33,1},{65,33},{97,65},{2,98}... | collective-permute-start | bytes 786440 | tf_op jit(solution)/shard_map/ppermute | solution.py:20
  198.5 9.4 %collective-permute-start.35 = (bf16[64,2048]{1,0:T(8,128)(2,1)S(1)}, bf16[64,2048]{1,0:T(8,128)(2,1)S(1)}, u32[]{:S(2)}, u32[]{:S(2)}) collective-permute-start(bf16[64,2048]{1,0:T(8,128)(2,1)S(1)} %get-tuple-element.99), channel_id=1, source_target_pairs={{0,32},{32,64},{64,96},{96,0},{1,33},{33,65},{65,97},{97,1},{2,34}... | collective-permute-start | bytes 786440 | tf_op jit(solution)/shard_map/ppermute | solution.py:20
  210.4 16.0 %copy-start.10 = (f32[2048]{0:T(1024)S(1)}, f32[2048]{0:T(1024)}, u32[]{:S(2)}) copy-start(f32[2048]{0:T(1024)} %param.25) | copy-start | bytes 24580
  210.5 7.9 %collective-permute-start.38 = (bf16[64,2048]{1,0:T(8,128)(2,1)S(1)}, bf16[64,2048]{1,0:T(8,128)(2,1)S(1)}, u32[]{:S(2)}, u32[]{:S(2)}) collective-permute-start(bf16[64,2048]{1,0:T(8,128)(2,1)S(1)} %get-tuple-element.98), channel_id=1, source_target_pairs={{0,32},{32,64},{64,96},{96,0},{1,33},{33,65},{65,97},{97,1},{2,34}... | collective-permute-start | bytes 786440 | tf_op jit(solution)/shard_map/ppermute | solution.py:20
  210.6 8.4 %collective-permute-start.36 = (bf16[64,2048]{1,0:T(8,128)(2,1)S(1)}, bf16[64,2048]{1,0:T(8,128)(2,1)S(1)}, u32[]{:S(2)}, u32[]{:S(2)}) collective-permute-start(bf16[64,2048]{1,0:T(8,128)(2,1)S(1)} %add_convert_fusion.4), channel_id=1, source_target_pairs={{0,96},{32,0},{64,32},{96,64},{1,97},{33,1},{65,33},{97,65},{2,98}... | collective-permute-start | bytes 786440 | tf_op jit(solution)/shard_map/ppermute | solution.py:20
  213.8 8.0 %collective-permute-start.37 = (bf16[64,2048]{1,0:T(8,128)(2,1)S(1)}, bf16[64,2048]{1,0:T(8,128)(2,1)S(1)}, u32[]{:S(2)}, u32[]{:S(2)}) collective-permute-start(bf16[64,2048]{1,0:T(8,128)(2,1)S(1)} %get-tuple-element.97), channel_id=1, source_target_pairs={{0,96},{32,0},{64,32},{96,64},{1,97},{33,1},{65,33},{97,65},{2,98}... | collective-permute-start | bytes 786440 | tf_op jit(solution)/shard_map/ppermute | solution.py:20
  218.4 7.9 %collective-permute-start.39 = (bf16[64,2048]{1,0:T(8,128)(2,1)S(1)}, bf16[64,2048]{1,0:T(8,128)(2,1)S(1)}, u32[]{:S(2)}, u32[]{:S(2)}) collective-permute-start(bf16[64,2048]{1,0:T(8,128)(2,1)S(1)} %add_convert_fusion.3), channel_id=1, source_target_pairs={{0,32},{32,64},{64,96},{96,0},{1,33},{33,65},{65,97},{97,1},{2,34}... | collective-permute-start | bytes 786440 | tf_op jit(solution)/shard_map/ppermute | solution.py:20

commit v12 on v11

--- a/solution.py
+++ b/solution.py
@@ -219,13 +219,15 @@
     foll = shift(foll, "z", 1)
     part = second(hidden, right, right_pair)
     via, foll, _ = hold(via, foll, part)
-    prev = shift(down(up(prev) + up(via)), "z", -1)
+    added = down(up(prev) + up(via))
+    prev = shift(added, "z", -1)
     sum_l = up(own) + up(prev) + up(foll)
     back_l = swap_column(down(sum_l[2 * count :]))
 
     back = swap_column(part[10 * count : 14 * count])
     via = shift(part[14 * count :], "z", 1)
-    prev = shift(part[8 * count : 10 * count], "z", -1)
+    held, _ = hold(part[8 * count : 10 * count], added)
+    prev = shift(held, "z", -1)
     foll = shift(down(up(part[6 * count : 8 * count]) + up(via)), "z", 1)
     sum_b = up(part[4 * count : 6 * count]) + up(prev) + up(foll)
     back_b = swap_column(down(sum_b[count:]))

time: 228 us -> 230 us (level)
  waiting for transfers between devices: 107 us -> 110 us
  transfers between devices with their start and end apart: 42 -> 42, of which waited for: 25 -> 26; matrix products, arithmetic and copies ran while one was open for 13% -> 13% of each run, Pallas kernels for 3% -> 3%
where the time goes in v12:
time: 230 us; the launch traced here: 229 us
  waiting for transfers between devices  110 us (48%)
  starting transfers between devices  70.2 us (31%)
  matrix products  28.3 us (12%)
  local copies, waits for them, and re-layouts  8.44 us (4%)
  Pallas kernels  6.17 us (3%)
  other arithmetic  5.34 us (2%)
    ppermute x27, waiting for transfers between devices, shift(): lax.ppermute(value, axis, [(i, (i + step) % size) for i in range(size)])  58.9 us
    ppermute x27, starting transfers between devices, shift(): lax.ppermute(value, axis, [(i, (i + step) % size) for i in range(size)])  42.3 us
    ppermute x4, waiting for transfers between devices, swap_blocks(): return lax.ppermute(value, X, [(0, 3), (3, 0), (1, 2), (2, 1)])  22.3 us
    all_to_all x2, waiting for transfers between devices, exchange(): lax.all_to_all(value, ('y', 'core'), split_axis=0, concat_axis=0, tiled=T...  18.2 us
    ppermute x4, starting transfers between devices, swap_blocks(): return lax.ppermute(value, X, [(0, 3), (3, 0), (1, 2), (2, 1)])  11 us
    ppermute x6, waiting for transfers between devices, swap_column(): return lax.ppermute(value, 'xl', [(0, 1), (1, 0)])  10.7 us
    all_to_all x2, starting transfers between devices, exchange(): lax.all_to_all(value, ('y', 'core'), split_axis=0, concat_axis=0, tiled=T...  10.2 us
    dot_general x2, matrix products, first(): jnp.dot(rows, w1, preferred_element_type=jnp.float32) + b1  8.84 us
  transfers between devices with their start and end apart: 42, of which 26 were waited for; matrix products, arithmetic and copies ran while one was open for 13% of the time, Pallas kernels for 3%

profile of v12, /device:TPU:0, one launch (start us, length us, event | category | flops | bytes accessed | tf_op | source)
XLA Modules:
  0.0 229.1 jit_solution(6273035823495439603)
XLA Ops:
  3.2 1.8 dispatch.1
  5.0 4.6 %all-to-all-start = ((bf16[8,24,2048]{2,1,0:T(8,128)(2,1)}), bf16[8,24,2048]{2,1,0:T(8,128)(2,1)S(1)}, u32[]{:S(2)}, u32[]{:S(2)}) async-start(bf16[8,24,2048]{2,1,0:T(8,128)(2,1)} %bitcast.2), calls=%async_computation | async-start | bytes 1572864 | tf_op jit(solution)/shard_map/all_to_all | solution.py:169
  10.0 2.8 %collective-permute-start.9 = (f32[512]{0:T(512)S(1)}, f32[512]{0:T(512)S(1)}, u32[]{:S(2)}, u32[]{:S(2)}) collective-permute-start(f32[512]{0:T(512)S(1)} %bitcast.46), channel_id=1, source_target_pairs={{0,3},{3,0},{1,2},{2,1},{4,7},{7,4},{5,6},{6,5},{8,11},{11,8},{9,1... | collective-permute-start | bytes 6152 | tf_op jit(solution)/shard_map/ppermute | solution.py:28
  12.8 2.0 collective-permute-done.9
  14.8 2.8 %collective-permute-start.10 = (bf16[2048,512]{1,0:T(8,128)(2,1)}, bf16[2048,512]{1,0:T(8,128)(2,1)}, u32[]{:S(2)}, u32[]{:S(2)}) collective-permute-start(bf16[2048,512]{1,0:T(8,128)(2,1)} %bitcast.48), channel_id=1, source_target_pairs={{0,3},{3,0},{1,2},{2,1},{4,7},{7,4},{5,6},{6,5},{8,11},{11,8},{9,1... | collective-permute-start | bytes 6291464 | tf_op jit(solution)/shard_map/ppermute | solution.py:28
  17.6 5.1 %all-to-all-done = bf16[8,24,2048]{2,1,0:T(8,128)(2,1)S(1)} async-done(((bf16[8,24,2048]{2,1,0:T(8,128)(2,1)}), bf16[8,24,2048]{2,1,0:T(8,128)(2,1)S(1)}, u32[]{:S(2)}, u32[]{:S(2)}) %all-to-all-start) | async-done | bytes 786464 | tf_op jit(solution)/shard_map/all_to_all | solution.py:169
  22.8 2.0 collective-permute-start.3
  24.7 2.2 collective-permute-start.4
  26.9 1.5 collective-permute-start.5
  28.7 7.1 %collective-permute-done.3 = bf16[96,2048]{1,0:T(8,128)(2,1)S(1)} collective-permute-done((bf16[96,2048]{1,0:T(8,128)(2,1)S(1)}, bf16[96,2048]{1,0:T(8,128)(2,1)S(1)}, u32[]{:S(2)}, u32[]{:S(2)}) %collective-permute-start.3) | collective-permute-done | bytes 393248 | tf_op jit(solution)/shard_map/ppermute | solution.py:20
  35.9 1.5 collective-permute-done.5
  37.3 1.5 collective-permute-start.11
  38.9 1.9 collective-permute-start.7
  40.8 6.3 %collective-permute-done.6 = bf16[96,2048]{1,0:T(8,128)(2,1)S(1)} collective-permute-done((bf16[96,2048]{1,0:T(8,128)(2,1)S(1)}, bf16[96,2048]{1,0:T(8,128)(2,1)S(1)}, u32[]{:S(2)}, u32[]{:S(2)}) %collective-permute-start.6) | collective-permute-done | bytes 393248 | tf_op jit(solution)/shard_map/ppermute | solution.py:20
  47.3 2.2 on_chip.2
  49.5 2.0 copy-done.2
  51.5 2.2 on_chip.3
  53.7 2.0 copy-done
  55.7 2.8 %collective-permute-start.14 = (bf16[512,1024]{1,0:T(8,128)(2,1)S(1)}, bf16[512,1024]{1,0:T(8,128)(2,1)S(1)}, u32[]{:S(2)}, u32[]{:S(2)}) collective-permute-start(bf16[512,1024]{1,0:T(8,128)(2,1)S(1)} %get-tuple-element.59), channel_id=1, source_target_pairs={{0,3},{3,0},{1,2},{2,1},{4,7},{7,4},{5,6},{6,5},{8,11},{11,8},{9,1... | collective-permute-start | bytes 3145736 | tf_op jit(solution)/shard_map/ppermute | solution.py:28
  58.5 3.3 %collective-permute-start.13 = (bf16[192,2048]{1,0:T(8,128)(2,1)S(1)}, bf16[192,2048]{1,0:T(8,128)(2,1)S(1)}, u32[]{:S(2)}, u32[]{:S(2)}) collective-permute-start(bf16[192,2048]{1,0:T(8,128)(2,1)S(1)} %collective-permute-done.7), channel_id=1, source_target_pairs={{0,12},{4,0},{8,4},{12,8},{1,13},{5,1},{9,5},{13,9},{2,14},{6,2},{... | collective-permute-start | bytes 2359304 | tf_op jit(solution)/shard_map/ppermute | solution.py:20
  61.9 1.8 collective-permute-done.11
  66.2 2.8 %collective-permute-start.17 = (bf16[512,1024]{1,0:T(8,128)(2,1)S(1)}, bf16[512,1024]{1,0:T(8,128)(2,1)S(1)}, u32[]{:S(2)}, u32[]{:S(2)}) collective-permute-start(bf16[512,1024]{1,0:T(8,128)(2,1)S(1)} %get-tuple-element.60), channel_id=1, source_target_pairs={{0,3},{3,0},{1,2},{2,1},{4,7},{7,4},{5,6},{6,5},{8,11},{11,8},{9,1... | collective-permute-start | bytes 3145736 | tf_op jit(solution)/shard_map/ppermute | solution.py:28
  69.1 5.9 %maximum_convert_fusion = bf16[1248,1024]{1,0:T(8,128)(2,1)S(1)} fusion(bf16[1248,2048]{1,0:T(8,128)(2,1)S(1)} %constant_dynamic-update-slice_fusion, bf16[2048,512]{1,0:T(8,128)(2,1)} %collective-permute-done.10, bf16[2048,512]{1,0:T(8,128)(2,1)S(1)} %bitcast.49, f32[1024]{0:T(1024)S(1)} %pad_maximum_fusion.22), kind=kOutput, calls=%fused_computation | convolution fusion | flops 5246713856 | bytes 11866112 | tf_op jit(solution)/shard_map/dot_general | solution.py:202
  75.0 1.6 collective-permute-done.13
  76.6 3.0 %fusion.12 = bf16[288,1024]{1,0:T(8,128)(2,1)S(1)} fusion(bf16[2048,512]{1,0:T(8,128)(2,1)} %collective-permute-done.10, bf16[2048,512]{1,0:T(8,128)(2,1)S(1)} %bitcast.50, bf16[192,2048]{1,0:T(8,128)(2,1)S(1)} %collective-permute-done.13, bf16[96,2048]{1,0:T(8,128)(2,1)S(1)} %collective-permute-done.12, f32[1024]{0:T(1024)S(1)} %pad_maximum_fusion.22), kind=kOutput, calls=%fused_computation.23 | convolution fusion | flops 1219592192 | bytes 5967872 | tf_op jit(solution)/shard_map/dot_general | solution.py:202
  79.6 7.7 %collective-permute-done.14 = bf16[512,1024]{1,0:T(8,128)(2,1)S(1)} collective-permute-done((bf16[512,1024]{1,0:T(8,128)(2,1)S(1)}, bf16[512,1024]{1,0:T(8,128)(2,1)S(1)}, u32[]{:S(2)}, u32[]{:S(2)}) %collective-permute-start.14) | collective-permute-done | bytes 1048608 | tf_op jit(solution)/shard_map/ppermute | solution.py:28
  87.3 4.3 %convolution_convert_fusion.1 = bf16[1536,1024]{1,0:T(8,128)(2,1)S(1)} fusion(bf16[512,1024]{1,0:T(8,128)(2,1)S(1)} %collective-permute-done.14, bf16[512,1024]{1,0:T(8,128)(2,1)S(1)} %get-tuple-element.59, bf16[288,1024]{1,0:T(8,128)(2,1)S(1)} %fusion.12, bf16[1248,1024]{1,0:T(8,128)(2,1)S(1)} %maximum_convert_fusion), kind=kOutput, calls=%fused_computation.3 | convolution fusion | flops 3233284096 | bytes 8388608 | tf_op jit(solution)/shard_map/dot_general | solution.py:208
  92.1 2.0 collective-permute-start.16
  94.1 2.2 collective-permute-start.15
  96.3 11.3 %collective-permute-done.17 = bf16[512,1024]{1,0:T(8,128)(2,1)S(1)} collective-permute-done((bf16[512,1024]{1,0:T(8,128)(2,1)S(1)}, bf16[512,1024]{1,0:T(8,128)(2,1)S(1)}, u32[]{:S(2)}, u32[]{:S(2)}) %collective-permute-start.17) | collective-permute-done | bytes 1048608 | tf_op jit(solution)/shard_map/ppermute | solution.py:28
  107.7 4.3 %convolution_convert_fusion = bf16[1536,1024]{1,0:T(8,128)(2,1)S(1)} fusion(bf16[512,1024]{1,0:T(8,128)(2,1)S(1)} %collective-permute-done.17, bf16[512,1024]{1,0:T(8,128)(2,1)S(1)} %get-tuple-element.60, bf16[288,1024]{1,0:T(8,128)(2,1)S(1)} %fusion.12, bf16[1248,1024]{1,0:T(8,128)(2,1)S(1)} %maximum_convert_fusion), kind=kOutput, calls=%fused_computation.2 | convolution fusion | flops 3233284096 | bytes 8388608 | tf_op jit(solution)/shard_map/dot_general | solution.py:208
  112.2 2.0 collective-permute-start.24
  114.5 2.2 collective-permute-start.18
  116.7 2.0 collective-permute-start.23
  118.7 4.9 %collective-permute-done.24 = bf16[192,1024]{1,0:T(8,128)(2,1)S(1)} collective-permute-done((bf16[192,1024]{1,0:T(8,128)(2,1)S(1)}, bf16[192,1024]{1,0:T(8,128)(2,1)S(1)}, u32[]{:S(2)}, u32[]{:S(2)}) %collective-permute-start.24) | collective-permute-done | bytes 393248 | tf_op jit(solution)/shard_map/ppermute | solution.py:20
  123.8 5.8 %collective-permute-done.19 = bf16[384,1024]{1,0:T(8,128)(2,1)S(1)} collective-permute-done((bf16[384,1024]{1,0:T(8,128)(2,1)S(1)}, bf16[384,1024]{1,0:T(8,128)(2,1)S(1)}, u32[]{:S(2)}, u32[]{:S(2)}) %collective-permute-start.19) | collective-permute-done | bytes 786464 | tf_op jit(solution)/shard_map/ppermute | solution.py:24
  129.9 2.0 collective-permute-start.21
  131.9 2.4 %collective-permute-start.20 = (bf16[96,1024]{1,0:T(8,128)(2,1)S(1)}, bf16[96,1024]{1,0:T(8,128)(2,1)S(1)}, u32[]{:S(2)}, u32[]{:S(2)}) collective-permute-start(bf16[96,1024]{1,0:T(8,128)(2,1)S(1)} %get-tuple-element.104), channel_id=1, source_target_pairs={{0,12},{4,0},{8,4},{12,8},{1,13},{5,1},{9,5},{13,9},{2,14},{6,2},{... | collective-permute-start | bytes 589832 | tf_op jit(solution)/shard_map/ppermute | solution.py:20
  134.3 8.1 %collective-permute-done.23 = bf16[192,1024]{1,0:T(8,128)(2,1)S(1)} collective-permute-done((bf16[192,1024]{1,0:T(8,128)(2,1)S(1)}, bf16[192,1024]{1,0:T(8,128)(2,1)S(1)}, u32[]{:S(2)}, u32[]{:S(2)}) %collective-permute-start.23) | collective-permute-done | bytes 393248 | tf_op jit(solution)/shard_map/ppermute | solution.py:20
  142.7 1.8 collective-permute-start.26
  145.4 1.8 collective-permute-start.22
  147.2 1.4 collective-permute-done.26
  148.6 3.9 %collective-permute-done.22 = bf16[96,1024]{1,0:T(8,128)(2,1)S(1)} collective-permute-done((bf16[96,1024]{1,0:T(8,128)(2,1)S(1)}, bf16[96,1024]{1,0:T(8,128)(2,1)S(1)}, u32[]{:S(2)}, u32[]{:S(2)}) %collective-permute-start.22) | collective-permute-done | bytes 196640 | tf_op jit(solution)/shard_map/ppermute | solution.py:20
  154.1 5.6 %all-to-all-start.1 = ((bf16[8,24,2048]{2,1,0:T(8,128)(2,1)}), bf16[8,24,2048]{2,1,0:T(8,128)(2,1)S(1)}, u32[]{:S(2)}, u32[]{:S(2)}) async-start(bf16[8,24,2048]{2,1,0:T(8,128)(2,1)} %bitcast.8), calls=%async_computation.1 | async-start | bytes 1572864 | tf_op jit(solution)/shard_map/all_to_all | solution.py:169
  159.8 13.1 %all-to-all-done.1 = bf16[8,24,2048]{2,1,0:T(8,128)(2,1)S(1)} async-done(((bf16[8,24,2048]{2,1,0:T(8,128)(2,1)}), bf16[8,24,2048]{2,1,0:T(8,128)(2,1)S(1)}, u32[]{:S(2)}, u32[]{:S(2)}) %all-to-all-start.1) | async-done | bytes 786464 | tf_op jit(solution)/shard_map/all_to_all | solution.py:169
  174.9 2.7 %collective-permute-start.29 = (bf16[64,2048]{1,0:T(8,128)(2,1)S(1)}, bf16[64,2048]{1,0:T(8,128)(2,1)S(1)}, u32[]{:S(2)}, u32[]{:S(2)}) collective-permute-start(bf16[64,2048]{1,0:T(8,128)(2,1)S(1)} %get-tuple-element.107), channel_id=1, source_target_pairs={{0,96},{32,0},{64,32},{96,64},{1,97},{33,1},{65,33},{97,65},{2,98}... | collective-permute-start | bytes 786440 | tf_op jit(solution)/shard_map/ppermute | solution.py:20
  177.6 5.8 %collective-permute-done.28 = bf16[64,2048]{1,0:T(8,128)(2,1)S(1)} collective-permute-done((bf16[64,2048]{1,0:T(8,128)(2,1)S(1)}, bf16[64,2048]{1,0:T(8,128)(2,1)S(1)}, u32[]{:S(2)}, u32[]{:S(2)}) %collective-permute-start.28) | collective-permute-done | bytes 262176 | tf_op jit(solution)/shard_map/ppermute | solution.py:20
  183.4 3.2 %collective-permute-start.31 = (bf16[64,2048]{1,0:T(8,128)(2,1)S(1)}, bf16[64,2048]{1,0:T(8,128)(2,1)S(1)}, u32[]{:S(2)}, u32[]{:S(2)}) collective-permute-start(bf16[64,2048]{1,0:T(8,128)(2,1)S(1)} %get-tuple-element.74), channel_id=1, source_target_pairs={{0,96},{32,0},{64,32},{96,64},{1,97},{33,1},{65,33},{97,65},{2,98}... | collective-permute-start | bytes 786440 | tf_op jit(solution)/shard_map/ppermute | solution.py:20
  186.6 4.9 %collective-permute-done.30 = bf16[64,2048]{1,0:T(8,128)(2,1)S(1)} collective-permute-done((bf16[64,2048]{1,0:T(8,128)(2,1)S(1)}, bf16[64,2048]{1,0:T(8,128)(2,1)S(1)}, u32[]{:S(2)}, u32[]{:S(2)}) %collective-permute-start.30) | collective-permute-done | bytes 262176 | tf_op jit(solution)/shard_map/ppermute | solution.py:20
  191.6 1.2 fusion.17
  192.8 1.3 fusion.18
  196.5 1.3 fusion.1
  197.8 2.2 collective-permute-start.33
  200.2 2.0 collective-permute-start.35
  202.2 4.5 %collective-permute-done.33 = bf16[64,2048]{1,0:T(8,128)(2,1)S(1)} collective-permute-done((bf16[64,2048]{1,0:T(8,128)(2,1)S(1)}, bf16[64,2048]{1,0:T(8,128)(2,1)S(1)}, u32[]{:S(2)}, u32[]{:S(2)}) %collective-permute-start.33) | collective-permute-done | bytes 262176 | tf_op jit(solution)/shard_map/ppermute | solution.py:20
  206.7 1.2 fusion.20
  207.9 1.3 fusion.19
  209.6 1.2 fusion.47
  210.8 1.3 fusion.2
  212.2 3.2 %collective-permute-start.36 = (bf16[64,2048]{1,0:T(8,128)(2,1)S(1)}, bf16[64,2048]{1,0:T(8,128)(2,1)S(1)}, u32[]{:S(2)}, u32[]{:S(2)}) collective-permute-start(bf16[64,2048]{1,0:T(8,128)(2,1)S(1)} %add_convert_fusion.4), channel_id=1, source_target_pairs={{0,96},{32,0},{64,32},{96,64},{1,97},{33,1},{65,33},{97,65},{2,98}... | collective-permute-start | bytes 786440 | tf_op jit(solution)/shard_map/ppermute | solution.py:20
  215.5 1.9 collective-permute-start.37
  217.4 2.7 %collective-permute-done.38 = bf16[64,2048]{1,0:T(8,128)(2,1)S(1)} collective-permute-done((bf16[64,2048]{1,0:T(8,128)(2,1)S(1)}, bf16[64,2048]{1,0:T(8,128)(2,1)S(1)}, u32[]{:S(2)}, u32[]{:S(2)}) %collective-permute-start.38) | collective-permute-done | bytes 262176 | tf_op jit(solution)/shard_map/ppermute | solution.py:20
  220.7 2.7 %collective-permute-done.37 = bf16[64,2048]{1,0:T(8,128)(2,1)S(1)} collective-permute-done((bf16[64,2048]{1,0:T(8,128)(2,1)S(1)}, bf16[64,2048]{1,0:T(8,128)(2,1)S(1)}, u32[]{:S(2)}, u32[]{:S(2)}) %collective-permute-start.37) | collective-permute-done | bytes 262176 | tf_op jit(solution)/shard_map/ppermute | solution.py:20
  223.4 4.6 %collective-permute-done.39 = bf16[64,2048]{1,0:T(8,128)(2,1)S(1)} collective-permute-done((bf16[64,2048]{1,0:T(8,128)(2,1)S(1)}, bf16[64,2048]{1,0:T(8,128)(2,1)S(1)}, u32[]{:S(2)}, u32[]{:S(2)}) %collective-permute-start.39) | collective-permute-done | bytes 262176 | tf_op jit(solution)/shard_map/ppermute | solution.py:20
  (111 shorter events, 17.8 us)
Async XLA Ops:
  0.0 10.0 %copy-start.11 = (f32[1,512]{1,0:T(1,128)S(1)}, f32[1,512]{1,0:T(1,128)}, u32[]{:S(2)}) copy-start(f32[1,512]{1,0:T(1,128)} %param.18) | copy-start | bytes 6148
  0.0 22.7 %collective-permute-start = (bf16[2048,1024]{1,0:T(8,128)(2,1)}, bf16[2048,1024]{1,0:T(8,128)(2,1)}, u32[]{:S(2)}, u32[]{:S(2)}) collective-permute-start(bf16[2048,1024]{1,0:T(8,128)(2,1)} %param.22), channel_id=1, source_target_pairs={{0,16},{16,0},{1,17},{17,1},{2,18},{18,2},{3,19},{19,3},{4,20},{20... | collective-permute-start | bytes 12582920 | tf_op jit(solution)/shard_map/ppermute | solution.py:32
  0.0 22.7 %collective-permute-start.1 = (bf16[1024,2048]{1,0:T(8,128)(2,1)}, bf16[1024,2048]{1,0:T(8,128)(2,1)}, u32[]{:S(2)}, u32[]{:S(2)}) collective-permute-start(bf16[1024,2048]{1,0:T(8,128)(2,1)} %param.24), channel_id=1, source_target_pairs={{0,16},{16,0},{1,17},{17,1},{2,18},{18,2},{3,19},{19,3},{4,20},{20... | collective-permute-start | bytes 12582920 | tf_op jit(solution)/shard_map/ppermute | solution.py:32
  1.3 1.0 copy-start.4
  2.3 0.8 copy-start.6
  3.2 6.3 %copy-start.15 = (f32[1024]{0:T(1024)S(1)}, f32[1024]{0:T(1024)}, u32[]{:S(2)}) copy-start(f32[1024]{0:T(1024)} %param.23) | copy-start | bytes 12292
  3.2 25.3 %copy-start.7 = (bf16[1,512,2048]{2,1,0:T(8,128)(2,1)S(1)}, bf16[1,512,2048]{2,1,0:T(8,128)(2,1)}, u32[]{:S(2)}) copy-start(bf16[1,512,2048]{2,1,0:T(8,128)(2,1)} %param.19) | copy-start | bytes 6291460
  5.0 17.7 %all-to-all-start = ((bf16[8,24,2048]{2,1,0:T(8,128)(2,1)}), bf16[8,24,2048]{2,1,0:T(8,128)(2,1)S(1)}, u32[]{:S(2)}, u32[]{:S(2)}) async-start(bf16[8,24,2048]{2,1,0:T(8,128)(2,1)} %bitcast.2), calls=%async_computation | async-start | bytes 1572864 | tf_op jit(solution)/shard_map/all_to_all | solution.py:169
  9.5 8.1 %collective-permute-start.2 = (f32[1024]{0:T(1024)S(1)}, f32[1024]{0:T(1024)S(1)}, u32[]{:S(2)}, u32[]{:S(2)}) collective-permute-start(f32[1024]{0:T(1024)S(1)} %copy-done.15), channel_id=1, source_target_pairs={{0,16},{16,0},{1,17},{17,1},{2,18},{18,2},{3,19},{19,3},{4,20},{20... | collective-permute-start | bytes 12296 | tf_op jit(solution)/shard_map/ppermute | solution.py:32
  10.0 4.8 %collective-permute-start.9 = (f32[512]{0:T(512)S(1)}, f32[512]{0:T(512)S(1)}, u32[]{:S(2)}, u32[]{:S(2)}) collective-permute-start(f32[512]{0:T(512)S(1)} %bitcast.46), channel_id=1, source_target_pairs={{0,3},{3,0},{1,2},{2,1},{4,7},{7,4},{5,6},{6,5},{8,11},{11,8},{9,1... | collective-permute-start | bytes 6152 | tf_op jit(solution)/shard_map/ppermute | solution.py:28
  14.8 50.1 %collective-permute-start.10 = (bf16[2048,512]{1,0:T(8,128)(2,1)}, bf16[2048,512]{1,0:T(8,128)(2,1)}, u32[]{:S(2)}, u32[]{:S(2)}) collective-permute-start(bf16[2048,512]{1,0:T(8,128)(2,1)} %bitcast.48), channel_id=1, source_target_pairs={{0,3},{3,0},{1,2},{2,1},{4,7},{7,4},{5,6},{6,5},{8,11},{11,8},{9,1... | collective-permute-start | bytes 6291464 | tf_op jit(solution)/shard_map/ppermute | solution.py:28
  22.8 13.0 %collective-permute-start.3 = (bf16[96,2048]{1,0:T(8,128)(2,1)S(1)}, bf16[96,2048]{1,0:T(8,128)(2,1)S(1)}, u32[]{:S(2)}, u32[]{:S(2)}) collective-permute-start(bf16[96,2048]{1,0:T(8,128)(2,1)S(1)} %get-tuple-element.106), channel_id=1, source_target_pairs={{0,4},{4,8},{8,12},{12,0},{1,5},{5,9},{9,13},{13,1},{2,6},{6,10},{... | collective-permute-start | bytes 1179656 | tf_op jit(solution)/shard_map/ppermute | solution.py:20
  24.7 11.0 %collective-permute-start.4 = (bf16[96,2048]{1,0:T(8,128)(2,1)S(1)}, bf16[96,2048]{1,0:T(8,128)(2,1)S(1)}, u32[]{:S(2)}, u32[]{:S(2)}) collective-permute-start(bf16[96,2048]{1,0:T(8,128)(2,1)S(1)} %get-tuple-element.106), channel_id=1, source_target_pairs={{0,12},{4,0},{8,4},{12,8},{1,13},{5,1},{9,5},{13,9},{2,14},{6,2},{... | collective-permute-start | bytes 1179656 | tf_op jit(solution)/shard_map/ppermute | solution.py:20
  26.9 10.4 %collective-permute-start.5 = (bf16[96,2048]{1,0:T(8,128)(2,1)S(1)}, bf16[96,2048]{1,0:T(8,128)(2,1)S(1)}, u32[]{:S(2)}, u32[]{:S(2)}) collective-permute-start(bf16[96,2048]{1,0:T(8,128)(2,1)S(1)} %get-tuple-element.105), channel_id=1, source_target_pairs={{0,1},{1,0},{2,3},{3,2},{4,5},{5,4},{6,7},{7,6},{8,9},{9,8},{10,11... | collective-permute-start | bytes 1179656 | tf_op jit(solution)/shard_map/ppermute | solution.py:24
  35.8 11.4 %collective-permute-start.6 = (bf16[96,2048]{1,0:T(8,128)(2,1)S(1)}, bf16[96,2048]{1,0:T(8,128)(2,1)S(1)}, u32[]{:S(2)}, u32[]{:S(2)}) collective-permute-start(bf16[96,2048]{1,0:T(8,128)(2,1)S(1)} %collective-permute-done.3), channel_id=1, source_target_pairs={{0,4},{4,8},{8,12},{12,0},{1,5},{5,9},{9,13},{13,1},{2,6},{6,10},{... | collective-permute-start | bytes 1179656 | tf_op jit(solution)/shard_map/ppermute | solution.py:20
  37.3 26.4 %collective-permute-start.11 = (bf16[288,2048]{1,0:T(8,128)(2,1)S(1)}, bf16[288,2048]{1,0:T(8,128)(2,1)S(1)}, u32[]{:S(2)}, u32[]{:S(2)}) collective-permute-start(bf16[288,2048]{1,0:T(8,128)(2,1)S(1)} %pad_maximum_fusion.12), channel_id=1, source_target_pairs={{0,1},{1,0},{2,3},{3,2},{4,5},{5,4},{6,7},{7,6},{8,9},{9,8},{10,11... | collective-permute-start | bytes 3538952 | tf_op jit(solution)/shard_map/ppermute | solution.py:24
  38.9 19.6 %collective-permute-start.7 = (bf16[192,2048]{1,0:T(8,128)(2,1)S(1)}, bf16[192,2048]{1,0:T(8,128)(2,1)S(1)}, u32[]{:S(2)}, u32[]{:S(2)}) collective-permute-start(bf16[192,2048]{1,0:T(8,128)(2,1)S(1)} %pad_maximum_fusion.15), channel_id=1, source_target_pairs={{0,12},{4,0},{8,4},{12,8},{1,13},{5,1},{9,5},{13,9},{2,14},{6,2},{... | collective-permute-start | bytes 2359304 | tf_op jit(solution)/shard_map/ppermute | solution.py:20
  47.2 19.0 %collective-permute-start.8 = (bf16[192,2048]{1,0:T(8,128)(2,1)S(1)}, bf16[192,2048]{1,0:T(8,128)(2,1)S(1)}, u32[]{:S(2)}, u32[]{:S(2)}) collective-permute-start(bf16[192,2048]{1,0:T(8,128)(2,1)S(1)} %pad_maximum_fusion.15), channel_id=1, source_target_pairs={{0,4},{4,8},{8,12},{12,0},{1,5},{5,9},{9,13},{13,1},{2,6},{6,10},{... | collective-permute-start | bytes 2359304 | tf_op jit(solution)/shard_map/ppermute | solution.py:20
  49.5 2.0 copy-start.2
  53.7 2.0 copy-start
  55.7 31.6 %collective-permute-start.14 = (bf16[512,1024]{1,0:T(8,128)(2,1)S(1)}, bf16[512,1024]{1,0:T(8,128)(2,1)S(1)}, u32[]{:S(2)}, u32[]{:S(2)}) collective-permute-start(bf16[512,1024]{1,0:T(8,128)(2,1)S(1)} %get-tuple-element.59), channel_id=1, source_target_pairs={{0,3},{3,0},{1,2},{2,1},{4,7},{7,4},{5,6},{6,5},{8,11},{11,8},{9,1... | collective-permute-start | bytes 3145736 | tf_op jit(solution)/shard_map/ppermute | solution.py:28
  58.5 18.1 %collective-permute-start.13 = (bf16[192,2048]{1,0:T(8,128)(2,1)S(1)}, bf16[192,2048]{1,0:T(8,128)(2,1)S(1)}, u32[]{:S(2)}, u32[]{:S(2)}) collective-permute-start(bf16[192,2048]{1,0:T(8,128)(2,1)S(1)} %collective-permute-done.7), channel_id=1, source_target_pairs={{0,12},{4,0},{8,4},{12,8},{1,13},{5,1},{9,5},{13,9},{2,14},{6,2},{... | collective-permute-start | bytes 2359304 | tf_op jit(solution)/shard_map/ppermute | solution.py:20
  61.9 7.2 %copy-start.14 = (bf16[1,2048,512]{2,1,0:T(8,128)(2,1)S(1)}, bf16[1,2048,512]{2,1,0:T(8,128)(2,1)}, u32[]{:S(2)}) copy-start(bf16[1,2048,512]{2,1,0:T(8,128)(2,1)} %param.17) | copy-start | bytes 6291460
  64.9 11.7 %collective-permute-start.12 = (bf16[96,2048]{1,0:T(8,128)(2,1)S(1)}, bf16[96,2048]{1,0:T(8,128)(2,1)S(1)}, u32[]{:S(2)}, u32[]{:S(2)}) collective-permute-start(bf16[96,2048]{1,0:T(8,128)(2,1)S(1)} %collective-permute-done.6), channel_id=1, source_target_pairs={{0,1},{1,0},{2,3},{3,2},{4,5},{5,4},{6,7},{7,6},{8,9},{9,8},{10,11... | collective-permute-start | bytes 1179656 | tf_op jit(solution)/shard_map/ppermute | solution.py:24
  66.2 41.5 %collective-permute-start.17 = (bf16[512,1024]{1,0:T(8,128)(2,1)S(1)}, bf16[512,1024]{1,0:T(8,128)(2,1)S(1)}, u32[]{:S(2)}, u32[]{:S(2)}) collective-permute-start(bf16[512,1024]{1,0:T(8,128)(2,1)S(1)} %get-tuple-element.60), channel_id=1, source_target_pairs={{0,3},{3,0},{1,2},{2,1},{4,7},{7,4},{5,6},{6,5},{8,11},{11,8},{9,1... | collective-permute-start | bytes 3145736 | tf_op jit(solution)/shard_map/ppermute | solution.py:28
  92.1 22.1 %collective-permute-start.16 = (bf16[384,1024]{1,0:T(8,128)(2,1)S(1)}, bf16[384,1024]{1,0:T(8,128)(2,1)S(1)}, u32[]{:S(2)}, u32[]{:S(2)}) collective-permute-start(bf16[384,1024]{1,0:T(8,128)(2,1)S(1)} %pad_maximum_fusion.17), channel_id=1, source_target_pairs={{0,4},{4,8},{8,12},{12,0},{1,5},{5,9},{9,13},{13,1},{2,6},{6,10},{... | collective-permute-start | bytes 2359304 | tf_op jit(solution)/shard_map/ppermute | solution.py:20
  94.1 20.1 %collective-permute-start.15 = (bf16[384,1024]{1,0:T(8,128)(2,1)S(1)}, bf16[384,1024]{1,0:T(8,128)(2,1)S(1)}, u32[]{:S(2)}, u32[]{:S(2)}) collective-permute-start(bf16[384,1024]{1,0:T(8,128)(2,1)S(1)} %pad_maximum_fusion.16), channel_id=1, source_target_pairs={{0,12},{4,0},{8,4},{12,8},{1,13},{5,1},{9,5},{13,9},{2,14},{6,2},{... | collective-permute-start | bytes 2359304 | tf_op jit(solution)/shard_map/ppermute | solution.py:20
  112.0 17.5 %collective-permute-start.19 = (bf16[384,1024]{1,0:T(8,128)(2,1)S(1)}, bf16[384,1024]{1,0:T(8,128)(2,1)S(1)}, u32[]{:S(2)}, u32[]{:S(2)}) collective-permute-start(bf16[384,1024]{1,0:T(8,128)(2,1)S(1)} %slice.180), channel_id=1, source_target_pairs={{0,1},{1,0},{2,3},{3,2},{4,5},{5,4},{6,7},{7,6},{8,9},{9,8},{10,11... | collective-permute-start | bytes 2359304 | tf_op jit(solution)/shard_map/ppermute | solution.py:24
  112.2 11.4 %collective-permute-start.24 = (bf16[192,1024]{1,0:T(8,128)(2,1)S(1)}, bf16[192,1024]{1,0:T(8,128)(2,1)S(1)}, u32[]{:S(2)}, u32[]{:S(2)}) collective-permute-start(bf16[192,1024]{1,0:T(8,128)(2,1)S(1)} %get-tuple-element.96), channel_id=1, source_target_pairs={{0,4},{4,8},{8,12},{12,0},{1,5},{5,9},{9,13},{13,1},{2,6},{6,10},{... | collective-permute-start | bytes 1179656 | tf_op jit(solution)/shard_map/ppermute | solution.py:20
  114.5 30.0 %collective-permute-start.18 = (bf16[384,1024]{1,0:T(8,128)(2,1)S(1)}, bf16[384,1024]{1,0:T(8,128)(2,1)S(1)}, u32[]{:S(2)}, u32[]{:S(2)}) collective-permute-start(bf16[384,1024]{1,0:T(8,128)(2,1)S(1)} %add_convert_fusion.1), channel_id=1, source_target_pairs={{0,12},{4,0},{8,4},{12,8},{1,13},{5,1},{9,5},{13,9},{2,14},{6,2},{... | collective-permute-start | bytes 2359304 | tf_op jit(solution)/shard_map/ppermute | solution.py:20
  116.7 25.7 %collective-permute-start.23 = (bf16[192,1024]{1,0:T(8,128)(2,1)S(1)}, bf16[192,1024]{1,0:T(8,128)(2,1)S(1)}, u32[]{:S(2)}, u32[]{:S(2)}) collective-permute-start(bf16[192,1024]{1,0:T(8,128)(2,1)S(1)} %get-tuple-element.63), channel_id=1, source_target_pairs={{0,12},{4,0},{8,4},{12,8},{1,13},{5,1},{9,5},{13,9},{2,14},{6,2},{... | collective-permute-start | bytes 1179656 | tf_op jit(solution)/shard_map/ppermute | solution.py:20
  123.7 18.7 %collective-permute-start.25 = (bf16[192,1024]{1,0:T(8,128)(2,1)S(1)}, bf16[192,1024]{1,0:T(8,128)(2,1)S(1)}, u32[]{:S(2)}, u32[]{:S(2)}) collective-permute-start(bf16[192,1024]{1,0:T(8,128)(2,1)S(1)} %add_convert_fusion.2), channel_id=1, source_target_pairs={{0,4},{4,8},{8,12},{12,0},{1,5},{5,9},{9,13},{13,1},{2,6},{6,10},{... | collective-permute-start | bytes 1179656 | tf_op jit(solution)/shard_map/ppermute | solution.py:20
  129.9 15.4 %collective-permute-start.21 = (bf16[96,1024]{1,0:T(8,128)(2,1)S(1)}, bf16[96,1024]{1,0:T(8,128)(2,1)S(1)}, u32[]{:S(2)}, u32[]{:S(2)}) collective-permute-start(bf16[96,1024]{1,0:T(8,128)(2,1)S(1)} %get-tuple-element.103), channel_id=1, source_target_pairs={{0,4},{4,8},{8,12},{12,0},{1,5},{5,9},{9,13},{13,1},{2,6},{6,10},{... | collective-permute-start | bytes 589832 | tf_op jit(solution)/shard_map/ppermute | solution.py:20
  131.9 15.3 %collective-permute-start.20 = (bf16[96,1024]{1,0:T(8,128)(2,1)S(1)}, bf16[96,1024]{1,0:T(8,128)(2,1)S(1)}, u32[]{:S(2)}, u32[]{:S(2)}) collective-permute-start(bf16[96,1024]{1,0:T(8,128)(2,1)S(1)} %get-tuple-element.104), channel_id=1, source_target_pairs={{0,12},{4,0},{8,4},{12,8},{1,13},{5,1},{9,5},{13,9},{2,14},{6,2},{... | collective-permute-start | bytes 589832 | tf_op jit(solution)/shard_map/ppermute | solution.py:20
  142.7 6.0 %collective-permute-start.26 = (bf16[96,1024]{1,0:T(8,128)(2,1)S(1)}, bf16[96,1024]{1,0:T(8,128)(2,1)S(1)}, u32[]{:S(2)}, u32[]{:S(2)}) collective-permute-start(bf16[96,1024]{1,0:T(8,128)(2,1)S(1)} %slice.204), channel_id=1, source_target_pairs={{0,1},{1,0},{2,3},{3,2},{4,5},{5,4},{6,7},{7,6},{8,9},{9,8},{10,11... | collective-permute-start | bytes 589832 | tf_op jit(solution)/shard_map/ppermute | solution.py:24
  145.0 7.9 %collective-permute-start.27 = (bf16[192,1024]{1,0:T(8,128)(2,1)S(1)}, bf16[192,1024]{1,0:T(8,128)(2,1)S(1)}, u32[]{:S(2)}, u32[]{:S(2)}) collective-permute-start(bf16[192,1024]{1,0:T(8,128)(2,1)S(1)} %slice.203), channel_id=1, source_target_pairs={{0,1},{1,0},{2,3},{3,2},{4,5},{5,4},{6,7},{7,6},{8,9},{9,8},{10,11... | collective-permute-start | bytes 1179656 | tf_op jit(solution)/shard_map/ppermute | solution.py:24
  145.4 7.2 %collective-permute-start.22 = (bf16[96,1024]{1,0:T(8,128)(2,1)S(1)}, bf16[96,1024]{1,0:T(8,128)(2,1)S(1)}, u32[]{:S(2)}, u32[]{:S(2)}) collective-permute-start(bf16[96,1024]{1,0:T(8,128)(2,1)S(1)} %add_convert_fusion.6), channel_id=1, source_target_pairs={{0,4},{4,8},{8,12},{12,0},{1,5},{5,9},{9,13},{13,1},{2,6},{6,10},{... | collective-permute-start | bytes 589832 | tf_op jit(solution)/shard_map/ppermute | solution.py:20
  152.9 6.8 %copy-start.8 = (f32[8,2048]{1,0:T(8,128)S(1)}, f32[8,2048]{1,0:T(8,128)}, u32[]{:S(2)}) copy-start(f32[8,2048]{1,0:T(8,128)} %param.20) | copy-start | bytes 196612
  153.0 19.9 %copy-start.5 = (bf16[128,2048]{1,0:T(8,128)(2,1)S(1)}, bf16[128,2048]{1,0:T(8,128)(2,1)}, u32[]{:S(2)}) copy-start(bf16[128,2048]{1,0:T(8,128)(2,1)} %tokens_ref.1) | copy-start | bytes 1572868
  154.1 18.8 %all-to-all-start.1 = ((bf16[8,24,2048]{2,1,0:T(8,128)(2,1)}), bf16[8,24,2048]{2,1,0:T(8,128)(2,1)S(1)}, u32[]{:S(2)}, u32[]{:S(2)}) async-start(bf16[8,24,2048]{2,1,0:T(8,128)(2,1)} %bitcast.8), calls=%async_computation.1 | async-start | bytes 1572864 | tf_op jit(solution)/shard_map/all_to_all | solution.py:169
  172.9 1.1 copy-start.9
  172.9 18.7 %copy-start.12 = (bf16[2048,1024]{1,0:T(8,128)(2,1)S(1)}, bf16[2048,1024]{1,0:T(8,128)(2,1)}, u32[]{:S(2)}) copy-start(bf16[2048,1024]{1,0:T(8,128)(2,1)} %param.22) | copy-start | bytes 12582916
  174.3 9.1 %collective-permute-start.28 = (bf16[64,2048]{1,0:T(8,128)(2,1)S(1)}, bf16[64,2048]{1,0:T(8,128)(2,1)S(1)}, u32[]{:S(2)}, u32[]{:S(2)}) collective-permute-start(bf16[64,2048]{1,0:T(8,128)(2,1)S(1)} %get-tuple-element.107), channel_id=1, source_target_pairs={{0,32},{32,64},{64,96},{96,0},{1,33},{33,65},{65,97},{97,1},{2,34}... | collective-permute-start | bytes 786440 | tf_op jit(solution)/shard_map/ppermute | solution.py:20
  174.9 8.5 %collective-permute-start.29 = (bf16[64,2048]{1,0:T(8,128)(2,1)S(1)}, bf16[64,2048]{1,0:T(8,128)(2,1)S(1)}, u32[]{:S(2)}, u32[]{:S(2)}) collective-permute-start(bf16[64,2048]{1,0:T(8,128)(2,1)S(1)} %get-tuple-element.107), channel_id=1, source_target_pairs={{0,96},{32,0},{64,32},{96,64},{1,97},{33,1},{65,33},{97,65},{2,98}... | collective-permute-start | bytes 786440 | tf_op jit(solution)/shard_map/ppermute | solution.py:20
  183.4 8.2 %collective-permute-start.30 = (bf16[64,2048]{1,0:T(8,128)(2,1)S(1)}, bf16[64,2048]{1,0:T(8,128)(2,1)S(1)}, u32[]{:S(2)}, u32[]{:S(2)}) collective-permute-start(bf16[64,2048]{1,0:T(8,128)(2,1)S(1)} %collective-permute-done.28), channel_id=1, source_target_pairs={{0,32},{32,64},{64,96},{96,0},{1,33},{33,65},{65,97},{97,1},{2,34}... | collective-permute-start | bytes 786440 | tf_op jit(solution)/shard_map/ppermute | solution.py:20
  183.4 9.4 %copy-start.3 = (bf16[2048,1024]{1,0:T(8,128)(2,1)S(1)}, bf16[2048,1024]{1,0:T(8,128)(2,1)}, u32[]{:S(2)}) copy-start(bf16[2048,1024]{1,0:T(8,128)(2,1)} %copy-done.2) | copy-start | bytes 12582916
  183.4 10.7 %collective-permute-start.31 = (bf16[64,2048]{1,0:T(8,128)(2,1)S(1)}, bf16[64,2048]{1,0:T(8,128)(2,1)S(1)}, u32[]{:S(2)}, u32[]{:S(2)}) collective-permute-start(bf16[64,2048]{1,0:T(8,128)(2,1)S(1)} %get-tuple-element.74), channel_id=1, source_target_pairs={{0,96},{32,0},{64,32},{96,64},{1,97},{33,1},{65,33},{97,65},{2,98}... | collective-permute-start | bytes 786440 | tf_op jit(solution)/shard_map/ppermute | solution.py:20
  192.8 2.2 copy-start.1
  194.1 2.4 %copy-start.13 = (bf16[1024,2048]{1,0:T(8,128)(2,1)S(1)}, bf16[1024,2048]{1,0:T(8,128)(2,1)}, u32[]{:S(2)}) copy-start(bf16[1024,2048]{1,0:T(8,128)(2,1)} %param.24) | copy-start | bytes 12582916
  194.1 8.0 %collective-permute-start.32 = (bf16[64,2048]{1,0:T(8,128)(2,1)S(1)}, bf16[64,2048]{1,0:T(8,128)(2,1)S(1)}, u32[]{:S(2)}, u32[]{:S(2)}) collective-permute-start(bf16[64,2048]{1,0:T(8,128)(2,1)S(1)} %get-tuple-element.74), channel_id=1, source_target_pairs={{0,32},{32,64},{64,96},{96,0},{1,33},{33,65},{65,97},{97,1},{2,34}... | collective-permute-start | bytes 786440 | tf_op jit(solution)/shard_map/ppermute | solution.py:20
  197.8 8.9 %collective-permute-start.33 = (bf16[64,2048]{1,0:T(8,128)(2,1)S(1)}, bf16[64,2048]{1,0:T(8,128)(2,1)S(1)}, u32[]{:S(2)}, u32[]{:S(2)}) collective-permute-start(bf16[64,2048]{1,0:T(8,128)(2,1)S(1)} %collective-permute-done.31), channel_id=1, source_target_pairs={{0,96},{32,0},{64,32},{96,64},{1,97},{33,1},{65,33},{97,65},{2,98}... | collective-permute-start | bytes 786440 | tf_op jit(solution)/shard_map/ppermute | solution.py:20
  200.1 9.4 %collective-permute-start.34 = (bf16[64,2048]{1,0:T(8,128)(2,1)S(1)}, bf16[64,2048]{1,0:T(8,128)(2,1)S(1)}, u32[]{:S(2)}, u32[]{:S(2)}) collective-permute-start(bf16[64,2048]{1,0:T(8,128)(2,1)S(1)} %get-tuple-element.102), channel_id=1, source_target_pairs={{0,96},{32,0},{64,32},{96,64},{1,97},{33,1},{65,33},{97,65},{2,98}... | collective-permute-start | bytes 786440 | tf_op jit(solution)/shard_map/ppermute | solution.py:20
  200.2 9.4 %collective-permute-start.35 = (bf16[64,2048]{1,0:T(8,128)(2,1)S(1)}, bf16[64,2048]{1,0:T(8,128)(2,1)S(1)}, u32[]{:S(2)}, u32[]{:S(2)}) collective-permute-start(bf16[64,2048]{1,0:T(8,128)(2,1)S(1)} %get-tuple-element.101), channel_id=1, source_target_pairs={{0,32},{32,64},{64,96},{96,0},{1,33},{33,65},{65,97},{97,1},{2,34}... | collective-permute-start | bytes 786440 | tf_op jit(solution)/shard_map/ppermute | solution.py:20
  212.1 16.0 %copy-start.10 = (f32[2048]{0:T(1024)S(1)}, f32[2048]{0:T(1024)}, u32[]{:S(2)}) copy-start(f32[2048]{0:T(1024)} %param.25) | copy-start | bytes 24580
  212.2 7.9 %collective-permute-start.38 = (bf16[64,2048]{1,0:T(8,128)(2,1)S(1)}, bf16[64,2048]{1,0:T(8,128)(2,1)S(1)}, u32[]{:S(2)}, u32[]{:S(2)}) collective-permute-start(bf16[64,2048]{1,0:T(8,128)(2,1)S(1)} %get-tuple-element.100), channel_id=1, source_target_pairs={{0,32},{32,64},{64,96},{96,0},{1,33},{33,65},{65,97},{97,1},{2,34}... | collective-permute-start | bytes 786440 | tf_op jit(solution)/shard_map/ppermute | solution.py:20
  212.2 8.4 %collective-permute-start.36 = (bf16[64,2048]{1,0:T(8,128)(2,1)S(1)}, bf16[64,2048]{1,0:T(8,128)(2,1)S(1)}, u32[]{:S(2)}, u32[]{:S(2)}) collective-permute-start(bf16[64,2048]{1,0:T(8,128)(2,1)S(1)} %add_convert_fusion.4), channel_id=1, source_target_pairs={{0,96},{32,0},{64,32},{96,64},{1,97},{33,1},{65,33},{97,65},{2,98}... | collective-permute-start | bytes 786440 | tf_op jit(solution)/shard_map/ppermute | solution.py:20
  215.5 8.0 %collective-permute-start.37 = (bf16[64,2048]{1,0:T(8,128)(2,1)S(1)}, bf16[64,2048]{1,0:T(8,128)(2,1)S(1)}, u32[]{:S(2)}, u32[]{:S(2)}) collective-permute-start(bf16[64,2048]{1,0:T(8,128)(2,1)S(1)} %get-tuple-element.99), channel_id=1, source_target_pairs={{0,96},{32,0},{64,32},{96,64},{1,97},{33,1},{65,33},{97,65},{2,98}... | collective-permute-start | bytes 786440 | tf_op jit(solution)/shard_map/ppermute | solution.py:20
  220.1 7.9 %collective-permute-start.39 = (bf16[64,2048]{1,0:T(8,128)(2,1)S(1)}, bf16[64,2048]{1,0:T(8,128)(2,1)S(1)}, u32[]{:S(2)}, u32[]{:S(2)}) collective-permute-start(bf16[64,2048]{1,0:T(8,128)(2,1)S(1)} %add_convert_fusion.3), channel_id=1, source_target_pairs={{0,32},{32,64},{64,96},{96,0},{1,33},{33,65},{65,97},{97,1},{2,34}... | collective-permute-start | bytes 786440 | tf_op jit(solution)/shard_map/ppermute | solution.py:20
